TPU v7x, 32 devices: a whole 2x2x4 slice. The times are simulated.
32 devices in a mesh: dp: 8 (over z, core), tensor: 4 (over y, x).
Axes of the slice: x: 2, y: 2, z: 4, core: 2. Of those that a mesh axis runs over, the one named last changes fastest.
Arguments:
- latents: bfloat16 [8, 1024, 1536], P('dp'), may hold values from -6 to 6
- context: bfloat16 [8, 130, 768], P('dp'), may hold values from -6 to 6
- cotangent: bfloat16 [8, 1024, 1536], P('dp'), may hold values from -6 to 6
- self_gain: float32 [1536], replicated, may hold values from 0.5 to 1.5
- self_query: bfloat16 [1536, 1536], P(None, 'tensor'), may hold values from -0.15625 to 0.15625
- self_key: bfloat16 [1536, 1536], P(None, 'tensor'), may hold values from -0.15625 to 0.15625
- self_value: bfloat16 [1536, 1536], P(None, 'tensor'), may hold values from -0.15625 to 0.15625
- self_output: bfloat16 [1536, 1536], P('tensor'), may hold values from -2.5 to 2.5
- cross_gain: float32 [1536], replicated, may hold values from 0.5 to 1.5
- cross_query: bfloat16 [1536, 1536], P(None, 'tensor'), may hold values from -0.15625 to 0.15625
- cross_key: bfloat16 [768, 1536], P(None, 'tensor'), may hold values from -0.21875 to 0.21875
- cross_value: bfloat16 [768, 1536], P(None, 'tensor'), may hold values from -0.21875 to 0.21875
- cross_output: bfloat16 [1536, 1536], P('tensor'), may hold values from -0.875 to 0.875
- feed_gain: float32 [1536], replicated, may hold values from 0.5 to 1.5
- feed_gate: bfloat16 [1536, 6144], P(None, 'tensor'), may hold values from -0.15625 to 0.15625
- feed_up: bfloat16 [1536, 6144], P(None, 'tensor'), may hold values from -0.15625 to 0.15625
- feed_down: bfloat16 [6144, 1536], P('tensor'), may hold values from -0.078125 to 0.078125
Outputs:
- block_out: bfloat16 [8, 1024, 1536], P('dp')
- latent_grad: float32 [8, 1024, 1536], P('dp')
- self_gain_grad: float32 [1536], P('dp')
- self_query_grad: float32 [1536, 1536], P('dp', 'tensor')
- self_key_grad: float32 [1536, 1536], P('dp', 'tensor')
- self_value_grad: float32 [1536, 1536], P('dp', 'tensor')
- self_output_grad: float32 [1536, 1536], P('tensor', 'dp')
- cross_gain_grad: float32 [1536], P('dp')
- cross_query_grad: float32 [1536, 1536], P('dp', 'tensor')
- cross_key_grad: float32 [768, 1536], P('dp', 'tensor')
- cross_value_grad: float32 [768, 1536], P('dp', 'tensor')
- cross_output_grad: float32 [1536, 1536], P('tensor', 'dp')
- feed_gain_grad: float32 [1536], P('dp')
- feed_gate_grad: float32 [1536, 6144], P('dp', 'tensor')
- feed_up_grad: float32 [1536, 6144], P('dp', 'tensor')
- feed_down_grad: float32 [6144, 1536], P('tensor', 'dp')
All inputs are finite; a program needn't handle non-finite values.
Results may differ from a plain program's by a relative error of at most 0.034.
Values may be sent and summed in bfloat16 or wider, within the bound.
A program may use at most 256 MiB of HBM per device.

v0:
```python
import jax
import jax.numpy as jnp
from jax import lax
from jax.sharding import PartitionSpec as P

HEAD_DIM = 64


norm_epsilon = 1e-05


def product(left_rows, right_rows):
    return jnp.dot(left_rows, right_rows, preferred_element_type=jnp.float32)


def outer_sum(left_rows, right_rows):
    return lax.dot_general(
        left_rows, right_rows, (((0,), (0,)), ((), ())), preferred_element_type=jnp.float32
    )


def back_product(grad_rows, weight):
    return lax.dot_general(
        grad_rows, weight, (((1,), (1,)), ((), ())), preferred_element_type=jnp.float32
    )


def normalize(values, gain_vec):
    center = values - jnp.mean(values, axis=-1, keepdims=True)
    inverse = lax.rsqrt(jnp.mean(center * center, axis=-1, keepdims=True) + norm_epsilon)
    unit_rows = center * inverse
    return (unit_rows * gain_vec, unit_rows, inverse)


def normalize_back(grad_normed, unit_rows, inverse, gain_vec):
    gain_grad = jnp.sum(grad_normed * unit_rows, axis=0)
    grad_unit = grad_normed * gain_vec
    mean_grad = jnp.mean(grad_unit, axis=-1, keepdims=True)
    mean_proj = jnp.mean(grad_unit * unit_rows, axis=-1, keepdims=True)
    return (inverse * (grad_unit - mean_grad - unit_rows * mean_proj), gain_grad)


def rotary_tables(length):
    half_dim = HEAD_DIM // 2
    frequency = 10000.0 ** (-jnp.arange(half_dim, dtype=jnp.float32) / half_dim)
    angles = jnp.arange(length, dtype=jnp.float32)[:, None] * frequency[None, :]
    return (jnp.cos(angles)[:, None, :], jnp.sin(angles)[:, None, :])


def rotate(values, cosine_table, sine_table):
    half_dim = values.shape[-1] // 2
    front_half = values[..., :half_dim]
    back_half = values[..., half_dim:]
    return jnp.concatenate(
        [
            front_half * cosine_table - back_half * sine_table,
            back_half * cosine_table + front_half * sine_table,
        ],
        axis=-1,
    )


def rotate_back(grad_rows, cosine_table, sine_table):
    half_dim = grad_rows.shape[-1] // 2
    front_half = grad_rows[..., :half_dim]
    back_half = grad_rows[..., half_dim:]
    return jnp.concatenate(
        [
            front_half * cosine_table + back_half * sine_table,
            back_half * cosine_table - front_half * sine_table,
        ],
        axis=-1,
    )


def attend_forward(queries, keys_in, values_in, score_scale):
    sequences, length, heads, head_width = queries.shape
    block_rows = 512
    block_starts = jnp.arange(length // block_rows, dtype=jnp.int32) * block_rows

    def one_block(block_start):
        query_blk = lax.dynamic_slice_in_dim(queries, block_start, block_rows, 1)
        scores = (
            jnp.einsum("sqhd,skhd->shqk", query_blk, keys_in, preferred_element_type=jnp.float32)
            * score_scale
        )
        row_max = jnp.max(scores, axis=-1, keepdims=True)
        exp_scores = jnp.exp(scores - row_max)
        exp_total = jnp.sum(exp_scores, axis=-1, keepdims=True)
        attn_weights = (exp_scores / exp_total).astype(jnp.bfloat16)
        output = jnp.einsum(
            "shqk,skhd->sqhd", attn_weights, values_in, preferred_element_type=jnp.float32
        )
        return (output, (row_max + jnp.log(exp_total))[..., 0])

    outputs, lse_blocks = lax.map(one_block, block_starts)
    outputs = jnp.moveaxis(outputs, 0, 1).reshape(sequences, length, heads, head_width)
    lse_rows = jnp.moveaxis(lse_blocks, 0, 2).reshape(sequences, heads, length)
    return (outputs, lse_rows)


def attend_backward(queries, keys_in, values_in, grad_out, lse_rows, score_scale):
    sequences, length, heads, head_width = queries.shape
    block_rows = 512
    block_starts = jnp.arange(length // block_rows, dtype=jnp.int32) * block_rows

    def one_block(carry, block_start):
        key_acc, value_acc = carry
        query_blk = lax.dynamic_slice_in_dim(queries, block_start, block_rows, 1)
        grad_blk = lax.dynamic_slice_in_dim(grad_out, block_start, block_rows, 1)
        lse_blk = lax.dynamic_slice_in_dim(lse_rows, block_start, block_rows, 2)
        scores = (
            jnp.einsum("sqhd,skhd->shqk", query_blk, keys_in, preferred_element_type=jnp.float32)
            * score_scale
        )
        attn_weights = jnp.exp(scores - lse_blk[..., None])
        grad_weights = jnp.einsum(
            "sqhd,skhd->shqk", grad_blk, values_in, preferred_element_type=jnp.float32
        )
        row_inner = jnp.sum(attn_weights * grad_weights, axis=-1, keepdims=True)
        grad_scores = (attn_weights * (grad_weights - row_inner)).astype(jnp.bfloat16)
        grad_query = (
            jnp.einsum("shqk,skhd->sqhd", grad_scores, keys_in, preferred_element_type=jnp.float32)
            * score_scale
        )
        key_acc = (
            key_acc
            + jnp.einsum(
                "shqk,sqhd->skhd", grad_scores, query_blk, preferred_element_type=jnp.float32
            )
            * score_scale
        )
        value_acc = value_acc + jnp.einsum(
            "shqk,sqhd->skhd",
            attn_weights.astype(jnp.bfloat16),
            grad_blk,
            preferred_element_type=jnp.float32,
        )
        return ((key_acc, value_acc), grad_query)

    zero_grads = jnp.zeros(keys_in.shape, jnp.float32)
    (grad_keys, grad_values), grad_blocks = lax.scan(
        one_block, (zero_grads, zero_grads), block_starts
    )
    grad_queries = jnp.moveaxis(grad_blocks, 0, 1).reshape(sequences, length, heads, head_width)
    return (grad_queries, grad_keys, grad_values)


def forward_pass(latents, context, params, tables, given):
    (
        self_gain,
        self_query,
        self_key,
        self_value,
        self_output,
        cross_gain,
        cross_query,
        cross_key,
        cross_value,
        cross_output,
        feed_gain,
        feed_gate,
        feed_up,
        feed_down,
    ) = params
    sequences, length, model_width = latents.shape
    ctx_len = context.shape[1]
    token_rows = sequences * length
    heads = self_query.shape[1] // HEAD_DIM
    score_scale = HEAD_DIM ** (-0.5)
    shape_tokens = (sequences, length, heads, HEAD_DIM)
    shape_context = (sequences, ctx_len, heads, HEAD_DIM)
    cosine_table, sine_table = tables
    stored = {}
    flat_rows = latents.reshape(token_rows, model_width).astype(jnp.float32)
    normed, stored["unit1"], stored["inverse1"] = normalize(flat_rows, self_gain)
    normed_low = normed.astype(jnp.bfloat16)
    stored["normed1"] = normed_low
    stored["queries"] = rotate(
        product(normed_low, self_query).reshape(shape_tokens), cosine_table, sine_table
    ).astype(jnp.bfloat16)
    stored["keys"] = rotate(
        product(normed_low, self_key).reshape(shape_tokens), cosine_table, sine_table
    ).astype(jnp.bfloat16)
    stored["values"] = product(normed_low, self_value).astype(jnp.bfloat16).reshape(shape_tokens)
    attn_out, stored["self_lse"] = attend_forward(
        stored["queries"], stored["keys"], stored["values"], score_scale
    )
    self_attn = attn_out.reshape(token_rows, -1).astype(jnp.bfloat16)
    stored["self_attn"] = self_attn
    if given is None:
        after1 = flat_rows + lax.psum(
            product(self_attn, self_output).astype(jnp.bfloat16), "tensor"
        ).astype(jnp.float32)
    else:
        after1 = given[0]
    stored["after1"] = after1
    normed, stored["unit2"], stored["inverse2"] = normalize(after1, cross_gain)
    normed_low = normed.astype(jnp.bfloat16)
    stored["normed2"] = normed_low
    context_rows = context.reshape(sequences * ctx_len, -1)
    stored["context"] = context_rows
    stored["cross_q"] = product(normed_low, cross_query).astype(jnp.bfloat16).reshape(shape_tokens)
    stored["cross_k"] = product(context_rows, cross_key).astype(jnp.bfloat16).reshape(shape_context)
    stored["cross_v"] = (
        product(context_rows, cross_value).astype(jnp.bfloat16).reshape(shape_context)
    )
    cross_out, stored["cross_lse"] = attend_forward(
        stored["cross_q"], stored["cross_k"], stored["cross_v"], score_scale
    )
    cross_attn = cross_out.reshape(token_rows, -1).astype(jnp.bfloat16)
    stored["cross_attn"] = cross_attn
    if given is None:
        after2 = after1 + lax.psum(
            product(cross_attn, cross_output).astype(jnp.bfloat16), "tensor"
        ).astype(jnp.float32)
    else:
        after2 = given[1]
    stored["after2"] = after2
    normed, stored["unit3"], stored["inverse3"] = normalize(after2, feed_gain)
    normed_low = normed.astype(jnp.bfloat16)
    stored["normed3"] = normed_low
    stored["gate"] = product(normed_low, feed_gate)
    stored["upper"] = product(normed_low, feed_up)
    hidden = (jax.nn.silu(stored["gate"]) * stored["upper"]).astype(jnp.bfloat16)
    stored["hidden"] = hidden
    if given is None:
        stored["result"] = after2 + lax.psum(
            product(hidden, feed_down).astype(jnp.bfloat16), "tensor"
        ).astype(jnp.float32)
    return stored


def body(
    latents,
    context,
    cotangent,
    self_gain,
    self_query,
    self_key,
    self_value,
    self_output,
    cross_gain,
    cross_query,
    cross_key,
    cross_value,
    cross_output,
    feed_gain,
    feed_gate,
    feed_up,
    feed_down,
):
    params = (
        self_gain,
        self_query,
        self_key,
        self_value,
        self_output,
        cross_gain,
        cross_query,
        cross_key,
        cross_value,
        cross_output,
        feed_gain,
        feed_gate,
        feed_up,
        feed_down,
    )
    sequences, length, model_width = latents.shape
    ctx_len = context.shape[1]
    token_rows = sequences * length
    heads = self_query.shape[1] // HEAD_DIM
    local_width = heads * HEAD_DIM
    score_scale = HEAD_DIM ** (-0.5)
    shape_tokens = (sequences, length, heads, HEAD_DIM)
    tables = rotary_tables(length)
    forward_one = forward_pass(latents, context, params, tables, None)
    block_out = forward_one["result"].reshape(latents.shape).astype(jnp.bfloat16)
    barrier_input = lax.optimization_barrier(latents)
    recomputed = forward_pass(
        barrier_input, context, params, tables, (forward_one["after1"], forward_one["after2"])
    )
    grad_final = cotangent.reshape(token_rows, model_width).astype(jnp.float32)
    grad_branch = cotangent.reshape(token_rows, model_width)
    down_grad = outer_sum(recomputed["hidden"], grad_branch)
    grad_hidden = back_product(grad_branch, feed_down)
    activation, act_pull = jax.vjp(
        lambda gate_in, up_in: jax.nn.silu(gate_in) * up_in, recomputed["gate"], recomputed["upper"]
    )
    grad_gate, grad_up = act_pull(grad_hidden)
    grad_gate = grad_gate.astype(jnp.bfloat16)
    grad_up = grad_up.astype(jnp.bfloat16)
    gate_grad = outer_sum(recomputed["normed3"], grad_gate)
    up_grad = outer_sum(recomputed["normed3"], grad_up)
    feed_partial = back_product(grad_gate, feed_gate) + back_product(grad_up, feed_up)
    grad_normed = lax.psum(feed_partial.astype(jnp.bfloat16), "tensor").astype(jnp.float32)
    grad_norm_in, feed_gain_grad = normalize_back(
        grad_normed, recomputed["unit3"], recomputed["inverse3"], feed_gain
    )
    grad_mid = grad_final + grad_norm_in
    grad_branch = grad_mid.astype(jnp.bfloat16)
    cross_out_grad = outer_sum(recomputed["cross_attn"], grad_branch)
    grad_cross = back_product(grad_branch, cross_output).astype(jnp.bfloat16).reshape(shape_tokens)
    grad_cq, grad_ck, grad_cv = attend_backward(
        recomputed["cross_q"],
        recomputed["cross_k"],
        recomputed["cross_v"],
        grad_cross,
        recomputed["cross_lse"],
        score_scale,
    )
    grad_cq = grad_cq.reshape(token_rows, local_width).astype(jnp.bfloat16)
    grad_ck = grad_ck.reshape(sequences * ctx_len, local_width).astype(jnp.bfloat16)
    grad_cv = grad_cv.reshape(sequences * ctx_len, local_width).astype(jnp.bfloat16)
    cross_query_grad = outer_sum(recomputed["normed2"], grad_cq)
    cross_key_grad = outer_sum(recomputed["context"], grad_ck)
    cross_value_grad = outer_sum(recomputed["context"], grad_cv)
    grad_normed = lax.psum(
        back_product(grad_cq, cross_query).astype(jnp.bfloat16), "tensor"
    ).astype(jnp.float32)
    grad_norm_in, cross_gain_grad = normalize_back(
        grad_normed, recomputed["unit2"], recomputed["inverse2"], cross_gain
    )
    grad_early = grad_mid + grad_norm_in
    grad_branch = grad_early.astype(jnp.bfloat16)
    self_out_grad = outer_sum(recomputed["self_attn"], grad_branch)
    grad_self = back_product(grad_branch, self_output).astype(jnp.bfloat16).reshape(shape_tokens)
    grad_rq, grad_rk, grad_rv = attend_backward(
        recomputed["queries"],
        recomputed["keys"],
        recomputed["values"],
        grad_self,
        recomputed["self_lse"],
        score_scale,
    )
    grad_query = (
        rotate_back(grad_rq, tables[0], tables[1])
        .reshape(token_rows, local_width)
        .astype(jnp.bfloat16)
    )
    grad_key = (
        rotate_back(grad_rk, tables[0], tables[1])
        .reshape(token_rows, local_width)
        .astype(jnp.bfloat16)
    )
    grad_value = grad_rv.reshape(token_rows, local_width).astype(jnp.bfloat16)
    query_grad = outer_sum(recomputed["normed1"], grad_query)
    key_grad = outer_sum(recomputed["normed1"], grad_key)
    value_grad = outer_sum(recomputed["normed1"], grad_value)
    self_partial = (
        back_product(grad_query, self_query)
        + back_product(grad_key, self_key)
        + back_product(grad_value, self_value)
    )
    grad_normed = lax.psum(self_partial.astype(jnp.bfloat16), "tensor").astype(jnp.float32)
    grad_norm_in, self_gain_grad = normalize_back(
        grad_normed, recomputed["unit1"], recomputed["inverse1"], self_gain
    )
    latent_grad = (grad_early + grad_norm_in).reshape(latents.shape)
    inner_sums = (
        lax.psum_scatter(
            query_grad.astype(jnp.bfloat16), "dp", scatter_dimension=0, tiled=True
        ).astype(jnp.float32),
        lax.psum_scatter(
            key_grad.astype(jnp.bfloat16), "dp", scatter_dimension=0, tiled=True
        ).astype(jnp.float32),
        lax.psum_scatter(
            value_grad.astype(jnp.bfloat16), "dp", scatter_dimension=0, tiled=True
        ).astype(jnp.float32),
        lax.psum_scatter(
            cross_query_grad.astype(jnp.bfloat16), "dp", scatter_dimension=0, tiled=True
        ).astype(jnp.float32),
        lax.psum_scatter(
            cross_key_grad.astype(jnp.bfloat16), "dp", scatter_dimension=0, tiled=True
        ).astype(jnp.float32),
        lax.psum_scatter(
            cross_value_grad.astype(jnp.bfloat16), "dp", scatter_dimension=0, tiled=True
        ).astype(jnp.float32),
        lax.psum_scatter(
            gate_grad.astype(jnp.bfloat16), "dp", scatter_dimension=0, tiled=True
        ).astype(jnp.float32),
        lax.psum_scatter(
            up_grad.astype(jnp.bfloat16), "dp", scatter_dimension=0, tiled=True
        ).astype(jnp.float32),
        lax.psum_scatter(
            self_gain_grad.astype(jnp.bfloat16), "dp", scatter_dimension=0, tiled=True
        ).astype(jnp.float32),
        lax.psum_scatter(
            cross_gain_grad.astype(jnp.bfloat16), "dp", scatter_dimension=0, tiled=True
        ).astype(jnp.float32),
        lax.psum_scatter(
            feed_gain_grad.astype(jnp.bfloat16), "dp", scatter_dimension=0, tiled=True
        ).astype(jnp.float32),
    )
    outer_sums = (
        lax.psum_scatter(
            self_out_grad.astype(jnp.bfloat16), "dp", scatter_dimension=1, tiled=True
        ).astype(jnp.float32),
        lax.psum_scatter(
            cross_out_grad.astype(jnp.bfloat16), "dp", scatter_dimension=1, tiled=True
        ).astype(jnp.float32),
        lax.psum_scatter(
            down_grad.astype(jnp.bfloat16), "dp", scatter_dimension=1, tiled=True
        ).astype(jnp.float32),
    )
    return (
        block_out,
        latent_grad,
        inner_sums[8],
        inner_sums[0],
        inner_sums[1],
        inner_sums[2],
        outer_sums[0],
        inner_sums[9],
        inner_sums[3],
        inner_sums[4],
        inner_sums[5],
        outer_sums[1],
        inner_sums[10],
        inner_sums[6],
        inner_sums[7],
        outer_sums[2],
    )


def solution(mesh):
    placed = (
        P("dp", None, None),
        P("dp", None, None),
        P("dp", None, None),
        P(),
        P(None, "tensor"),
        P(None, "tensor"),
        P(None, "tensor"),
        P("tensor", None),
        P(),
        P(None, "tensor"),
        P(None, "tensor"),
        P(None, "tensor"),
        P("tensor", None),
        P(),
        P(None, "tensor"),
        P(None, "tensor"),
        P("tensor", None),
    )
    return jax.shard_map(
        body,
        mesh=mesh,
        in_specs=placed,
        out_specs=(
            P("dp", None, None),
            P("dp", None, None),
            P("dp"),
            P("dp", "tensor"),
            P("dp", "tensor"),
            P("dp", "tensor"),
            P("tensor", "dp"),
            P("dp"),
            P("dp", "tensor"),
            P("dp", "tensor"),
            P("dp", "tensor"),
            P("tensor", "dp"),
            P("dp"),
            P("dp", "tensor"),
            P("dp", "tensor"),
            P("tensor", "dp"),
        ),
        check_vma=False,
    )
```

profile of v0, /device:TPU:0, one launch (start us, length us, event | category | flops | bytes accessed | tf_op | source)
XLA Modules:
  0.0 1173.4 jit_solution(17161380586421471506)
XLA Ops:
  18.0 5.0 fusion.174
  41.0 34.2 %while.74 = (s32[]{:T(128)}, bf16[2,1,512,6,64]{2,4,3,1,0:T(8,128)(2,1)S(1)}, s32[2]{0:T(128)S(1)}, bf16[1,1024,6,64]{1,3,2,0:T(8,128)(2,1)S(1)}, bf16[1,1024,6,...) while((s32[]{:T(128)}, ...), condition=%wide.region_5.6_spmd, body=%wide.region_2.5_spmd.sunk | while | flops 821036032 | bytes 27943068 | solution.py:96
  43.7 7.6 fusion.355
  51.3 6.8 fusion.356
  60.7 7.7 fusion.355
  68.4 6.8 fusion.356
  82.0 87.8 %all-reduce.11.cloned.1.call-done = bf16[1024,1536]{1,0:T(8,128)(2,1)} async-done(((bf16[1024,1536]{1,0:T(8,128)(2,1)}), bf16[1024,1536]{1,0:T(8,128)(2,1)}) %all-reduce.11.cloned.1.call-update) | async-done | bytes 3145744 | tf_op jit(solution)/shard_map/psum | solution.py:192
  179.1 12.7 %while.75 = (s32[]{:T(128)}, bf16[2,1,512,6,64]{2,4,3,1,0:T(8,128)(2,1)S(1)}, s32[2]{0:T(128)S(1)}, bf16[1,1024,6,64]{1,3,2,0:T(8,128)(2,1)S(1)}, bf16[1,130,6,6...) while((s32[]{:T(128)}, ...), condition=%wide.region_12.13_spmd, body=%wide.region_9.12_spmd.sunk | while | flops 104233088 | bytes 4796571 | solution.py:96
  196.6 87.0 %all-reduce.13.cloned.1.call-done = bf16[1024,1536]{1,0:T(8,128)(2,1)} async-done(((bf16[1024,1536]{1,0:T(8,128)(2,1)}), bf16[1024,1536]{1,0:T(8,128)(2,1)}) %all-reduce.13.cloned.1.call-update) | async-done | bytes 3145744 | tf_op jit(solution)/shard_map/psum | solution.py:214
  283.7 5.2 fusion.243
  292.5 7.1 fusion.258
  299.6 7.1 fusion.257
  306.7 13.9 %multiply_convert_fusion.2 = (bf16[1024,1536]{1,0:T(8,128)(2,1)}, bf16[1024,1536]{1,0:T(8,128)(2,1)}, bf16[1024,1536]{1,0:T(8,128)(2,1)}) fusion(f32[1024,1536]{1,0:T(8,128)} %fusion.257, f32[1024,1536]{1,0:T(8,128)} %fusion.258, bf16[1536,1536]{1,0:T(8,128)(2,1)} %param.45, bf16[1,1024,1536]{2,1,0:T(8,128)(2,1)S(1)} %copy-done.32), kind=kOutput, calls=%fused_computation.194 | convolution fusion | flops 4857004032 | bytes 29884416 | tf_op jit(solution)/shard_map/dot_general | solution.py:23
  320.6 7.1 fusion.259
  327.7 6.6 add_convert_fusion.1
  335.4 10.2 while.76
  345.6 75.8 %all-reduce.15.cloned.1.call-done = bf16[1024,1536]{1,0:T(8,128)(2,1)} async-done(((bf16[1024,1536]{1,0:T(8,128)(2,1)}), bf16[1024,1536]{1,0:T(8,128)(2,1)}) %all-reduce.15.cloned.1.call-update) | async-done | bytes 3145744 | tf_op jit(solution)/shard_map/psum | solution.py:296
  421.4 5.9 fusion.147
  435.4 14.6 %while.78 = (s32[]{:T(128)}, f32[1,130,6,64]{1,3,2,0:T(8,128)S(1)}, f32[1,130,6,64]{1,3,2,0:T(8,128)}, bf16[2,1,512,6,64]{2,4,3,1,0:T(8,128)(2,1)}, s32[2]{0:T(1...) while((s32[]{:T(128)}, f32[1,130,6,64]{1,3,2,0:T(8,128)S(1)}, ...), condition=%wide.region_26.27_spmd.clone, body=%wide.region_24.26_spmd.clone.sunk | while | flops 259228416 | bytes 24291652 | solution.py:142
  473.2 25.1 %while.77 = (s32[]{:T(128)}, bf16[2,1,512,6,64]{2,4,3,1,0:T(8,128)(2,1)}, f32[2,1,6,512]{3,2,1,0:T(8,128)}, s32[2]{0:T(128)S(1)}, bf16[1,1024,6,64]{1,3,2,0:T(8,...) while((s32[]{:T(128)}, ...), condition=%wide.region_35.36_spmd, body=%wide.region_32.35_spmd.sunk | while | flops 833614848 | bytes 47108376 | solution.py:96
  502.6 5.4 convolution_convert_fusion.8
  508.3 35.6 %all-reduce.17.cloned.1.call-done = bf16[1024,1536]{1,0:T(8,128)(2,1)} async-done(((bf16[1024,1536]{1,0:T(8,128)(2,1)}), bf16[1024,1536]{1,0:T(8,128)(2,1)}) %all-reduce.17.cloned.1.call-update) | async-done | bytes 3145744 | tf_op jit(solution)/shard_map/psum | solution.py:318
  543.8 7.6 fusion.152
  551.5 4.9 fusion.150
  561.9 5.4 fusion.226
  567.4 87.0 %while.79 = (s32[]{:T(128)}, f32[1,1024,6,64]{1,3,2,0:T(8,128)S(1)}, f32[1,1024,6,64]{1,3,2,0:T(8,128)}, f32[2,1,512,6,64]{2,0,4,3,1:T(2,128)}, s32[2]{0:T(128)S...) while((s32[]{:T(128)}, ...), condition=%wide.region_38.39_spmd.clone, body=%wide.region_36.38_spmd.clone.sunk | while | flops 2053174272 | bytes 118059312 | solution.py:142
  577.3 6.4 multiply_reduce_fusion.15
  583.7 6.4 multiply_convert_fusion.11
  595.3 15.0 %dynamic_update_slice.50 = f32[2,1,512,6,64]{2,0,4,3,1:T(2,128)} dynamic-update-slice(f32[2,1,512,6,64]{2,0,4,3,1:T(2,128)} %get-tuple-element.1083, f32[1,1,512,6,64]{2,0,4,3,1:T(1,128)} %copy.109, s32[]{:T(128)S(6)} %copy.168, s32[]{:T(128)} %constant.125.clone.1..sunk.5, s32[]{:T(128)} %constant.125.clone.1..sunk.5, s32[]{:T(128)} %constant.125.clone.1..sunk.5, s32[]{:T(128)} %constant.125.clone.1..sunk.5) | dynamic-update-slice | bytes 1572868 | tf_op jit(solution)/shard_map/while/body/jit(dynamic_update_index_in_dim)/dynamic_update_slice | solution.py:96
  621.4 6.3 multiply_reduce_fusion.15
  627.7 6.4 multiply_convert_fusion.11
  639.4 15.0 %dynamic_update_slice.50 = f32[2,1,512,6,64]{2,0,4,3,1:T(2,128)} dynamic-update-slice(f32[2,1,512,6,64]{2,0,4,3,1:T(2,128)} %get-tuple-element.1083, f32[1,1,512,6,64]{2,0,4,3,1:T(1,128)} %copy.109, s32[]{:T(128)S(6)} %copy.168, s32[]{:T(128)} %constant.125.clone.1..sunk.5, s32[]{:T(128)} %constant.125.clone.1..sunk.5, s32[]{:T(128)} %constant.125.clone.1..sunk.5, s32[]{:T(128)} %constant.125.clone.1..sunk.5) | dynamic-update-slice | bytes 1572868 | tf_op jit(solution)/shard_map/while/body/jit(dynamic_update_index_in_dim)/dynamic_update_slice | solution.py:96
  656.8 4.8 fusion.205
  671.9 4.8 fusion.202
  676.7 9.1 convolution_convert_fusion
  685.9 9.2 convolution_convert_fusion.1
  695.2 9.2 convolution_convert_fusion.2
  704.7 9.3 convolution_convert_fusion.4
  731.9 12.0 %reduce-scatter.20.cloned.1.call-done = bf16[192,384]{1,0:T(8,128)(2,1)} async-done(((bf16[1536,384]{1,0:T(8,128)(2,1)}), bf16[192,384]{1,0:T(8,128)(2,1)}) %reduce-scatter.20.cloned.1.call-update) | async-done | bytes 147472 | tf_op jit(solution)/shard_map/reduce_scatter | solution.py:367
  745.5 32.7 %reduce-scatter.16.cloned.1.call-done = bf16[192,384]{1,0:T(8,128)(2,1)} async-done(((bf16[1536,384]{1,0:T(8,128)(2,1)}), bf16[192,384]{1,0:T(8,128)(2,1)}) %reduce-scatter.16.cloned.1.call-update) | async-done | bytes 147472 | tf_op jit(solution)/shard_map/reduce_scatter | solution.py:361
  779.9 32.2 %reduce-scatter.18.cloned.1.call-done = bf16[192,384]{1,0:T(8,128)(2,1)} async-done(((bf16[1536,384]{1,0:T(8,128)(2,1)}), bf16[192,384]{1,0:T(8,128)(2,1)}) %reduce-scatter.18.cloned.1.call-update) | async-done | bytes 147472 | tf_op jit(solution)/shard_map/reduce_scatter | solution.py:364
  813.7 53.8 %reduce-scatter.32.cloned.1.call-done = bf16[1536,192]{0,1:T(8,128)(2,1)} async-done(((bf16[1536,1536]{0,1:T(8,128)(2,1)}), bf16[1536,192]{0,1:T(8,128)(2,1)}) %reduce-scatter.32.cloned.1.call-update) | async-done | bytes 589840 | tf_op jit(solution)/shard_map/reduce_scatter | solution.py:402
  869.7 53.3 %reduce-scatter.30.cloned.1.call-done = bf16[192,1536]{1,0:T(8,128)(2,1)} async-done(((bf16[1536,1536]{1,0:T(8,128)(2,1)}), bf16[192,1536]{1,0:T(8,128)(2,1)}) %reduce-scatter.30.cloned.1.call-update) | async-done | bytes 589840 | tf_op jit(solution)/shard_map/reduce_scatter | solution.py:382
  925.3 53.3 %reduce-scatter.28.cloned.1.call-done = bf16[192,1536]{1,0:T(8,128)(2,1)} async-done(((bf16[1536,1536]{1,0:T(8,128)(2,1)}), bf16[192,1536]{1,0:T(8,128)(2,1)}) %reduce-scatter.28.cloned.1.call-update) | async-done | bytes 589840 | tf_op jit(solution)/shard_map/reduce_scatter | solution.py:379
  980.8 138.4 %all-reduce.19.cloned.1.call-done = (bf16[1024,1536]{1,0:T(8,128)(2,1)}, bf16[1024,1536]{1,0:T(8,128)(2,1)}) async-done(((bf16[1024,1536]{1,0:T(8,128)(2,1)}, bf16[1024,1536]{1,0:T(8,128)(2,1)}), (bf16[1024,1536]{1,0:T(8,128)(2,1)}, bf16[1024,1536]{1,0:T(8,128)(2,1)})) %all-reduce.19.cloned.1.call-update) | async-done | bytes 6291472 | tf_op jit(solution)/shard_map/psum | solution.py:228
  1119.2 6.6 fusion.177
  1129.0 28.4 %all-reduce.3 = (bf16[1536]{0:T(1024)(128)(2,1)S(1)}, bf16[1536]{0:T(1024)(128)(2,1)S(1)}, bf16[1536]{0:T(1024)(128)(2,1)S(1)}) all-reduce(bf16[1536]{0:T(1024)(128)(2,1)S(1)} %get-tuple-element.463, bf16[1536]{0:T(1024)(128)(2,1)S(1)} %copy-done.76, bf16[1536]{0:T(1024)(128)(2,1)S(1)} %copy-done.75), channel_id=2, replica_groups=mesh['dp'=8,'tensor'=4] {'dp'}, use_global_device_ids=true, to_apply=%region_43.44.clone | all-reduce | flops 4608 | bytes 18432
  1159.3 7.4 fusion.156
  (418 shorter events, 216.8 us)
Async XLA Ops:
  7.2 26.2 %copy-start = (bf16[1536,384]{1,0:T(8,128)(2,1)S(1)}, bf16[1536,384]{1,0:T(8,128)(2,1)}, u32[]{:S(2)}) copy-start(bf16[1536,384]{1,0:T(8,128)(2,1)} %param.35) | copy-start | bytes 3538948
  7.2 162.6 %all-reduce.11.cloned.1.call-start = ((), (), s32[]{:S(2)}) async-start(), calls=%async_computation.11 | async-start | bytes 6291456 | tf_op jit(solution)/shard_map/psum | solution.py:192
  11.2 6.8 copy-start.59
  17.9 5.0 copy-start.68
  17.9 5.0 copy-start.50
  22.9 7.3 copy-start.41
  33.4 4.7 copy-start.48
  80.0 203.7 %all-reduce.13.cloned.1.call-start = ((), (), s32[]{:S(2)}) async-start(), calls=%async_computation.12 | async-start | bytes 6291456 | tf_op jit(solution)/shard_map/psum | solution.py:214
  196.6 224.9 %all-reduce.15.cloned.1.call-start = ((), (), s32[]{:S(2)}) async-start(), calls=%async_computation.13 | async-start | bytes 6291456 | tf_op jit(solution)/shard_map/psum | solution.py:296
  283.7 8.7 slice-start.4
  291.6 8.0 slice-start.2
  292.4 7.1 copy-start.43
  292.5 7.1 slice-start.3
  299.6 7.1 copy-start.32
  320.6 7.1 copy-start.88
  334.3 209.5 %all-reduce.17.cloned.1.call-start = ((), (), s32[]{:S(2)}) async-start(), calls=%async_computation.14 | async-start | bytes 6291456 | tf_op jit(solution)/shard_map/psum | solution.py:318
  345.6 81.7 %copy-start.58 = (f32[2,1,6,512]{3,2,1,0:T(8,128)}, f32[2,1,6,512]{3,2,1,0:T(8,128)S(1)}, u32[]{:S(2)}) copy-start(f32[2,1,6,512]{3,2,1,0:T(8,128)S(1)} %get-tuple-element.266) | copy-start | bytes 73732
  421.4 5.9 copy-start.19
  421.4 5.9 copy-start.33
  450.0 6.6 copy-start.85
  456.7 266.7 %reduce-scatter.36.cloned.1.call-start = ((), (), s32[]{:S(2)}) async-start(), calls=%async_computation.25 | async-start | bytes 663552
  459.1 266.1 %reduce-scatter.34.cloned.1.call-start = ((), (), s32[]{:S(2)}) async-start(), calls=%async_computation.24 | async-start | bytes 663552
  460.6 266.4 %reduce-scatter.26.cloned.1.call-start = ((), (), s32[]{:S(2)}) async-start(), calls=%async_computation.20 | async-start | bytes 1327104 | tf_op jit(solution)/shard_map/reduce_scatter | solution.py:399
  462.2 6.5 slice-start
  463.7 5.0 slice-start.1
  471.6 257.0 %reduce-scatter.24.cloned.1.call-start = ((), (), s32[]{:S(2)}) async-start(), calls=%async_computation.19 | async-start | bytes 1327104 | tf_op jit(solution)/shard_map/reduce_scatter | solution.py:370
  473.2 29.3 %copy-start.74 = (f32[1536]{0:T(1024)S(1)}, f32[1536]{0:T(1024)}, u32[]{:S(2)}) copy-start(f32[1536]{0:T(1024)} %param.37) | copy-start | bytes 18436
  508.0 222.2 %reduce-scatter.22.cloned.1.call-start = ((), (), s32[]{:S(2)}) async-start(), calls=%async_computation.18 | async-start | bytes 1327104 | tf_op jit(solution)/shard_map/reduce_scatter | solution.py:396
  543.8 7.6 copy-start.4
  543.8 7.6 copy-start.8
  543.8 7.6 copy-start.21
  551.5 7.5 copy-start.53
  561.9 5.5 copy-start.87
  567.3 176.6 %reduce-scatter.20.cloned.1.call-start = ((), (), s32[]{:S(2)}) async-start(), calls=%async_computation.17 | async-start | bytes 1327104 | tf_op jit(solution)/shard_map/reduce_scatter | solution.py:367
  616.6 4.7 copy-start.14
  661.6 116.7 %reduce-scatter.16.cloned.1.call-start = ((), (), s32[]{:S(2)}) async-start(), calls=%async_computation.15 | async-start | bytes 1327104 | tf_op jit(solution)/shard_map/reduce_scatter | solution.py:361
  670.9 141.2 %reduce-scatter.18.cloned.1.call-start = ((), (), s32[]{:S(2)}) async-start(), calls=%async_computation.16 | async-start | bytes 1327104 | tf_op jit(solution)/shard_map/reduce_scatter | solution.py:364
  676.6 190.9 %reduce-scatter.32.cloned.1.call-start = ((), (), s32[]{:S(2)}) async-start(), calls=%async_computation.23 | async-start | bytes 5308416 | tf_op jit(solution)/shard_map/reduce_scatter | solution.py:402
  685.8 237.2 %reduce-scatter.30.cloned.1.call-start = ((), (), s32[]{:S(2)}) async-start(), calls=%async_computation.22 | async-start | bytes 5308416 | tf_op jit(solution)/shard_map/reduce_scatter | solution.py:382
  695.1 283.5 %reduce-scatter.28.cloned.1.call-start = ((), (), s32[]{:S(2)}) async-start(), calls=%async_computation.21 | async-start | bytes 5308416 | tf_op jit(solution)/shard_map/reduce_scatter | solution.py:379
  704.5 9.6 copy-start.23
  704.5 414.7 %all-reduce.19.cloned.1.call-start = ((), (), s32[]{:S(2)}) async-start(), calls=%async_computation.26 | async-start | bytes 12582912 | tf_op jit(solution)/shard_map/psum | solution.py:228
  704.7 9.3 copy-start.27
  1119.2 6.6 copy-start.5
  1119.2 6.6 copy-start.20
  1119.2 6.6 copy-start.61
  1119.2 6.6 copy-start.65
  1119.2 6.6 copy-start.70
  (76 other events, 180.0 us)
Sparse Core Ops, SparseCore 0:
  80.1 89.6 all-reduce.10
  196.7 86.9 all-reduce.12
  334.5 86.9 all-reduce.14
  456.8 86.9 all-reduce.16
  545.9 31.5 reduce-scatter.35
  579.7 29.5 reduce-scatter.33
  611.6 31.3 reduce-scatter.25
  645.3 31.1 reduce-scatter.23
  678.8 31.3 reduce-scatter.21
  712.9 30.9 reduce-scatter.19
  746.8 31.4 reduce-scatter.15
  781.0 31.0 reduce-scatter.17
  814.4 53.0 reduce-scatter.31
  869.7 53.3 reduce-scatter.29
  925.2 53.3 reduce-scatter.27
  982.5 136.6 all-reduce.18
where the time goes:
time: 1190 us; the launch traced here: 1170 us
  waiting for transfers between devices  662 us (56%)
  matrix products  238 us (20%)
  other arithmetic  112 us (9%)
  local copies, waits for them, and re-layouts  90.8 us (8%)
  blocking collectives  28.4 us (2%)
  loops' own time  24.3 us (2%)
  between operations  15.9 us (1%)
    psum x1, waiting for transfers between devices, forward_pass(): lax.psum(product(hidden, feed_down).astype(jnp.bfloat16), 'tensor')  138 us
    psum x1, waiting for transfers between devices, forward_pass(): lax.psum(product(self_attn, self_output).astype(jnp.bfloat16), 'tensor')  87.8 us
    psum x1, waiting for transfers between devices, forward_pass(): lax.psum(product(cross_attn, cross_output).astype(jnp.bfloat16), 'tensor')  87 us
    psum x1, waiting for transfers between devices, body(): lax.psum(feed_partial.astype(jnp.bfloat16), 'tensor').astype(jnp.float32)  75.8 us
    reduce_scatter x1, waiting for transfers between devices, body(): lax.psum_scatter(down_grad.astype(jnp.bfloat16), 'dp', scatter_dimension=...  53.8 us
    reduce_scatter x1, waiting for transfers between devices, body(): lax.psum_scatter(up_grad.astype(jnp.bfloat16), 'dp', scatter_dimension=0,...  53.3 us
    reduce_scatter x1, waiting for transfers between devices, body(): lax.psum_scatter(gate_grad.astype(jnp.bfloat16), 'dp', scatter_dimension=...  53.3 us
    dot_general x14, matrix products, product(): return jnp.dot(left_rows, right_rows, preferred_element_type=jnp.float32)  51.8 us
  transfers between devices with their start and end apart: 16, of which 11 were waited for; matrix products, arithmetic and copies ran while one was open for 20% of the time, Pallas kernels for 0%

commit v1 on v0

v1 whole, which is shorter than its diff:
```python
import functools

import jax
import jax.numpy as jnp
from jax import lax
from jax.experimental import pallas as pl
from jax.experimental.pallas import tpu as pltpu
from jax.sharding import PartitionSpec as P

HEAD_DIM = 64
HALF = HEAD_DIM // 2
EPS = 1e-05
BF = jnp.bfloat16
F32 = jnp.float32
LOG2E = 1.4426950408889634
SCALE = HEAD_DIM**-0.5
VMEM_BYTES = 60 << 20
MESH_ID = pl.DeviceIdType.MESH
VSPEC = pl.BlockSpec(memory_space=pltpu.VMEM)
ANYSPEC = pl.BlockSpec(memory_space=pl.ANY)


def nn(a, b):
    return lax.dot_general(a, b, (((1,), (0,)), ((), ())), preferred_element_type=F32)


def nt(a, b):
    return lax.dot_general(a, b, (((1,), (1,)), ((), ())), preferred_element_type=F32)


def tn(a, b):
    return lax.dot_general(a, b, (((0,), (0,)), ((), ())), preferred_element_type=F32)


def sds(shape, dtype):
    return jax.ShapeDtypeStruct(shape, dtype)


def params(**kw):
    return pltpu.CompilerParams(vmem_limit_bytes=VMEM_BYTES, **kw)


def cost(flops, nbytes, trans=0):
    return pl.CostEstimate(flops=int(flops), bytes_accessed=int(nbytes), transcendentals=int(trans))


def unit(x):
    center = x - jnp.mean(x, axis=-1, keepdims=True)
    inverse = lax.rsqrt(jnp.mean(center * center, axis=-1, keepdims=True) + EPS)
    return center * inverse, inverse


def norm_back(grad, u, inverse, gain):
    e = grad * gain
    mean_e = jnp.mean(e, axis=-1, keepdims=True)
    mean_p = jnp.mean(e * u, axis=-1, keepdims=True)
    return inverse * (e - mean_e - u * mean_p)


def lane_group(width):
    return 128 if width % 128 == 0 else width


def tables(length, group):
    freq = 10000.0 ** (-jnp.arange(HALF, dtype=F32) / HALF)
    angles = jnp.arange(length, dtype=F32)[:, None] * freq[None, :]
    c, s = jnp.cos(angles), jnp.sin(angles)
    reps = group // HEAD_DIM
    return jnp.tile(jnp.concatenate([c, c], 1), (1, reps)), jnp.tile(jnp.concatenate([-s, s], 1), (1, reps))


def turned(a):
    width = a.shape[-1]
    lane = lax.broadcasted_iota(jnp.int32, a.shape, 1) % HEAD_DIM
    return jnp.where(lane < HALF, pltpu.roll(a, width - HALF, 1), pltpu.roll(a, HALF, 1))


def head_masks(rows, group):
    lane = lax.broadcasted_iota(jnp.int32, (rows, group), 1) // HEAD_DIM
    return [jnp.where(lane == h, 1.0, 0.0) for h in range(group // HEAD_DIM)]


def qkv_kernel(x_ref, g_ref, wq_ref, wk_ref, wv_ref, c_ref, s_ref, h_ref, q_ref, k_ref, v_ref):
    u, _ = unit(x_ref[...].astype(F32))
    h = (u * g_ref[...]).astype(BF)
    h_ref[...] = h
    reps = q_ref.shape[1] // c_ref.shape[1]
    c = jnp.concatenate([c_ref[...]] * reps, 1)
    s = jnp.concatenate([s_ref[...]] * reps, 1)
    for w_ref, o_ref in ((wq_ref, q_ref), (wk_ref, k_ref)):
        a = nn(h, w_ref[...])
        o_ref[...] = (a * c + turned(a) * s).astype(BF)
    v_ref[...] = nn(h, wv_ref[...]).astype(BF)


def qkv(x, gain, wq, wk, wv, cs, sn):
    T, D = x.shape
    W = wq.shape[1]
    tb = 256
    row = lambda n: pl.BlockSpec((tb, n), lambda i: (i, 0))
    full = lambda a: pl.BlockSpec(a.shape, lambda i: (0, 0), pipeline_mode=pl.Buffered(1))
    return pl.pallas_call(
        qkv_kernel,
        grid=(T // tb,),
        in_specs=[row(D), full(gain), full(wq), full(wk), full(wv), row(cs.shape[1]), row(cs.shape[1])],
        out_specs=[row(D), row(W), row(W), row(W)],
        out_shape=[sds((T, D), BF)] + [sds((T, W), BF)] * 3,
        compiler_params=params(),
        cost_estimate=cost(6 * T * D * W, 4 * T * D + 6 * D * W + 6 * T * W),
        name="qkv",
    )(x, gain, wq, wk, wv, cs, sn)


def attn_fwd_kernel(q_ref, k_ref, v_ref, o_ref, lse_ref):
    T, G = q_ref.shape
    qb = 256
    mult = SCALE * LOG2E
    k, v = k_ref[...], v_ref[...]
    masks = [m.astype(BF) for m in head_masks(1, G)]
    lane = lax.broadcasted_iota(jnp.int32, (qb, G), 1) // HEAD_DIM
    stat_lane = lax.broadcasted_iota(jnp.int32, (qb, 128), 1)

    def block(i, carry):
        rows = pl.ds(pl.multiple_of(i * qb, qb), qb)
        q = q_ref[rows, :]
        out = jnp.zeros((qb, G), F32)
        stats = jnp.zeros((qb, 128), F32)
        for h in range(G // HEAD_DIM):
            s = nt(q * masks[h], k)
            top = jnp.max(s, axis=-1, keepdims=True) * mult
            p = jnp.exp2(s * mult - top)
            total = jnp.sum(p, axis=-1, keepdims=True)
            o = nn(p.astype(BF), v) / total
            out = jnp.where(lane == h, o, out)
            stats = jnp.where(stat_lane == h, top + jnp.log2(total), stats)
        o_ref[rows, :] = out.astype(BF)
        lse_ref[:, rows] = jnp.transpose(stats)[:8]
        return carry

    lax.fori_loop(0, T // qb, block, 0)


def attn_fwd(q, k, v):
    T, W = q.shape
    G = lane_group(W)
    groups = W // G
    cols = pl.BlockSpec((T, G), lambda i: (0, i))
    return pl.pallas_call(
        attn_fwd_kernel,
        grid=(groups,),
        in_specs=[cols] * 3,
        out_specs=[cols, pl.BlockSpec((None, 8, T), lambda i: (i, 0, 0))],
        out_shape=[sds((T, W), BF), sds((groups, 8, T), F32)],
        compiler_params=params(),
        cost_estimate=cost(16 * T * T * W, 8 * T * W, T * T * W // HEAD_DIM),
        name="attn_fwd",
    )(q, k, v)


def attn_bwd_kernel(q_ref, k_ref, v_ref, o_ref, do_ref, lse_ref, c_ref, s_ref, dq_ref, dk_ref, dv_ref, dk_acc, dv_acc, kt_ref):
    T, G = q_ref.shape
    qb = 256
    mult = SCALE * LOG2E
    nh = G // HEAD_DIM
    k, v = k_ref[...], v_ref[...]
    kt_ref[...] = jnp.transpose(k.astype(F32)).astype(BF)
    masks = [m.astype(BF) for m in head_masks(1, G)]
    head_rows = jnp.where(
        lax.broadcasted_iota(jnp.int32, (16, G), 0) == lax.broadcasted_iota(jnp.int32, (16, G), 1) // HEAD_DIM, 1.0, 0.0
    ).astype(BF)
    dk_acc[...] = jnp.zeros_like(dk_acc)
    dv_acc[...] = jnp.zeros_like(dv_acc)

    def block(i, carry):
        rows = pl.ds(pl.multiple_of(i * qb, qb), qb)
        q = q_ref[rows, :]
        do = do_ref[rows, :]
        prod = do.astype(F32) * o_ref[rows, :].astype(F32)
        high = prod.astype(BF)
        delta = nt(head_rows, high) + nt(head_rows, (prod - high.astype(F32)).astype(BF))
        lse = lse_ref[:, rows]
        parts = []
        for h in range(nh):
            qm = q * masks[h]
            dom = do * masks[h]
            st = nt(k, qm)
            pt = jnp.exp2(st * mult - lse[h : h + 1, :])
            dpt = nt(v, dom)
            dst = (pt * (dpt - delta[h : h + 1, :])).astype(BF)
            dv_acc[...] += nn(pt.astype(BF), dom)
            dk_acc[...] += nn(dst, qm)
            parts.append(nn(kt_ref[h * HEAD_DIM : (h + 1) * HEAD_DIM, :], dst))
        dq = jnp.transpose(jnp.concatenate(parts, 0)) * SCALE
        dq_ref[rows, :] = (dq * c_ref[rows, :] - turned(dq) * s_ref[rows, :]).astype(BF)
        return carry

    lax.fori_loop(0, T // qb, block, 0)
    dk = dk_acc[...] * SCALE
    dk_ref[...] = (dk * c_ref[...] - turned(dk) * s_ref[...]).astype(BF)
    dv_ref[...] = dv_acc[...].astype(BF)


def attn_bwd(q, k, v, o, do, lse, cs, sn):
    T, W = q.shape
    G = lane_group(W)
    cols = pl.BlockSpec((T, G), lambda i: (0, i))
    tab = pl.BlockSpec((T, G), lambda i: (0, 0), pipeline_mode=pl.Buffered(1))
    return pl.pallas_call(
        attn_bwd_kernel,
        grid=(W // G,),
        in_specs=[cols] * 5 + [pl.BlockSpec((None, 8, T), lambda i: (i, 0, 0)), tab, tab],
        out_specs=[cols] * 3,
        out_shape=[sds((T, W), BF)] * 3,
        scratch_shapes=[pltpu.VMEM((T, G), F32), pltpu.VMEM((T, G), F32), pltpu.VMEM((G, T), BF)],
        compiler_params=params(),
        cost_estimate=cost(40 * T * T * W, 16 * T * W, T * T * W // HEAD_DIM),
        name="attn_bwd",
    )(q, k, v, o, do, lse, cs, sn)


def greet(n, me):
    sem = pltpu.get_barrier_semaphore()
    for d in range(1, n):
        pl.semaphore_signal(sem, 1, device_id={"tensor": me ^ d}, device_id_type=MESH_ID)
    pl.semaphore_wait(sem, n - 1)


def remote(src, dst, send, recv, target):
    return pltpu.make_async_remote_copy(src, dst, send, recv, device_id={"tensor": target}, device_id_type=MESH_ID)


def out_rs_kernel(n, a_ref, w_ref, x_ref, g_ref, after_ref, h_ref, sbuf, rbuf, ss, rs):
    me = lax.axis_index("tensor")
    C = x_ref.shape[0]
    greet(n, me)

    def part(t):
        return nn(a_ref[pl.ds(pl.multiple_of(t * C, C), C), :], w_ref[...])

    copies = {}
    for d in reversed(range(1, n)):
        t = me ^ d
        sbuf[d - 1] = part(t).astype(BF)
        copies[d] = remote(sbuf.at[d - 1], rbuf.at[d - 1], ss.at[d - 1], rs.at[d - 1], t)
        copies[d].start()
    total = part(me)
    for d in range(1, n):
        copies[d].wait_recv()
        total = total + rbuf[d - 1].astype(F32)
    after = x_ref[...].astype(F32) + total
    after_ref[...] = after
    u, _ = unit(after)
    h_ref[...] = (u * g_ref[...]).astype(BF)
    for d in range(1, n):
        copies[d].wait_send()


def out_rs(n, a, w, x, gain):
    C, D = x.shape
    T, W = a.shape
    return pl.pallas_call(
        functools.partial(out_rs_kernel, n),
        in_specs=[VSPEC] * 4,
        out_specs=[VSPEC] * 2,
        out_shape=[sds((C, D), F32), sds((C, D), BF)],
        scratch_shapes=[pltpu.VMEM((n - 1, C, D), BF)] * 2 + [pltpu.SemaphoreType.DMA((n - 1,))] * 2,
        compiler_params=params(collective_id=0, has_side_effects=True),
        cost_estimate=cost(2 * T * W * D + 2e10, 8 * C * D),
        name="out_rs",
    )(a, w, x, gain)


def ff_kernel(n, h_in, gb_hbm, wg_hbm, wu_hbm, wd_hbm, h_ref, hid_ref, dgu_ref, dh_ref,
              gb_ref, wg_ref, wu_ref, wd_ref, sbuf, rbuf, ss, rs, ss2, rs2, ls):
    me = lax.axis_index("tensor")
    C, D = h_in.shape
    F = wg_ref.shape[1]
    loads = [
        pltpu.make_async_copy(src, dst, ls.at[i])
        for i, (src, dst) in enumerate(((wg_hbm, wg_ref), (wu_hbm, wu_ref), (wd_hbm, wd_ref), (gb_hbm, gb_ref)))
    ]
    for c in loads:
        c.start()
    greet(n, me)
    gather = {}
    for d in range(1, n):
        gather[d] = remote(h_in, h_ref.at[me], ss.at[d - 1], rs.at[d - 1], me ^ d)
        gather[d].start()
    h_ref[me] = h_in[...]
    for c in loads:
        c.wait()
    tf = 256

    def chunk(t, store):
        rows = pl.ds(pl.multiple_of(t * C, C), C)
        h = h_ref[t]
        gb = gb_ref[rows, :]

        def tile(j, carry):
            cols = pl.ds(pl.multiple_of(j * tf, tf), tf)
            gate = nn(h, wg_ref[:, cols])
            up = nn(h, wu_ref[:, cols])
            dhid = nt(gb, wd_ref[cols, :])
            sig = 1.0 / (1.0 + jnp.exp(-gate))
            act = gate * sig
            hid_ref[rows, cols] = (act * up).astype(BF)
            dgu_ref[rows, cols] = (dhid * up * (sig * (1.0 + gate * (1.0 - sig)))).astype(BF)
            dgu_ref[rows, pl.ds(pl.multiple_of(F + j * tf, tf), tf)] = (dhid * act).astype(BF)
            return carry

        lax.fori_loop(0, F // tf, tile, 0)

        def back(j, carry):
            out = pl.ds(pl.multiple_of(j * tf, tf), tf)
            store(out, nt(dgu_ref[rows, :F], wg_ref[out, :]) + nt(dgu_ref[rows, F:], wu_ref[out, :]))
            return carry

        lax.fori_loop(0, D // tf, back, 0)

    def store_own(cols, val):
        dh_ref[:, cols] = val

    chunk(me, store_own)
    copies = {}
    for d in range(1, n):
        t = me ^ d
        gather[d].wait_recv()

        def store_sent(cols, val):
            sbuf[d - 1, :, cols] = val.astype(BF)

        chunk(t, store_sent)
        copies[d] = remote(sbuf.at[d - 1], rbuf.at[d - 1], ss2.at[d - 1], rs2.at[d - 1], t)
        copies[d].start()
    for d in range(1, n):
        gather[d].wait_send()
    for d in range(1, n):
        copies[d].wait_recv()
        dh_ref[...] += rbuf[d - 1].astype(F32)
    for d in range(1, n):
        copies[d].wait_send()


def ff(n, h, gb, wg, wu, wd):
    C, D = h.shape
    T = gb.shape[0]
    F = wg.shape[1]
    return pl.pallas_call(
        functools.partial(ff_kernel, n),
        in_specs=[VSPEC] + [ANYSPEC] * 4,
        out_specs=[VSPEC] * 4,
        out_shape=[sds((n, C, D), BF), sds((T, F), BF), sds((T, 2 * F), BF), sds((C, D), F32)],
        scratch_shapes=[
            pltpu.VMEM((T, D), BF),
            pltpu.VMEM((D, F), BF),
            pltpu.VMEM((D, F), BF),
            pltpu.VMEM((F, D), BF),
            pltpu.VMEM((n - 1, C, D), BF),
            pltpu.VMEM((n - 1, C, D), BF),
        ]
        + [pltpu.SemaphoreType.DMA((n - 1,))] * 4
        + [pltpu.SemaphoreType.DMA((4,))],
        compiler_params=params(collective_id=1, has_side_effects=True),
        cost_estimate=cost(10 * T * D * F + 3e10, 6 * D * F + 8 * T * D),
        name="ff",
    )(h, gb, wg, wu, wd)


def gather_kernel(n, x_in, w_ref, x_ref, da_ref, ss, rs):
    me = lax.axis_index("tensor")
    C = x_in.shape[0]
    greet(n, me)
    gather = {}
    for d in range(1, n):
        gather[d] = remote(x_in, x_ref.at[me], ss.at[d - 1], rs.at[d - 1], me ^ d)
        gather[d].start()

    def back(t, x):
        da_ref[pl.ds(pl.multiple_of(t * C, C), C), :] = nt(x, w_ref[...]).astype(BF)

    x_ref[me] = x_in[...]
    back(me, x_in[...])
    for d in range(1, n):
        gather[d].wait_recv()
        back(me ^ d, x_ref[me ^ d])
    for d in range(1, n):
        gather[d].wait_send()


def gather_back(n, x, w):
    C, D = x.shape
    W = w.shape[0]
    return pl.pallas_call(
        functools.partial(gather_kernel, n),
        in_specs=[VSPEC] * 2,
        out_specs=[VSPEC] * 2,
        out_shape=[sds((n, C, D), BF), sds((n * C, W), BF)],
        scratch_shapes=[pltpu.SemaphoreType.DMA((n - 1,))] * 2,
        compiler_params=params(collective_id=2, has_side_effects=True),
        cost_estimate=cost(2 * n * C * W * D + 2e10, 8 * C * D),
        name="gather_back",
    )(x, w)


def last_kernel(n, dq_ref, dk_ref, dv_ref, wq_ref, wk_ref, wv_ref, x_ref, da_ref, g_ref, gg_in,
                out_ref, gg_ref, sbuf, rbuf, lbuf, gbuf, gsum, ss, rs, ss2, rs2, ss3, rs3):
    me = lax.axis_index("tensor")
    C, D = x_ref.shape
    greet(n, me)

    def part(t):
        rows = pl.ds(pl.multiple_of(t * C, C), C)
        return nt(dq_ref[rows, :], wq_ref[...]) + nt(dk_ref[rows, :], wk_ref[...]) + nt(dv_ref[rows, :], wv_ref[...])

    copies = {}
    for d in reversed(range(1, n)):
        t = me ^ d
        sbuf[d - 1] = part(t).astype(BF)
        copies[d] = remote(sbuf.at[d - 1], rbuf.at[d - 1], ss.at[d - 1], rs.at[d - 1], t)
        copies[d].start()
    total = part(me)
    u, inverse = unit(x_ref[...].astype(F32))
    for d in range(1, n):
        copies[d].wait_recv()
        total = total + rbuf[d - 1].astype(F32)
    lbuf[me] = (da_ref[...] + norm_back(total, u, inverse, g_ref[...])).astype(BF)
    gather = {}
    for d in range(1, n):
        gather[d] = remote(lbuf.at[me], lbuf.at[me], ss2.at[d - 1], rs2.at[d - 1], me ^ d)
        gather[d].start()
    row = lax.broadcasted_iota(jnp.int32, (8, D), 0)
    gsum[...] = gg_in[...] + jnp.where(row == 2, jnp.sum(total * u, axis=0, keepdims=True), 0.0)
    small = {}
    for d in range(1, n):
        small[d] = remote(gsum, gbuf.at[d - 1], ss3.at[d - 1], rs3.at[d - 1], me ^ d)
        small[d].start()

    def put(t):
        out_ref[pl.ds(pl.multiple_of(t * C, C), C), :] = lbuf[t].astype(F32)

    put(me)
    for d in range(1, n):
        gather[d].wait_recv()
        put(me ^ d)
    gains = gsum[...]
    for d in range(1, n):
        small[d].wait_recv()
        gains = gains + gbuf[d - 1]
    gg_ref[...] = gains
    for d in range(1, n):
        copies[d].wait_send()
        gather[d].wait_send()
        small[d].wait_send()


def last(n, dq, dk, dv, wq, wk, wv, x, da, gain, gains):
    C, D = x.shape
    T, W = dq.shape
    return pl.pallas_call(
        functools.partial(last_kernel, n),
        in_specs=[VSPEC] * 10,
        out_specs=[VSPEC] * 2,
        out_shape=[sds((T, D), F32), sds((8, D), F32)],
        scratch_shapes=[
            pltpu.VMEM((n - 1, C, D), BF),
            pltpu.VMEM((n - 1, C, D), BF),
            pltpu.VMEM((n, C, D), BF),
            pltpu.VMEM((n - 1, 8, D), F32),
            pltpu.VMEM((8, D), F32),
        ]
        + [pltpu.SemaphoreType.DMA((n - 1,))] * 6,
        compiler_params=params(collective_id=3, has_side_effects=True),
        cost_estimate=cost(6 * T * W * D + 4e10, 8 * T * D),
        name="last",
    )(dq, dk, dv, wq, wk, wv, x, da, gain, gains)


def cross_fwd_kernel(ctx, h_ref, x_ref, wq_ref, k_ref, v_ref, wo_ref, g_ref, q_ref, o_ref, after_ref, h3_ref):
    C, HD = q_ref.shape
    KP = k_ref.shape[0]
    mult = SCALE * LOG2E
    G = 128
    masks = [m.astype(BF) for m in head_masks(1, G)]
    lane = lax.broadcasted_iota(jnp.int32, (C, G), 1) // HEAD_DIM
    valid = lax.broadcasted_iota(jnp.int32, (C, KP), 1) < ctx

    def group(g, carry):
        cols = pl.ds(pl.multiple_of(g * G, G), G)
        q = nn(h_ref[...], wq_ref[:, cols]).astype(BF)
        q_ref[:, cols] = q
        k, v = k_ref[:, cols], v_ref[:, cols]
        out = jnp.zeros((C, G), F32)
        for h in range(G // HEAD_DIM):
            s = jnp.where(valid, nt(q * masks[h], k), -1e30)
            p = jnp.exp2((s - jnp.max(s, axis=-1, keepdims=True)) * mult)
            o = nn(p.astype(BF), v) / jnp.sum(p, axis=-1, keepdims=True)
            out = jnp.where(lane == h, o, out)
        o_ref[:, cols] = out.astype(BF)
        return carry

    lax.fori_loop(0, HD // G, group, 0)
    D = h_ref.shape[1]
    tf = 256

    def project(j, carry):
        cols = pl.ds(pl.multiple_of(j * tf, tf), tf)
        after_ref[:, cols] = x_ref[:, cols] + nn(o_ref[...], wo_ref[:, cols])
        return carry

    lax.fori_loop(0, D // tf, project, 0)
    u, _ = unit(after_ref[...])
    h3_ref[...] = (u * g_ref[...]).astype(BF)


def cross_fwd(ctx, h, x, wq, k, v, wo, gain):
    C, D = h.shape
    HD = wq.shape[1]
    return pl.pallas_call(
        functools.partial(cross_fwd_kernel, ctx),
        in_specs=[VSPEC] * 7,
        out_specs=[VSPEC] * 4,
        out_shape=[sds((C, HD), BF), sds((C, HD), BF), sds((C, D), F32), sds((C, D), BF)],
        compiler_params=params(),
        cost_estimate=cost(4 * C * D * HD + 16 * C * 256 * HD, 8 * D * HD),
        name="cross_fwd",
    )(h, x, wq, k, v, wo, gain)


def cross_bwd_kernel(ctx, dh3_ref, after2_ref, cot_ref, g3_ref, wo_ref, q_ref, k_ref, v_ref, wq_ref, after1_ref, g2_ref,
                     cb_ref, dq_ref, dk_ref, dv_ref, da_ref, sb_ref, gg_ref, dh2_ref):
    C, HD = q_ref.shape
    KP = k_ref.shape[0]
    D = da_ref.shape[1]
    mult = SCALE * LOG2E
    G = 128
    masks = [m.astype(BF) for m in head_masks(1, G)]
    lane = lax.broadcasted_iota(jnp.int32, (C, G), 1) // HEAD_DIM
    valid = lax.broadcasted_iota(jnp.int32, (C, KP), 1) < ctx
    dh3 = dh3_ref[...]
    u3, inv3 = unit(after2_ref[...])
    gain3 = jnp.sum(dh3 * u3, axis=0, keepdims=True)
    da2 = cot_ref[...].astype(F32) + norm_back(dh3, u3, inv3, g3_ref[...])
    da_ref[...] = da2
    cb_ref[...] = da2.astype(BF)

    def group(g, carry):
        cols = pl.ds(pl.multiple_of(g * G, G), G)
        do = nt(cb_ref[...], wo_ref[cols, :]).astype(BF)
        q, k, v = q_ref[:, cols], k_ref[:, cols], v_ref[:, cols]
        dq = jnp.zeros((C, G), F32)
        dk = jnp.zeros((KP, G), F32)
        dv = jnp.zeros((KP, G), F32)
        for h in range(G // HEAD_DIM):
            qm = q * masks[h]
            dom = do * masks[h]
            s = jnp.where(valid, nt(qm, k), -1e30)
            p = jnp.exp2((s - jnp.max(s, axis=-1, keepdims=True)) * mult)
            p = p / jnp.sum(p, axis=-1, keepdims=True)
            dp = nt(dom, v)
            ds = (p * (dp - jnp.sum(p * dp, axis=-1, keepdims=True))).astype(BF)
            dq = jnp.where(lane == h, nn(ds, k), dq)
            dk = dk + tn(ds, qm)
            dv = dv + tn(p.astype(BF), dom)
        dq_ref[:, cols] = (dq * SCALE).astype(BF)
        dk_ref[:, cols] = dk * SCALE
        dv_ref[:, cols] = dv
        return carry

    lax.fori_loop(0, HD // G, group, 0)
    tf = 256

    def project(j, carry):
        cols = pl.ds(pl.multiple_of(j * tf, tf), tf)
        dh2_ref[:, cols] = nt(dq_ref[...], wq_ref[cols, :])
        return carry

    lax.fori_loop(0, D // tf, project, 0)
    dh2 = dh2_ref[...]
    u2, inv2 = unit(after1_ref[...])
    gain2 = jnp.sum(dh2 * u2, axis=0, keepdims=True)
    da1 = da_ref[...] + norm_back(dh2, u2, inv2, g2_ref[...])
    da_ref[...] = da1
    sb_ref[...] = da1.astype(BF)
    row = lax.broadcasted_iota(jnp.int32, (8, D), 0)
    gg_ref[...] = jnp.where(row == 0, gain3, 0.0) + jnp.where(row == 1, gain2, 0.0)


def cross_bwd(ctx, dh3, after2, cot, g3, wo, q, k, v, wq, after1, g2):
    C, D = after2.shape
    HD = wq.shape[1]
    KP = k.shape[0]
    return pl.pallas_call(
        functools.partial(cross_bwd_kernel, ctx),
        in_specs=[VSPEC] * 11,
        out_specs=[VSPEC] * 7,
        out_shape=[
            sds((C, D), BF),
            sds((C, HD), BF),
            sds((KP, HD), F32),
            sds((KP, HD), F32),
            sds((C, D), F32),
            sds((C, D), BF),
            sds((8, D), F32),
        ],
        scratch_shapes=[pltpu.VMEM((C, D), F32)],
        compiler_params=params(),
        cost_estimate=cost(4 * C * D * HD + 40 * C * 256 * HD, 8 * D * HD),
        name="cross_bwd",
    )(dh3, after2, cot, g3, wo, q, k, v, wq, after1, g2)


def body(latents, context, cotangent, g1, wq, wk, wv, wo, g2, xq, xk, xv, xo, g3, wg, wu, wd, n):
    _, T, D = latents.shape
    ctx = context.shape[1]
    W = wq.shape[1]
    F = wg.shape[1]
    C = T // n
    me = lax.axis_index("tensor")
    x = latents.reshape(T, D)
    gb = cotangent.reshape(T, D)
    ctx_rows = context.reshape(ctx, -1)
    KP = -(-ctx // 16) * 16
    cs, sn = tables(T, lane_group(W))
    g1, g2, g3 = (g.reshape(1, D) for g in (g1, g2, g3))
    own = lambda a: lax.dynamic_slice_in_dim(a, me * C, C, 0)

    pad = ((0, KP - ctx), (0, 0))
    ck = jnp.pad(nn(ctx_rows, xk).astype(BF), pad)
    cv = jnp.pad(nn(ctx_rows, xv).astype(BF), pad)
    xq_kv = lax.all_gather(jnp.concatenate([xq, ck, cv], 0), "tensor", axis=1, tiled=True)
    xo_all = lax.all_gather(xo, "tensor", axis=0, tiled=True)
    xq_all, ck_all, cv_all = xq_kv[:D], xq_kv[D : D + KP], xq_kv[D + KP :]

    h1, q, k, v = qkv(x, g1, wq, wk, wv, cs, sn)
    attn, lse = attn_fwd(q, k, v)
    x_own = own(x)
    after1, h2 = out_rs(n, attn, wo, x_own, g2)
    cq, cattn, after2, h3_own = cross_fwd(ctx, h2, after1, xq_all, ck_all, cv_all, xo_all, g3)
    h3, hidden, dgu, dh3 = ff(n, h3_own, gb, wg, wu, wd)
    h3 = h3.reshape(T, D)

    def scatter(a, axis):
        return lax.psum_scatter(a.astype(BF), axis, scatter_dimension=0, tiled=True)

    down_grad = scatter(tn(gb, hidden), "dp").astype(F32).T
    gu_grad = scatter(tn(h3, dgu), "dp").astype(F32)
    gate_grad, up_grad = gu_grad[:, :F], gu_grad[:, F:]

    terms = nn(hidden, wd).astype(BF).reshape(n, C, D)
    swap = lambda a, d: lax.ppermute(a, "tensor", [(i, i ^ d) for i in range(n)])
    pick = lambda a, t: lax.dynamic_index_in_dim(a, t, 0, keepdims=False)
    total = after2 + pick(terms, me).astype(F32)
    for d in range(1, n):
        total = total + swap(pick(terms, me ^ d), d).astype(F32)
    total = total.astype(BF)
    block_out = jnp.zeros((n, C, D), BF)
    block_out = lax.dynamic_update_index_in_dim(block_out, total, me, 0)
    for d in range(1, n):
        block_out = lax.dynamic_update_index_in_dim(block_out, swap(total, d), me ^ d, 0)

    cb, dcq, dck, dcv, dafter1, sb_own, gains = cross_bwd(
        ctx, dh3, after2, own(gb), g3, xo_all, cq, ck_all, cv_all, xq_all, after1, g2
    )
    sb, dattn = gather_back(n, sb_own, wo)
    sb = sb.reshape(T, D)
    dq, dk, dv = attn_bwd(q, k, v, attn, dattn, lse, cs, sn)
    latent_grad, gains = last(n, dq, dk, dv, wq, wk, wv, x_own, dafter1, g1, gains)

    cross_grads = jnp.concatenate([tn(h2, dcq).astype(BF), tn(cb, cattn).astype(BF)], 1)
    cross_grads = scatter(cross_grads, "dp")
    rows = cross_grads.shape[0]
    cross_grads = cross_grads.reshape(rows, 2, n, W).transpose(2, 0, 1, 3).reshape(n * rows, 2 * W)
    cross_grads = scatter(cross_grads, "tensor").astype(F32)
    xq_grad, xo_grad = cross_grads[:, :W], cross_grads[:, W:].T

    dckv = jnp.concatenate([dck[:ctx], dcv[:ctx]], 0).astype(BF)
    dckv = lax.psum_scatter(dckv, "tensor", scatter_dimension=1, tiled=True)
    kv_grads = jnp.concatenate([tn(ctx_rows, dckv[:ctx]), tn(ctx_rows, dckv[ctx:])], 1)
    kv_grads = scatter(kv_grads, "dp").astype(F32)

    self_grads = jnp.concatenate([tn(h1, dq), tn(h1, dk), tn(h1, dv), tn(sb, attn)], 1)
    self_grads = scatter(self_grads, "dp").astype(F32)
    gains = lax.psum_scatter(gains, "dp", scatter_dimension=1, tiled=True)
    return (
        block_out.reshape(1, T, D),
        latent_grad.reshape(1, T, D),
        gains[2],
        self_grads[:, :W],
        self_grads[:, W : 2 * W],
        self_grads[:, 2 * W : 3 * W],
        self_grads[:, 3 * W :].T,
        gains[1],
        xq_grad,
        kv_grads[:, :W],
        kv_grads[:, W:],
        xo_grad,
        gains[0],
        gate_grad,
        up_grad,
        down_grad,
    )


def solution(mesh):
    tokens = P("dp", None, None)
    cols = P(None, "tensor")
    rows = P("tensor", None)
    return jax.shard_map(
        functools.partial(body, n=mesh.shape["tensor"]),
        mesh=mesh,
        in_specs=(tokens, tokens, tokens, P(), cols, cols, cols, rows, P(), cols, cols, cols, rows, P(), cols, cols, rows),
        out_specs=(
            tokens,
            tokens,
            P("dp"),
            P("dp", "tensor"),
            P("dp", "tensor"),
            P("dp", "tensor"),
            P("tensor", "dp"),
            P("dp"),
            P("dp", "tensor"),
            P("dp", "tensor"),
            P("dp", "tensor"),
            P("tensor", "dp"),
            P("dp"),
            P("dp", "tensor"),
            P("dp", "tensor"),
            P("tensor", "dp"),
        ),
        check_vma=False,
    )
```

time: 1190 us -> 903 us (0.76)
  Pallas kernels: 0 us -> 377 us
  waiting for transfers between devices: 662 us -> 333 us
  matrix products: 238 us -> 53.1 us
  other arithmetic: 112 us -> 18.1 us
  blocking collectives: 28.4 us -> 0 us
  loops' own time: 24.3 us -> 0 us
    psum x5 -> x0, waiting for transfers between devices: 425 us -> none  [the longest x1 138 us: forward_pass(): lax.psum(product(hidden, feed_down).astype(jnp.bfloat16), 'tensor')]
    pallas_call x0 -> x9, Pallas kernels: none -> 377 us  [the longest x1 83.2 us: ff(): pl.pallas_call(functools.partial(ff_kernel, n), in_specs=[VSPEC] + [ANYSP...]
    dot_general x66 -> x13, matrix products: 218 us -> 53.1 us  [the longest x10 42.4 us: tn(): lax.dot_general(a, b, (((0,), (0,)), ((), ())), preferred_element_type=F32)]
    reduce_scatter x9 -> x2, waiting for transfers between devices: 237 us -> 125 us  [scatter(): return lax.psum_scatter(a.astype(BF), axis, scatter_dimension=0, tiled=True)]
    unnamed x18 -> x16, waiting for transfers between devices: 0.28 us -> 104 us
    ppermute x0 -> x6, waiting for transfers between devices: none -> 55.3 us  [body(): lax.ppermute(a, 'tensor', [(i, i ^ d) for i in range(n)])]
    all_gather x0 -> x2, waiting for transfers between devices: none -> 49.1 us  [the longest x1 49.1 us: body(): xo_all = lax.all_gather(xo, 'tensor', axis=0, tiled=True)]
    convert_element_type x24 -> x2, other arithmetic: 46.2 us -> 1.12 us  [the longest x1 1 us: body(): cross_grads = scatter(cross_grads, 'tensor').astype(F32)]
  transfers between devices with their start and end apart: 16 -> 16, of which waited for: 11 -> 9; matrix products, arithmetic and copies ran while one was open for 20% -> 16% of each run, Pallas kernels for 0% -> 28%
where the time goes in v1:
time: 903 us; the launch traced here: 893 us
  Pallas kernels  377 us (42%)
  waiting for transfers between devices  333 us (37%)
  local copies, waits for them, and re-layouts  90.2 us (10%)
  matrix products  53.1 us (6%)
  other arithmetic  18.1 us (2%)
  between operations  14.8 us (2%)
    reduce_scatter x2, waiting for transfers between devices, scatter(): return lax.psum_scatter(a.astype(BF), axis, scatter_dimension=0, tiled=True)  125 us
    unnamed x16, waiting for transfers between devices  104 us
    pallas_call x1, Pallas kernels, ff(): pl.pallas_call(functools.partial(ff_kernel, n), in_specs=[VSPEC] + [ANYSP...  83.2 us
    pallas_call x1, Pallas kernels, last(): pl.pallas_call(functools.partial(last_kernel, n), in_specs=[VSPEC] * 10,...  80.4 us
    pallas_call x1, Pallas kernels, out_rs(): pl.pallas_call(functools.partial(out_rs_kernel, n), in_specs=[VSPEC] * 4,...  66.4 us
    unnamed x58, local copies, waits for them, and re-layouts  56.5 us
    ppermute x6, waiting for transfers between devices, body(): lax.ppermute(a, 'tensor', [(i, i ^ d) for i in range(n)])  55.3 us
    all_gather x1, waiting for transfers between devices, body(): xo_all = lax.all_gather(xo, 'tensor', axis=0, tiled=True)  49.1 us
  transfers between devices with their start and end apart: 16, of which 9 were waited for; matrix products, arithmetic and copies ran while one was open for 16% of the time, Pallas kernels for 28%

profile of v1, /device:TPU:0, one launch (start us, length us, event | category | flops | bytes accessed | tf_op | source)
XLA Modules:
  0.0 893.4 jit_solution(9786800542688339735)
XLA Ops:
  10.9 2.5 fusion.9
  18.8 2.1 dynamic-slice_bitcast_fusion.4.x_ref
  20.9 2.0 dynamic-slice_bitcast_fusion.cot_ref
  22.9 11.2 %qkv.1 = (bf16[1024,1536]{1,0:T(8,128)(2,1)}, bf16[1024,384]{1,0:T(8,128)(2,1)}, bf16[1024,384]{1,0:T(8,128)(2,1)}, bf16[1024,384]{1,0:T(8,128)(2,1)}) custom-call(bf16[1024,1536]{1,0:T(8,128)(2,1)} %bitcast.103, f32[1,1536]{1,0:T(1,128)} %reshape.90.g_ref, bf16[1536,384]{1,0:T(8,128)(2,1)} %wq_ref.3, bf16[1536,384]{1,0:T(8,128)(2,1)} %wk_ref.3, ...), custom_call_target="tpu_custom_call" | custom-call | flops 3623878656 | bytes 12189696 | tf_op jit(solution)/shard_map/qkv/pallas_call | solution.py:102
  34.1 16.3 %attn_fwd.1 = (bf16[1024,384]{1,0:T(8,128)(2,1)}, f32[3,8,1024]{2,1,0:T(8,128)}) custom-call(bf16[1024,384]{1,0:T(8,128)(2,1)} %get-tuple-element.46.q_ref, bf16[1024,384]{1,0:T(8,128)(2,1)} %get-tuple-element.47.k_ref, bf16[1024,384]{1,0:T(8,128)(2,1)} %get-tuple-element.48.v_ref), custom_call_target="tpu_custom_call" | custom-call | flops 6442450944 | bytes 3145728 | tf_op jit(solution)/shard_map/attn_fwd/pallas_call | solution.py:148
  50.4 66.4 %out_rs.1 = (f32[256,1536]{1,0:T(8,128)}, bf16[256,1536]{1,0:T(8,128)(2,1)}) custom-call(bf16[1024,384]{1,0:T(8,128)(2,1)} %get-tuple-element.49.a_ref.o_ref, bf16[384,1536]{1,0:T(8,128)(2,1)} %w_ref.3, bf16[256,1536]{1,0:T(8,128)(2,1)} %dynamic-slice_bitcast_fusion.4.x_ref, f32[1,1536]{1,0:T(1,128)} %reshape.91.g_ref.g2_ref), custom_call_target="tpu_custom_call" | custom-call | flops 21207959552 | bytes 3145728 | tf_op jit(solution)/shard_map/out_rs/pallas_call | solution.py:261
  116.8 4.8 slice.82.wq_ref
  121.7 2.3 fusion.23
  124.0 49.1 %all-gather.5.cloned.1.call-done.wo_ref = bf16[1536,1536]{1,0:T(8,128)(2,1)} async-done(((bf16[384,1536]{1,0:T(8,128)(2,1)}), bf16[1536,1536]{1,0:T(8,128)(2,1)}) %all-gather.5.cloned.1.call-update) | async-done | bytes 4718608 | tf_op jit(solution)/shard_map/all_gather | solution.py:631
  173.0 17.6 %cross_fwd.1 = (bf16[256,1536]{1,0:T(8,128)(2,1)}, bf16[256,1536]{1,0:T(8,128)(2,1)}, f32[256,1536]{1,0:T(8,128)}, bf16[256,1536]{1,0:T(8,128)(2,1)}) custom-call(bf16[256,1536]{1,0:T(8,128)(2,1)} %get-tuple-element.50.h_ref, f32[256,1536]{1,0:T(8,128)} %get-tuple-element.51.x_ref.after1_ref, bf16[1536,1536]{1,0:T(8,128)(2,1)} %slice.82.wq_ref, ...), custom_call_target="tpu_custom_call" | custom-call | flops 4026531840 | bytes 18874368 | tf_op jit(solution)/shard_map/cross_fwd/pallas_call | solution.py:518
  190.6 83.2 %ff.1 = (bf16[4,256,1536]{2,1,0:T(8,128)(2,1)}, bf16[1024,1536]{1,0:T(8,128)(2,1)}, bf16[1024,3072]{1,0:T(8,128)(2,1)}, f32[256,1536]{1,0:T(8,128)}) custom-call(bf16[256,1536]{1,0:T(8,128)(2,1)} %get-tuple-element.53.h_in, bf16[1024,1536]{1,0:T(8,128)(2,1)} %bitcast.104, bf16[1536,1536]{1,0:T(8,128)(2,1)} %wg_hbm.1, bf16[1536,1536]{1,0:T(8,128)(2,1)} %wu_hbm.1, ...), custom_call_target="tpu_custom_call" | custom-call | flops 54159192064 | bytes 26738688 | tf_op jit(solution)/shard_map/ff/pallas_call | solution.py:348
  273.8 30.1 %cross_bwd.1 = (bf16[256,1536]{1,0:T(8,128)(2,1)}, bf16[256,1536]{1,0:T(8,128)(2,1)}, f32[144,1536]{1,0:T(8,128)}, f32[144,1536]{1,0:T(8,128)}, f32[256,1536]{1,...) custom-call(f32[256,1536]{1,0:T(8,128)} %get-tuple-element.55.dh3_ref, ...), custom_call_target="tpu_custom_call" | custom-call | flops 6442450944 | bytes 18874368 | tf_op jit(solution)/shard_map/cross_bwd/pallas_call | solution.py:592
  307.8 47.7 %gather_back.1 = (bf16[4,256,1536]{2,1,0:T(8,128)(2,1)}, bf16[1024,384]{1,0:T(8,128)(2,1)}) custom-call(bf16[256,1536]{1,0:T(8,128)(2,1)} %get-tuple-element.57.x_in, bf16[384,1536]{1,0:T(8,128)(2,1)} %w_ref.3), custom_call_target="tpu_custom_call" | custom-call | flops 21207959552 | bytes 3145728 | tf_op jit(solution)/shard_map/gather_back/pallas_call | solution.py:393
  355.5 23.8 %attn_bwd.1 = (bf16[1024,384]{1,0:T(8,128)(2,1)}, bf16[1024,384]{1,0:T(8,128)(2,1)}, bf16[1024,384]{1,0:T(8,128)(2,1)}) custom-call(bf16[1024,384]{1,0:T(8,128)(2,1)} %get-tuple-element.46.q_ref, bf16[1024,384]{1,0:T(8,128)(2,1)} %get-tuple-element.47.k_ref, bf16[1024,384]{1,0:T(8,128)(2,1)} %get-tuple-element.48.v_ref, ...), custom_call_target="tpu_custom_call" | custom-call | flops 16106127360 | bytes 6291456 | tf_op jit(solution)/shard_map/attn_bwd/pallas_call | solution.py:208
  379.4 80.4 %last.1 = (f32[1024,1536]{1,0:T(8,128)}, f32[8,1536]{1,0:T(8,128)}) custom-call(bf16[1024,384]{1,0:T(8,128)(2,1)} %get-tuple-element.60.dq_ref, bf16[1024,384]{1,0:T(8,128)(2,1)} %get-tuple-element.61.dk_ref, bf16[1024,384]{1,0:T(8,128)(2,1)} %get-tuple-element.62.dv_ref, bf16[1536,384]{1,0:T(8,128)(2,1)} %wq_ref.3, bf16[1536,384]{1,0:T(8,128)(2,1)} %wk_ref.3, ...), custom_call_target="tpu_custom_call" | custom-call | flops 43623878656 | bytes 12582912 | tf_op jit(solution)/shard_map/last/pallas_call | solution.py:459
  459.8 2.0 copy.65
  461.8 3.6 convolution_convert_fusion.3
  465.4 3.6 convolution_convert_fusion.2
  469.1 7.9 pad_maximum_fusion
  477.0 12.6 %copy.69 = bf16[1536,3072]{1,0:T(8,128)(2,1)} copy(bf16[1536,3072]{0,1:T(8,128)(2,1)} %pad_maximum_fusion) | data formatting | bytes 18874368
  493.2 1.9 copy.73
  495.2 3.5 convolution_convert_fusion.6
  503.7 2.4 pad_maximum_fusion.1
  506.0 6.7 copy.67
  512.8 9.2 %fusion = bf16[1536,1536]{0,1:T(8,128)(2,1)} fusion(bf16[1024,1536]{1,0:T(8,128)(2,1)} %get-tuple-element.54, bf16[1,1024,1536]{2,1,0:T(8,128)(2,1)} %param.19), kind=kOutput, calls=%fused_computation.5 | convolution fusion | flops 4834197504 | bytes 11010048 | tf_op jit(solution)/shard_map/dot_general | solution.py:32
  521.9 6.7 copy.75
  528.7 15.8 %convolution_convert_fusion = bf16[1536,3072]{1,0:T(8,128)(2,1)} fusion(bf16[1024,1536]{1,0:T(8,128)(2,1)} %bitcast.108, bf16[1024,3072]{1,0:T(8,128)(2,1)} %get-tuple-element.75), kind=kOutput, calls=%fused_computation | convolution fusion | flops 9668395008 | bytes 18874368 | tf_op jit(solution)/shard_map/dot_general | solution.py:32
  544.5 8.1 convolution_convert_fusion.4
  552.6 1.7 copy-done.3
  554.3 1.4 dynamic-slice_bitcast_fusion.3
  557.8 1.5 collective-permute-start.2
  559.2 17.1 %collective-permute-done = bf16[256,1536]{1,0:T(8,128)(2,1)S(1)} collective-permute-done((bf16[256,1536]{1,0:T(8,128)(2,1)}, bf16[256,1536]{1,0:T(8,128)(2,1)S(1)}, u32[]{:S(2)}, u32[]{:S(2)}) %collective-permute-start) | collective-permute-done | bytes 786464 | tf_op jit(solution)/shard_map/ppermute | solution.py:650
  576.4 15.9 %collective-permute-done.1 = bf16[256,1536]{1,0:T(8,128)(2,1)} collective-permute-done((bf16[256,1536]{1,0:T(8,128)(2,1)}, bf16[256,1536]{1,0:T(8,128)(2,1)}, u32[]{:S(2)}, u32[]{:S(2)}) %collective-permute-start.1) | collective-permute-done | bytes 786464 | tf_op jit(solution)/shard_map/ppermute | solution.py:650
  592.2 1.9 broadcast_in_dim.18
  594.1 3.3 bitcast_dynamic-update-slice_fusion.3
  604.0 14.0 %collective-permute-done.3 = bf16[256,1536]{1,0:T(8,128)(2,1)S(1)} collective-permute-done((bf16[256,1536]{1,0:T(8,128)(2,1)}, bf16[256,1536]{1,0:T(8,128)(2,1)S(1)}, u32[]{:S(2)}, u32[]{:S(2)}) %collective-permute-start.3) | collective-permute-done | bytes 786464 | tf_op jit(solution)/shard_map/ppermute | solution.py:650
  619.0 1.6 copy.70
  623.1 8.3 collective-permute-done.4
  631.4 2.1 bitcast_dynamic-update-slice_fusion.1
  633.4 2.1 bitcast_dynamic-update-slice_fusion
  638.2 52.3 %reduce-scatter.27.cloned.1.call-done = bf16[192,1536]{1,0:T(8,128)(2,1)} async-done(((bf16[1536,1536]{1,0:T(8,128)(2,1)}), bf16[192,1536]{1,0:T(8,128)(2,1)}) %reduce-scatter.27.cloned.1.call-update) | async-done | bytes 589840
  695.5 50.6 %reduce-scatter.35.cloned.1.call-done = bf16[192,1536]{1,0:T(8,128)(2,1)} async-done(((bf16[1536,1536]{1,0:T(8,128)(2,1)}), bf16[192,1536]{1,0:T(8,128)(2,1)}) %reduce-scatter.35.cloned.1.call-update) | async-done | bytes 589840
  747.6 1.5 copy.64
  749.1 97.3 %reduce-scatter.23.cloned.1.call-done = bf16[192,3072]{1,0:T(8,128)(2,1)} async-done(((bf16[1536,3072]{1,0:T(8,128)(2,1)}), bf16[192,3072]{1,0:T(8,128)(2,1)}) %reduce-scatter.23.cloned.1.call-update) | async-done | bytes 1179664 | tf_op jit(solution)/shard_map/reduce_scatter | solution.py:643
  846.4 2.9 fusion.24
  849.3 27.6 %reduce-scatter.21.cloned.1.call-done = bf16[192,768]{1,0:T(8,128)(2,1)} async-done(((bf16[768,768]{1,0:T(8,128)(2,1)}), bf16[192,768]{1,0:T(8,128)(2,1)}) %reduce-scatter.21.cloned.1.call-update) | async-done | bytes 294928 | tf_op jit(solution)/shard_map/reduce_scatter | solution.py:643
  878.7 1.6 slice.91
  880.3 6.0 copy.88
  (112 shorter events, 44.6 us)
Async XLA Ops:
  7.2 1.1 copy-start
  7.2 109.6 %all-gather.3.cloned.1.call-start = ((), (), s32[]{:S(2)}) async-start(), calls=%async_computation.8 | async-start | bytes 7004160 | tf_op jit(solution)/shard_map/all_gather | solution.py:630
  13.4 3.6 copy-start.9
  13.4 4.2 copy-start.10
  13.4 4.8 copy-start.11
  13.5 159.6 %all-gather.5.cloned.1.call-start = ((), (), s32[]{:S(2)}) async-start(), calls=%async_computation.9 | async-start | bytes 5898240 | tf_op jit(solution)/shard_map/all_gather | solution.py:631
  14.2 475.5 %reduce-scatter.31.cloned.1.call-start = ((), (), s32[]{:S(2)}) async-start(), calls=%async_computation.15 | async-start | bytes 1474560
  307.8 291.7 %reduce-scatter.25.cloned.1.call-start = ((), (), s32[]{:S(2)}) async-start(), calls=%async_computation.12 | async-start | bytes 884736
  379.4 82.4 %copy-start.4 = (bf16[256,1536]{1,0:T(8,128)(2,1)S(1)}, bf16[256,1536]{1,0:T(8,128)(2,1)}, u32[]{:S(2)}) copy-start(bf16[256,1536]{1,0:T(8,128)(2,1)} %get-tuple-element.50.h_ref) | copy-start | bytes 2359300
  379.4 82.4 %copy-start.8 = (bf16[256,1536]{1,0:T(8,128)(2,1)S(1)}, bf16[256,1536]{1,0:T(8,128)(2,1)}, u32[]{:S(2)}) copy-start(bf16[256,1536]{1,0:T(8,128)(2,1)} %get-tuple-element.69) | copy-start | bytes 2359300
  461.8 3.6 copy-start.5
  461.8 3.6 copy-start.7
  469.0 149.9 %reduce-scatter.29.cloned.1.call-start = ((), (), s32[]{:S(2)}) async-start(), calls=%async_computation.14 | async-start | bytes 10616832
  489.7 0.9 copy-start.2
  489.7 145.8 %reduce-scatter.33.cloned.1.call-start = ((), (), s32[]{:S(2)}) async-start(), calls=%async_computation.16 | async-start | bytes 1327104
  493.1 2.0 copy-start.17
  495.1 195.4 %reduce-scatter.27.cloned.1.call-start = ((), (), s32[]{:S(2)}) async-start(), calls=%async_computation.13 | async-start | bytes 5308416
  495.2 3.5 copy-start.13
  495.2 3.5 copy-start.16
  498.7 1.5 copy-start.15
  500.1 1.9 copy-start.12
  500.1 2.1 copy-start.14
  512.7 233.4 %reduce-scatter.35.cloned.1.call-start = ((), (), s32[]{:S(2)}) async-start(), calls=%async_computation.17 | async-start | bytes 5308416
  528.6 317.8 %reduce-scatter.23.cloned.1.call-start = ((), (), s32[]{:S(2)}) async-start(), calls=%async_computation.11 | async-start | bytes 10616832 | tf_op jit(solution)/shard_map/reduce_scatter | solution.py:643
  544.5 332.5 %reduce-scatter.21.cloned.1.call-start = ((), (), s32[]{:S(2)}) async-start(), calls=%async_computation.10 | async-start | bytes 1474560 | tf_op jit(solution)/shard_map/reduce_scatter | solution.py:643
  552.6 1.7 copy-start.3
  554.3 39.8 %copy-start.6 = (f32[256,1536]{1,0:T(8,128)S(1)}, f32[256,1536]{1,0:T(8,128)}, u32[]{:S(2)}) copy-start(f32[256,1536]{1,0:T(8,128)} %get-tuple-element.52.after2_ref) | copy-start | bytes 4718596
  555.7 20.6 %collective-permute-start = (bf16[256,1536]{1,0:T(8,128)(2,1)}, bf16[256,1536]{1,0:T(8,128)(2,1)S(1)}, u32[]{:S(2)}, u32[]{:S(2)}) collective-permute-start(bf16[256,1536]{1,0:T(8,128)(2,1)} %get-tuple-element.128), channel_id=1, source_target_pairs={{0,1},{1,0},{2,3},{3,2},{4,5},{5,4},{6,7},{7,6},{8,9},{9,8},{10,11... | collective-permute-start | bytes 2359304 | tf_op jit(solution)/shard_map/ppermute | solution.py:650
  556.8 35.4 %collective-permute-start.1 = (bf16[256,1536]{1,0:T(8,128)(2,1)}, bf16[256,1536]{1,0:T(8,128)(2,1)}, u32[]{:S(2)}, u32[]{:S(2)}) collective-permute-start(bf16[256,1536]{1,0:T(8,128)(2,1)} %get-tuple-element.130), channel_id=1, source_target_pairs={{0,2},{1,3},{2,0},{3,1},{4,6},{5,7},{6,4},{7,5},{8,10},{9,11},{10,... | collective-permute-start | bytes 2359304 | tf_op jit(solution)/shard_map/ppermute | solution.py:650
  557.8 34.4 %collective-permute-start.2 = (bf16[256,1536]{1,0:T(8,128)(2,1)}, bf16[256,1536]{1,0:T(8,128)(2,1)}, u32[]{:S(2)}, u32[]{:S(2)}) collective-permute-start(bf16[256,1536]{1,0:T(8,128)(2,1)} %get-tuple-element.129), channel_id=1, source_target_pairs={{0,3},{1,2},{2,1},{3,0},{4,7},{5,6},{6,5},{7,4},{8,11},{9,10},{10,... | collective-permute-start | bytes 2359304 | tf_op jit(solution)/shard_map/ppermute | solution.py:650
  597.4 20.6 %collective-permute-start.3 = (bf16[256,1536]{1,0:T(8,128)(2,1)}, bf16[256,1536]{1,0:T(8,128)(2,1)S(1)}, u32[]{:S(2)}, u32[]{:S(2)}) collective-permute-start(bf16[256,1536]{1,0:T(8,128)(2,1)} %get-tuple-element.125), channel_id=1, source_target_pairs={{0,1},{1,0},{2,3},{3,2},{4,5},{5,4},{6,7},{7,6},{8,9},{9,8},{10,11... | collective-permute-start | bytes 2359304 | tf_op jit(solution)/shard_map/ppermute | solution.py:650
  598.7 32.6 %collective-permute-start.4 = (bf16[256,1536]{1,0:T(8,128)(2,1)}, bf16[256,1536]{1,0:T(8,128)(2,1)}, u32[]{:S(2)}, u32[]{:S(2)}) collective-permute-start(bf16[256,1536]{1,0:T(8,128)(2,1)} %get-tuple-element.125), channel_id=1, source_target_pairs={{0,2},{1,3},{2,0},{3,1},{4,6},{5,7},{6,4},{7,5},{8,10},{9,11},{10,... | collective-permute-start | bytes 2359304 | tf_op jit(solution)/shard_map/ppermute | solution.py:650
  602.5 30.9 %collective-permute-start.5 = (bf16[256,1536]{1,0:T(8,128)(2,1)}, bf16[256,1536]{1,0:T(8,128)(2,1)}, u32[]{:S(2)}, u32[]{:S(2)}) collective-permute-start(bf16[256,1536]{1,0:T(8,128)(2,1)} %get-tuple-element.125), channel_id=1, source_target_pairs={{0,3},{1,2},{2,1},{3,0},{4,7},{5,6},{6,5},{7,4},{8,11},{9,10},{10,... | collective-permute-start | bytes 2359304 | tf_op jit(solution)/shard_map/ppermute | solution.py:650
  880.3 6.0 copy-start.1
Sparse Core Ops, SparseCore 0:
  13.5 100.5 all-gather.2
  116.0 56.9 all-gather.4
  307.9 38.1 reduce-scatter.30
  469.1 31.7 reduce-scatter.24
  503.1 97.7 reduce-scatter.28
  603.6 31.4 reduce-scatter.32
  637.4 53.0 reduce-scatter.26
  692.8 53.3 reduce-scatter.34
  748.5 97.8 reduce-scatter.22
  849.7 27.1 reduce-scatter.20

commit v2 on v1

--- a/solution.py
+++ b/solution.py
@@ -41,7 +41,7 @@
 
 
 def cost(flops, nbytes, trans=0):
-    return pl.CostEstimate(flops=int(flops), bytes_accessed=int(nbytes), transcendentals=int(trans))
+    return pl.CostEstimate(flops=1000, bytes_accessed=1000, transcendentals=0)
 
 
 def unit(x):
@@ -366,44 +366,121 @@
     )(h, gb, wg, wu, wd)
 
 
-def gather_kernel(n, x_in, w_ref, x_ref, da_ref, ss, rs):
+def feed_kernel(h_ref, gb_ref, dgu_ref, hid_ref, o_ref, od_ref):
+    F2 = dgu_ref.shape[1]
+    h, gb = h_ref[...], gb_ref[...]
+    tf = 512
+
+    def feed(j, carry):
+        cols = pl.ds(pl.multiple_of(j * tf, tf), tf)
+        o_ref[:, cols] = tn(h, dgu_ref[:, cols]).astype(BF)
+        return carry
+
+    def down(j, carry):
+        cols = pl.ds(pl.multiple_of(j * tf, tf), tf)
+        od_ref[:, cols] = tn(gb, hid_ref[:, cols]).astype(BF)
+        return carry
+
+    lax.fori_loop(0, F2 // tf, feed, 0)
+    lax.fori_loop(0, F2 // 2 // tf, down, 0)
+
+
+def feed_grads(h, gb, dgu, hidden):
+    T, D = h.shape
+    F = hidden.shape[1]
+    tb = 256
+    cols = pl.BlockSpec((T, tb), lambda i: (0, i))
+    full = lambda a: pl.BlockSpec(a.shape, lambda i: (0, 0), pipeline_mode=pl.Buffered(1))
+    return pl.pallas_call(
+        feed_kernel,
+        grid=(D // tb,),
+        in_specs=[cols, cols, full(dgu), full(hidden)],
+        out_specs=[pl.BlockSpec((tb, 2 * F), lambda i: (i, 0)), pl.BlockSpec((tb, F), lambda i: (i, 0))],
+        out_shape=[sds((D, 2 * F), BF), sds((D, F), BF)],
+        compiler_params=params(),
+        cost_estimate=cost(6 * T * D * F, 6 * D * F),
+        name="feed_grads",
+    )(h, gb, dgu, hidden)
+
+
+def shard_of(ref, t, n, width):
+    if width % 128 == 0:
+        return ref[:, pl.ds(pl.multiple_of(t * width, width), width)]
+    out = ref[:, :width]
+    for i in range(1, n):
+        out = jnp.where(t == i, ref[:, i * width : (i + 1) * width], out)
+    return out
+
+
+def gather_kernel(n, ndp, x_in, w_ref, h2_ref, dcq_ref, cb_ref, ca_ref, dck_ref, dcv_ref, ctx_ref,
+                  x_ref, da_ref, gr_ref, ksend, krecv, ss, rs, ss2, rs2):
     me = lax.axis_index("tensor")
-    C = x_in.shape[0]
+    C, D = x_in.shape
+    HD = dcq_ref.shape[1]
+    W = w_ref.shape[0]
+    KP = dck_ref.shape[0]
     greet(n, me)
     gather = {}
     for d in range(1, n):
         gather[d] = remote(x_in, x_ref.at[me], ss.at[d - 1], rs.at[d - 1], me ^ d)
         gather[d].start()
+    kv = {}
+    for d in range(1, n):
+        ksend[d - 1, :KP] = shard_of(dck_ref, me ^ d, n, W).astype(BF)
+        ksend[d - 1, KP:] = shard_of(dcv_ref, me ^ d, n, W).astype(BF)
+        kv[d] = remote(ksend.at[d - 1], krecv.at[d - 1], ss2.at[d - 1], rs2.at[d - 1], me ^ d)
+        kv[d].start()
 
     def back(t, x):
         da_ref[pl.ds(pl.multiple_of(t * C, C), C), :] = nt(x, w_ref[...]).astype(BF)
 
     x_ref[me] = x_in[...]
     back(me, x_in[...])
+    tf = 256
+
+    def weights(j, carry):
+        rows = pl.ds(pl.multiple_of(j * tf, tf), tf)
+        gr_ref[rows, :HD] = tn(h2_ref[:, rows], dcq_ref[...]).astype(BF)
+        gr_ref[rows, HD : 2 * HD] = tn(cb_ref[:, rows], ca_ref[...]).astype(BF)
+        return carry
+
+    lax.fori_loop(0, D // tf, weights, 0)
+    dk, dv = shard_of(dck_ref, me, n, W), shard_of(dcv_ref, me, n, W)
+    for d in range(1, n):
+        kv[d].wait_recv()
+        dk = dk + krecv[d - 1, :KP].astype(F32)
+        dv = dv + krecv[d - 1, KP:].astype(F32)
+    for half, g in enumerate((dk, dv)):
+        kvg = tn(ctx_ref[...], g.astype(BF)).astype(BF)
+        R = kvg.shape[0] // ndp
+        for i in range(ndp):
+            gr_ref[(2 * i + half) * R : (2 * i + half + 1) * R, 2 * HD :] = kvg[i * R : (i + 1) * R]
     for d in range(1, n):
         gather[d].wait_recv()
         back(me ^ d, x_ref[me ^ d])
     for d in range(1, n):
         gather[d].wait_send()
-
-
-def gather_back(n, x, w):
+        kv[d].wait_send()
+
+
+def gather_back(n, ndp, x, w, h2, dcq, cb, ca, dck, dcv, ctx):
     C, D = x.shape
-    W = w.shape[0]
-    return pl.pallas_call(
-        functools.partial(gather_kernel, n),
-        in_specs=[VSPEC] * 2,
-        out_specs=[VSPEC] * 2,
-        out_shape=[sds((n, C, D), BF), sds((n * C, W), BF)],
-        scratch_shapes=[pltpu.SemaphoreType.DMA((n - 1,))] * 2,
+    W, HD = w.shape[0], dcq.shape[1]
+    KP = dck.shape[0]
+    return pl.pallas_call(
+        functools.partial(gather_kernel, n, ndp),
+        in_specs=[VSPEC] * 9,
+        out_specs=[VSPEC] * 3,
+        out_shape=[sds((n, C, D), BF), sds((n * C, W), BF), sds((D, 2 * HD + W), BF)],
+        scratch_shapes=[pltpu.VMEM((n - 1, 2 * KP, W), BF)] * 2 + [pltpu.SemaphoreType.DMA((n - 1,))] * 4,
         compiler_params=params(collective_id=2, has_side_effects=True),
         cost_estimate=cost(2 * n * C * W * D + 2e10, 8 * C * D),
         name="gather_back",
-    )(x, w)
-
-
-def last_kernel(n, dq_ref, dk_ref, dv_ref, wq_ref, wk_ref, wv_ref, x_ref, da_ref, g_ref, gg_in,
-                out_ref, gg_ref, sbuf, rbuf, lbuf, gbuf, gsum, ss, rs, ss2, rs2, ss3, rs3):
+    )(x, w, h2, dcq, cb, ca, dck, dcv, ctx)
+
+
+def last_kernel(n, dq_ref, dk_ref, dv_ref, wq_ref, wk_ref, wv_ref, x_ref, da_ref, g_ref, gg_in, h1_ref, sb_ref, at_ref,
+                out_ref, gg_ref, gr_ref, sbuf, rbuf, lbuf, gbuf, gsum, ss, rs, ss2, rs2, ss3, rs3):
     me = lax.axis_index("tensor")
     C, D = x_ref.shape
     greet(n, me)
@@ -419,6 +496,18 @@
         copies[d] = remote(sbuf.at[d - 1], rbuf.at[d - 1], ss.at[d - 1], rs.at[d - 1], t)
         copies[d].start()
     total = part(me)
+    W = dq_ref.shape[1]
+    tf = 256
+
+    def weights(j, carry):
+        rows = pl.ds(pl.multiple_of(j * tf, tf), tf)
+        h = h1_ref[:, rows]
+        for i, a_ref in enumerate((dq_ref, dk_ref, dv_ref)):
+            gr_ref[rows, i * W : (i + 1) * W] = tn(h, a_ref[...]).astype(BF)
+        gr_ref[rows, 3 * W :] = tn(sb_ref[:, rows], at_ref[...]).astype(BF)
+        return carry
+
+    lax.fori_loop(0, D // tf, weights, 0)
     u, inverse = unit(x_ref[...].astype(F32))
     for d in range(1, n):
         copies[d].wait_recv()
@@ -453,14 +542,14 @@
         small[d].wait_send()
 
 
-def last(n, dq, dk, dv, wq, wk, wv, x, da, gain, gains):
+def last(n, dq, dk, dv, wq, wk, wv, x, da, gain, gains, h1, sb, attn):
     C, D = x.shape
     T, W = dq.shape
     return pl.pallas_call(
         functools.partial(last_kernel, n),
-        in_specs=[VSPEC] * 10,
-        out_specs=[VSPEC] * 2,
-        out_shape=[sds((T, D), F32), sds((8, D), F32)],
+        in_specs=[VSPEC] * 13,
+        out_specs=[VSPEC] * 3,
+        out_shape=[sds((T, D), F32), sds((8, D), F32), sds((D, 4 * W), BF)],
         scratch_shapes=[
             pltpu.VMEM((n - 1, C, D), BF),
             pltpu.VMEM((n - 1, C, D), BF),
@@ -472,7 +561,7 @@
         compiler_params=params(collective_id=3, has_side_effects=True),
         cost_estimate=cost(6 * T * W * D + 4e10, 8 * T * D),
         name="last",
-    )(dq, dk, dv, wq, wk, wv, x, da, gain, gains)
+    )(dq, dk, dv, wq, wk, wv, x, da, gain, gains, h1, sb, attn)
 
 
 def cross_fwd_kernel(ctx, h_ref, x_ref, wq_ref, k_ref, v_ref, wo_ref, g_ref, q_ref, o_ref, after_ref, h3_ref):
@@ -609,7 +698,7 @@
     )(dh3, after2, cot, g3, wo, q, k, v, wq, after1, g2)
 
 
-def body(latents, context, cotangent, g1, wq, wk, wv, wo, g2, xq, xk, xv, xo, g3, wg, wu, wd, n):
+def body(latents, context, cotangent, g1, wq, wk, wv, wo, g2, xq, xk, xv, xo, g3, wg, wu, wd, n, ndp):
     _, T, D = latents.shape
     ctx = context.shape[1]
     W = wq.shape[1]
@@ -640,12 +729,25 @@
     h3 = h3.reshape(T, D)
 
     def scatter(a, axis):
-        return lax.psum_scatter(a.astype(BF), axis, scatter_dimension=0, tiled=True)
-
-    down_grad = scatter(tn(gb, hidden), "dp").astype(F32).T
-    gu_grad = scatter(tn(h3, dgu), "dp").astype(F32)
-    gate_grad, up_grad = gu_grad[:, :F], gu_grad[:, F:]
-
+        return lax.psum_scatter(a, axis, scatter_dimension=0, tiled=True)
+
+    gu_part, down_part = feed_grads(h3, gb, dgu, hidden)
+    dh3, gu_part, down_part = lax.optimization_barrier((dh3, gu_part, down_part))
+    gu_grad = scatter(gu_part, "dp")
+    down_grad = scatter(down_part, "dp")
+
+    cb, dcq, dck, dcv, dafter1, sb_own, gains = cross_bwd(
+        ctx, dh3, after2, own(gb), g3, xo_all, cq, ck_all, cv_all, xq_all, after1, g2
+    )
+    sb, dattn, cross_grads = gather_back(
+        n, ndp, sb_own, wo, h2, dcq, cb, cattn, dck, dcv, jnp.pad(ctx_rows, pad)
+    )
+    sb = sb.reshape(T, D)
+    dq, dk, dv = attn_bwd(q, k, v, attn, dattn, lse, cs, sn)
+    dq, gu_grad = lax.optimization_barrier((dq, gu_grad))
+    latent_grad, gains, self_grads = last(n, dq, dk, dv, wq, wk, wv, x_own, dafter1, g1, gains, h1, sb, attn)
+
+    hidden, gains = lax.optimization_barrier((hidden, gains))
     terms = nn(hidden, wd).astype(BF).reshape(n, C, D)
     swap = lambda a, d: lax.ppermute(a, "tensor", [(i, i ^ d) for i in range(n)])
     pick = lambda a, t: lax.dynamic_index_in_dim(a, t, 0, keepdims=False)
@@ -658,27 +760,15 @@
     for d in range(1, n):
         block_out = lax.dynamic_update_index_in_dim(block_out, swap(total, d), me ^ d, 0)
 
-    cb, dcq, dck, dcv, dafter1, sb_own, gains = cross_bwd(
-        ctx, dh3, after2, own(gb), g3, xo_all, cq, ck_all, cv_all, xq_all, after1, g2
-    )
-    sb, dattn = gather_back(n, sb_own, wo)
-    sb = sb.reshape(T, D)
-    dq, dk, dv = attn_bwd(q, k, v, attn, dattn, lse, cs, sn)
-    latent_grad, gains = last(n, dq, dk, dv, wq, wk, wv, x_own, dafter1, g1, gains)
-
-    cross_grads = jnp.concatenate([tn(h2, dcq).astype(BF), tn(cb, cattn).astype(BF)], 1)
     cross_grads = scatter(cross_grads, "dp")
+    gains, down_grad, cross_grads, block_out = lax.optimization_barrier((gains, down_grad, cross_grads, block_out))
+    gu_grad = gu_grad.astype(F32)
+    gate_grad, up_grad, down_grad = gu_grad[:, :F], gu_grad[:, F:], down_grad.astype(F32).T
     rows = cross_grads.shape[0]
-    cross_grads = cross_grads.reshape(rows, 2, n, W).transpose(2, 0, 1, 3).reshape(n * rows, 2 * W)
+    kv_grads = cross_grads[:, 2 * n * W :].reshape(2, rows // 2, W).astype(F32)
+    cross_grads = cross_grads[:, : 2 * n * W].reshape(rows, 2, n, W).transpose(2, 0, 1, 3).reshape(n * rows, 2 * W)
     cross_grads = scatter(cross_grads, "tensor").astype(F32)
     xq_grad, xo_grad = cross_grads[:, :W], cross_grads[:, W:].T
-
-    dckv = jnp.concatenate([dck[:ctx], dcv[:ctx]], 0).astype(BF)
-    dckv = lax.psum_scatter(dckv, "tensor", scatter_dimension=1, tiled=True)
-    kv_grads = jnp.concatenate([tn(ctx_rows, dckv[:ctx]), tn(ctx_rows, dckv[ctx:])], 1)
-    kv_grads = scatter(kv_grads, "dp").astype(F32)
-
-    self_grads = jnp.concatenate([tn(h1, dq), tn(h1, dk), tn(h1, dv), tn(sb, attn)], 1)
     self_grads = scatter(self_grads, "dp").astype(F32)
     gains = lax.psum_scatter(gains, "dp", scatter_dimension=1, tiled=True)
     return (
@@ -691,8 +781,8 @@
         self_grads[:, 3 * W :].T,
         gains[1],
         xq_grad,
-        kv_grads[:, :W],
-        kv_grads[:, W:],
+        kv_grads[0],
+        kv_grads[1],
         xo_grad,
         gains[0],
         gate_grad,
@@ -706,7 +796,7 @@
     cols = P(None, "tensor")
     rows = P("tensor", None)
     return jax.shard_map(
-        functools.partial(body, n=mesh.shape["tensor"]),
+        functools.partial(body, n=mesh.shape["tensor"], ndp=mesh.shape["dp"]),
         mesh=mesh,
         in_specs=(tokens, tokens, tokens, P(), cols, cols, cols, rows, P(), cols, cols, cols, rows, P(), cols, cols, rows),
         out_specs=(

time: 903 us -> 738 us (0.82)
  waiting for transfers between devices: 333 us -> 221 us
  local copies, waits for them, and re-layouts: 90.2 us -> 45.4 us
  matrix products: 53.1 us -> 10.5 us
  Pallas kernels: 377 us -> 419 us
    unnamed x16 -> x9, waiting for transfers between devices: 104 us -> 25.1 us
    reduce_scatter x2 -> x5, waiting for transfers between devices: 125 us -> 81.4 us  [scatter(): return lax.psum_scatter(a, axis, scatter_dimension=0, tiled=True)]
    pallas_call x2 -> x3, Pallas kernels: 128 us -> 171 us  [the longest x1 84.8 us: last(): pl.pallas_call(functools.partial(last_kernel, n), in_specs=[VSPEC] * 13,...]
    unnamed x58 -> x34, local copies, waits for them, and re-layouts: 56.5 us -> 13.9 us
    dot_general x10 -> x0, matrix products: 42.4 us -> none  [tn(): lax.dot_general(a, b, (((0,), (0,)), ((), ())), preferred_element_type=F32)]
    ppermute x6, waiting for transfers between devices: 55.3 us -> 66.5 us  [body(): lax.ppermute(a, 'tensor', [(i, i ^ d) for i in range(n)])]
    concatenate x4 -> x0, other arithmetic: 10.5 us -> none  [the longest x1 7.95 us: body(): jnp.concatenate([tn(h2, dcq).astype(BF), tn(cb, cattn).astype(BF)], 1)]
  transfers between devices with their start and end apart: 16 -> 14, of which waited for: 9 -> 9; matrix products, arithmetic and copies ran while one was open for 16% -> 6% of each run, Pallas kernels for 28% -> 40%
where the time goes in v2:
time: 738 us; the launch traced here: 728 us
  Pallas kernels  419 us (57%)
  waiting for transfers between devices  221 us (30%)
  local copies, waits for them, and re-layouts  45.4 us (6%)
  between operations  14.8 us (2%)
  matrix products  10.5 us (1%)
  other arithmetic  9.51 us (1%)
    pallas_call x1, Pallas kernels, last(): pl.pallas_call(functools.partial(last_kernel, n), in_specs=[VSPEC] * 13,...  84.8 us
    reduce_scatter x5, waiting for transfers between devices, scatter(): return lax.psum_scatter(a, axis, scatter_dimension=0, tiled=True)  81.4 us
    pallas_call x1, Pallas kernels, ff(): pl.pallas_call(functools.partial(ff_kernel, n), in_specs=[VSPEC] + [ANYSP...  78.1 us
    pallas_call x1, Pallas kernels, out_rs(): pl.pallas_call(functools.partial(out_rs_kernel, n), in_specs=[VSPEC] * 4,...  69.8 us
    ppermute x6, waiting for transfers between devices, body(): lax.ppermute(a, 'tensor', [(i, i ^ d) for i in range(n)])  66.5 us
    pallas_call x1, Pallas kernels, gather_back(): pl.pallas_call(functools.partial(gather_kernel, n, ndp), in_specs=[VSPEC]...  55.1 us
    all_gather x1, waiting for transfers between devices, body(): xo_all = lax.all_gather(xo, 'tensor', axis=0, tiled=True)  48.4 us
    pallas_call x1, Pallas kernels, feed_grads(): pl.pallas_call(feed_kernel, grid=(D // tb,), in_specs=[cols, cols, full(d...  31.5 us
  transfers between devices with their start and end apart: 14, of which 9 were waited for; matrix products, arithmetic and copies ran while one was open for 6% of the time, Pallas kernels for 40%

profile of v2, /device:TPU:0, one launch (start us, length us, event | category | flops | bytes accessed | tf_op | source)
XLA Modules:
  0.0 727.5 jit_solution(10583045523430919766)
XLA Ops:
  7.2 1.0 copy-done
  8.3 1.2 convolution_convert_fusion.1
  9.5 1.4 convolution_convert_fusion.2
  10.9 2.5 fusion.8
  15.5 1.0 copy.39.c_ref
  16.6 1.0 copy.40.s_ref
  17.6 10.6 %qkv.1 = (bf16[1024,1536]{1,0:T(8,128)(2,1)}, bf16[1024,384]{1,0:T(8,128)(2,1)}, bf16[1024,384]{1,0:T(8,128)(2,1)}, bf16[1024,384]{1,0:T(8,128)(2,1)}) custom-call(bf16[1024,1536]{1,0:T(8,128)(2,1)} %bitcast.58, f32[1,1536]{1,0:T(1,128)} %reshape.96.g_ref, bf16[1536,384]{1,0:T(8,128)(2,1)} %wq_ref.3, bf16[1536,384]{1,0:T(8,128)(2,1)} %wk_ref.3, ...), custom_call_target="tpu_custom_call" | custom-call | flops 1000 | bytes 1000 | tf_op jit(solution)/shard_map/qkv/pallas_call | solution.py:102
  28.2 16.3 %attn_fwd.1 = (bf16[1024,384]{1,0:T(8,128)(2,1)}, f32[3,8,1024]{2,1,0:T(8,128)}) custom-call(bf16[1024,384]{1,0:T(8,128)(2,1)} %get-tuple-element.61.q_ref, bf16[1024,384]{1,0:T(8,128)(2,1)} %get-tuple-element.62.k_ref, bf16[1024,384]{1,0:T(8,128)(2,1)} %get-tuple-element.63.v_ref), custom_call_target="tpu_custom_call" | custom-call | flops 1000 | bytes 1000 | tf_op jit(solution)/shard_map/attn_fwd/pallas_call | solution.py:148
  45.1 2.1 dynamic-slice_bitcast_fusion.4.x_ref
  47.2 69.8 %out_rs.1 = (f32[256,1536]{1,0:T(8,128)}, bf16[256,1536]{1,0:T(8,128)(2,1)}) custom-call(bf16[1024,384]{1,0:T(8,128)(2,1)} %get-tuple-element.64.a_ref.o_ref.at_ref, bf16[384,1536]{1,0:T(8,128)(2,1)} %w_ref.3, bf16[256,1536]{1,0:T(8,128)(2,1)} %dynamic-slice_bitcast_fusion.4.x_ref, f32[1,1536]{1,0:T(1,128)} %reshape.97.g_ref.g2_ref), custom_call_target="tpu_custom_call" | custom-call | flops 1000 | bytes 1000 | tf_op jit(solution)/shard_map/out_rs/pallas_call | solution.py:261
  117.6 4.8 slice.74.wq_ref
  122.4 2.2 fusion.15
  124.6 48.4 %all-gather.5.cloned.1.call-done.wo_ref = bf16[1536,1536]{1,0:T(8,128)(2,1)} async-done(((bf16[384,1536]{1,0:T(8,128)(2,1)}), bf16[1536,1536]{1,0:T(8,128)(2,1)}) %all-gather.5.cloned.1.call-update) | async-done | bytes 4718608 | tf_op jit(solution)/shard_map/all_gather | solution.py:720
  173.0 17.6 %cross_fwd.1 = (bf16[256,1536]{1,0:T(8,128)(2,1)}, bf16[256,1536]{1,0:T(8,128)(2,1)}, f32[256,1536]{1,0:T(8,128)}, bf16[256,1536]{1,0:T(8,128)(2,1)}) custom-call(bf16[256,1536]{1,0:T(8,128)(2,1)} %get-tuple-element.65.h_ref.h2_ref, f32[256,1536]{1,0:T(8,128)} %get-tuple-element.66.x_ref.after1_ref, bf16[1536,1536]{1,0:T(8,128)(2,1)} %slice.74.wq_ref, ...), custom_call_target="tpu_custom_call" | custom-call | flops 1000 | bytes 1000 | tf_op jit(solution)/shard_map/cross_fwd/pallas_call | solution.py:607
  190.6 78.1 %ff.1 = (bf16[4,256,1536]{2,1,0:T(8,128)(2,1)}, bf16[1024,1536]{1,0:T(8,128)(2,1)}, bf16[1024,3072]{1,0:T(8,128)(2,1)}, f32[256,1536]{1,0:T(8,128)}) custom-call(bf16[256,1536]{1,0:T(8,128)(2,1)} %get-tuple-element.67.h_in, bf16[1024,1536]{1,0:T(8,128)(2,1)} %bitcast.55, bf16[1536,1536]{1,0:T(8,128)(2,1)} %wg_hbm.1, bf16[1536,1536]{1,0:T(8,128)(2,1)} %wu_hbm.1, ...), custom_call_target="tpu_custom_call" | custom-call | flops 1000 | bytes 1000 | tf_op jit(solution)/shard_map/ff/pallas_call | solution.py:348
  268.7 31.5 %feed_grads.1 = (bf16[1536,3072]{1,0:T(8,128)(2,1)}, bf16[1536,1536]{1,0:T(8,128)(2,1)}) custom-call(bf16[1024,1536]{1,0:T(8,128)(2,1)} %bitcast.66, bf16[1024,1536]{1,0:T(8,128)(2,1)} %bitcast.56, bf16[1024,3072]{1,0:T(8,128)(2,1)} %get-tuple-element.71.dgu_ref, bf16[1024,1536]{1,0:T(8,128)(2,1)} %get-tuple-element.98.hid_ref), custom_call_target="tpu_custom_call" | custom-call | flops 1000 | bytes 1000 | tf_op jit(solution)/shard_map/feed_grads/pallas_call | solution.py:394
  301.9 2.1 dynamic-slice_bitcast_fusion.3.cot_ref
  304.0 30.9 %cross_bwd.1 = (bf16[256,1536]{1,0:T(8,128)(2,1)}, bf16[256,1536]{1,0:T(8,128)(2,1)}, f32[144,1536]{1,0:T(8,128)}, f32[144,1536]{1,0:T(8,128)}, f32[256,1536]{1,...) custom-call(f32[256,1536]{1,0:T(8,128)} %get-tuple-element.74.dh3_ref, ...), custom_call_target="tpu_custom_call" | custom-call | flops 1000 | bytes 1000 | tf_op jit(solution)/shard_map/cross_bwd/pallas_call | solution.py:681
  334.9 55.1 %gather_back.1 = (bf16[4,256,1536]{2,1,0:T(8,128)(2,1)}, bf16[1024,384]{1,0:T(8,128)(2,1)}, bf16[1536,3456]{1,0:T(8,128)(2,1)}) custom-call(bf16[256,1536]{1,0:T(8,128)(2,1)} %get-tuple-element.77.x_in, bf16[384,1536]{1,0:T(8,128)(2,1)} %w_ref.3, bf16[256,1536]{1,0:T(8,128)(2,1)} %get-tuple-element.65.h_ref.h2_ref, ...), custom_call_target="tpu_custom_call" | custom-call | flops 1000 | bytes 1000 | tf_op jit(solution)/shard_map/gather_back/pallas_call | solution.py:470
  390.0 24.0 %attn_bwd.1 = (bf16[1024,384]{1,0:T(8,128)(2,1)}, bf16[1024,384]{1,0:T(8,128)(2,1)}, bf16[1024,384]{1,0:T(8,128)(2,1)}) custom-call(bf16[1024,384]{1,0:T(8,128)(2,1)} %get-tuple-element.61.q_ref, bf16[1024,384]{1,0:T(8,128)(2,1)} %get-tuple-element.62.k_ref, bf16[1024,384]{1,0:T(8,128)(2,1)} %get-tuple-element.63.v_ref, ...), custom_call_target="tpu_custom_call" | custom-call | flops 1000 | bytes 1000 | tf_op jit(solution)/shard_map/attn_bwd/pallas_call | solution.py:208
  414.1 84.8 %last.1 = (f32[1024,1536]{1,0:T(8,128)}, f32[8,1536]{1,0:T(8,128)}, bf16[1536,1536]{1,0:T(8,128)(2,1)}) custom-call(bf16[1024,384]{1,0:T(8,128)(2,1)} %get-tuple-element.87.dq_ref, bf16[1024,384]{1,0:T(8,128)(2,1)} %get-tuple-element.88.dk_ref, bf16[1024,384]{1,0:T(8,128)(2,1)} %get-tuple-element.89.dv_ref, bf16[1536,384]{1,0:T(8,128)(2,1)} %wq_ref.3, ...), custom_call_target="tpu_custom_call" | custom-call | flops 1000 | bytes 1000 | tf_op jit(solution)/shard_map/last/pallas_call | solution.py:548
  498.9 7.9 %convolution_convert_fusion = bf16[1024,1536]{1,0:T(8,128)(2,1)S(1)} fusion(bf16[1024,1536]{1,0:T(8,128)(2,1)S(1)} %copy-done.7, bf16[1536,1536]{1,0:T(8,128)(2,1)} %wd_hbm.1), kind=kOutput, calls=%fused_computation.2 | convolution fusion | flops 4833411072 | bytes 11010048 | tf_op jit(solution)/shard_map/dot_general | solution.py:24
  506.8 1.7 copy-done.6
  508.4 1.4 dynamic-slice_bitcast_fusion.2
  509.9 1.7 collective-permute-start.2
  511.6 1.1 collective-permute-start.1
  513.4 18.1 %collective-permute-done.2 = bf16[256,1536]{1,0:T(8,128)(2,1)S(1)} collective-permute-done((bf16[256,1536]{1,0:T(8,128)(2,1)}, bf16[256,1536]{1,0:T(8,128)(2,1)S(1)}, u32[]{:S(2)}, u32[]{:S(2)}) %collective-permute-start.2) | collective-permute-done | bytes 786464 | tf_op jit(solution)/shard_map/ppermute | solution.py:752
  531.4 15.3 %collective-permute-done.1 = bf16[256,1536]{1,0:T(8,128)(2,1)} collective-permute-done((bf16[256,1536]{1,0:T(8,128)(2,1)}, bf16[256,1536]{1,0:T(8,128)(2,1)}, u32[]{:S(2)}, u32[]{:S(2)}) %collective-permute-start.1) | collective-permute-done | bytes 786464 | tf_op jit(solution)/shard_map/ppermute | solution.py:752
  546.9 1.9 broadcast_in_dim.18
  548.8 3.0 bitcast_dynamic-update-slice_fusion.3
  551.8 1.4 collective-permute-start.3
  554.0 1.2 collective-permute-start.5
  555.2 16.9 %collective-permute-done.3 = bf16[256,1536]{1,0:T(8,128)(2,1)S(1)} collective-permute-done((bf16[256,1536]{1,0:T(8,128)(2,1)S(1)}, bf16[256,1536]{1,0:T(8,128)(2,1)S(1)}, u32[]{:S(2)}, u32[]{:S(2)}) %collective-permute-start.3) | collective-permute-done | bytes 786464 | tf_op jit(solution)/shard_map/ppermute | solution.py:752
  572.2 0.9 bitcast_dynamic-update-slice_fusion.2
  573.1 16.1 %collective-permute-done.4 = bf16[256,1536]{1,0:T(8,128)(2,1)S(1)} collective-permute-done((bf16[256,1536]{1,0:T(8,128)(2,1)S(1)}, bf16[256,1536]{1,0:T(8,128)(2,1)S(1)}, u32[]{:S(2)}, u32[]{:S(2)}) %collective-permute-start.4) | collective-permute-done | bytes 786464 | tf_op jit(solution)/shard_map/ppermute | solution.py:752
  590.1 0.9 bitcast_dynamic-update-slice_fusion
  591.0 1.2 copy.44
  594.3 1.2 copy.49
  596.8 1.7 fusion.16
  599.2 1.1 convert_bitcast_fusion
  600.4 23.1 %reduce-scatter.19.cloned.1.call-done = f32[192,8]{1,0:T(8,128)} async-done(((f32[1536,8]{1,0:T(8,128)}), f32[192,8]{1,0:T(8,128)}) %reduce-scatter.19.cloned.1.call-update) | async-done | bytes 6160
  623.5 1.1 fusion.19
  626.6 27.5 %reduce-scatter.17.cloned.1.call-done = bf16[192,768]{1,0:T(8,128)(2,1)} async-done(((bf16[768,768]{1,0:T(8,128)(2,1)}), bf16[192,768]{1,0:T(8,128)(2,1)}) %reduce-scatter.17.cloned.1.call-update) | async-done | bytes 294928 | tf_op jit(solution)/shard_map/reduce_scatter | solution.py:732
  654.1 1.6 slice.83
  655.7 1.0 convert_element_type.56
  657.5 53.8 %reduce-scatter.15.cloned.1.call-done = bf16[192,1536]{1,0:T(8,128)(2,1)} async-done(((bf16[1536,1536]{1,0:T(8,128)(2,1)}), bf16[192,1536]{1,0:T(8,128)(2,1)}) %reduce-scatter.15.cloned.1.call-update) | async-done | bytes 589840 | tf_op jit(solution)/shard_map/reduce_scatter | solution.py:732
  711.3 1.3 convert_element_type.55
  714.2 6.0 copy.55
  (72 shorter events, 16.0 us)
Async XLA Ops:
  7.2 1.1 copy-start
  7.2 110.4 %all-gather.3.cloned.1.call-start = ((), (), s32[]{:S(2)}) async-start(), calls=%async_computation.6 | async-start | bytes 7004160 | tf_op jit(solution)/shard_map/all_gather | solution.py:719
  10.9 3.3 copy-start.11
  13.4 159.6 %all-gather.5.cloned.1.call-start = ((), (), s32[]{:S(2)}) async-start(), calls=%async_computation.7 | async-start | bytes 5898240 | tf_op jit(solution)/shard_map/all_gather | solution.py:720
  14.2 399.9 %reduce-scatter.9.cloned.1.call-start = ((), (), s32[]{:S(2)}) async-start(), calls=%async_computation.8 | async-start | bytes 10616832 | tf_op jit(solution)/shard_map/reduce_scatter | solution.py:732
  17.6 26.9 %copy-start.12 = (f32[1536]{0:T(1024)S(1)}, f32[1536]{0:T(1024)}, u32[]{:S(2)}) copy-start(f32[1536]{0:T(1024)} %param.25) | copy-start | bytes 18436
  28.2 88.8 %copy-start.13 = (f32[1536]{0:T(1024)S(1)}, f32[1536]{0:T(1024)}, u32[]{:S(2)}) copy-start(f32[1536]{0:T(1024)} %param.30) | copy-start | bytes 18436
  300.3 0.9 copy-start.8
  300.3 290.8 %reduce-scatter.11.cloned.1.call-start = ((), (), s32[]{:S(2)}) async-start(), calls=%async_computation.9 | async-start | bytes 5308416 | tf_op jit(solution)/shard_map/reduce_scatter | solution.py:732
  300.9 290.2 %reduce-scatter.13.cloned.1.call-start = ((), (), s32[]{:S(2)}) async-start(), calls=%async_computation.10 | async-start | bytes 11943936 | tf_op jit(solution)/shard_map/reduce_scatter | solution.py:732
  390.0 233.5 %reduce-scatter.19.cloned.1.call-start = ((), (), s32[]{:S(2)}) async-start(), calls=%async_computation.13 | async-start | bytes 884736
  414.1 84.8 %copy-start.7 = (bf16[1024,1536]{1,0:T(8,128)(2,1)S(1)}, bf16[1024,1536]{1,0:T(8,128)(2,1)}, u32[]{:S(2)}) copy-start(bf16[1024,1536]{1,0:T(8,128)(2,1)} %get-tuple-element.98.hid_ref) | copy-start | bytes 9437188
  506.8 1.7 copy-start.6
  508.4 40.3 %copy-start.2 = (f32[256,1536]{1,0:T(8,128)S(1)}, f32[256,1536]{1,0:T(8,128)}, u32[]{:S(2)}) copy-start(f32[256,1536]{1,0:T(8,128)} %get-tuple-element.75.after2_ref) | copy-start | bytes 4718596
  509.9 21.6 %collective-permute-start.2 = (bf16[256,1536]{1,0:T(8,128)(2,1)}, bf16[256,1536]{1,0:T(8,128)(2,1)S(1)}, u32[]{:S(2)}, u32[]{:S(2)}) collective-permute-start(bf16[256,1536]{1,0:T(8,128)(2,1)} %get-tuple-element.111), channel_id=1, source_target_pairs={{0,3},{1,2},{2,1},{3,0},{4,7},{5,6},{6,5},{7,4},{8,11},{9,10},{10,... | collective-permute-start | bytes 2359304 | tf_op jit(solution)/shard_map/ppermute | solution.py:752
  511.6 35.1 %collective-permute-start.1 = (bf16[256,1536]{1,0:T(8,128)(2,1)}, bf16[256,1536]{1,0:T(8,128)(2,1)}, u32[]{:S(2)}, u32[]{:S(2)}) collective-permute-start(bf16[256,1536]{1,0:T(8,128)(2,1)} %get-tuple-element.112), channel_id=1, source_target_pairs={{0,2},{1,3},{2,0},{3,1},{4,6},{5,7},{6,4},{7,5},{8,10},{9,11},{10,... | collective-permute-start | bytes 2359304 | tf_op jit(solution)/shard_map/ppermute | solution.py:752
  512.7 34.2 %collective-permute-start = (bf16[256,1536]{1,0:T(8,128)(2,1)}, bf16[256,1536]{1,0:T(8,128)(2,1)}, u32[]{:S(2)}, u32[]{:S(2)}) collective-permute-start(bf16[256,1536]{1,0:T(8,128)(2,1)} %get-tuple-element.110), channel_id=1, source_target_pairs={{0,1},{1,0},{2,3},{3,2},{4,5},{5,4},{6,7},{7,6},{8,9},{9,8},{10,11... | collective-permute-start | bytes 2359304 | tf_op jit(solution)/shard_map/ppermute | solution.py:752
  551.8 39.3 %copy-start.10 = (f32[8,1536]{1,0:T(8,128)S(1)}, f32[8,1536]{1,0:T(8,128)}, u32[]{:S(2)}) copy-start(f32[8,1536]{1,0:T(8,128)} %get-tuple-element.101) | copy-start | bytes 147460
  551.8 20.4 %collective-permute-start.3 = (bf16[256,1536]{1,0:T(8,128)(2,1)S(1)}, bf16[256,1536]{1,0:T(8,128)(2,1)S(1)}, u32[]{:S(2)}, u32[]{:S(2)}) collective-permute-start(bf16[256,1536]{1,0:T(8,128)(2,1)S(1)} %get-tuple-element.107), channel_id=1, source_target_pairs={{0,1},{1,0},{2,3},{3,2},{4,5},{5,4},{6,7},{7,6},{8,9},{9,8},{10,11... | collective-permute-start | bytes 2359304 | tf_op jit(solution)/shard_map/ppermute | solution.py:752
  553.1 36.0 %collective-permute-start.4 = (bf16[256,1536]{1,0:T(8,128)(2,1)S(1)}, bf16[256,1536]{1,0:T(8,128)(2,1)S(1)}, u32[]{:S(2)}, u32[]{:S(2)}) collective-permute-start(bf16[256,1536]{1,0:T(8,128)(2,1)S(1)} %get-tuple-element.107), channel_id=1, source_target_pairs={{0,2},{1,3},{2,0},{3,1},{4,6},{5,7},{6,4},{7,5},{8,10},{9,11},{10,... | collective-permute-start | bytes 2359304 | tf_op jit(solution)/shard_map/ppermute | solution.py:752
  554.0 36.1 %collective-permute-start.5 = (bf16[256,1536]{1,0:T(8,128)(2,1)S(1)}, bf16[256,1536]{1,0:T(8,128)(2,1)S(1)}, u32[]{:S(2)}, u32[]{:S(2)}) collective-permute-start(bf16[256,1536]{1,0:T(8,128)(2,1)S(1)} %get-tuple-element.107), channel_id=1, source_target_pairs={{0,3},{1,2},{2,1},{3,0},{4,7},{5,6},{6,5},{7,4},{8,11},{9,10},{10,... | collective-permute-start | bytes 2359304 | tf_op jit(solution)/shard_map/ppermute | solution.py:752
  591.0 1.4 slice-start
  592.3 61.8 %reduce-scatter.17.cloned.1.call-start = ((), (), s32[]{:S(2)}) async-start(), calls=%async_computation.12 | async-start | bytes 1474560 | tf_op jit(solution)/shard_map/reduce_scatter | solution.py:732
  595.5 1.3 copy-start.3
  595.5 115.8 %reduce-scatter.15.cloned.1.call-start = ((), (), s32[]{:S(2)}) async-start(), calls=%async_computation.11 | async-start | bytes 5308416 | tf_op jit(solution)/shard_map/reduce_scatter | solution.py:732
  596.3 2.2 copy-start.4
  596.8 2.4 copy-start.9
  711.3 2.0 copy-start.5
  714.2 6.0 copy-start.1
Sparse Core Ops, SparseCore 0:
  13.6 100.5 all-gather.2
  116.0 56.9 all-gather.4
  300.4 99.3 reduce-scatter.8
  402.0 53.3 reduce-scatter.10
  457.5 109.0 reduce-scatter.12
  592.4 31.0 reduce-scatter.18
  627.0 27.0 reduce-scatter.16
  656.4 54.8 reduce-scatter.14

commit v3 on v2

--- a/solution.py
+++ b/solution.py
@@ -80,81 +80,136 @@
     return [jnp.where(lane == h, 1.0, 0.0) for h in range(group // HEAD_DIM)]
 
 
-def qkv_kernel(x_ref, g_ref, wq_ref, wk_ref, wv_ref, c_ref, s_ref, h_ref, q_ref, k_ref, v_ref):
-    u, _ = unit(x_ref[...].astype(F32))
-    h = (u * g_ref[...]).astype(BF)
-    h_ref[...] = h
-    reps = q_ref.shape[1] // c_ref.shape[1]
-    c = jnp.concatenate([c_ref[...]] * reps, 1)
-    s = jnp.concatenate([s_ref[...]] * reps, 1)
-    for w_ref, o_ref in ((wq_ref, q_ref), (wk_ref, k_ref)):
-        a = nn(h, w_ref[...])
-        o_ref[...] = (a * c + turned(a) * s).astype(BF)
-    v_ref[...] = nn(h, wv_ref[...]).astype(BF)
-
-
-def qkv(x, gain, wq, wk, wv, cs, sn):
+def front_kernel(n, ctx, x_ref, g_ref, wq_ref, wk_ref, wv_ref, c_ref, s_ref, xq_ref, xo_ref, ctx_ref, xk_ref, xv_ref,
+                 h_ref, q_ref, k_ref, v_ref, o_ref, lse_ref, xqa_ref, xoa_ref, kva_ref,
+                 kv_own, sq, rq, so, ro, sk, rk, fsq, frq, fso, fro, local):
+    me = lax.axis_index("tensor")
+    dp = lax.axis_index("dp")
+    core = dp % 2
+    partner = dp + 1 - 2 * core
+    T, D = x_ref.shape
+    W = q_ref.shape[1]
+    KP = ctx_ref.shape[0]
+    sem = pltpu.get_barrier_semaphore()
+    for d in range(1, n):
+        pl.semaphore_signal(sem, 1, device_id={"tensor": me ^ d}, device_id_type=MESH_ID)
+    pl.semaphore_signal(sem, 1, device_id={"dp": partner}, device_id_type=MESH_ID)
+    pl.semaphore_wait(sem, n)
+
+    rows_q = pl.ds(pl.multiple_of(core * (D // 2), 16), D // 2)
+    rows_o = pl.ds(pl.multiple_of(core * (W // 2), 16), W // 2)
+    gq, go, gk = {}, {}, {}
+    for d in range(1, n):
+        gq[d] = remote(xq_ref.at[rows_q], xqa_ref.at[me, rows_q], sq.at[d - 1], rq.at[d - 1], me ^ d)
+        gq[d].start()
+    for d in range(1, n):
+        go[d] = remote(xo_ref.at[rows_o], xoa_ref.at[me, rows_o], so.at[d - 1], ro.at[d - 1], me ^ d)
+        go[d].start()
+    own = [
+        pltpu.make_async_copy(xq_ref, xqa_ref.at[me], local.at[0]),
+        pltpu.make_async_copy(xo_ref, xoa_ref.at[me], local.at[1]),
+    ]
+    for copy in own:
+        copy.start()
+    kv_own[:KP] = nn(ctx_ref[...], xk_ref[...]).astype(BF)
+    kv_own[KP:] = nn(ctx_ref[...], xv_ref[...]).astype(BF)
+    for d in range(1, n):
+        gk[d] = remote(kv_own, kva_ref.at[me], sk.at[d - 1], rk.at[d - 1], me ^ d)
+        gk[d].start()
+    kva_ref[me] = kv_own[...]
+
+    tb = 256
+    reps = W // c_ref.shape[1]
+
+    def project(i, carry):
+        rows = pl.ds(pl.multiple_of(i * tb, tb), tb)
+        u, _ = unit(x_ref[rows, :].astype(F32))
+        h = (u * g_ref[...]).astype(BF)
+        h_ref[rows, :] = h
+        c = jnp.concatenate([c_ref[rows, :]] * reps, 1)
+        s = jnp.concatenate([s_ref[rows, :]] * reps, 1)
+        for w_ref, out_ref in ((wq_ref, q_ref), (wk_ref, k_ref)):
+            a = nn(h, w_ref[...])
+            out_ref[rows, :] = (a * c + turned(a) * s).astype(BF)
+        v_ref[rows, :] = nn(h, wv_ref[...]).astype(BF)
+        return carry
+
+    lax.fori_loop(0, T // tb, project, 0)
+
+    G = lane_group(W)
+    mult = SCALE * LOG2E
+    masks = [m.astype(BF) for m in head_masks(1, G)]
+    lane = lax.broadcasted_iota(jnp.int32, (tb, G), 1) // HEAD_DIM
+    stat_lane = lax.broadcasted_iota(jnp.int32, (tb, 128), 1)
+
+    def heads(g, carry):
+        cols = pl.ds(pl.multiple_of(g * G, G), G) if G < W else slice(None)
+        k, v = k_ref[:, cols], v_ref[:, cols]
+
+        def block(i, inner):
+            rows = pl.ds(pl.multiple_of(i * tb, tb), tb)
+            q = q_ref[rows, cols]
+            out = jnp.zeros((tb, G), F32)
+            stats = jnp.zeros((tb, 128), F32)
+            for h in range(G // HEAD_DIM):
+                s = nt(q * masks[h], k)
+                top = jnp.max(s, axis=-1, keepdims=True) * mult
+                p = jnp.exp2(s * mult - top)
+                total = jnp.sum(p, axis=-1, keepdims=True)
+                o = nn(p.astype(BF), v) / total
+                out = jnp.where(lane == h, o, out)
+                stats = jnp.where(stat_lane == h, top + jnp.log2(total), stats)
+            o_ref[rows, cols] = out.astype(BF)
+            lse_ref[g, :, rows] = jnp.transpose(stats)[:8]
+            return inner
+
+        return lax.fori_loop(0, T // tb, block, carry)
+
+    lax.fori_loop(0, W // G, heads, 0)
+
+    def pass_on(ref, rows, send, recv, t):
+        return pltpu.make_async_remote_copy(
+            ref.at[t, rows], ref.at[t, rows], send, recv, device_id={"dp": partner}, device_id_type=MESH_ID
+        )
+
+    fq, fo = {}, {}
+    for d in range(1, n):
+        gq[d].wait_recv()
+        fq[d] = pass_on(xqa_ref, rows_q, fsq.at[d - 1], frq.at[d - 1], me ^ d)
+        fq[d].start()
+    for d in range(1, n):
+        go[d].wait_recv()
+        fo[d] = pass_on(xoa_ref, rows_o, fso.at[d - 1], fro.at[d - 1], me ^ d)
+        fo[d].start()
+    for copy in own:
+        copy.wait()
+    for d in range(1, n):
+        gk[d].wait_recv()
+        fq[d].wait_recv()
+        fo[d].wait_recv()
+    for d in range(1, n):
+        for copy in (gq[d], go[d], gk[d], fq[d], fo[d]):
+            copy.wait_send()
+
+
+def front(n, ctx, x, gain, wq, wk, wv, cs, sn, xq, xo, ctx_rows, xk, xv):
     T, D = x.shape
     W = wq.shape[1]
-    tb = 256
-    row = lambda n: pl.BlockSpec((tb, n), lambda i: (i, 0))
-    full = lambda a: pl.BlockSpec(a.shape, lambda i: (0, 0), pipeline_mode=pl.Buffered(1))
-    return pl.pallas_call(
-        qkv_kernel,
-        grid=(T // tb,),
-        in_specs=[row(D), full(gain), full(wq), full(wk), full(wv), row(cs.shape[1]), row(cs.shape[1])],
-        out_specs=[row(D), row(W), row(W), row(W)],
-        out_shape=[sds((T, D), BF)] + [sds((T, W), BF)] * 3,
-        compiler_params=params(),
+    KP = ctx_rows.shape[0]
+    groups = W // lane_group(W)
+    dma = pltpu.SemaphoreType.DMA((n - 1,))
+    return pl.pallas_call(
+        functools.partial(front_kernel, n, ctx),
+        in_specs=[VSPEC] * 12,
+        out_specs=[VSPEC] * 6 + [ANYSPEC] * 2 + [VSPEC],
+        out_shape=[sds((T, D), BF)]
+        + [sds((T, W), BF)] * 4
+        + [sds((groups, 8, T), F32), sds((n, D, W), BF), sds((n, W, D), BF), sds((n, 2 * KP, W), BF)],
+        scratch_shapes=[pltpu.VMEM((2 * KP, W), BF)] + [dma] * 10 + [pltpu.SemaphoreType.DMA((2,))],
+        compiler_params=params(collective_id=4, has_side_effects=True),
         cost_estimate=cost(6 * T * D * W, 4 * T * D + 6 * D * W + 6 * T * W),
-        name="qkv",
-    )(x, gain, wq, wk, wv, cs, sn)
-
-
-def attn_fwd_kernel(q_ref, k_ref, v_ref, o_ref, lse_ref):
-    T, G = q_ref.shape
-    qb = 256
-    mult = SCALE * LOG2E
-    k, v = k_ref[...], v_ref[...]
-    masks = [m.astype(BF) for m in head_masks(1, G)]
-    lane = lax.broadcasted_iota(jnp.int32, (qb, G), 1) // HEAD_DIM
-    stat_lane = lax.broadcasted_iota(jnp.int32, (qb, 128), 1)
-
-    def block(i, carry):
-        rows = pl.ds(pl.multiple_of(i * qb, qb), qb)
-        q = q_ref[rows, :]
-        out = jnp.zeros((qb, G), F32)
-        stats = jnp.zeros((qb, 128), F32)
-        for h in range(G // HEAD_DIM):
-            s = nt(q * masks[h], k)
-            top = jnp.max(s, axis=-1, keepdims=True) * mult
-            p = jnp.exp2(s * mult - top)
-            total = jnp.sum(p, axis=-1, keepdims=True)
-            o = nn(p.astype(BF), v) / total
-            out = jnp.where(lane == h, o, out)
-            stats = jnp.where(stat_lane == h, top + jnp.log2(total), stats)
-        o_ref[rows, :] = out.astype(BF)
-        lse_ref[:, rows] = jnp.transpose(stats)[:8]
-        return carry
-
-    lax.fori_loop(0, T // qb, block, 0)
-
-
-def attn_fwd(q, k, v):
-    T, W = q.shape
-    G = lane_group(W)
-    groups = W // G
-    cols = pl.BlockSpec((T, G), lambda i: (0, i))
-    return pl.pallas_call(
-        attn_fwd_kernel,
-        grid=(groups,),
-        in_specs=[cols] * 3,
-        out_specs=[cols, pl.BlockSpec((None, 8, T), lambda i: (i, 0, 0))],
-        out_shape=[sds((T, W), BF), sds((groups, 8, T), F32)],
-        compiler_params=params(),
-        cost_estimate=cost(16 * T * T * W, 8 * T * W, T * T * W // HEAD_DIM),
-        name="attn_fwd",
-    )(q, k, v)
+        name="front",
+    )(x, gain, wq, wk, wv, cs, sn, xq, xo, ctx_rows, xk, xv)
 
 
 def attn_bwd_kernel(q_ref, k_ref, v_ref, o_ref, do_ref, lse_ref, c_ref, s_ref, dq_ref, dk_ref, dv_ref, dk_acc, dv_acc, kt_ref):
@@ -403,22 +458,13 @@
     )(h, gb, dgu, hidden)
 
 
-def shard_of(ref, t, n, width):
-    if width % 128 == 0:
-        return ref[:, pl.ds(pl.multiple_of(t * width, width), width)]
-    out = ref[:, :width]
-    for i in range(1, n):
-        out = jnp.where(t == i, ref[:, i * width : (i + 1) * width], out)
-    return out
-
-
-def gather_kernel(n, ndp, x_in, w_ref, h2_ref, dcq_ref, cb_ref, ca_ref, dck_ref, dcv_ref, ctx_ref,
+def gather_kernel(n, ndp, x_in, w_ref, h2_ref, dcq_ref, cb_ref, ca_ref, dkv_ref, ctx_ref,
                   x_ref, da_ref, gr_ref, ksend, krecv, ss, rs, ss2, rs2):
     me = lax.axis_index("tensor")
     C, D = x_in.shape
-    HD = dcq_ref.shape[1]
     W = w_ref.shape[0]
-    KP = dck_ref.shape[0]
+    HD = n * W
+    KP = ctx_ref.shape[0]
     greet(n, me)
     gather = {}
     for d in range(1, n):
@@ -426,8 +472,7 @@
         gather[d].start()
     kv = {}
     for d in range(1, n):
-        ksend[d - 1, :KP] = shard_of(dck_ref, me ^ d, n, W).astype(BF)
-        ksend[d - 1, KP:] = shard_of(dcv_ref, me ^ d, n, W).astype(BF)
+        ksend[d - 1] = dkv_ref[me ^ d].astype(BF)
         kv[d] = remote(ksend.at[d - 1], krecv.at[d - 1], ss2.at[d - 1], rs2.at[d - 1], me ^ d)
         kv[d].start()
 
@@ -440,18 +485,19 @@
 
     def weights(j, carry):
         rows = pl.ds(pl.multiple_of(j * tf, tf), tf)
-        gr_ref[rows, :HD] = tn(h2_ref[:, rows], dcq_ref[...]).astype(BF)
-        gr_ref[rows, HD : 2 * HD] = tn(cb_ref[:, rows], ca_ref[...]).astype(BF)
+        h2, cb = h2_ref[:, rows], cb_ref[:, rows]
+        for t in range(n):
+            gr_ref[rows, t * W : (t + 1) * W] = tn(h2, dcq_ref[t]).astype(BF)
+            gr_ref[rows, HD + t * W : HD + (t + 1) * W] = tn(cb, ca_ref[t]).astype(BF)
         return carry
 
     lax.fori_loop(0, D // tf, weights, 0)
-    dk, dv = shard_of(dck_ref, me, n, W), shard_of(dcv_ref, me, n, W)
+    dkv = dkv_ref[me]
     for d in range(1, n):
         kv[d].wait_recv()
-        dk = dk + krecv[d - 1, :KP].astype(F32)
-        dv = dv + krecv[d - 1, KP:].astype(F32)
-    for half, g in enumerate((dk, dv)):
-        kvg = tn(ctx_ref[...], g.astype(BF)).astype(BF)
+        dkv = dkv + krecv[d - 1].astype(F32)
+    for half in range(2):
+        kvg = tn(ctx_ref[...], dkv[half * KP : (half + 1) * KP].astype(BF)).astype(BF)
         R = kvg.shape[0] // ndp
         for i in range(ndp):
             gr_ref[(2 * i + half) * R : (2 * i + half + 1) * R, 2 * HD :] = kvg[i * R : (i + 1) * R]
@@ -463,24 +509,24 @@
         kv[d].wait_send()
 
 
-def gather_back(n, ndp, x, w, h2, dcq, cb, ca, dck, dcv, ctx):
+def gather_back(n, ndp, x, w, h2, dcq, cb, ca, dkv, ctx):
     C, D = x.shape
-    W, HD = w.shape[0], dcq.shape[1]
-    KP = dck.shape[0]
+    W = w.shape[0]
+    KP = ctx.shape[0]
     return pl.pallas_call(
         functools.partial(gather_kernel, n, ndp),
-        in_specs=[VSPEC] * 9,
+        in_specs=[VSPEC] * 8,
         out_specs=[VSPEC] * 3,
-        out_shape=[sds((n, C, D), BF), sds((n * C, W), BF), sds((D, 2 * HD + W), BF)],
+        out_shape=[sds((n, C, D), BF), sds((n * C, W), BF), sds((D, (2 * n + 1) * W), BF)],
         scratch_shapes=[pltpu.VMEM((n - 1, 2 * KP, W), BF)] * 2 + [pltpu.SemaphoreType.DMA((n - 1,))] * 4,
         compiler_params=params(collective_id=2, has_side_effects=True),
         cost_estimate=cost(2 * n * C * W * D + 2e10, 8 * C * D),
         name="gather_back",
-    )(x, w, h2, dcq, cb, ca, dck, dcv, ctx)
+    )(x, w, h2, dcq, cb, ca, dkv, ctx)
 
 
 def last_kernel(n, dq_ref, dk_ref, dv_ref, wq_ref, wk_ref, wv_ref, x_ref, da_ref, g_ref, gg_in, h1_ref, sb_ref, at_ref,
-                out_ref, gg_ref, gr_ref, sbuf, rbuf, lbuf, gbuf, gsum, ss, rs, ss2, rs2, ss3, rs3):
+                lbuf, gr_ref, sbuf, rbuf, gbuf, gsum, ss, rs, ss2, rs2, ss3, rs3):
     me = lax.axis_index("tensor")
     C, D = x_ref.shape
     greet(n, me)
@@ -504,7 +550,7 @@
         h = h1_ref[:, rows]
         for i, a_ref in enumerate((dq_ref, dk_ref, dv_ref)):
             gr_ref[rows, i * W : (i + 1) * W] = tn(h, a_ref[...]).astype(BF)
-        gr_ref[rows, 3 * W :] = tn(sb_ref[:, rows], at_ref[...]).astype(BF)
+        gr_ref[rows, 3 * W : 4 * W] = tn(sb_ref[:, rows], at_ref[...]).astype(BF)
         return carry
 
     lax.fori_loop(0, D // tf, weights, 0)
@@ -524,18 +570,14 @@
         small[d] = remote(gsum, gbuf.at[d - 1], ss3.at[d - 1], rs3.at[d - 1], me ^ d)
         small[d].start()
 
-    def put(t):
-        out_ref[pl.ds(pl.multiple_of(t * C, C), C), :] = lbuf[t].astype(F32)
-
-    put(me)
-    for d in range(1, n):
-        gather[d].wait_recv()
-        put(me ^ d)
     gains = gsum[...]
     for d in range(1, n):
         small[d].wait_recv()
         gains = gains + gbuf[d - 1]
-    gg_ref[...] = gains
+    gains = jnp.concatenate([gains, jnp.zeros((120, D), F32)], 0)
+    gr_ref[:, 4 * W :] = jnp.transpose(gains).astype(BF)
+    for d in range(1, n):
+        gather[d].wait_recv()
     for d in range(1, n):
         copies[d].wait_send()
         gather[d].wait_send()
@@ -548,12 +590,11 @@
     return pl.pallas_call(
         functools.partial(last_kernel, n),
         in_specs=[VSPEC] * 13,
-        out_specs=[VSPEC] * 3,
-        out_shape=[sds((T, D), F32), sds((8, D), F32), sds((D, 4 * W), BF)],
+        out_specs=[VSPEC] * 2,
+        out_shape=[sds((n, C, D), BF), sds((D, 4 * W + 128), BF)],
         scratch_shapes=[
             pltpu.VMEM((n - 1, C, D), BF),
             pltpu.VMEM((n - 1, C, D), BF),
-            pltpu.VMEM((n, C, D), BF),
             pltpu.VMEM((n - 1, 8, D), F32),
             pltpu.VMEM((8, D), F32),
         ]
@@ -564,36 +605,41 @@
     )(dq, dk, dv, wq, wk, wv, x, da, gain, gains, h1, sb, attn)
 
 
-def cross_fwd_kernel(ctx, h_ref, x_ref, wq_ref, k_ref, v_ref, wo_ref, g_ref, q_ref, o_ref, after_ref, h3_ref):
-    C, HD = q_ref.shape
-    KP = k_ref.shape[0]
+def cross_fwd_kernel(n, ctx, h_ref, x_ref, wq_ref, kv_ref, wo_ref, g_ref, q_ref, o_ref, after_ref, h3_ref):
+    _, C, W = q_ref.shape
+    KP = kv_ref.shape[1] // 2
     mult = SCALE * LOG2E
-    G = 128
+    G = lane_group(W)
+    per = W // G
     masks = [m.astype(BF) for m in head_masks(1, G)]
     lane = lax.broadcasted_iota(jnp.int32, (C, G), 1) // HEAD_DIM
     valid = lax.broadcasted_iota(jnp.int32, (C, KP), 1) < ctx
 
     def group(g, carry):
-        cols = pl.ds(pl.multiple_of(g * G, G), G)
-        q = nn(h_ref[...], wq_ref[:, cols]).astype(BF)
-        q_ref[:, cols] = q
-        k, v = k_ref[:, cols], v_ref[:, cols]
+        t = g // per
+        cols = pl.ds(pl.multiple_of(g % per * G, G), G) if per > 1 else slice(None)
+        q = nn(h_ref[...], wq_ref[t, :, cols]).astype(BF)
+        q_ref[t, :, cols] = q
+        k, v = kv_ref[t, :KP, cols], kv_ref[t, KP:, cols]
         out = jnp.zeros((C, G), F32)
         for h in range(G // HEAD_DIM):
             s = jnp.where(valid, nt(q * masks[h], k), -1e30)
             p = jnp.exp2((s - jnp.max(s, axis=-1, keepdims=True)) * mult)
             o = nn(p.astype(BF), v) / jnp.sum(p, axis=-1, keepdims=True)
             out = jnp.where(lane == h, o, out)
-        o_ref[:, cols] = out.astype(BF)
-        return carry
-
-    lax.fori_loop(0, HD // G, group, 0)
+        o_ref[t, :, cols] = out.astype(BF)
+        return carry
+
+    lax.fori_loop(0, n * per, group, 0)
     D = h_ref.shape[1]
     tf = 256
 
     def project(j, carry):
         cols = pl.ds(pl.multiple_of(j * tf, tf), tf)
-        after_ref[:, cols] = x_ref[:, cols] + nn(o_ref[...], wo_ref[:, cols])
+        total = nn(o_ref[0], wo_ref[0, :, cols])
+        for t in range(1, n):
+            total = total + nn(o_ref[t], wo_ref[t, :, cols])
+        after_ref[:, cols] = x_ref[:, cols] + total
         return carry
 
     lax.fori_loop(0, D // tf, project, 0)
@@ -601,27 +647,28 @@
     h3_ref[...] = (u * g_ref[...]).astype(BF)
 
 
-def cross_fwd(ctx, h, x, wq, k, v, wo, gain):
+def cross_fwd(ctx, h, x, wq, kv, wo, gain):
     C, D = h.shape
-    HD = wq.shape[1]
-    return pl.pallas_call(
-        functools.partial(cross_fwd_kernel, ctx),
-        in_specs=[VSPEC] * 7,
+    n, W = wq.shape[0], wq.shape[2]
+    return pl.pallas_call(
+        functools.partial(cross_fwd_kernel, n, ctx),
+        in_specs=[VSPEC] * 6,
         out_specs=[VSPEC] * 4,
-        out_shape=[sds((C, HD), BF), sds((C, HD), BF), sds((C, D), F32), sds((C, D), BF)],
+        out_shape=[sds((n, C, W), BF), sds((n, C, W), BF), sds((C, D), F32), sds((C, D), BF)],
         compiler_params=params(),
-        cost_estimate=cost(4 * C * D * HD + 16 * C * 256 * HD, 8 * D * HD),
+        cost_estimate=cost(4 * C * D * n * W + 16 * C * 256 * n * W, 8 * D * n * W),
         name="cross_fwd",
-    )(h, x, wq, k, v, wo, gain)
-
-
-def cross_bwd_kernel(ctx, dh3_ref, after2_ref, cot_ref, g3_ref, wo_ref, q_ref, k_ref, v_ref, wq_ref, after1_ref, g2_ref,
-                     cb_ref, dq_ref, dk_ref, dv_ref, da_ref, sb_ref, gg_ref, dh2_ref):
-    C, HD = q_ref.shape
-    KP = k_ref.shape[0]
+    )(h, x, wq, kv, wo, gain)
+
+
+def cross_bwd_kernel(n, ctx, dh3_ref, after2_ref, cot_ref, g3_ref, wo_ref, q_ref, kv_ref, wq_ref, after1_ref, g2_ref,
+                     cb_ref, dq_ref, dkv_ref, da_ref, sb_ref, gg_ref, dh2_ref):
+    _, C, W = q_ref.shape
+    KP = kv_ref.shape[1] // 2
     D = da_ref.shape[1]
     mult = SCALE * LOG2E
-    G = 128
+    G = lane_group(W)
+    per = W // G
     masks = [m.astype(BF) for m in head_masks(1, G)]
     lane = lax.broadcasted_iota(jnp.int32, (C, G), 1) // HEAD_DIM
     valid = lax.broadcasted_iota(jnp.int32, (C, KP), 1) < ctx
@@ -633,9 +680,10 @@
     cb_ref[...] = da2.astype(BF)
 
     def group(g, carry):
-        cols = pl.ds(pl.multiple_of(g * G, G), G)
-        do = nt(cb_ref[...], wo_ref[cols, :]).astype(BF)
-        q, k, v = q_ref[:, cols], k_ref[:, cols], v_ref[:, cols]
+        t = g // per
+        cols = pl.ds(pl.multiple_of(g % per * G, G), G) if per > 1 else slice(None)
+        do = nt(cb_ref[...], wo_ref[t, cols, :]).astype(BF)
+        q, k, v = q_ref[t, :, cols], kv_ref[t, :KP, cols], kv_ref[t, KP:, cols]
         dq = jnp.zeros((C, G), F32)
         dk = jnp.zeros((KP, G), F32)
         dv = jnp.zeros((KP, G), F32)
@@ -650,17 +698,20 @@
             dq = jnp.where(lane == h, nn(ds, k), dq)
             dk = dk + tn(ds, qm)
             dv = dv + tn(p.astype(BF), dom)
-        dq_ref[:, cols] = (dq * SCALE).astype(BF)
-        dk_ref[:, cols] = dk * SCALE
-        dv_ref[:, cols] = dv
-        return carry
-
-    lax.fori_loop(0, HD // G, group, 0)
+        dq_ref[t, :, cols] = (dq * SCALE).astype(BF)
+        dkv_ref[t, :KP, cols] = dk * SCALE
+        dkv_ref[t, KP:, cols] = dv
+        return carry
+
+    lax.fori_loop(0, n * per, group, 0)
     tf = 256
 
     def project(j, carry):
         cols = pl.ds(pl.multiple_of(j * tf, tf), tf)
-        dh2_ref[:, cols] = nt(dq_ref[...], wq_ref[cols, :])
+        total = nt(dq_ref[0], wq_ref[0, cols, :])
+        for t in range(1, n):
+            total = total + nt(dq_ref[t], wq_ref[t, cols, :])
+        dh2_ref[:, cols] = total
         return carry
 
     lax.fori_loop(0, D // tf, project, 0)
@@ -674,28 +725,56 @@
     gg_ref[...] = jnp.where(row == 0, gain3, 0.0) + jnp.where(row == 1, gain2, 0.0)
 
 
-def cross_bwd(ctx, dh3, after2, cot, g3, wo, q, k, v, wq, after1, g2):
+def cross_bwd(ctx, dh3, after2, cot, g3, wo, q, kv, wq, after1, g2):
     C, D = after2.shape
-    HD = wq.shape[1]
-    KP = k.shape[0]
-    return pl.pallas_call(
-        functools.partial(cross_bwd_kernel, ctx),
-        in_specs=[VSPEC] * 11,
-        out_specs=[VSPEC] * 7,
+    n, W = wq.shape[0], wq.shape[2]
+    return pl.pallas_call(
+        functools.partial(cross_bwd_kernel, n, ctx),
+        in_specs=[VSPEC] * 10,
+        out_specs=[VSPEC] * 6,
         out_shape=[
             sds((C, D), BF),
-            sds((C, HD), BF),
-            sds((KP, HD), F32),
-            sds((KP, HD), F32),
+            sds((n, C, W), BF),
+            sds(kv.shape, F32),
             sds((C, D), F32),
             sds((C, D), BF),
             sds((8, D), F32),
         ],
         scratch_shapes=[pltpu.VMEM((C, D), F32)],
         compiler_params=params(),
-        cost_estimate=cost(4 * C * D * HD + 40 * C * 256 * HD, 8 * D * HD),
+        cost_estimate=cost(4 * C * D * n * W + 40 * C * 256 * n * W, 8 * D * n * W),
         name="cross_bwd",
-    )(dh3, after2, cot, g3, wo, q, k, v, wq, after1, g2)
+    )(dh3, after2, cot, g3, wo, q, kv, wq, after1, g2)
+
+
+def swap_sum_kernel(n, a_ref, o_ref, rbuf, ss, rs):
+    me = lax.axis_index("tensor")
+    greet(n, me)
+    copies = {}
+    for d in range(1, n):
+        copies[d] = remote(a_ref.at[me ^ d], rbuf.at[d - 1], ss.at[d - 1], rs.at[d - 1], me ^ d)
+        copies[d].start()
+    total = a_ref[me].astype(F32)
+    for d in range(1, n):
+        copies[d].wait_recv()
+        total = total + rbuf[d - 1].astype(F32)
+    o_ref[...] = total
+    for d in range(1, n):
+        copies[d].wait_send()
+
+
+def swap_sum(a):
+    n, R, N = a.shape
+    return pl.pallas_call(
+        functools.partial(swap_sum_kernel, n),
+        in_specs=[VSPEC],
+        out_specs=VSPEC,
+        out_shape=sds((R, N), F32),
+        scratch_shapes=[pltpu.VMEM((n - 1, R, N), BF)] + [pltpu.SemaphoreType.DMA((n - 1,))] * 2,
+        compiler_params=params(collective_id=5, has_side_effects=True),
+        cost_estimate=cost(n * R * N, 8 * R * N),
+        name="swap_sum",
+    )(a)
 
 
 def body(latents, context, cotangent, g1, wq, wk, wv, wo, g2, xq, xk, xv, xo, g3, wg, wu, wd, n, ndp):
@@ -713,18 +792,11 @@
     g1, g2, g3 = (g.reshape(1, D) for g in (g1, g2, g3))
     own = lambda a: lax.dynamic_slice_in_dim(a, me * C, C, 0)
 
-    pad = ((0, KP - ctx), (0, 0))
-    ck = jnp.pad(nn(ctx_rows, xk).astype(BF), pad)
-    cv = jnp.pad(nn(ctx_rows, xv).astype(BF), pad)
-    xq_kv = lax.all_gather(jnp.concatenate([xq, ck, cv], 0), "tensor", axis=1, tiled=True)
-    xo_all = lax.all_gather(xo, "tensor", axis=0, tiled=True)
-    xq_all, ck_all, cv_all = xq_kv[:D], xq_kv[D : D + KP], xq_kv[D + KP :]
-
-    h1, q, k, v = qkv(x, g1, wq, wk, wv, cs, sn)
-    attn, lse = attn_fwd(q, k, v)
+    ctx_pad = jnp.pad(ctx_rows, ((0, KP - ctx), (0, 0)))
+    h1, q, k, v, attn, lse, xq_all, xo_all, kv_all = front(n, ctx, x, g1, wq, wk, wv, cs, sn, xq, xo, ctx_pad, xk, xv)
     x_own = own(x)
     after1, h2 = out_rs(n, attn, wo, x_own, g2)
-    cq, cattn, after2, h3_own = cross_fwd(ctx, h2, after1, xq_all, ck_all, cv_all, xo_all, g3)
+    cq, cattn, after2, h3_own = cross_fwd(ctx, h2, after1, xq_all, kv_all, xo_all, g3)
     h3, hidden, dgu, dh3 = ff(n, h3_own, gb, wg, wu, wd)
     h3 = h3.reshape(T, D)
 
@@ -736,18 +808,17 @@
     gu_grad = scatter(gu_part, "dp")
     down_grad = scatter(down_part, "dp")
 
-    cb, dcq, dck, dcv, dafter1, sb_own, gains = cross_bwd(
-        ctx, dh3, after2, own(gb), g3, xo_all, cq, ck_all, cv_all, xq_all, after1, g2
+    cb, dcq, dckv, dafter1, sb_own, gains = cross_bwd(
+        ctx, dh3, after2, own(gb), g3, xo_all, cq, kv_all, xq_all, after1, g2
     )
-    sb, dattn, cross_grads = gather_back(
-        n, ndp, sb_own, wo, h2, dcq, cb, cattn, dck, dcv, jnp.pad(ctx_rows, pad)
-    )
+    sb, dattn, cross_grads = gather_back(n, ndp, sb_own, wo, h2, dcq, cb, cattn, dckv, ctx_pad)
     sb = sb.reshape(T, D)
     dq, dk, dv = attn_bwd(q, k, v, attn, dattn, lse, cs, sn)
     dq, gu_grad = lax.optimization_barrier((dq, gu_grad))
-    latent_grad, gains, self_grads = last(n, dq, dk, dv, wq, wk, wv, x_own, dafter1, g1, gains, h1, sb, attn)
-
-    hidden, gains = lax.optimization_barrier((hidden, gains))
+    latent_grad, self_grads = last(n, dq, dk, dv, wq, wk, wv, x_own, dafter1, g1, gains, h1, sb, attn)
+    self_grads = scatter(self_grads, "dp")
+
+    hidden, latent_grad = lax.optimization_barrier((hidden, latent_grad))
     terms = nn(hidden, wd).astype(BF).reshape(n, C, D)
     swap = lambda a, d: lax.ppermute(a, "tensor", [(i, i ^ d) for i in range(n)])
     pick = lambda a, t: lax.dynamic_index_in_dim(a, t, 0, keepdims=False)
@@ -761,30 +832,30 @@
         block_out = lax.dynamic_update_index_in_dim(block_out, swap(total, d), me ^ d, 0)
 
     cross_grads = scatter(cross_grads, "dp")
-    gains, down_grad, cross_grads, block_out = lax.optimization_barrier((gains, down_grad, cross_grads, block_out))
+    cross_grads, down_grad, block_out = lax.optimization_barrier((cross_grads, down_grad, block_out))
     gu_grad = gu_grad.astype(F32)
     gate_grad, up_grad, down_grad = gu_grad[:, :F], gu_grad[:, F:], down_grad.astype(F32).T
     rows = cross_grads.shape[0]
     kv_grads = cross_grads[:, 2 * n * W :].reshape(2, rows // 2, W).astype(F32)
-    cross_grads = cross_grads[:, : 2 * n * W].reshape(rows, 2, n, W).transpose(2, 0, 1, 3).reshape(n * rows, 2 * W)
-    cross_grads = scatter(cross_grads, "tensor").astype(F32)
+    cross_grads = cross_grads[:, : 2 * n * W].reshape(rows, 2, n, W).transpose(2, 0, 1, 3).reshape(n, rows, 2 * W)
+    cross_grads = swap_sum(cross_grads)
     xq_grad, xo_grad = cross_grads[:, :W], cross_grads[:, W:].T
-    self_grads = scatter(self_grads, "dp").astype(F32)
-    gains = lax.psum_scatter(gains, "dp", scatter_dimension=1, tiled=True)
+    self_grads = self_grads.astype(F32)
+    gains = self_grads[:, 4 * W :]
     return (
         block_out.reshape(1, T, D),
-        latent_grad.reshape(1, T, D),
-        gains[2],
+        latent_grad.astype(F32).reshape(1, T, D),
+        gains[:, 2],
         self_grads[:, :W],
         self_grads[:, W : 2 * W],
         self_grads[:, 2 * W : 3 * W],
-        self_grads[:, 3 * W :].T,
-        gains[1],
+        self_grads[:, 3 * W : 4 * W].T,
+        gains[:, 1],
         xq_grad,
         kv_grads[0],
         kv_grads[1],
         xo_grad,
-        gains[0],
+        gains[:, 0],
         gate_grad,
         up_grad,
         down_grad,

time: 738 us -> 604 us (0.82)
  waiting for transfers between devices: 221 us -> 74.5 us
  Pallas kernels: 419 us -> 452 us
  local copies, waits for them, and re-layouts: 45.4 us -> 29.2 us
    reduce_scatter x5 -> x4, waiting for transfers between devices: 81.4 us -> 11.4 us  [scatter(): return lax.psum_scatter(a, axis, scatter_dimension=0, tiled=True)]
    pallas_call x4, Pallas kernels: 75.3 us -> 137 us  [the longest x1 72.9 us: front(): pl.pallas_call(functools.partial(front_kernel, n, ctx), in_specs=[VSPEC]...]
    all_gather x2 -> x0, waiting for transfers between devices: 48.4 us -> none  [the longest x1 48.4 us: body(): xo_all = lax.all_gather(xo, 'tensor', axis=0, tiled=True)]
    pallas_call x1, Pallas kernels: 69.8 us -> 41.1 us  [out_rs(): pl.pallas_call(functools.partial(out_rs_kernel, n), in_specs=[VSPEC] * 4,...]
    unnamed x9 -> x4, waiting for transfers between devices: 25.1 us -> 0.75 us
    unnamed x34 -> x22, local copies, waits for them, and re-layouts: 13.9 us -> 3.63 us
    slice x4 -> x1, local copies, waits for them, and re-layouts: 9.85 us -> 0.82 us  [body(): gains[:, 0]]
  transfers between devices with their start and end apart: 14 -> 10, of which waited for: 9 -> 5; matrix products, arithmetic and copies ran while one was open for 6% -> 5% of each run, Pallas kernels for 40% -> 35%
where the time goes in v3:
time: 604 us; the launch traced here: 594 us
  Pallas kernels  452 us (75%)
  waiting for transfers between devices  74.5 us (12%)
  local copies, waits for them, and re-layouts  29.2 us (5%)
  between operations  14.4 us (2%)
  other arithmetic  9.47 us (2%)
  matrix products  7.81 us (1%)
  starting transfers between devices  7.14 us (1%)
    pallas_call x1, Pallas kernels, last(): pl.pallas_call(functools.partial(last_kernel, n), in_specs=[VSPEC] * 13,...  84.3 us
    pallas_call x1, Pallas kernels, ff(): pl.pallas_call(functools.partial(ff_kernel, n), in_specs=[VSPEC] + [ANYSP...  78.2 us
    pallas_call x1, Pallas kernels, front(): pl.pallas_call(functools.partial(front_kernel, n, ctx), in_specs=[VSPEC]...  72.9 us
    ppermute x6, waiting for transfers between devices, body(): lax.ppermute(a, 'tensor', [(i, i ^ d) for i in range(n)])  62.4 us
    pallas_call x1, Pallas kernels, gather_back(): pl.pallas_call(functools.partial(gather_kernel, n, ndp), in_specs=[VSPEC]...  55 us
    pallas_call x1, Pallas kernels, out_rs(): pl.pallas_call(functools.partial(out_rs_kernel, n), in_specs=[VSPEC] * 4,...  41.1 us
    pallas_call x1, Pallas kernels, feed_grads(): pl.pallas_call(feed_kernel, grid=(D // tb,), in_specs=[cols, cols, full(d...  31.4 us
    pallas_call x1, Pallas kernels, cross_bwd(): pl.pallas_call(functools.partial(cross_bwd_kernel, n, ctx), in_specs=[VSP...  30.6 us
  transfers between devices with their start and end apart: 10, of which 5 were waited for; matrix products, arithmetic and copies ran while one was open for 5% of the time, Pallas kernels for 35%

profile of v3, /device:TPU:0, one launch (start us, length us, event | category | flops | bytes accessed | tf_op | source)
XLA Modules:
  0.0 594.1 jit_solution(15789480211543919719)
XLA Ops:
  7.3 1.3 reshape.99.g_ref
  9.2 1.0 copy.34.c_ref
  10.3 1.0 copy.35.s_ref
  12.5 0.7 pad.4.ctx_ref
  13.2 2.6 dynamic-slice_bitcast_fusion.3
  15.8 72.9 %front.1 = (bf16[1024,1536]{1,0:T(8,128)(2,1)}, bf16[1024,384]{1,0:T(8,128)(2,1)}, bf16[1024,384]{1,0:T(8,128)(2,1)}, bf16[1024,384]{1,0:T(8,128)(2,1)}, bf16[10...) custom-call(bf16[1024,1536]{1,0:T(8,128)(2,1)} %bitcast.48, ...), custom_call_target="tpu_custom_call" | custom-call | flops 1000 | bytes 1000 | tf_op jit(solution)/shard_map/front/pallas_call | solution.py:201
  88.7 41.1 %out_rs.1 = (f32[256,1536]{1,0:T(8,128)}, bf16[256,1536]{1,0:T(8,128)(2,1)}) custom-call(bf16[1024,384]{1,0:T(8,128)(2,1)} %get-tuple-element.61.a_ref.o_ref.at_ref, bf16[384,1536]{1,0:T(8,128)(2,1)} %w_ref.3, bf16[256,1536]{1,0:T(8,128)(2,1)} %get-tuple-element.129.x_ref, f32[1,1536]{1,0:T(1,128)} %reshape.101.g_ref.g2_ref), custom_call_target="tpu_custom_call" | custom-call | flops 1000 | bytes 1000 | tf_op jit(solution)/shard_map/out_rs/pallas_call | solution.py:316
  129.8 17.8 %cross_fwd.1 = (bf16[4,256,384]{2,1,0:T(8,128)(2,1)}, bf16[4,256,384]{2,1,0:T(8,128)(2,1)}, f32[256,1536]{1,0:T(8,128)}, bf16[256,1536]{1,0:T(8,128)(2,1)}) custom-call(bf16[256,1536]{1,0:T(8,128)(2,1)} %get-tuple-element.62.h_ref.h2_ref, f32[256,1536]{1,0:T(8,128)} %get-tuple-element.63.x_ref.after1_ref, bf16[4,1536,384]{2,1,0:T(8,128)(2,1)} %get-tuple-element.64.wq_ref, ...), custom_call_target="tpu_custom_call" | custom-call | flops 1000 | bytes 1000 | tf_op jit(solution)/shard_map/cross_fwd/pallas_call | solution.py:653
  147.6 78.2 %ff.1 = (bf16[4,256,1536]{2,1,0:T(8,128)(2,1)}, bf16[1024,1536]{1,0:T(8,128)(2,1)}, bf16[1024,3072]{1,0:T(8,128)(2,1)}, f32[256,1536]{1,0:T(8,128)}) custom-call(bf16[256,1536]{1,0:T(8,128)(2,1)} %get-tuple-element.67.h_in, bf16[1024,1536]{1,0:T(8,128)(2,1)} %bitcast.46, bf16[1536,1536]{1,0:T(8,128)(2,1)} %wg_hbm.1, bf16[1536,1536]{1,0:T(8,128)(2,1)} %wu_hbm.1, ...), custom_call_target="tpu_custom_call" | custom-call | flops 1000 | bytes 1000 | tf_op jit(solution)/shard_map/ff/pallas_call | solution.py:403
  225.8 31.4 %feed_grads.1 = (bf16[1536,3072]{1,0:T(8,128)(2,1)}, bf16[1536,1536]{1,0:T(8,128)(2,1)}) custom-call(bf16[1024,1536]{1,0:T(8,128)(2,1)} %bitcast.54, bf16[1024,1536]{1,0:T(8,128)(2,1)} %bitcast.47, bf16[1024,3072]{1,0:T(8,128)(2,1)} %get-tuple-element.70.dgu_ref, bf16[1024,1536]{1,0:T(8,128)(2,1)} %get-tuple-element.99.hid_ref), custom_call_target="tpu_custom_call" | custom-call | flops 1000 | bytes 1000 | tf_op jit(solution)/shard_map/feed_grads/pallas_call | solution.py:449
  258.1 30.6 %cross_bwd.1 = (bf16[256,1536]{1,0:T(8,128)(2,1)}, bf16[4,256,384]{2,1,0:T(8,128)(2,1)}, f32[4,288,384]{2,1,0:T(8,128)}, f32[256,1536]{1,0:T(8,128)}, bf16[256,1536]{1,0:T(8,128)(2,1)}, /*index=5*/f32[8,1536]{1,0:T(8,128)}) custom-call(f32[256,1536]{1,0:T(8,128)} %get-tuple-element.74.dh3_ref, f32[256,1536]{1,0:T(8,128)} %get-tuple-element.75.after2_ref, ...), custom_call_target="tpu_custom_call" | custom-call | flops 1000 | bytes 1000 | tf_op jit(solution)/shard_map/cross_bwd/pallas_call | solution.py:731
  288.7 55.0 %gather_back.1 = (bf16[4,256,1536]{2,1,0:T(8,128)(2,1)}, bf16[1024,384]{1,0:T(8,128)(2,1)}, bf16[1536,3456]{1,0:T(8,128)(2,1)}) custom-call(bf16[256,1536]{1,0:T(8,128)(2,1)} %get-tuple-element.77.x_in, bf16[384,1536]{1,0:T(8,128)(2,1)} %w_ref.3, bf16[256,1536]{1,0:T(8,128)(2,1)} %get-tuple-element.62.h_ref.h2_ref, ...), custom_call_target="tpu_custom_call" | custom-call | flops 1000 | bytes 1000 | tf_op jit(solution)/shard_map/gather_back/pallas_call | solution.py:516
  343.8 24.0 %attn_bwd.1 = (bf16[1024,384]{1,0:T(8,128)(2,1)}, bf16[1024,384]{1,0:T(8,128)(2,1)}, bf16[1024,384]{1,0:T(8,128)(2,1)}) custom-call(bf16[1024,384]{1,0:T(8,128)(2,1)} %get-tuple-element.84.q_ref, bf16[1024,384]{1,0:T(8,128)(2,1)} %get-tuple-element.85.k_ref, bf16[1024,384]{1,0:T(8,128)(2,1)} %get-tuple-element.86.v_ref, ...), custom_call_target="tpu_custom_call" | custom-call | flops 1000 | bytes 1000 | tf_op jit(solution)/shard_map/attn_bwd/pallas_call | solution.py:263
  367.8 84.3 %last.1 = (bf16[4,256,1536]{2,1,0:T(8,128)(2,1)}, bf16[1536,1664]{1,0:T(8,128)(2,1)}) custom-call(bf16[1024,384]{1,0:T(8,128)(2,1)} %get-tuple-element.91.dq_ref, bf16[1024,384]{1,0:T(8,128)(2,1)} %get-tuple-element.92.dk_ref, bf16[1024,384]{1,0:T(8,128)(2,1)} %get-tuple-element.93.dv_ref, bf16[1536,384]{1,0:T(8,128)(2,1)} %wq_ref.3, ...), custom_call_target="tpu_custom_call" | custom-call | flops 1000 | bytes 1000 | tf_op jit(solution)/shard_map/last/pallas_call | solution.py:590
  452.2 1.9 copy-done.6
  454.1 7.8 %convolution_convert_fusion = bf16[1024,1536]{1,0:T(8,128)(2,1)S(1)} fusion(bf16[1024,1536]{1,0:T(8,128)(2,1)S(1)} %copy-done.6, bf16[1536,1536]{1,0:T(8,128)(2,1)} %wd_hbm.1), kind=kOutput, calls=%fused_computation | convolution fusion | flops 4833411072 | bytes 11010048 | tf_op jit(solution)/shard_map/dot_general | solution.py:24
  462.0 1.7 copy-done.4
  463.6 1.4 dynamic-slice_bitcast_fusion.2
  465.1 1.0 collective-permute-start.2
  466.1 1.2 collective-permute-start.1
  467.3 1.3 collective-permute-start
  468.6 18.0 %collective-permute-done.2 = bf16[256,1536]{1,0:T(8,128)(2,1)S(1)} collective-permute-done((bf16[256,1536]{1,0:T(8,128)(2,1)}, bf16[256,1536]{1,0:T(8,128)(2,1)S(1)}, u32[]{:S(2)}, u32[]{:S(2)}) %collective-permute-start.2) | collective-permute-done | bytes 786464 | tf_op jit(solution)/shard_map/ppermute | solution.py:823
  486.6 15.3 %collective-permute-done.1 = bf16[256,1536]{1,0:T(8,128)(2,1)S(1)} collective-permute-done((bf16[256,1536]{1,0:T(8,128)(2,1)}, bf16[256,1536]{1,0:T(8,128)(2,1)S(1)}, u32[]{:S(2)}, u32[]{:S(2)}) %collective-permute-start.1) | collective-permute-done | bytes 786464 | tf_op jit(solution)/shard_map/ppermute | solution.py:823
  501.9 1.9 broadcast_in_dim.18
  503.8 2.9 bitcast_dynamic-update-slice_fusion.3
  506.7 1.0 collective-permute-start.3
  507.7 0.8 collective-permute-start.4
  508.5 3.6 bitcast_convert_fusion
  512.0 1.7 collective-permute-start.5
  513.8 13.3 %collective-permute-done.3 = bf16[256,1536]{1,0:T(8,128)(2,1)S(1)} collective-permute-done((bf16[256,1536]{1,0:T(8,128)(2,1)S(1)}, bf16[256,1536]{1,0:T(8,128)(2,1)S(1)}, u32[]{:S(2)}, u32[]{:S(2)}) %collective-permute-start.3) | collective-permute-done | bytes 786464 | tf_op jit(solution)/shard_map/ppermute | solution.py:823
  527.1 0.9 bitcast_dynamic-update-slice_fusion.2
  528.0 15.7 %collective-permute-done.4 = bf16[256,1536]{1,0:T(8,128)(2,1)S(1)} collective-permute-done((bf16[256,1536]{1,0:T(8,128)(2,1)S(1)}, bf16[256,1536]{1,0:T(8,128)(2,1)S(1)}, u32[]{:S(2)}, u32[]{:S(2)}) %collective-permute-start.4) | collective-permute-done | bytes 786464 | tf_op jit(solution)/shard_map/ppermute | solution.py:823
  543.8 0.9 bitcast_dynamic-update-slice_fusion.1
  544.7 0.9 bitcast_dynamic-update-slice_fusion
  545.6 1.3 slice-done
  546.9 0.9 reshape.110
  547.8 0.9 copy.40
  548.7 1.6 reshape.111.a_ref
  550.3 1.7 fusion.8
  552.0 16.1 %swap_sum.1 = f32[192,768]{1,0:T(8,128)} custom-call(bf16[4,192,768]{2,1,0:T(8,128)(2,1)} %reshape.111.a_ref), custom_call_target="tpu_custom_call" | custom-call | flops 1000 | bytes 1000 | tf_op jit(solution)/shard_map/swap_sum/pallas_call | solution.py:768
  568.2 0.7 fusion.10
  568.9 1.9 slice_bitcast_fusion.1
  570.8 1.1 convert_bitcast_fusion
  572.0 11.4 %reduce-scatter.11.cloned.1.call-done = bf16[192,1664]{1,0:T(8,128)(2,1)} async-done(((bf16[1536,1664]{1,0:T(8,128)(2,1)}), bf16[192,1664]{1,0:T(8,128)(2,1)}) %reduce-scatter.11.cloned.1.call-update) | async-done | bytes 638992 | tf_op jit(solution)/shard_map/reduce_scatter | solution.py:804
  583.4 1.2 convert_element_type.42
  584.6 0.8 slice_reduce_fusion
  585.4 0.7 slice_bitcast_fusion
  586.2 0.9 fusion.9
  (42 shorter events, 2.9 us)
Async XLA Ops:
  7.2 4.1 copy-start.9
  7.2 4.7 copy-start.10
  7.2 5.3 copy-start.8
  7.2 360.6 %reduce-scatter.9.cloned.1.call-start = ((), (), s32[]{:S(2)}) async-start(), calls=%async_computation.6 | async-start | bytes 10616832 | tf_op jit(solution)/shard_map/reduce_scatter | solution.py:804
  257.3 288.3 %reduce-scatter.7.cloned.1.call-start = ((), (), s32[]{:S(2)}) async-start(), calls=%async_computation.5 | async-start | bytes 5308416 | tf_op jit(solution)/shard_map/reduce_scatter | solution.py:804
  258.0 287.6 %reduce-scatter.5.cloned.1.call-start = ((), (), s32[]{:S(2)}) async-start(), calls=%async_computation.4 | async-start | bytes 11943936 | tf_op jit(solution)/shard_map/reduce_scatter | solution.py:804
  343.7 239.6 %reduce-scatter.11.cloned.1.call-start = ((), (), s32[]{:S(2)}) async-start(), calls=%async_computation.7 | async-start | bytes 5750784 | tf_op jit(solution)/shard_map/reduce_scatter | solution.py:804
  452.2 2.0 copy-start.6
  462.0 1.7 copy-start.4
  463.6 40.1 %copy-start = (f32[256,1536]{1,0:T(8,128)S(1)}, f32[256,1536]{1,0:T(8,128)}, u32[]{:S(2)}) copy-start(f32[256,1536]{1,0:T(8,128)} %get-tuple-element.75.after2_ref) | copy-start | bytes 4718596
  465.1 21.5 %collective-permute-start.2 = (bf16[256,1536]{1,0:T(8,128)(2,1)}, bf16[256,1536]{1,0:T(8,128)(2,1)S(1)}, u32[]{:S(2)}, u32[]{:S(2)}) collective-permute-start(bf16[256,1536]{1,0:T(8,128)(2,1)} %get-tuple-element.112), channel_id=1, source_target_pairs={{0,3},{1,2},{2,1},{3,0},{4,7},{5,6},{6,5},{7,4},{8,11},{9,10},{10,... | collective-permute-start | bytes 2359304 | tf_op jit(solution)/shard_map/ppermute | solution.py:823
  466.1 35.8 %collective-permute-start.1 = (bf16[256,1536]{1,0:T(8,128)(2,1)}, bf16[256,1536]{1,0:T(8,128)(2,1)S(1)}, u32[]{:S(2)}, u32[]{:S(2)}) collective-permute-start(bf16[256,1536]{1,0:T(8,128)(2,1)} %get-tuple-element.113), channel_id=1, source_target_pairs={{0,2},{1,3},{2,0},{3,1},{4,6},{5,7},{6,4},{7,5},{8,10},{9,11},{10,... | collective-permute-start | bytes 2359304 | tf_op jit(solution)/shard_map/ppermute | solution.py:823
  467.3 34.6 %collective-permute-start = (bf16[256,1536]{1,0:T(8,128)(2,1)}, bf16[256,1536]{1,0:T(8,128)(2,1)}, u32[]{:S(2)}, u32[]{:S(2)}) collective-permute-start(bf16[256,1536]{1,0:T(8,128)(2,1)} %get-tuple-element.111), channel_id=1, source_target_pairs={{0,1},{1,0},{2,3},{3,2},{4,5},{5,4},{6,7},{7,6},{8,9},{9,8},{10,11... | collective-permute-start | bytes 2359304 | tf_op jit(solution)/shard_map/ppermute | solution.py:823
  503.8 4.7 copy-start.5
  506.7 20.4 %collective-permute-start.3 = (bf16[256,1536]{1,0:T(8,128)(2,1)S(1)}, bf16[256,1536]{1,0:T(8,128)(2,1)S(1)}, u32[]{:S(2)}, u32[]{:S(2)}) collective-permute-start(bf16[256,1536]{1,0:T(8,128)(2,1)S(1)} %get-tuple-element.110), channel_id=1, source_target_pairs={{0,1},{1,0},{2,3},{3,2},{4,5},{5,4},{6,7},{7,6},{8,9},{9,8},{10,11... | collective-permute-start | bytes 2359304 | tf_op jit(solution)/shard_map/ppermute | solution.py:823
  507.7 36.1 %collective-permute-start.4 = (bf16[256,1536]{1,0:T(8,128)(2,1)S(1)}, bf16[256,1536]{1,0:T(8,128)(2,1)S(1)}, u32[]{:S(2)}, u32[]{:S(2)}) collective-permute-start(bf16[256,1536]{1,0:T(8,128)(2,1)S(1)} %get-tuple-element.110), channel_id=1, source_target_pairs={{0,2},{1,3},{2,0},{3,1},{4,6},{5,7},{6,4},{7,5},{8,10},{9,11},{10,... | collective-permute-start | bytes 2359304 | tf_op jit(solution)/shard_map/ppermute | solution.py:823
  512.0 32.6 %collective-permute-start.5 = (bf16[256,1536]{1,0:T(8,128)(2,1)S(1)}, bf16[256,1536]{1,0:T(8,128)(2,1)S(1)}, u32[]{:S(2)}, u32[]{:S(2)}) collective-permute-start(bf16[256,1536]{1,0:T(8,128)(2,1)S(1)} %get-tuple-element.110), channel_id=1, source_target_pairs={{0,3},{1,2},{2,1},{3,0},{4,7},{5,6},{6,5},{7,4},{8,11},{9,10},{10,... | collective-permute-start | bytes 2359304 | tf_op jit(solution)/shard_map/ppermute | solution.py:823
  545.6 1.3 slice-start
  546.9 3.4 copy-start.1
  550.3 17.8 %copy-start.2 = (bf16[192,3456]{1,0:T(8,128)(2,1)S(1)}, bf16[192,3456]{1,0:T(8,128)(2,1)}, u32[]{:S(2)}) copy-start(bf16[192,3456]{1,0:T(8,128)(2,1)} %reduce-scatter.5.cloned.1.call-done) | copy-start | bytes 3981316
  552.0 18.8 %copy-start.7 = (bf16[192,1536]{1,0:T(8,128)(2,1)S(1)}, bf16[192,1536]{1,0:T(8,128)(2,1)}, u32[]{:S(2)}) copy-start(bf16[192,1536]{1,0:T(8,128)(2,1)} %reduce-scatter.7.cloned.1.call-done) | copy-start | bytes 1769476
  583.4 2.8 copy-start.3
Sparse Core Ops, SparseCore 0:
  257.4 99.5 reduce-scatter.8
  359.3 53.3 reduce-scatter.6
  415.0 109.0 reduce-scatter.4
  526.3 57.0 reduce-scatter.10

commit v4 on v3

--- a/solution.py
+++ b/solution.py
@@ -98,13 +98,14 @@
 
     rows_q = pl.ds(pl.multiple_of(core * (D // 2), 16), D // 2)
     rows_o = pl.ds(pl.multiple_of(core * (W // 2), 16), W // 2)
-    gq, go, gk = {}, {}, {}
-    for d in range(1, n):
-        gq[d] = remote(xq_ref.at[rows_q], xqa_ref.at[me, rows_q], sq.at[d - 1], rq.at[d - 1], me ^ d)
-        gq[d].start()
-    for d in range(1, n):
-        go[d] = remote(xo_ref.at[rows_o], xoa_ref.at[me, rows_o], so.at[d - 1], ro.at[d - 1], me ^ d)
-        go[d].start()
+    def quarter(ref, rows):
+        return lambda t, i: ref.at[t, pl.ds(pl.multiple_of(core * (rows // 2) + i * (rows // 4), 16), rows // 4)]
+
+    gq = Gather(n, me, xq_ref.at[rows_q], lambda t: xqa_ref.at[t, rows_q], quarter(xqa_ref, D), sq, rq)
+    go = Gather(n, me, xo_ref.at[rows_o], lambda t: xoa_ref.at[t, rows_o], quarter(xoa_ref, W), so, ro)
+    gk = Gather(n, me, kv_own, lambda t: kva_ref.at[t], lambda t, i: kva_ref.at[t, pl.ds(i * KP, KP)], sk, rk)
+    gq.start()
+    go.start()
     own = [
         pltpu.make_async_copy(xq_ref, xqa_ref.at[me], local.at[0]),
         pltpu.make_async_copy(xo_ref, xoa_ref.at[me], local.at[1]),
@@ -113,9 +114,7 @@
         copy.start()
     kv_own[:KP] = nn(ctx_ref[...], xk_ref[...]).astype(BF)
     kv_own[KP:] = nn(ctx_ref[...], xv_ref[...]).astype(BF)
-    for d in range(1, n):
-        gk[d] = remote(kv_own, kva_ref.at[me], sk.at[d - 1], rk.at[d - 1], me ^ d)
-        gk[d].start()
+    gk.start()
     kva_ref[me] = kv_own[...]
 
     tb = 256
@@ -135,6 +134,7 @@
         return carry
 
     lax.fori_loop(0, T // tb, project, 0)
+    gq.relay()
 
     G = lane_group(W)
     mult = SCALE * LOG2E
@@ -172,24 +172,25 @@
             ref.at[t, rows], ref.at[t, rows], send, recv, device_id={"dp": partner}, device_id_type=MESH_ID
         )
 
-    fq, fo = {}, {}
-    for d in range(1, n):
-        gq[d].wait_recv()
-        fq[d] = pass_on(xqa_ref, rows_q, fsq.at[d - 1], frq.at[d - 1], me ^ d)
-        fq[d].start()
-    for d in range(1, n):
-        go[d].wait_recv()
-        fo[d] = pass_on(xoa_ref, rows_o, fso.at[d - 1], fro.at[d - 1], me ^ d)
-        fo[d].start()
+    go.relay()
+    gk.relay()
+    passed = []
+    for gather, ref, rows, send, recv in ((gq, xqa_ref, rows_q, fsq, frq), (go, xoa_ref, rows_o, fso, fro)):
+        for d in range(1, n):
+            gather.wait(d)
+            copy = pass_on(ref, rows, send.at[d - 1], recv.at[d - 1], me ^ d)
+            copy.start()
+            passed.append(copy)
     for copy in own:
         copy.wait()
     for d in range(1, n):
-        gk[d].wait_recv()
-        fq[d].wait_recv()
-        fo[d].wait_recv()
-    for d in range(1, n):
-        for copy in (gq[d], go[d], gk[d], fq[d], fo[d]):
-            copy.wait_send()
+        gk.wait(d)
+    for copy in passed:
+        copy.wait_recv()
+    for copy in (gq, go, gk):
+        copy.finish()
+    for copy in passed:
+        copy.wait_send()
 
 
 def front(n, ctx, x, gain, wq, wk, wv, cs, sn, xq, xo, ctx_rows, xk, xv):
@@ -197,7 +198,7 @@
     W = wq.shape[1]
     KP = ctx_rows.shape[0]
     groups = W // lane_group(W)
-    dma = pltpu.SemaphoreType.DMA((n - 1,))
+    link, pair = pltpu.SemaphoreType.DMA((links(n),)), pltpu.SemaphoreType.DMA((n - 1,))
     return pl.pallas_call(
         functools.partial(front_kernel, n, ctx),
         in_specs=[VSPEC] * 12,
@@ -205,7 +206,7 @@
         out_shape=[sds((T, D), BF)]
         + [sds((T, W), BF)] * 4
         + [sds((groups, 8, T), F32), sds((n, D, W), BF), sds((n, W, D), BF), sds((n, 2 * KP, W), BF)],
-        scratch_shapes=[pltpu.VMEM((2 * KP, W), BF)] + [dma] * 10 + [pltpu.SemaphoreType.DMA((2,))],
+        scratch_shapes=[pltpu.VMEM((2 * KP, W), BF)] + [link] * 6 + [pair] * 4 + [pltpu.SemaphoreType.DMA((2,))],
         compiler_params=params(collective_id=4, has_side_effects=True),
         cost_estimate=cost(6 * T * D * W, 4 * T * D + 6 * D * W + 6 * T * W),
         name="front",
@@ -284,6 +285,84 @@
     return pltpu.make_async_remote_copy(src, dst, send, recv, device_id={"tensor": target}, device_id_type=MESH_ID)
 
 
+def links(n):
+    return 4 if n == 4 else n - 1
+
+
+class Gather:
+    def __init__(self, n, me, src, slot, half, ss, rs):
+        self.n, self.me, self.half, self.ss, self.rs = n, me, half, ss, rs
+        self.copies = {
+            d: remote(src, slot(me), ss.at[d - 1], rs.at[d - 1], me ^ d) for d in (range(1, n) if n != 4 else (1, 2))
+        }
+        self.passed = []
+
+    def start(self):
+        for copy in self.copies.values():
+            copy.start()
+
+    def relay(self):
+        if self.n == 4:
+            for i, d in enumerate((1, 2)):
+                self.copies[d].wait_recv()
+                block = self.half(self.me ^ d, i)
+                copy = remote(block, block, self.ss.at[2 + i], self.rs.at[2 + i], self.me ^ (3 - d))
+                copy.start()
+                self.passed.append(copy)
+
+    def wait(self, d):
+        if self.n != 4:
+            self.copies[d].wait_recv()
+        elif d == 3:
+            for copy in self.passed:
+                copy.wait_recv()
+
+    def finish(self):
+        for copy in (*self.copies.values(), *self.passed):
+            copy.wait_send()
+
+
+def reduce_bufs(n, C, D):
+    shape = (6, C, D // 2) if n == 4 else (n - 1, C, D)
+    return [pltpu.VMEM(shape, BF)] * 2 + [pltpu.SemaphoreType.DMA((shape[0],))] * 2
+
+
+def reduce_parts(n, me, part, filler, sbuf, rbuf, ss, rs):
+    copies = {}
+
+    def send(i, val, d):
+        sbuf[i] = val.astype(BF)
+        copies[i] = remote(sbuf.at[i], rbuf.at[i], ss.at[i], rs.at[i], me ^ d)
+        copies[i].start()
+
+    def got(i):
+        copies[i].wait_recv()
+        return rbuf[i].astype(F32)
+
+    if n == 4:
+        across = part(me ^ 3)
+        H = across.shape[1] // 2
+        send(0, across[:, :H], 1)
+        send(2, across[:, H:], 2)
+        one = part(me ^ 1)
+        send(1, one[:, :H], 1)
+        two = part(me ^ 2)
+        send(3, two[:, H:], 2)
+        total = part(me)
+        filler()
+        send(4, two[:, :H] + got(0), 2)
+        send(5, one[:, H:] + got(2), 1)
+        total = jnp.concatenate([total[:, :H] + got(1) + got(4), total[:, H:] + got(3) + got(5)], 1)
+    else:
+        for d in reversed(range(1, n)):
+            send(d - 1, part(me ^ d), d)
+        total = part(me)
+        filler()
+        for d in range(1, n):
+            total = total + got(d - 1)
+    return total, copies
+
+
 def out_rs_kernel(n, a_ref, w_ref, x_ref, g_ref, after_ref, h_ref, sbuf, rbuf, ss, rs):
     me = lax.axis_index("tensor")
     C = x_ref.shape[0]
@@ -292,22 +371,13 @@
     def part(t):
         return nn(a_ref[pl.ds(pl.multiple_of(t * C, C), C), :], w_ref[...])
 
-    copies = {}
-    for d in reversed(range(1, n)):
-        t = me ^ d
-        sbuf[d - 1] = part(t).astype(BF)
-        copies[d] = remote(sbuf.at[d - 1], rbuf.at[d - 1], ss.at[d - 1], rs.at[d - 1], t)
-        copies[d].start()
-    total = part(me)
-    for d in range(1, n):
-        copies[d].wait_recv()
-        total = total + rbuf[d - 1].astype(F32)
+    total, copies = reduce_parts(n, me, part, lambda: None, sbuf, rbuf, ss, rs)
     after = x_ref[...].astype(F32) + total
     after_ref[...] = after
     u, _ = unit(after)
     h_ref[...] = (u * g_ref[...]).astype(BF)
-    for d in range(1, n):
-        copies[d].wait_send()
+    for copy in copies.values():
+        copy.wait_send()
 
 
 def out_rs(n, a, w, x, gain):
@@ -318,7 +388,7 @@
         in_specs=[VSPEC] * 4,
         out_specs=[VSPEC] * 2,
         out_shape=[sds((C, D), F32), sds((C, D), BF)],
-        scratch_shapes=[pltpu.VMEM((n - 1, C, D), BF)] * 2 + [pltpu.SemaphoreType.DMA((n - 1,))] * 2,
+        scratch_shapes=reduce_bufs(n, C, D),
         compiler_params=params(collective_id=0, has_side_effects=True),
         cost_estimate=cost(2 * T * W * D + 2e10, 8 * C * D),
         name="out_rs",
@@ -337,10 +407,8 @@
     for c in loads:
         c.start()
     greet(n, me)
-    gather = {}
-    for d in range(1, n):
-        gather[d] = remote(h_in, h_ref.at[me], ss.at[d - 1], rs.at[d - 1], me ^ d)
-        gather[d].start()
+    gather = Gather(n, me, h_in, lambda t: h_ref.at[t], lambda t, i: h_ref.at[t, pl.ds(i * C // 2, C // 2)], ss, rs)
+    gather.start()
     h_ref[me] = h_in[...]
     for c in loads:
         c.wait()
@@ -376,10 +444,11 @@
         dh_ref[:, cols] = val
 
     chunk(me, store_own)
+    gather.relay()
     copies = {}
     for d in range(1, n):
         t = me ^ d
-        gather[d].wait_recv()
+        gather.wait(d)
 
         def store_sent(cols, val):
             sbuf[d - 1, :, cols] = val.astype(BF)
@@ -387,8 +456,7 @@
         chunk(t, store_sent)
         copies[d] = remote(sbuf.at[d - 1], rbuf.at[d - 1], ss2.at[d - 1], rs2.at[d - 1], t)
         copies[d].start()
-    for d in range(1, n):
-        gather[d].wait_send()
+    gather.finish()
     for d in range(1, n):
         copies[d].wait_recv()
         dh_ref[...] += rbuf[d - 1].astype(F32)
@@ -413,7 +481,8 @@
             pltpu.VMEM((n - 1, C, D), BF),
             pltpu.VMEM((n - 1, C, D), BF),
         ]
-        + [pltpu.SemaphoreType.DMA((n - 1,))] * 4
+        + [pltpu.SemaphoreType.DMA((links(n),))] * 2
+        + [pltpu.SemaphoreType.DMA((n - 1,))] * 2
         + [pltpu.SemaphoreType.DMA((4,))],
         compiler_params=params(collective_id=1, has_side_effects=True),
         cost_estimate=cost(10 * T * D * F + 3e10, 6 * D * F + 8 * T * D),
@@ -421,41 +490,77 @@
     )(h, gb, wg, wu, wd)
 
 
-def feed_kernel(h_ref, gb_ref, dgu_ref, hid_ref, o_ref, od_ref):
-    F2 = dgu_ref.shape[1]
-    h, gb = h_ref[...], gb_ref[...]
-    tf = 512
-
-    def feed(j, carry):
-        cols = pl.ds(pl.multiple_of(j * tf, tf), tf)
-        o_ref[:, cols] = tn(h, dgu_ref[:, cols]).astype(BF)
-        return carry
+def down_kernel(gb_ref, hid_ref, o_ref):
+    gb = gb_ref[...]
+    tf = 512 if hid_ref.shape[1] % 512 == 0 else 256
 
     def down(j, carry):
         cols = pl.ds(pl.multiple_of(j * tf, tf), tf)
-        od_ref[:, cols] = tn(gb, hid_ref[:, cols]).astype(BF)
+        o_ref[:, cols] = tn(gb, hid_ref[:, cols]).astype(BF)
         return carry
 
-    lax.fori_loop(0, F2 // tf, feed, 0)
-    lax.fori_loop(0, F2 // 2 // tf, down, 0)
-
-
-def feed_grads(h, gb, dgu, hidden):
-    T, D = h.shape
+    lax.fori_loop(0, hid_ref.shape[1] // tf, down, 0)
+
+
+def down_grads(gb, hidden):
+    T, D = gb.shape
     F = hidden.shape[1]
     tb = 256
-    cols = pl.BlockSpec((T, tb), lambda i: (0, i))
-    full = lambda a: pl.BlockSpec(a.shape, lambda i: (0, 0), pipeline_mode=pl.Buffered(1))
-    return pl.pallas_call(
-        feed_kernel,
+    return pl.pallas_call(
+        down_kernel,
         grid=(D // tb,),
-        in_specs=[cols, cols, full(dgu), full(hidden)],
-        out_specs=[pl.BlockSpec((tb, 2 * F), lambda i: (i, 0)), pl.BlockSpec((tb, F), lambda i: (i, 0))],
-        out_shape=[sds((D, 2 * F), BF), sds((D, F), BF)],
+        in_specs=[
+            pl.BlockSpec((T, tb), lambda i: (0, i)),
+            pl.BlockSpec(hidden.shape, lambda i: (0, 0), pipeline_mode=pl.Buffered(1)),
+        ],
+        out_specs=pl.BlockSpec((tb, F), lambda i: (i, 0)),
+        out_shape=sds((D, F), BF),
         compiler_params=params(),
-        cost_estimate=cost(6 * T * D * F, 6 * D * F),
+        cost_estimate=cost(2 * T * D * F, 2 * D * F),
+        name="down_grads",
+    )(gb, hidden)
+
+
+def feed_kernel(n, hid_ref, wd_ref, after_ref, h_ref, dgu_ref, out_ref, gr_ref, sbuf, rbuf, ss, rs):
+    me = lax.axis_index("tensor")
+    C, D = after_ref.shape
+    F2 = dgu_ref.shape[1]
+    greet(n, me)
+
+    def part(t):
+        return nn(hid_ref[pl.ds(pl.multiple_of(t * C, C), C), :], wd_ref[...])
+
+    tb, tf = 256, 512
+
+    def tile(j, carry):
+        cols = pl.ds(pl.multiple_of(j * tf, tf), tf)
+        for i in range(D // tb):
+            rows = slice(i * tb, (i + 1) * tb)
+            gr_ref[rows, cols] = tn(h_ref[:, rows], dgu_ref[:, cols]).astype(BF)
+        return carry
+
+    def filler():
+        lax.fori_loop(0, F2 // tf, tile, 0)
+
+    total, copies = reduce_parts(n, me, part, filler, sbuf, rbuf, ss, rs)
+    out_ref[...] = (after_ref[...] + total).astype(BF)
+    for copy in copies.values():
+        copy.wait_send()
+
+
+def feed_grads(n, hidden, wd, after, h, dgu):
+    C, D = after.shape
+    T, F2 = dgu.shape
+    return pl.pallas_call(
+        functools.partial(feed_kernel, n),
+        in_specs=[VSPEC] * 5,
+        out_specs=[VSPEC] * 2,
+        out_shape=[sds((C, D), BF), sds((D, F2), BF)],
+        scratch_shapes=reduce_bufs(n, C, D),
+        compiler_params=params(collective_id=6, has_side_effects=True),
+        cost_estimate=cost(3 * T * D * F2, 6 * D * F2),
         name="feed_grads",
-    )(h, gb, dgu, hidden)
+    )(hidden, wd, after, h, dgu)
 
 
 def gather_kernel(n, ndp, x_in, w_ref, h2_ref, dcq_ref, cb_ref, ca_ref, dkv_ref, ctx_ref,
@@ -466,10 +571,8 @@
     HD = n * W
     KP = ctx_ref.shape[0]
     greet(n, me)
-    gather = {}
-    for d in range(1, n):
-        gather[d] = remote(x_in, x_ref.at[me], ss.at[d - 1], rs.at[d - 1], me ^ d)
-        gather[d].start()
+    gather = Gather(n, me, x_in, lambda t: x_ref.at[t], lambda t, i: x_ref.at[t, pl.ds(i * C // 2, C // 2)], ss, rs)
+    gather.start()
     kv = {}
     for d in range(1, n):
         ksend[d - 1] = dkv_ref[me ^ d].astype(BF)
@@ -492,6 +595,7 @@
         return carry
 
     lax.fori_loop(0, D // tf, weights, 0)
+    gather.relay()
     dkv = dkv_ref[me]
     for d in range(1, n):
         kv[d].wait_recv()
@@ -502,10 +606,10 @@
         for i in range(ndp):
             gr_ref[(2 * i + half) * R : (2 * i + half + 1) * R, 2 * HD :] = kvg[i * R : (i + 1) * R]
     for d in range(1, n):
-        gather[d].wait_recv()
+        gather.wait(d)
         back(me ^ d, x_ref[me ^ d])
-    for d in range(1, n):
-        gather[d].wait_send()
+    gather.finish()
+    for d in range(1, n):
         kv[d].wait_send()
 
 
@@ -518,7 +622,9 @@
         in_specs=[VSPEC] * 8,
         out_specs=[VSPEC] * 3,
         out_shape=[sds((n, C, D), BF), sds((n * C, W), BF), sds((D, (2 * n + 1) * W), BF)],
-        scratch_shapes=[pltpu.VMEM((n - 1, 2 * KP, W), BF)] * 2 + [pltpu.SemaphoreType.DMA((n - 1,))] * 4,
+        scratch_shapes=[pltpu.VMEM((n - 1, 2 * KP, W), BF)] * 2
+        + [pltpu.SemaphoreType.DMA((links(n),))] * 2
+        + [pltpu.SemaphoreType.DMA((n - 1,))] * 2,
         compiler_params=params(collective_id=2, has_side_effects=True),
         cost_estimate=cost(2 * n * C * W * D + 2e10, 8 * C * D),
         name="gather_back",
@@ -535,13 +641,6 @@
         rows = pl.ds(pl.multiple_of(t * C, C), C)
         return nt(dq_ref[rows, :], wq_ref[...]) + nt(dk_ref[rows, :], wk_ref[...]) + nt(dv_ref[rows, :], wv_ref[...])
 
-    copies = {}
-    for d in reversed(range(1, n)):
-        t = me ^ d
-        sbuf[d - 1] = part(t).astype(BF)
-        copies[d] = remote(sbuf.at[d - 1], rbuf.at[d - 1], ss.at[d - 1], rs.at[d - 1], t)
-        copies[d].start()
-    total = part(me)
     W = dq_ref.shape[1]
     tf = 256
 
@@ -553,16 +652,16 @@
         gr_ref[rows, 3 * W : 4 * W] = tn(sb_ref[:, rows], at_ref[...]).astype(BF)
         return carry
 
-    lax.fori_loop(0, D // tf, weights, 0)
+    def filler():
+        lax.fori_loop(0, D // tf, weights, 0)
+
+    total, copies = reduce_parts(n, me, part, filler, sbuf, rbuf, ss, rs)
     u, inverse = unit(x_ref[...].astype(F32))
-    for d in range(1, n):
-        copies[d].wait_recv()
-        total = total + rbuf[d - 1].astype(F32)
     lbuf[me] = (da_ref[...] + norm_back(total, u, inverse, g_ref[...])).astype(BF)
-    gather = {}
-    for d in range(1, n):
-        gather[d] = remote(lbuf.at[me], lbuf.at[me], ss2.at[d - 1], rs2.at[d - 1], me ^ d)
-        gather[d].start()
+    gather = Gather(
+        n, me, lbuf.at[me], lambda t: lbuf.at[t], lambda t, i: lbuf.at[t, pl.ds(i * C // 2, C // 2)], ss2, rs2
+    )
+    gather.start()
     row = lax.broadcasted_iota(jnp.int32, (8, D), 0)
     gsum[...] = gg_in[...] + jnp.where(row == 2, jnp.sum(total * u, axis=0, keepdims=True), 0.0)
     small = {}
@@ -576,11 +675,13 @@
         gains = gains + gbuf[d - 1]
     gains = jnp.concatenate([gains, jnp.zeros((120, D), F32)], 0)
     gr_ref[:, 4 * W :] = jnp.transpose(gains).astype(BF)
-    for d in range(1, n):
-        gather[d].wait_recv()
-    for d in range(1, n):
-        copies[d].wait_send()
-        gather[d].wait_send()
+    gather.relay()
+    for d in range(1, n):
+        gather.wait(d)
+    gather.finish()
+    for copy in copies.values():
+        copy.wait_send()
+    for d in range(1, n):
         small[d].wait_send()
 
 
@@ -592,13 +693,11 @@
         in_specs=[VSPEC] * 13,
         out_specs=[VSPEC] * 2,
         out_shape=[sds((n, C, D), BF), sds((D, 4 * W + 128), BF)],
-        scratch_shapes=[
-            pltpu.VMEM((n - 1, C, D), BF),
-            pltpu.VMEM((n - 1, C, D), BF),
-            pltpu.VMEM((n - 1, 8, D), F32),
-            pltpu.VMEM((8, D), F32),
-        ]
-        + [pltpu.SemaphoreType.DMA((n - 1,))] * 6,
+        scratch_shapes=reduce_bufs(n, C, D)[:2]
+        + [pltpu.VMEM((n - 1, 8, D), F32), pltpu.VMEM((8, D), F32)]
+        + reduce_bufs(n, C, D)[2:]
+        + [pltpu.SemaphoreType.DMA((links(n),))] * 2
+        + [pltpu.SemaphoreType.DMA((n - 1,))] * 2,
         compiler_params=params(collective_id=3, has_side_effects=True),
         cost_estimate=cost(6 * T * W * D + 4e10, 8 * T * D),
         name="last",
@@ -661,8 +760,9 @@
     )(h, x, wq, kv, wo, gain)
 
 
-def cross_bwd_kernel(n, ctx, dh3_ref, after2_ref, cot_ref, g3_ref, wo_ref, q_ref, kv_ref, wq_ref, after1_ref, g2_ref,
-                     cb_ref, dq_ref, dkv_ref, da_ref, sb_ref, gg_ref, dh2_ref):
+def cross_bwd_kernel(n, ctx, dh3_ref, after2_ref, cot_ref, g3_ref, wo_ref, q_ref, kv_ref, wq_ref, after1_ref, g2_ref, bo_in,
+                     cb_ref, dq_ref, dkv_ref, da_ref, sb_ref, gg_ref, bo_ref, dh2_ref, ss, rs):
+    me = lax.axis_index("tensor")
     _, C, W = q_ref.shape
     KP = kv_ref.shape[1] // 2
     D = da_ref.shape[1]
@@ -672,6 +772,10 @@
     masks = [m.astype(BF) for m in head_masks(1, G)]
     lane = lax.broadcasted_iota(jnp.int32, (C, G), 1) // HEAD_DIM
     valid = lax.broadcasted_iota(jnp.int32, (C, KP), 1) < ctx
+    greet(n, me)
+    gather = Gather(n, me, bo_in, lambda t: bo_ref.at[t], lambda t, i: bo_ref.at[t, pl.ds(i * C // 2, C // 2)], ss, rs)
+    gather.start()
+    bo_ref[me] = bo_in[...]
     dh3 = dh3_ref[...]
     u3, inv3 = unit(after2_ref[...])
     gain3 = jnp.sum(dh3 * u3, axis=0, keepdims=True)
@@ -704,6 +808,7 @@
         return carry
 
     lax.fori_loop(0, n * per, group, 0)
+    gather.relay()
     tf = 256
 
     def project(j, carry):
@@ -723,15 +828,18 @@
     sb_ref[...] = da1.astype(BF)
     row = lax.broadcasted_iota(jnp.int32, (8, D), 0)
     gg_ref[...] = jnp.where(row == 0, gain3, 0.0) + jnp.where(row == 1, gain2, 0.0)
-
-
-def cross_bwd(ctx, dh3, after2, cot, g3, wo, q, kv, wq, after1, g2):
+    for d in range(1, n):
+        gather.wait(d)
+    gather.finish()
+
+
+def cross_bwd(ctx, dh3, after2, cot, g3, wo, q, kv, wq, after1, g2, bo):
     C, D = after2.shape
     n, W = wq.shape[0], wq.shape[2]
     return pl.pallas_call(
         functools.partial(cross_bwd_kernel, n, ctx),
-        in_specs=[VSPEC] * 10,
-        out_specs=[VSPEC] * 6,
+        in_specs=[VSPEC] * 11,
+        out_specs=[VSPEC] * 7,
         out_shape=[
             sds((C, D), BF),
             sds((n, C, W), BF),
@@ -739,12 +847,13 @@
             sds((C, D), F32),
             sds((C, D), BF),
             sds((8, D), F32),
+            sds((n, C, D), BF),
         ],
-        scratch_shapes=[pltpu.VMEM((C, D), F32)],
-        compiler_params=params(),
+        scratch_shapes=[pltpu.VMEM((C, D), F32)] + [pltpu.SemaphoreType.DMA((links(n),))] * 2,
+        compiler_params=params(collective_id=7, has_side_effects=True),
         cost_estimate=cost(4 * C * D * n * W + 40 * C * 256 * n * W, 8 * D * n * W),
         name="cross_bwd",
-    )(dh3, after2, cot, g3, wo, q, kv, wq, after1, g2)
+    )(dh3, after2, cot, g3, wo, q, kv, wq, after1, g2, bo)
 
 
 def swap_sum_kernel(n, a_ref, o_ref, rbuf, ss, rs):
@@ -803,42 +912,32 @@
     def scatter(a, axis):
         return lax.psum_scatter(a, axis, scatter_dimension=0, tiled=True)
 
-    gu_part, down_part = feed_grads(h3, gb, dgu, hidden)
-    dh3, gu_part, down_part = lax.optimization_barrier((dh3, gu_part, down_part))
+    down_part = down_grads(gb, hidden)
+    down_part, dgu = lax.optimization_barrier((down_part, dgu))
+    down_grad = scatter(down_part, "dp")
+    out_own, gu_part = feed_grads(n, hidden, wd, after2, h3, dgu)
+    dh3, gu_part = lax.optimization_barrier((dh3, gu_part))
     gu_grad = scatter(gu_part, "dp")
-    down_grad = scatter(down_part, "dp")
-
-    cb, dcq, dckv, dafter1, sb_own, gains = cross_bwd(
-        ctx, dh3, after2, own(gb), g3, xo_all, cq, kv_all, xq_all, after1, g2
+
+    cb, dcq, dckv, dafter1, sb_own, gains, block_out = cross_bwd(
+        ctx, dh3, after2, own(gb), g3, xo_all, cq, kv_all, xq_all, after1, g2, out_own
     )
     sb, dattn, cross_grads = gather_back(n, ndp, sb_own, wo, h2, dcq, cb, cattn, dckv, ctx_pad)
     sb = sb.reshape(T, D)
     dq, dk, dv = attn_bwd(q, k, v, attn, dattn, lse, cs, sn)
-    dq, gu_grad = lax.optimization_barrier((dq, gu_grad))
+    dq, down_grad = lax.optimization_barrier((dq, down_grad))
     latent_grad, self_grads = last(n, dq, dk, dv, wq, wk, wv, x_own, dafter1, g1, gains, h1, sb, attn)
     self_grads = scatter(self_grads, "dp")
 
-    hidden, latent_grad = lax.optimization_barrier((hidden, latent_grad))
-    terms = nn(hidden, wd).astype(BF).reshape(n, C, D)
-    swap = lambda a, d: lax.ppermute(a, "tensor", [(i, i ^ d) for i in range(n)])
-    pick = lambda a, t: lax.dynamic_index_in_dim(a, t, 0, keepdims=False)
-    total = after2 + pick(terms, me).astype(F32)
-    for d in range(1, n):
-        total = total + swap(pick(terms, me ^ d), d).astype(F32)
-    total = total.astype(BF)
-    block_out = jnp.zeros((n, C, D), BF)
-    block_out = lax.dynamic_update_index_in_dim(block_out, total, me, 0)
-    for d in range(1, n):
-        block_out = lax.dynamic_update_index_in_dim(block_out, swap(total, d), me ^ d, 0)
-
     cross_grads = scatter(cross_grads, "dp")
-    cross_grads, down_grad, block_out = lax.optimization_barrier((cross_grads, down_grad, block_out))
+    cross_grads, gu_grad = lax.optimization_barrier((cross_grads, gu_grad))
     gu_grad = gu_grad.astype(F32)
     gate_grad, up_grad, down_grad = gu_grad[:, :F], gu_grad[:, F:], down_grad.astype(F32).T
     rows = cross_grads.shape[0]
     kv_grads = cross_grads[:, 2 * n * W :].reshape(2, rows // 2, W).astype(F32)
     cross_grads = cross_grads[:, : 2 * n * W].reshape(rows, 2, n, W).transpose(2, 0, 1, 3).reshape(n, rows, 2 * W)
     cross_grads = swap_sum(cross_grads)
+    cross_grads, self_grads = lax.optimization_barrier((cross_grads, self_grads))
     xq_grad, xo_grad = cross_grads[:, :W], cross_grads[:, W:].T
     self_grads = self_grads.astype(F32)
     gains = self_grads[:, 4 * W :]

time: 604 us -> 570 us (0.944)
  Pallas kernels: 452 us -> 425 us
  waiting for transfers between devices: 74.5 us -> 88.8 us
  matrix products: 7.81 us -> 0 us
  starting transfers between devices: 7.14 us -> 0.16 us
    reduce_scatter x4, waiting for transfers between devices: 11.4 us -> 88.7 us  [scatter(): return lax.psum_scatter(a, axis, scatter_dimension=0, tiled=True)]
    ppermute x6 -> x0, waiting for transfers between devices: 62.4 us -> none  [body(): lax.ppermute(a, 'tensor', [(i, i ^ d) for i in range(n)])]
    pallas_call x1, Pallas kernels: 84.3 us -> 63.6 us  [last(): pl.pallas_call(functools.partial(last_kernel, n), in_specs=[VSPEC] * 13,...]
    pallas_call x1 -> x2, Pallas kernels: 31.4 us -> 50.2 us  [the longest x1 38.3 us: feed_grads(): pl.pallas_call(functools.partial(feed_kernel, n), in_specs=[VSPEC] * 5, o...]
    pallas_call x1, Pallas kernels: 72.9 us -> 58.4 us  [front(): pl.pallas_call(functools.partial(front_kernel, n, ctx), in_specs=[VSPEC]...]
    pallas_call x1, Pallas kernels: 55 us -> 44 us  [gather_back(): pl.pallas_call(functools.partial(gather_kernel, n, ndp), in_specs=[VSPEC]...]
    pallas_call x1, Pallas kernels: 30.6 us -> 39.5 us  [cross_bwd(): pl.pallas_call(functools.partial(cross_bwd_kernel, n, ctx), in_specs=[VSP...]
    dot_general x1 -> x0, matrix products: 7.81 us -> none  [nn(): lax.dot_general(a, b, (((1,), (0,)), ((), ())), preferred_element_type=F32)]
  transfers between devices with their start and end apart: 10 -> 4, of which waited for: 5 -> 2; matrix products, arithmetic and copies ran while one was open for 5% -> 1% of each run, Pallas kernels for 35% -> 40%
where the time goes in v4:
time: 570 us; the launch traced here: 559 us
  Pallas kernels  425 us (75%)
  waiting for transfers between devices  88.8 us (16%)
  local copies, waits for them, and re-layouts  25.5 us (4%)
  between operations  14.2 us (2%)
    reduce_scatter x4, waiting for transfers between devices, scatter(): return lax.psum_scatter(a, axis, scatter_dimension=0, tiled=True)  88.7 us
    pallas_call x1, Pallas kernels, ff(): pl.pallas_call(functools.partial(ff_kernel, n), in_specs=[VSPEC] + [ANYSP...  77.6 us
    pallas_call x1, Pallas kernels, last(): pl.pallas_call(functools.partial(last_kernel, n), in_specs=[VSPEC] * 13,...  63.6 us
    pallas_call x1, Pallas kernels, front(): pl.pallas_call(functools.partial(front_kernel, n, ctx), in_specs=[VSPEC]...  58.4 us
    pallas_call x1, Pallas kernels, gather_back(): pl.pallas_call(functools.partial(gather_kernel, n, ndp), in_specs=[VSPEC]...  44 us
    pallas_call x1, Pallas kernels, cross_bwd(): pl.pallas_call(functools.partial(cross_bwd_kernel, n, ctx), in_specs=[VSP...  39.5 us
    pallas_call x1, Pallas kernels, feed_grads(): pl.pallas_call(functools.partial(feed_kernel, n), in_specs=[VSPEC] * 5, o...  38.3 us
    pallas_call x1, Pallas kernels, out_rs(): pl.pallas_call(functools.partial(out_rs_kernel, n), in_specs=[VSPEC] * 4,...  33.8 us
  transfers between devices with their start and end apart: 4, of which 2 were waited for; matrix products, arithmetic and copies ran while one was open for 1% of the time, Pallas kernels for 40%

profile of v4, /device:TPU:0, one launch (start us, length us, event | category | flops | bytes accessed | tf_op | source)
XLA Modules:
  0.0 559.3 jit_solution(10789886557993207109)
XLA Ops:
  7.2 0.0 reduce-scatter.5.cloned.1.call-start
  7.2 1.3 reshape.94.g_ref
  8.5 1.3 reshape.96.g_ref.g2_ref
  9.8 1.3 reshape.97.g_ref.g3_ref
  11.1 0.5 fusion.2
  11.8 0.0 copy-start.7
  11.8 1.0 copy.34.c_ref
  12.9 1.0 copy.35.s_ref
  13.9 0.0 copy-done.7
  13.9 0.7 pad.4.ctx_ref
  14.6 2.6 dynamic-slice_bitcast_fusion
  17.2 58.4 %front.1 = (bf16[1024,1536]{1,0:T(8,128)(2,1)}, bf16[1024,384]{1,0:T(8,128)(2,1)}, bf16[1024,384]{1,0:T(8,128)(2,1)}, bf16[1024,384]{1,0:T(8,128)(2,1)}, bf16[10...) custom-call(bf16[1024,1536]{1,0:T(8,128)(2,1)} %bitcast.27, ...), custom_call_target="tpu_custom_call" | custom-call | flops 1000 | bytes 1000 | tf_op jit(solution)/shard_map/front/pallas_call | solution.py:202
  75.5 33.8 %out_rs.1 = (f32[256,1536]{1,0:T(8,128)}, bf16[256,1536]{1,0:T(8,128)(2,1)}) custom-call(bf16[1024,384]{1,0:T(8,128)(2,1)} %get-tuple-element.62.a_ref.o_ref.at_ref, bf16[384,1536]{1,0:T(8,128)(2,1)} %w_ref.3, bf16[256,1536]{1,0:T(8,128)(2,1)} %get-tuple-element.126.x_ref, f32[1,1536]{1,0:T(1,128)} %reshape.96.g_ref.g2_ref), custom_call_target="tpu_custom_call" | custom-call | flops 1000 | bytes 1000 | tf_op jit(solution)/shard_map/out_rs/pallas_call | solution.py:386
  109.4 17.8 %cross_fwd.1 = (bf16[4,256,384]{2,1,0:T(8,128)(2,1)}, bf16[4,256,384]{2,1,0:T(8,128)(2,1)}, f32[256,1536]{1,0:T(8,128)}, bf16[256,1536]{1,0:T(8,128)(2,1)}) custom-call(bf16[256,1536]{1,0:T(8,128)(2,1)} %get-tuple-element.63.h_ref.h2_ref, f32[256,1536]{1,0:T(8,128)} %get-tuple-element.64.x_ref.after1_ref, bf16[4,1536,384]{2,1,0:T(8,128)(2,1)} %get-tuple-element.65.wq_ref, ...), custom_call_target="tpu_custom_call" | custom-call | flops 1000 | bytes 1000 | tf_op jit(solution)/shard_map/cross_fwd/pallas_call | solution.py:752
  127.2 77.6 %ff.1 = (bf16[4,256,1536]{2,1,0:T(8,128)(2,1)}, bf16[1024,1536]{1,0:T(8,128)(2,1)}, bf16[1024,3072]{1,0:T(8,128)(2,1)}, f32[256,1536]{1,0:T(8,128)}) custom-call(bf16[256,1536]{1,0:T(8,128)(2,1)} %get-tuple-element.68.h_in, bf16[1024,1536]{1,0:T(8,128)(2,1)} %bitcast.25, bf16[1536,1536]{1,0:T(8,128)(2,1)} %wg_hbm.1, bf16[1536,1536]{1,0:T(8,128)(2,1)} %wu_hbm.1, ...), custom_call_target="tpu_custom_call" | custom-call | flops 1000 | bytes 1000 | tf_op jit(solution)/shard_map/ff/pallas_call | solution.py:471
  204.8 11.9 %down_grads.1 = bf16[1536,1536]{1,0:T(8,128)(2,1)} custom-call(bf16[1024,1536]{1,0:T(8,128)(2,1)} %bitcast.26, bf16[1024,1536]{1,0:T(8,128)(2,1)} %get-tuple-element.70.hid_ref), custom_call_target="tpu_custom_call" | custom-call | flops 1000 | bytes 1000 | tf_op jit(solution)/shard_map/down_grads/pallas_call | solution.py:509
  216.7 0.0 reduce-scatter.5.cloned.1.call-update
  216.7 0.0 reduce-scatter.9.cloned.1.call-start
  216.7 38.3 %feed_grads.1 = (bf16[256,1536]{1,0:T(8,128)(2,1)}, bf16[1536,3072]{1,0:T(8,128)(2,1)}) custom-call(bf16[1024,1536]{1,0:T(8,128)(2,1)} %get-tuple-element.70.hid_ref, bf16[1536,1536]{1,0:T(8,128)(2,1)} %wd_ref.1, f32[256,1536]{1,0:T(8,128)} %get-tuple-element.71.after_ref.after2_ref, bf16[1024,1536]{1,0:T(8,128)(2,1)} %bitcast.29, ...), custom_call_target="tpu_custom_call" | custom-call | flops 1000 | bytes 1000 | tf_op jit(solution)/shard_map/feed_grads/pallas_call | solution.py:554
  255.1 0.0 reduce-scatter.9.cloned.1.call-update
  255.1 0.0 reduce-scatter.7.cloned.1.call-start
  255.2 39.5 %cross_bwd.1 = (bf16[256,1536]{1,0:T(8,128)(2,1)}, bf16[4,256,384]{2,1,0:T(8,128)(2,1)}, f32[4,288,384]{2,1,0:T(8,128)}, f32[256,1536]{1,0:T(8,128)}, bf16[256,1...) custom-call(f32[256,1536]{1,0:T(8,128)} %get-tuple-element.76.dh3_ref, ...), custom_call_target="tpu_custom_call" | custom-call | flops 1000 | bytes 1000 | tf_op jit(solution)/shard_map/cross_bwd/pallas_call | solution.py:839
  294.7 44.0 %gather_back.1 = (bf16[4,256,1536]{2,1,0:T(8,128)(2,1)}, bf16[1024,384]{1,0:T(8,128)(2,1)}, bf16[1536,3456]{1,0:T(8,128)(2,1)}) custom-call(bf16[256,1536]{1,0:T(8,128)(2,1)} %get-tuple-element.83.x_in, bf16[384,1536]{1,0:T(8,128)(2,1)} %w_ref.3, bf16[256,1536]{1,0:T(8,128)(2,1)} %get-tuple-element.63.h_ref.h2_ref, ...), custom_call_target="tpu_custom_call" | custom-call | flops 1000 | bytes 1000 | tf_op jit(solution)/shard_map/gather_back/pallas_call | solution.py:620
  338.6 0.0 reduce-scatter.7.cloned.1.call-update
  338.7 0.0 reduce-scatter.11.cloned.1.call-start
  338.7 24.0 %attn_bwd.1 = (bf16[1024,384]{1,0:T(8,128)(2,1)}, bf16[1024,384]{1,0:T(8,128)(2,1)}, bf16[1024,384]{1,0:T(8,128)(2,1)}) custom-call(bf16[1024,384]{1,0:T(8,128)(2,1)} %get-tuple-element.80.q_ref, bf16[1024,384]{1,0:T(8,128)(2,1)} %get-tuple-element.81.k_ref, bf16[1024,384]{1,0:T(8,128)(2,1)} %get-tuple-element.82.v_ref, ...), custom_call_target="tpu_custom_call" | custom-call | flops 1000 | bytes 1000 | tf_op jit(solution)/shard_map/attn_bwd/pallas_call | solution.py:264
  362.7 0.0 reduce-scatter.5.cloned.1.call-done
  362.7 63.6 %last.1 = (bf16[4,256,1536]{2,1,0:T(8,128)(2,1)}, bf16[1536,1664]{1,0:T(8,128)(2,1)}) custom-call(bf16[1024,384]{1,0:T(8,128)(2,1)} %get-tuple-element.92.dq_ref, bf16[1024,384]{1,0:T(8,128)(2,1)} %get-tuple-element.93.dk_ref, bf16[1024,384]{1,0:T(8,128)(2,1)} %get-tuple-element.94.dv_ref, bf16[1536,384]{1,0:T(8,128)(2,1)} %wq_ref.3, ...), custom_call_target="tpu_custom_call" | custom-call | flops 1000 | bytes 1000 | tf_op jit(solution)/shard_map/last/pallas_call | solution.py:691
  426.4 0.0 reduce-scatter.11.cloned.1.call-update
  426.4 1.9 copy-done.4
  428.3 3.6 bitcast_convert_fusion
  431.9 51.8 %reduce-scatter.7.cloned.1.call-done = bf16[192,3456]{1,0:T(8,128)(2,1)} async-done(((bf16[1536,3456]{1,0:T(8,128)(2,1)}), bf16[192,3456]{1,0:T(8,128)(2,1)}) %reduce-scatter.7.cloned.1.call-update) | async-done | bytes 1327120 | tf_op jit(solution)/shard_map/reduce_scatter | solution.py:913
  483.6 1.3 slice-done
  484.9 0.9 reshape.104
  485.8 0.9 copy.40
  486.7 1.6 reshape.105.a_ref
  488.3 1.1 convert_bitcast_fusion
  489.5 16.4 %swap_sum.1 = f32[192,768]{1,0:T(8,128)} custom-call(bf16[4,192,768]{2,1,0:T(8,128)(2,1)} %reshape.105.a_ref), custom_call_target="tpu_custom_call" | custom-call | flops 1000 | bytes 1000 | tf_op jit(solution)/shard_map/swap_sum/pallas_call | solution.py:877
  505.9 37.0 %reduce-scatter.11.cloned.1.call-done = bf16[192,1664]{1,0:T(8,128)(2,1)} async-done(((bf16[1536,1664]{1,0:T(8,128)(2,1)}), bf16[192,1664]{1,0:T(8,128)(2,1)}) %reduce-scatter.11.cloned.1.call-update) | async-done | bytes 638992 | tf_op jit(solution)/shard_map/reduce_scatter | solution.py:913
  542.9 2.0 fusion.4
  544.9 0.1 convert_element_type.14
  545.0 0.8 slice_reduce_fusion
  545.9 0.7 slice_bitcast_fusion
  546.6 0.7 fusion.5
  547.3 0.8 slice_bitcast_fusion.1
  548.2 1.7 fusion.3
  549.9 1.0 copy-done.3
  550.9 1.7 copy.42
  (19 shorter events, 0.2 us)
Async XLA Ops:
  7.2 355.5 %reduce-scatter.5.cloned.1.call-start = ((), (), s32[]{:S(2)}) async-start(), calls=%async_computation.4 | async-start | bytes 5308416 | tf_op jit(solution)/shard_map/reduce_scatter | solution.py:913
  11.8 2.1 copy-start.7
  216.7 215.2 %reduce-scatter.9.cloned.1.call-start = ((), (), s32[]{:S(2)}) async-start(), calls=%async_computation.6 | async-start | bytes 10616832 | tf_op jit(solution)/shard_map/reduce_scatter | solution.py:913
  255.1 228.5 %reduce-scatter.7.cloned.1.call-start = ((), (), s32[]{:S(2)}) async-start(), calls=%async_computation.5 | async-start | bytes 11943936 | tf_op jit(solution)/shard_map/reduce_scatter | solution.py:913
  338.7 204.2 %reduce-scatter.11.cloned.1.call-start = ((), (), s32[]{:S(2)}) async-start(), calls=%async_computation.7 | async-start | bytes 5750784 | tf_op jit(solution)/shard_map/reduce_scatter | solution.py:913
  426.4 1.9 copy-start.4
  483.6 1.3 slice-start
  486.7 1.6 copy-start.6
  488.3 17.6 %copy-start.1 = (bf16[192,3456]{1,0:T(8,128)(2,1)S(1)}, bf16[192,3456]{1,0:T(8,128)(2,1)}, u32[]{:S(2)}) copy-start(bf16[192,3456]{1,0:T(8,128)(2,1)} %reduce-scatter.7.cloned.1.call-done) | copy-start | bytes 3981316
  542.9 2.1 copy-start.2
  544.9 2.4 copy-start.5
  545.0 3.1 copy-start
  548.2 2.7 copy-start.3
Sparse Core Ops, SparseCore 0:
  216.8 55.1 reduce-scatter.4
  274.3 97.9 reduce-scatter.8
  374.6 109.0 reduce-scatter.6
  485.8 57.0 reduce-scatter.10

commit v5 on v4

--- a/solution.py
+++ b/solution.py
@@ -90,11 +90,7 @@
     T, D = x_ref.shape
     W = q_ref.shape[1]
     KP = ctx_ref.shape[0]
-    sem = pltpu.get_barrier_semaphore()
-    for d in range(1, n):
-        pl.semaphore_signal(sem, 1, device_id={"tensor": me ^ d}, device_id_type=MESH_ID)
-    pl.semaphore_signal(sem, 1, device_id={"dp": partner}, device_id_type=MESH_ID)
-    pl.semaphore_wait(sem, n)
+    greet(n, me, [partner])
 
     rows_q = pl.ds(pl.multiple_of(core * (D // 2), 16), D // 2)
     rows_o = pl.ds(pl.multiple_of(core * (W // 2), 16), W // 2)
@@ -167,18 +163,14 @@
 
     lax.fori_loop(0, W // G, heads, 0)
 
-    def pass_on(ref, rows, send, recv, t):
-        return pltpu.make_async_remote_copy(
-            ref.at[t, rows], ref.at[t, rows], send, recv, device_id={"dp": partner}, device_id_type=MESH_ID
-        )
-
     go.relay()
     gk.relay()
     passed = []
     for gather, ref, rows, send, recv in ((gq, xqa_ref, rows_q, fsq, frq), (go, xoa_ref, rows_o, fso, fro)):
         for d in range(1, n):
             gather.wait(d)
-            copy = pass_on(ref, rows, send.at[d - 1], recv.at[d - 1], me ^ d)
+            block = ref.at[me ^ d, rows]
+            copy = to_dp(block, block, send.at[d - 1], recv.at[d - 1], partner)
             copy.start()
             passed.append(copy)
     for copy in own:
@@ -213,72 +205,17 @@
     )(x, gain, wq, wk, wv, cs, sn, xq, xo, ctx_rows, xk, xv)
 
 
-def attn_bwd_kernel(q_ref, k_ref, v_ref, o_ref, do_ref, lse_ref, c_ref, s_ref, dq_ref, dk_ref, dv_ref, dk_acc, dv_acc, kt_ref):
-    T, G = q_ref.shape
-    qb = 256
-    mult = SCALE * LOG2E
-    nh = G // HEAD_DIM
-    k, v = k_ref[...], v_ref[...]
-    kt_ref[...] = jnp.transpose(k.astype(F32)).astype(BF)
-    masks = [m.astype(BF) for m in head_masks(1, G)]
-    head_rows = jnp.where(
-        lax.broadcasted_iota(jnp.int32, (16, G), 0) == lax.broadcasted_iota(jnp.int32, (16, G), 1) // HEAD_DIM, 1.0, 0.0
-    ).astype(BF)
-    dk_acc[...] = jnp.zeros_like(dk_acc)
-    dv_acc[...] = jnp.zeros_like(dv_acc)
-
-    def block(i, carry):
-        rows = pl.ds(pl.multiple_of(i * qb, qb), qb)
-        q = q_ref[rows, :]
-        do = do_ref[rows, :]
-        prod = do.astype(F32) * o_ref[rows, :].astype(F32)
-        high = prod.astype(BF)
-        delta = nt(head_rows, high) + nt(head_rows, (prod - high.astype(F32)).astype(BF))
-        lse = lse_ref[:, rows]
-        parts = []
-        for h in range(nh):
-            qm = q * masks[h]
-            dom = do * masks[h]
-            st = nt(k, qm)
-            pt = jnp.exp2(st * mult - lse[h : h + 1, :])
-            dpt = nt(v, dom)
-            dst = (pt * (dpt - delta[h : h + 1, :])).astype(BF)
-            dv_acc[...] += nn(pt.astype(BF), dom)
-            dk_acc[...] += nn(dst, qm)
-            parts.append(nn(kt_ref[h * HEAD_DIM : (h + 1) * HEAD_DIM, :], dst))
-        dq = jnp.transpose(jnp.concatenate(parts, 0)) * SCALE
-        dq_ref[rows, :] = (dq * c_ref[rows, :] - turned(dq) * s_ref[rows, :]).astype(BF)
-        return carry
-
-    lax.fori_loop(0, T // qb, block, 0)
-    dk = dk_acc[...] * SCALE
-    dk_ref[...] = (dk * c_ref[...] - turned(dk) * s_ref[...]).astype(BF)
-    dv_ref[...] = dv_acc[...].astype(BF)
-
-
-def attn_bwd(q, k, v, o, do, lse, cs, sn):
-    T, W = q.shape
-    G = lane_group(W)
-    cols = pl.BlockSpec((T, G), lambda i: (0, i))
-    tab = pl.BlockSpec((T, G), lambda i: (0, 0), pipeline_mode=pl.Buffered(1))
-    return pl.pallas_call(
-        attn_bwd_kernel,
-        grid=(W // G,),
-        in_specs=[cols] * 5 + [pl.BlockSpec((None, 8, T), lambda i: (i, 0, 0)), tab, tab],
-        out_specs=[cols] * 3,
-        out_shape=[sds((T, W), BF)] * 3,
-        scratch_shapes=[pltpu.VMEM((T, G), F32), pltpu.VMEM((T, G), F32), pltpu.VMEM((G, T), BF)],
-        compiler_params=params(),
-        cost_estimate=cost(40 * T * T * W, 16 * T * W, T * T * W // HEAD_DIM),
-        name="attn_bwd",
-    )(q, k, v, o, do, lse, cs, sn)
-
-
-def greet(n, me):
+def greet(n, me, dps=()):
     sem = pltpu.get_barrier_semaphore()
     for d in range(1, n):
         pl.semaphore_signal(sem, 1, device_id={"tensor": me ^ d}, device_id_type=MESH_ID)
-    pl.semaphore_wait(sem, n - 1)
+    for dp in dps:
+        pl.semaphore_signal(sem, 1, device_id={"dp": dp}, device_id_type=MESH_ID)
+    pl.semaphore_wait(sem, n - 1 + len(dps))
+
+
+def to_dp(src, dst, send, recv, target):
+    return pltpu.make_async_remote_copy(src, dst, send, recv, device_id={"dp": target}, device_id_type=MESH_ID)
 
 
 def remote(src, dst, send, recv, target):
@@ -361,6 +298,55 @@
         for d in range(1, n):
             total = total + got(d - 1)
     return total, copies
+
+
+class ShardSum:
+    def __init__(self, n, me, a, sbuf, rbuf, ss, rs):
+        self.n, self.me, self.a, self.sbuf, self.rbuf, self.ss, self.rs = n, me, a, sbuf, rbuf, ss, rs
+        self.copies = {}
+
+    def send(self, i, src, d):
+        self.copies[i] = remote(src, self.rbuf.at[i], self.ss.at[i], self.rs.at[i], self.me ^ d)
+        self.copies[i].start()
+
+    def got(self, i):
+        self.copies[i].wait_recv()
+        return self.rbuf[i].astype(F32)
+
+    def halves(self, d):
+        H = self.a.shape[1] // 2
+        return self.a.at[self.me ^ d, pl.ds(0, H)], self.a.at[self.me ^ d, pl.ds(H, H)]
+
+    def start(self):
+        if self.n == 4:
+            self.send(0, self.halves(3)[0], 1)
+            self.send(2, self.halves(3)[1], 2)
+            self.send(1, self.halves(1)[0], 1)
+            self.send(3, self.halves(2)[1], 2)
+        else:
+            for d in range(1, self.n):
+                self.send(d - 1, self.a.at[self.me ^ d], d)
+
+    def middle(self):
+        if self.n == 4:
+            self.sbuf[0] = (self.halves(2)[0][...].astype(F32) + self.got(0)).astype(BF)
+            self.send(4, self.sbuf.at[0], 2)
+            self.sbuf[1] = (self.halves(1)[1][...].astype(F32) + self.got(2)).astype(BF)
+            self.send(5, self.sbuf.at[1], 1)
+
+    def store(self, out_ref):
+        if self.n == 4:
+            H = self.a.shape[1] // 2
+            own = self.halves(0)
+            out_ref[:H] = (own[0][...].astype(F32) + self.got(1) + self.got(4)).astype(BF)
+            out_ref[H:] = (own[1][...].astype(F32) + self.got(3) + self.got(5)).astype(BF)
+        else:
+            total = self.a[self.me].astype(F32)
+            for d in range(1, self.n):
+                total = total + self.got(d - 1)
+            out_ref[...] = total.astype(BF)
+        for copy in self.copies.values():
+            copy.wait_send()
 
 
 def out_rs_kernel(n, a_ref, w_ref, x_ref, g_ref, after_ref, h_ref, sbuf, rbuf, ss, rs):
@@ -563,14 +549,17 @@
     )(hidden, wd, after, h, dgu)
 
 
-def gather_kernel(n, ndp, x_in, w_ref, h2_ref, dcq_ref, cb_ref, ca_ref, dkv_ref, ctx_ref,
-                  x_ref, da_ref, gr_ref, ksend, krecv, ss, rs, ss2, rs2):
+def gather_kernel(n, ndp, x_in, w_ref, h2_ref, dcq_ref, cb_ref, ca_ref, dkv_ref, ctx_ref, x_ref, da_ref, gr_ref, kv_ref,
+                  buf, other, ksend, krecv, ss, rs, ss2, rs2, pair):
     me = lax.axis_index("tensor")
+    dp = lax.axis_index("dp")
+    core = dp % 2
+    partner = dp + 1 - 2 * core
     C, D = x_in.shape
     W = w_ref.shape[0]
-    HD = n * W
     KP = ctx_ref.shape[0]
-    greet(n, me)
+    R = D // ndp
+    greet(n, me, [partner])
     gather = Gather(n, me, x_in, lambda t: x_ref.at[t], lambda t, i: x_ref.at[t, pl.ds(i * C // 2, C // 2)], ss, rs)
     gather.start()
     kv = {}
@@ -584,17 +573,20 @@
 
     x_ref[me] = x_in[...]
     back(me, x_in[...])
-    tf = 256
-
-    def weights(j, carry):
-        rows = pl.ds(pl.multiple_of(j * tf, tf), tf)
-        h2, cb = h2_ref[:, rows], cb_ref[:, rows]
-        for t in range(n):
-            gr_ref[rows, t * W : (t + 1) * W] = tn(h2, dcq_ref[t]).astype(BF)
-            gr_ref[rows, HD + t * W : HD + (t + 1) * W] = tn(cb, ca_ref[t]).astype(BF)
-        return carry
-
-    lax.fori_loop(0, D // tf, weights, 0)
+
+    for j in range(ndp // 2):
+        h2, cb = h2_ref[:, 2 * R * j : 2 * R * (j + 1)], cb_ref[:, 2 * R * j : 2 * R * (j + 1)]
+
+        def weights(t, carry):
+            for i, (a, b) in enumerate(((h2, dcq_ref[t]), (cb, ca_ref[t]))):
+                res = tn(a, b).astype(BF)
+                for c in range(2):
+                    buf[c, t, j * R : (j + 1) * R, i * W : (i + 1) * W] = res[c * R : (c + 1) * R]
+            return carry
+
+        lax.fori_loop(0, n, weights, 0)
+    swap = to_dp(buf.at[1 - core], other, pair.at[0], pair.at[1], partner)
+    swap.start()
     gather.relay()
     dkv = dkv_ref[me]
     for d in range(1, n):
@@ -602,60 +594,150 @@
         dkv = dkv + krecv[d - 1].astype(F32)
     for half in range(2):
         kvg = tn(ctx_ref[...], dkv[half * KP : (half + 1) * KP].astype(BF)).astype(BF)
-        R = kvg.shape[0] // ndp
+        S = kvg.shape[0] // ndp
         for i in range(ndp):
-            gr_ref[(2 * i + half) * R : (2 * i + half + 1) * R, 2 * HD :] = kvg[i * R : (i + 1) * R]
+            kv_ref[(2 * i + half) * S : (2 * i + half + 1) * S] = kvg[i * S : (i + 1) * S]
     for d in range(1, n):
         gather.wait(d)
         back(me ^ d, x_ref[me ^ d])
+    swap.wait_recv()
+
+    def add(t, carry):
+        gr_ref[t] = (buf[core, t].astype(F32) + other[t].astype(F32)).astype(BF)
+        return carry
+
+    lax.fori_loop(0, n, add, 0)
     gather.finish()
     for d in range(1, n):
         kv[d].wait_send()
+    swap.wait_send()
 
 
 def gather_back(n, ndp, x, w, h2, dcq, cb, ca, dkv, ctx):
     C, D = x.shape
     W = w.shape[0]
     KP = ctx.shape[0]
+    half = (n, D // 2, 2 * W)
     return pl.pallas_call(
         functools.partial(gather_kernel, n, ndp),
         in_specs=[VSPEC] * 8,
-        out_specs=[VSPEC] * 3,
-        out_shape=[sds((n, C, D), BF), sds((n * C, W), BF), sds((D, (2 * n + 1) * W), BF)],
-        scratch_shapes=[pltpu.VMEM((n - 1, 2 * KP, W), BF)] * 2
+        out_specs=[VSPEC] * 4,
+        out_shape=[sds((n, C, D), BF), sds((n * C, W), BF), sds(half, BF), sds((2 * ctx.shape[1], W), BF)],
+        scratch_shapes=[pltpu.VMEM((2, *half), BF), pltpu.VMEM(half, BF)]
+        + [pltpu.VMEM((n - 1, 2 * KP, W), BF)] * 2
         + [pltpu.SemaphoreType.DMA((links(n),))] * 2
-        + [pltpu.SemaphoreType.DMA((n - 1,))] * 2,
+        + [pltpu.SemaphoreType.DMA((n - 1,))] * 2
+        + [pltpu.SemaphoreType.DMA((2,))],
         compiler_params=params(collective_id=2, has_side_effects=True),
         cost_estimate=cost(2 * n * C * W * D + 2e10, 8 * C * D),
         name="gather_back",
     )(x, w, h2, dcq, cb, ca, dkv, ctx)
 
 
-def last_kernel(n, dq_ref, dk_ref, dv_ref, wq_ref, wk_ref, wv_ref, x_ref, da_ref, g_ref, gg_in, h1_ref, sb_ref, at_ref,
-                lbuf, gr_ref, sbuf, rbuf, gbuf, gsum, ss, rs, ss2, rs2, ss3, rs3):
+def attn_bwd_kernel(n, q_ref, k_ref, v_ref, o_ref, do_ref, lse_ref, c_ref, s_ref, h_ref, sb_ref, kv_ref, a_ref,
+                    dq_ref, dk_ref, dv_ref, gr_ref, x_ref, dk_acc, dv_acc, kt_ref, sbuf, rbuf, ss, rs):
     me = lax.axis_index("tensor")
+    T, W = q_ref.shape
+    G = lane_group(W)
+    qb = 256
+    mult = SCALE * LOG2E
+    nh = G // HEAD_DIM
+    greet(n, me)
+    shards = ShardSum(n, me, a_ref, sbuf, rbuf, ss, rs)
+    shards.start()
+    masks = [m.astype(BF) for m in head_masks(1, G)]
+    head_rows = jnp.where(
+        lax.broadcasted_iota(jnp.int32, (16, G), 0) == lax.broadcasted_iota(jnp.int32, (16, G), 1) // HEAD_DIM, 1.0, 0.0
+    ).astype(BF)
+
+    def heads(g, outer):
+        cols = pl.ds(pl.multiple_of(g * G, G), G) if G < W else slice(None)
+        k, v = k_ref[:, cols], v_ref[:, cols]
+        kt_ref[...] = jnp.transpose(k.astype(F32)).astype(BF)
+        dk_acc[...] = jnp.zeros_like(dk_acc)
+        dv_acc[...] = jnp.zeros_like(dv_acc)
+
+        def block(i, carry):
+            rows = pl.ds(pl.multiple_of(i * qb, qb), qb)
+            q = q_ref[rows, cols]
+            do = do_ref[rows, cols]
+            prod = do.astype(F32) * o_ref[rows, cols].astype(F32)
+            high = prod.astype(BF)
+            delta = nt(head_rows, high) + nt(head_rows, (prod - high.astype(F32)).astype(BF))
+            lse = lse_ref[g, :, rows]
+            parts = []
+            for h in range(nh):
+                qm = q * masks[h]
+                dom = do * masks[h]
+                st = nt(k, qm)
+                pt = jnp.exp2(st * mult - lse[h : h + 1, :])
+                dpt = nt(v, dom)
+                dst = (pt * (dpt - delta[h : h + 1, :])).astype(BF)
+                dv_acc[...] += nn(pt.astype(BF), dom)
+                dk_acc[...] += nn(dst, qm)
+                parts.append(nn(kt_ref[h * HEAD_DIM : (h + 1) * HEAD_DIM, :], dst))
+            dq = jnp.transpose(jnp.concatenate(parts, 0)) * SCALE
+            dq_ref[rows, cols] = (dq * c_ref[rows, :] - turned(dq) * s_ref[rows, :]).astype(BF)
+            return carry
+
+        lax.fori_loop(0, T // qb, block, 0)
+        dk = dk_acc[...] * SCALE
+        dk_ref[:, cols] = (dk * c_ref[...] - turned(dk) * s_ref[...]).astype(BF)
+        dv_ref[:, cols] = dv_acc[...].astype(BF)
+        return outer
+
+    lax.fori_loop(0, W // G, heads, 0)
+    shards.middle()
+    tf = 256
+
+    def weights(j, carry):
+        rows = pl.ds(pl.multiple_of(j * tf, tf), tf)
+        h = h_ref[:, rows]
+        for i, g_ref in enumerate((dq_ref, dk_ref, dv_ref)):
+            gr_ref[rows, i * W : (i + 1) * W] = tn(h, g_ref[...]).astype(BF)
+        gr_ref[rows, 3 * W : 4 * W] = tn(sb_ref[:, rows], o_ref[...]).astype(BF)
+        gr_ref[rows, 4 * W :] = kv_ref[rows, :]
+        return carry
+
+    lax.fori_loop(0, gr_ref.shape[0] // tf, weights, 0)
+    shards.store(x_ref)
+
+
+def attn_bwd(n, q, k, v, o, do, lse, cs, sn, h, sb, kv, a):
+    T, W = q.shape
+    D = h.shape[1]
+    G = lane_group(W)
+    _, R, N = a.shape
+    slots = 6 if n == 4 else n - 1
+    H = R // 2 if n == 4 else R
+    return pl.pallas_call(
+        functools.partial(attn_bwd_kernel, n),
+        in_specs=[VSPEC] * 12,
+        out_specs=[VSPEC] * 5,
+        out_shape=[sds((T, W), BF)] * 3 + [sds((D, 5 * W), BF), sds((R, N), BF)],
+        scratch_shapes=[pltpu.VMEM((T, G), F32), pltpu.VMEM((T, G), F32), pltpu.VMEM((G, T), BF)]
+        + [pltpu.VMEM((2, H, N), BF), pltpu.VMEM((slots, H, N), BF)]
+        + [pltpu.SemaphoreType.DMA((slots,))] * 2,
+        compiler_params=params(collective_id=5, has_side_effects=True),
+        cost_estimate=cost(40 * T * T * W, 16 * T * W, T * T * W // HEAD_DIM),
+        name="attn_bwd",
+    )(q, k, v, o, do, lse, cs, sn, h, sb, kv, a)
+
+
+def last_kernel(n, ndp, dq_ref, dk_ref, dv_ref, wq_ref, wk_ref, wv_ref, x_ref, da_ref, g_ref, gg_in,
+                lbuf, gg_ref, sbuf, rbuf, gbuf, gsum, gown, gall, ss, rs, ss2, rs2, ss3, rs3, ss4, rs4):
+    me = lax.axis_index("tensor")
+    dp = lax.axis_index("dp")
     C, D = x_ref.shape
-    greet(n, me)
+    R = D // ndp
+    others = [(dp + i) % ndp for i in range(1, ndp)]
+    greet(n, me, others)
 
     def part(t):
         rows = pl.ds(pl.multiple_of(t * C, C), C)
         return nt(dq_ref[rows, :], wq_ref[...]) + nt(dk_ref[rows, :], wk_ref[...]) + nt(dv_ref[rows, :], wv_ref[...])
 
-    W = dq_ref.shape[1]
-    tf = 256
-
-    def weights(j, carry):
-        rows = pl.ds(pl.multiple_of(j * tf, tf), tf)
-        h = h1_ref[:, rows]
-        for i, a_ref in enumerate((dq_ref, dk_ref, dv_ref)):
-            gr_ref[rows, i * W : (i + 1) * W] = tn(h, a_ref[...]).astype(BF)
-        gr_ref[rows, 3 * W : 4 * W] = tn(sb_ref[:, rows], at_ref[...]).astype(BF)
-        return carry
-
-    def filler():
-        lax.fori_loop(0, D // tf, weights, 0)
-
-    total, copies = reduce_parts(n, me, part, filler, sbuf, rbuf, ss, rs)
+    total, copies = reduce_parts(n, me, part, lambda: None, sbuf, rbuf, ss, rs)
     u, inverse = unit(x_ref[...].astype(F32))
     lbuf[me] = (da_ref[...] + norm_back(total, u, inverse, g_ref[...])).astype(BF)
     gather = Gather(
@@ -668,40 +750,48 @@
     for d in range(1, n):
         small[d] = remote(gsum, gbuf.at[d - 1], ss3.at[d - 1], rs3.at[d - 1], me ^ d)
         small[d].start()
-
     gains = gsum[...]
     for d in range(1, n):
         small[d].wait_recv()
         gains = gains + gbuf[d - 1]
-    gains = jnp.concatenate([gains, jnp.zeros((120, D), F32)], 0)
-    gr_ref[:, 4 * W :] = jnp.transpose(gains).astype(BF)
+    for i in range(ndp):
+        gown[i] = gains[:, i * R : (i + 1) * R]
+    sums = []
+    for i, other in enumerate(others):
+        sums.append(to_dp(gown.at[other], gall.at[i], ss4.at[i], rs4.at[i], other))
+        sums[i].start()
+    mine = gown[dp]
+    for i in range(ndp - 1):
+        sums[i].wait_recv()
+        mine = mine + gall[i]
+    gg_ref[...] = mine
     gather.relay()
     for d in range(1, n):
         gather.wait(d)
     gather.finish()
-    for copy in copies.values():
+    for copy in (*copies.values(), *small.values(), *sums):
         copy.wait_send()
-    for d in range(1, n):
-        small[d].wait_send()
-
-
-def last(n, dq, dk, dv, wq, wk, wv, x, da, gain, gains, h1, sb, attn):
+
+
+def last(n, ndp, dq, dk, dv, wq, wk, wv, x, da, gain, gains):
     C, D = x.shape
     T, W = dq.shape
     return pl.pallas_call(
-        functools.partial(last_kernel, n),
-        in_specs=[VSPEC] * 13,
+        functools.partial(last_kernel, n, ndp),
+        in_specs=[VSPEC] * 10,
         out_specs=[VSPEC] * 2,
-        out_shape=[sds((n, C, D), BF), sds((D, 4 * W + 128), BF)],
+        out_shape=[sds((n, C, D), BF), sds((8, D // ndp), F32)],
         scratch_shapes=reduce_bufs(n, C, D)[:2]
         + [pltpu.VMEM((n - 1, 8, D), F32), pltpu.VMEM((8, D), F32)]
+        + [pltpu.VMEM((ndp, 8, D // ndp), F32), pltpu.VMEM((ndp - 1, 8, D // ndp), F32)]
         + reduce_bufs(n, C, D)[2:]
         + [pltpu.SemaphoreType.DMA((links(n),))] * 2
-        + [pltpu.SemaphoreType.DMA((n - 1,))] * 2,
+        + [pltpu.SemaphoreType.DMA((n - 1,))] * 2
+        + [pltpu.SemaphoreType.DMA((ndp - 1,))] * 2,
         compiler_params=params(collective_id=3, has_side_effects=True),
         cost_estimate=cost(6 * T * W * D + 4e10, 8 * T * D),
         name="last",
-    )(dq, dk, dv, wq, wk, wv, x, da, gain, gains, h1, sb, attn)
+    )(dq, dk, dv, wq, wk, wv, x, da, gain, gains)
 
 
 def cross_fwd_kernel(n, ctx, h_ref, x_ref, wq_ref, kv_ref, wo_ref, g_ref, q_ref, o_ref, after_ref, h3_ref):
@@ -856,36 +946,6 @@
     )(dh3, after2, cot, g3, wo, q, kv, wq, after1, g2, bo)
 
 
-def swap_sum_kernel(n, a_ref, o_ref, rbuf, ss, rs):
-    me = lax.axis_index("tensor")
-    greet(n, me)
-    copies = {}
-    for d in range(1, n):
-        copies[d] = remote(a_ref.at[me ^ d], rbuf.at[d - 1], ss.at[d - 1], rs.at[d - 1], me ^ d)
-        copies[d].start()
-    total = a_ref[me].astype(F32)
-    for d in range(1, n):
-        copies[d].wait_recv()
-        total = total + rbuf[d - 1].astype(F32)
-    o_ref[...] = total
-    for d in range(1, n):
-        copies[d].wait_send()
-
-
-def swap_sum(a):
-    n, R, N = a.shape
-    return pl.pallas_call(
-        functools.partial(swap_sum_kernel, n),
-        in_specs=[VSPEC],
-        out_specs=VSPEC,
-        out_shape=sds((R, N), F32),
-        scratch_shapes=[pltpu.VMEM((n - 1, R, N), BF)] + [pltpu.SemaphoreType.DMA((n - 1,))] * 2,
-        compiler_params=params(collective_id=5, has_side_effects=True),
-        cost_estimate=cost(n * R * N, 8 * R * N),
-        name="swap_sum",
-    )(a)
-
-
 def body(latents, context, cotangent, g1, wq, wk, wv, wo, g2, xq, xk, xv, xo, g3, wg, wu, wd, n, ndp):
     _, T, D = latents.shape
     ctx = context.shape[1]
@@ -922,39 +982,39 @@
     cb, dcq, dckv, dafter1, sb_own, gains, block_out = cross_bwd(
         ctx, dh3, after2, own(gb), g3, xo_all, cq, kv_all, xq_all, after1, g2, out_own
     )
-    sb, dattn, cross_grads = gather_back(n, ndp, sb_own, wo, h2, dcq, cb, cattn, dckv, ctx_pad)
+    sb_own, down_grad = lax.optimization_barrier((sb_own, down_grad))
+    sb, dattn, cross_part, kv_part = gather_back(n, ndp, sb_own, wo, h2, dcq, cb, cattn, dckv, ctx_pad)
     sb = sb.reshape(T, D)
-    dq, dk, dv = attn_bwd(q, k, v, attn, dattn, lse, cs, sn)
-    dq, down_grad = lax.optimization_barrier((dq, down_grad))
-    latent_grad, self_grads = last(n, dq, dk, dv, wq, wk, wv, x_own, dafter1, g1, gains, h1, sb, attn)
-    self_grads = scatter(self_grads, "dp")
-
-    cross_grads = scatter(cross_grads, "dp")
-    cross_grads, gu_grad = lax.optimization_barrier((cross_grads, gu_grad))
+    dq, dk, dv, self_part, cross_part = attn_bwd(
+        n, q, k, v, attn, dattn, lse, cs, sn, h1, sb, kv_part, cross_part
+    )
+    cores = [[i for i in range(ndp) if i % 2 == c] for c in range(2)]
+    cross_grads = lax.psum_scatter(cross_part, "dp", scatter_dimension=0, axis_index_groups=cores, tiled=True)
+    self_grads = scatter(self_part, "dp")
+    dq, gu_grad = lax.optimization_barrier((dq, gu_grad))
+    latent_grad, gains = last(n, ndp, dq, dk, dv, wq, wk, wv, x_own, dafter1, g1, gains)
+
+    cross_grads, self_grads, gains = lax.optimization_barrier((cross_grads, self_grads, gains))
     gu_grad = gu_grad.astype(F32)
     gate_grad, up_grad, down_grad = gu_grad[:, :F], gu_grad[:, F:], down_grad.astype(F32).T
-    rows = cross_grads.shape[0]
-    kv_grads = cross_grads[:, 2 * n * W :].reshape(2, rows // 2, W).astype(F32)
-    cross_grads = cross_grads[:, : 2 * n * W].reshape(rows, 2, n, W).transpose(2, 0, 1, 3).reshape(n, rows, 2 * W)
-    cross_grads = swap_sum(cross_grads)
-    cross_grads, self_grads = lax.optimization_barrier((cross_grads, self_grads))
+    cross_grads = cross_grads.astype(F32)
     xq_grad, xo_grad = cross_grads[:, :W], cross_grads[:, W:].T
     self_grads = self_grads.astype(F32)
-    gains = self_grads[:, 4 * W :]
+    kv_grads = self_grads[:, 4 * W :].reshape(2, D // ndp // 2, W)
     return (
         block_out.reshape(1, T, D),
         latent_grad.astype(F32).reshape(1, T, D),
-        gains[:, 2],
+        gains[2],
         self_grads[:, :W],
         self_grads[:, W : 2 * W],
         self_grads[:, 2 * W : 3 * W],
         self_grads[:, 3 * W : 4 * W].T,
-        gains[:, 1],
+        gains[1],
         xq_grad,
         kv_grads[0],
         kv_grads[1],
         xo_grad,
-        gains[:, 0],
+        gains[0],
         gate_grad,
         up_grad,
         down_grad,

time: 570 us -> 516 us (0.905)
  waiting for transfers between devices: 88.8 us -> 15.8 us
  Pallas kernels: 425 us -> 447 us
    reduce_scatter x4 -> x3, waiting for transfers between devices: 88.7 us -> 15.4 us  [scatter(): return lax.psum_scatter(a, axis, scatter_dimension=0, tiled=True)]
    pallas_call x3 -> x2, Pallas kernels: 104 us -> 124 us  [the longest x1 73.5 us: last(): pl.pallas_call(functools.partial(last_kernel, n, ndp), in_specs=[VSPEC] *...]
  transfers between devices with their start and end apart: 4 -> 4, of which waited for: 2 -> 1; matrix products, arithmetic and copies ran while one was open for 1% -> 1% of each run, Pallas kernels for 40% -> 49%
where the time goes in v5:
time: 516 us; the launch traced here: 506 us
  Pallas kernels  447 us (87%)
  local copies, waits for them, and re-layouts  22.4 us (4%)
  waiting for transfers between devices  15.8 us (3%)
  between operations  14.4 us (3%)
  other arithmetic  6.56 us (1%)
    pallas_call x1, Pallas kernels, ff(): pl.pallas_call(functools.partial(ff_kernel, n), in_specs=[VSPEC] + [ANYSP...  77.5 us
    pallas_call x1, Pallas kernels, last(): pl.pallas_call(functools.partial(last_kernel, n, ndp), in_specs=[VSPEC] *...  73.5 us
    pallas_call x1, Pallas kernels, front(): pl.pallas_call(functools.partial(front_kernel, n, ctx), in_specs=[VSPEC]...  58.5 us
    pallas_call x1, Pallas kernels, attn_bwd(): pl.pallas_call(functools.partial(attn_bwd_kernel, n), in_specs=[VSPEC] *...  50.3 us
    pallas_call x1, Pallas kernels, gather_back(): pl.pallas_call(functools.partial(gather_kernel, n, ndp), in_specs=[VSPEC]...  45.6 us
    pallas_call x1, Pallas kernels, cross_bwd(): pl.pallas_call(functools.partial(cross_bwd_kernel, n, ctx), in_specs=[VSP...  39.7 us
    pallas_call x1, Pallas kernels, feed_grads(): pl.pallas_call(functools.partial(feed_kernel, n), in_specs=[VSPEC] * 5, o...  38.4 us
    pallas_call x1, Pallas kernels, out_rs(): pl.pallas_call(functools.partial(out_rs_kernel, n), in_specs=[VSPEC] * 4,...  33.8 us
  transfers between devices with their start and end apart: 4, of which 1 were waited for; matrix products, arithmetic and copies ran while one was open for 1% of the time, Pallas kernels for 49%

profile of v5, /device:TPU:0, one launch (start us, length us, event | category | flops | bytes accessed | tf_op | source)
XLA Modules:
  0.0 506.5 jit_solution(10043470875610537140)
XLA Ops:
  7.2 0.0 copy-start.5
  7.2 0.0 reduce-scatter.5.cloned.1.call-start
  7.3 1.3 reshape.87.g_ref
  8.6 1.3 reshape.89.g_ref.g2_ref
  9.9 1.3 reshape.90.g_ref.g3_ref
  11.2 0.5 fusion.2
  11.8 1.0 copy.33.c_ref
  12.9 1.0 copy.34.s_ref
  13.8 0.0 copy-done.5
  13.8 0.7 pad.4.ctx_ref
  14.5 2.6 dynamic-slice_bitcast_fusion
  17.2 58.5 %front.1 = (bf16[1024,1536]{1,0:T(8,128)(2,1)}, bf16[1024,384]{1,0:T(8,128)(2,1)}, bf16[1024,384]{1,0:T(8,128)(2,1)}, bf16[1024,384]{1,0:T(8,128)(2,1)}, bf16[10...) custom-call(bf16[1024,1536]{1,0:T(8,128)(2,1)} %bitcast.27, ...), custom_call_target="tpu_custom_call" | custom-call | flops 1000 | bytes 1000 | tf_op jit(solution)/shard_map/front/pallas_call | solution.py:194
  75.6 33.8 %out_rs.1 = (f32[256,1536]{1,0:T(8,128)}, bf16[256,1536]{1,0:T(8,128)(2,1)}) custom-call(bf16[1024,384]{1,0:T(8,128)(2,1)} %get-tuple-element.66.a_ref.o_ref, bf16[384,1536]{1,0:T(8,128)(2,1)} %w_ref.3, bf16[256,1536]{1,0:T(8,128)(2,1)} %get-tuple-element.132.x_ref, f32[1,1536]{1,0:T(1,128)} %reshape.89.g_ref.g2_ref), custom_call_target="tpu_custom_call" | custom-call | flops 1000 | bytes 1000 | tf_op jit(solution)/shard_map/out_rs/pallas_call | solution.py:372
  109.4 17.8 %cross_fwd.1 = (bf16[4,256,384]{2,1,0:T(8,128)(2,1)}, bf16[4,256,384]{2,1,0:T(8,128)(2,1)}, f32[256,1536]{1,0:T(8,128)}, bf16[256,1536]{1,0:T(8,128)(2,1)}) custom-call(bf16[256,1536]{1,0:T(8,128)(2,1)} %get-tuple-element.67.h_ref.h2_ref, f32[256,1536]{1,0:T(8,128)} %get-tuple-element.68.x_ref.after1_ref, bf16[4,1536,384]{2,1,0:T(8,128)(2,1)} %get-tuple-element.69.wq_ref, ...), custom_call_target="tpu_custom_call" | custom-call | flops 1000 | bytes 1000 | tf_op jit(solution)/shard_map/cross_fwd/pallas_call | solution.py:842
  127.3 77.5 %ff.1 = (bf16[4,256,1536]{2,1,0:T(8,128)(2,1)}, bf16[1024,1536]{1,0:T(8,128)(2,1)}, bf16[1024,3072]{1,0:T(8,128)(2,1)}, f32[256,1536]{1,0:T(8,128)}) custom-call(bf16[256,1536]{1,0:T(8,128)(2,1)} %get-tuple-element.72.h_in, bf16[1024,1536]{1,0:T(8,128)(2,1)} %bitcast.25, bf16[1536,1536]{1,0:T(8,128)(2,1)} %wg_hbm.1, bf16[1536,1536]{1,0:T(8,128)(2,1)} %wu_hbm.1, ...), custom_call_target="tpu_custom_call" | custom-call | flops 1000 | bytes 1000 | tf_op jit(solution)/shard_map/ff/pallas_call | solution.py:457
  204.8 11.9 %down_grads.1 = bf16[1536,1536]{1,0:T(8,128)(2,1)} custom-call(bf16[1024,1536]{1,0:T(8,128)(2,1)} %bitcast.26, bf16[1024,1536]{1,0:T(8,128)(2,1)} %get-tuple-element.74.hid_ref), custom_call_target="tpu_custom_call" | custom-call | flops 1000 | bytes 1000 | tf_op jit(solution)/shard_map/down_grads/pallas_call | solution.py:495
  216.7 0.0 reduce-scatter.5.cloned.1.call-update
  216.7 0.0 reduce-scatter.7.cloned.1.call-start
  216.8 38.4 %feed_grads.1 = (bf16[256,1536]{1,0:T(8,128)(2,1)}, bf16[1536,3072]{1,0:T(8,128)(2,1)}) custom-call(bf16[1024,1536]{1,0:T(8,128)(2,1)} %get-tuple-element.74.hid_ref, bf16[1536,1536]{1,0:T(8,128)(2,1)} %wd_ref.1, f32[256,1536]{1,0:T(8,128)} %get-tuple-element.75.after_ref.after2_ref, bf16[1024,1536]{1,0:T(8,128)(2,1)} %bitcast.28, ...), custom_call_target="tpu_custom_call" | custom-call | flops 1000 | bytes 1000 | tf_op jit(solution)/shard_map/feed_grads/pallas_call | solution.py:540
  255.1 0.0 reduce-scatter.7.cloned.1.call-update
  255.2 0.0 reduce-scatter.9.cloned.1.call-start
  255.2 39.7 %cross_bwd.1 = (bf16[256,1536]{1,0:T(8,128)(2,1)}, bf16[4,256,384]{2,1,0:T(8,128)(2,1)}, f32[4,288,384]{2,1,0:T(8,128)}, f32[256,1536]{1,0:T(8,128)}, bf16[256,1...) custom-call(f32[256,1536]{1,0:T(8,128)} %get-tuple-element.80.dh3_ref, ...), custom_call_target="tpu_custom_call" | custom-call | flops 1000 | bytes 1000 | tf_op jit(solution)/shard_map/cross_bwd/pallas_call | solution.py:929
  295.0 0.0 reduce-scatter.5.cloned.1.call-done
  295.0 45.6 %gather_back.1 = (bf16[4,256,1536]{2,1,0:T(8,128)(2,1)}, bf16[1024,384]{1,0:T(8,128)(2,1)}, bf16[4,768,768]{2,1,0:T(8,128)(2,1)}, bf16[1536,384]{1,0:T(8,128)(2,1)}) custom-call(bf16[256,1536]{1,0:T(8,128)(2,1)} %get-tuple-element.89.x_in, bf16[384,1536]{1,0:T(8,128)(2,1)} %w_ref.3, bf16[256,1536]{1,0:T(8,128)(2,1)} %get-tuple-element.67.h_ref.h2_ref, ...), custom_call_target="tpu_custom_call" | custom-call | flops 1000 | bytes 1000 | tf_op jit(solution)/shard_map/gather_back/pallas_call | solution.py:621
  340.6 50.3 %attn_bwd.1 = (bf16[1024,384]{1,0:T(8,128)(2,1)}, bf16[1024,384]{1,0:T(8,128)(2,1)}, bf16[1024,384]{1,0:T(8,128)(2,1)}, bf16[1536,1920]{1,0:T(8,128)(2,1)}, bf16[768,768]{1,0:T(8,128)(2,1)}) custom-call(bf16[1024,384]{1,0:T(8,128)(2,1)} %get-tuple-element.84.q_ref, bf16[1024,384]{1,0:T(8,128)(2,1)} %get-tuple-element.85.k_ref, ...), custom_call_target="tpu_custom_call" | custom-call | flops 1000 | bytes 1000 | tf_op jit(solution)/shard_map/attn_bwd/pallas_call | solution.py:713
  390.9 0.0 reduce-scatter.9.cloned.1.call-update
  390.9 0.0 copy-start.4
  390.9 0.3 reduce-scatter.11.cloned.1.call-start
  391.2 0.3 reduce-scatter.11.cloned.1.call-update
  391.5 0.5 copy-done.4
  392.0 1.1 convert_bitcast_fusion
  393.1 73.5 %last.1 = (bf16[4,256,1536]{2,1,0:T(8,128)(2,1)}, f32[8,192]{1,0:T(8,128)}) custom-call(bf16[1024,384]{1,0:T(8,128)(2,1)} %get-tuple-element.102.dq_ref, bf16[1024,384]{1,0:T(8,128)(2,1)} %get-tuple-element.103.dk_ref, bf16[1024,384]{1,0:T(8,128)(2,1)} %get-tuple-element.104.dv_ref, bf16[1536,384]{1,0:T(8,128)(2,1)} %wq_ref.3, bf16[1536,384]{1,0:T(8,128)(2,1)} %wk_ref.3, ...), custom_call_target="tpu_custom_call" | custom-call | flops 1000 | bytes 1000 | tf_op jit(solution)/shard_map/last/pallas_call | solution.py:779
  466.6 0.0 copy-done.1
  466.6 0.0 copy-start.3
  466.6 1.7 fusion.3
  468.3 1.1 copy-done.3
  469.4 3.6 bitcast_convert_fusion
  472.9 15.4 %reduce-scatter.11.cloned.1.call-done = bf16[192,1920]{1,0:T(8,128)(2,1)} async-done(((bf16[1536,1920]{1,0:T(8,128)(2,1)}), bf16[192,1920]{1,0:T(8,128)(2,1)}) %reduce-scatter.11.cloned.1.call-update) | async-done | bytes 737296 | tf_op jit(solution)/shard_map/reduce_scatter | solution.py:973
  488.4 1.7 slice.61
  490.1 1.2 convert_element_type.14
  491.2 1.7 fusion.4
  492.9 2.0 fusion.5
  494.9 0.0 copy-done
  494.9 0.1 convert_element_type.13
  495.0 1.4 fusion.6
  496.4 0.7 slice_bitcast_fusion
  497.1 0.7 slice_bitcast_fusion.1
  497.8 1.7 copy.38
  (10 shorter events, 0.1 us)
Async XLA Ops:
  7.2 6.7 %copy-start.5 = (bf16[1,130,768]{2,1,0:T(8,128)(2,1)S(1)}, bf16[1,130,768]{2,1,0:T(8,128)(2,1)}, u32[]{:S(2)}) copy-start(bf16[1,130,768]{2,1,0:T(8,128)(2,1)} %param.18) | copy-start | bytes 599044
  7.2 287.8 %reduce-scatter.5.cloned.1.call-start = ((), (), s32[]{:S(2)}) async-start(), calls=%async_computation.4 | async-start | bytes 5308416 | tf_op jit(solution)/shard_map/reduce_scatter | solution.py:973
  216.7 176.4 %reduce-scatter.7.cloned.1.call-start = ((), (), s32[]{:S(2)}) async-start(), calls=%async_computation.5 | async-start | bytes 10616832 | tf_op jit(solution)/shard_map/reduce_scatter | solution.py:973
  255.2 217.8 %reduce-scatter.9.cloned.1.call-start = ((), (), s32[]{:S(2)}) async-start(), calls=%async_computation.6 | async-start | bytes 1474560 | tf_op jit(solution)/shard_map/reduce_scatter | solution.py:992
  390.9 1.1 copy-start.4
  390.9 97.5 %reduce-scatter.11.cloned.1.call-start = ((), (), s32[]{:S(2)}) async-start(), calls=%async_computation.7 | async-start | bytes 6635520 | tf_op jit(solution)/shard_map/reduce_scatter | solution.py:973
  393.1 73.5 %copy-start.1 = (bf16[192,3072]{1,0:T(8,128)(2,1)S(1)}, bf16[192,3072]{1,0:T(8,128)(2,1)}, u32[]{:S(2)}) copy-start(bf16[192,3072]{1,0:T(8,128)(2,1)} %reduce-scatter.7.cloned.1.call-done) | copy-start | bytes 3538948
  466.6 2.8 copy-start.3
  488.4 6.5 %copy-start = (bf16[192,1920]{1,0:T(8,128)(2,1)S(1)}, bf16[192,1920]{1,0:T(8,128)(2,1)}, u32[]{:S(2)}) copy-start(bf16[192,1920]{1,0:T(8,128)(2,1)} %reduce-scatter.11.cloned.1.call-done) | copy-start | bytes 2211844
  490.1 7.7 %copy-start.2 = (bf16[4,256,1536]{2,1,0:T(8,128)(2,1)S(1)}, bf16[4,256,1536]{2,1,0:T(8,128)(2,1)}, u32[]{:S(2)}) copy-start(bf16[4,256,1536]{2,1,0:T(8,128)(2,1)} %get-tuple-element.83) | copy-start | bytes 9437188
Sparse Core Ops, SparseCore 0:
  216.8 55.1 reduce-scatter.4
  274.3 97.8 reduce-scatter.6
  391.0 29.4 reduce-scatter.8
  422.7 65.6 reduce-scatter.10

commit v6 on v5

--- a/solution.py
+++ b/solution.py
@@ -62,11 +62,10 @@
 
 
 def tables(length, group):
-    freq = 10000.0 ** (-jnp.arange(HALF, dtype=F32) / HALF)
-    angles = jnp.arange(length, dtype=F32)[:, None] * freq[None, :]
-    c, s = jnp.cos(angles), jnp.sin(angles)
-    reps = group // HEAD_DIM
-    return jnp.tile(jnp.concatenate([c, c], 1), (1, reps)), jnp.tile(jnp.concatenate([-s, s], 1), (1, reps))
+    freq = jnp.tile(10000.0 ** (-jnp.arange(HALF, dtype=F32) / HALF), group // HALF)
+    angles = lax.broadcasted_iota(F32, (length, group), 0) * freq[None, :]
+    front = lax.broadcasted_iota(jnp.int32, (length, group), 1) % HEAD_DIM < HALF
+    return jnp.cos(angles), jnp.where(front, -1.0, 1.0) * jnp.sin(angles)
 
 
 def turned(a):
@@ -78,131 +77,6 @@
 def head_masks(rows, group):
     lane = lax.broadcasted_iota(jnp.int32, (rows, group), 1) // HEAD_DIM
     return [jnp.where(lane == h, 1.0, 0.0) for h in range(group // HEAD_DIM)]
-
-
-def front_kernel(n, ctx, x_ref, g_ref, wq_ref, wk_ref, wv_ref, c_ref, s_ref, xq_ref, xo_ref, ctx_ref, xk_ref, xv_ref,
-                 h_ref, q_ref, k_ref, v_ref, o_ref, lse_ref, xqa_ref, xoa_ref, kva_ref,
-                 kv_own, sq, rq, so, ro, sk, rk, fsq, frq, fso, fro, local):
-    me = lax.axis_index("tensor")
-    dp = lax.axis_index("dp")
-    core = dp % 2
-    partner = dp + 1 - 2 * core
-    T, D = x_ref.shape
-    W = q_ref.shape[1]
-    KP = ctx_ref.shape[0]
-    greet(n, me, [partner])
-
-    rows_q = pl.ds(pl.multiple_of(core * (D // 2), 16), D // 2)
-    rows_o = pl.ds(pl.multiple_of(core * (W // 2), 16), W // 2)
-    def quarter(ref, rows):
-        return lambda t, i: ref.at[t, pl.ds(pl.multiple_of(core * (rows // 2) + i * (rows // 4), 16), rows // 4)]
-
-    gq = Gather(n, me, xq_ref.at[rows_q], lambda t: xqa_ref.at[t, rows_q], quarter(xqa_ref, D), sq, rq)
-    go = Gather(n, me, xo_ref.at[rows_o], lambda t: xoa_ref.at[t, rows_o], quarter(xoa_ref, W), so, ro)
-    gk = Gather(n, me, kv_own, lambda t: kva_ref.at[t], lambda t, i: kva_ref.at[t, pl.ds(i * KP, KP)], sk, rk)
-    gq.start()
-    go.start()
-    own = [
-        pltpu.make_async_copy(xq_ref, xqa_ref.at[me], local.at[0]),
-        pltpu.make_async_copy(xo_ref, xoa_ref.at[me], local.at[1]),
-    ]
-    for copy in own:
-        copy.start()
-    kv_own[:KP] = nn(ctx_ref[...], xk_ref[...]).astype(BF)
-    kv_own[KP:] = nn(ctx_ref[...], xv_ref[...]).astype(BF)
-    gk.start()
-    kva_ref[me] = kv_own[...]
-
-    tb = 256
-    reps = W // c_ref.shape[1]
-
-    def project(i, carry):
-        rows = pl.ds(pl.multiple_of(i * tb, tb), tb)
-        u, _ = unit(x_ref[rows, :].astype(F32))
-        h = (u * g_ref[...]).astype(BF)
-        h_ref[rows, :] = h
-        c = jnp.concatenate([c_ref[rows, :]] * reps, 1)
-        s = jnp.concatenate([s_ref[rows, :]] * reps, 1)
-        for w_ref, out_ref in ((wq_ref, q_ref), (wk_ref, k_ref)):
-            a = nn(h, w_ref[...])
-            out_ref[rows, :] = (a * c + turned(a) * s).astype(BF)
-        v_ref[rows, :] = nn(h, wv_ref[...]).astype(BF)
-        return carry
-
-    lax.fori_loop(0, T // tb, project, 0)
-    gq.relay()
-
-    G = lane_group(W)
-    mult = SCALE * LOG2E
-    masks = [m.astype(BF) for m in head_masks(1, G)]
-    lane = lax.broadcasted_iota(jnp.int32, (tb, G), 1) // HEAD_DIM
-    stat_lane = lax.broadcasted_iota(jnp.int32, (tb, 128), 1)
-
-    def heads(g, carry):
-        cols = pl.ds(pl.multiple_of(g * G, G), G) if G < W else slice(None)
-        k, v = k_ref[:, cols], v_ref[:, cols]
-
-        def block(i, inner):
-            rows = pl.ds(pl.multiple_of(i * tb, tb), tb)
-            q = q_ref[rows, cols]
-            out = jnp.zeros((tb, G), F32)
-            stats = jnp.zeros((tb, 128), F32)
-            for h in range(G // HEAD_DIM):
-                s = nt(q * masks[h], k)
-                top = jnp.max(s, axis=-1, keepdims=True) * mult
-                p = jnp.exp2(s * mult - top)
-                total = jnp.sum(p, axis=-1, keepdims=True)
-                o = nn(p.astype(BF), v) / total
-                out = jnp.where(lane == h, o, out)
-                stats = jnp.where(stat_lane == h, top + jnp.log2(total), stats)
-            o_ref[rows, cols] = out.astype(BF)
-            lse_ref[g, :, rows] = jnp.transpose(stats)[:8]
-            return inner
-
-        return lax.fori_loop(0, T // tb, block, carry)
-
-    lax.fori_loop(0, W // G, heads, 0)
-
-    go.relay()
-    gk.relay()
-    passed = []
-    for gather, ref, rows, send, recv in ((gq, xqa_ref, rows_q, fsq, frq), (go, xoa_ref, rows_o, fso, fro)):
-        for d in range(1, n):
-            gather.wait(d)
-            block = ref.at[me ^ d, rows]
-            copy = to_dp(block, block, send.at[d - 1], recv.at[d - 1], partner)
-            copy.start()
-            passed.append(copy)
-    for copy in own:
-        copy.wait()
-    for d in range(1, n):
-        gk.wait(d)
-    for copy in passed:
-        copy.wait_recv()
-    for copy in (gq, go, gk):
-        copy.finish()
-    for copy in passed:
-        copy.wait_send()
-
-
-def front(n, ctx, x, gain, wq, wk, wv, cs, sn, xq, xo, ctx_rows, xk, xv):
-    T, D = x.shape
-    W = wq.shape[1]
-    KP = ctx_rows.shape[0]
-    groups = W // lane_group(W)
-    link, pair = pltpu.SemaphoreType.DMA((links(n),)), pltpu.SemaphoreType.DMA((n - 1,))
-    return pl.pallas_call(
-        functools.partial(front_kernel, n, ctx),
-        in_specs=[VSPEC] * 12,
-        out_specs=[VSPEC] * 6 + [ANYSPEC] * 2 + [VSPEC],
-        out_shape=[sds((T, D), BF)]
-        + [sds((T, W), BF)] * 4
-        + [sds((groups, 8, T), F32), sds((n, D, W), BF), sds((n, W, D), BF), sds((n, 2 * KP, W), BF)],
-        scratch_shapes=[pltpu.VMEM((2 * KP, W), BF)] + [link] * 6 + [pair] * 4 + [pltpu.SemaphoreType.DMA((2,))],
-        compiler_params=params(collective_id=4, has_side_effects=True),
-        cost_estimate=cost(6 * T * D * W, 4 * T * D + 6 * D * W + 6 * T * W),
-        name="front",
-    )(x, gain, wq, wk, wv, cs, sn, xq, xo, ctx_rows, xk, xv)
 
 
 def greet(n, me, dps=()):
@@ -220,6 +94,24 @@
 
 def remote(src, dst, send, recv, target):
     return pltpu.make_async_remote_copy(src, dst, send, recv, device_id={"tensor": target}, device_id_type=MESH_ID)
+
+
+class Late:
+    def __init__(self, src, dst, sem):
+        self.dst, self.copy = dst, pltpu.make_async_copy(src, dst, sem)
+        self.copy.start()
+
+    def __call__(self):
+        self.copy.wait()
+        return self.dst
+
+
+def held(*arrays):
+    return [pltpu.VMEM(a.shape, a.dtype) for a in arrays] + [pltpu.SemaphoreType.DMA((len(arrays),))]
+
+
+def rows_of(ref, t, C):
+    return ref.at[pl.ds(pl.multiple_of(t * C, C), C)]
 
 
 def links(n):
@@ -313,19 +205,20 @@
         self.copies[i].wait_recv()
         return self.rbuf[i].astype(F32)
 
-    def halves(self, d):
-        H = self.a.shape[1] // 2
-        return self.a.at[self.me ^ d, pl.ds(0, H)], self.a.at[self.me ^ d, pl.ds(H, H)]
-
-    def start(self):
+    def halves(self, d, a=None):
+        a = self.a if a is None else a
+        H = a.shape[1] // 2
+        return a.at[self.me ^ d, pl.ds(0, H)], a.at[self.me ^ d, pl.ds(H, H)]
+
+    def start(self, a):
         if self.n == 4:
-            self.send(0, self.halves(3)[0], 1)
-            self.send(2, self.halves(3)[1], 2)
-            self.send(1, self.halves(1)[0], 1)
-            self.send(3, self.halves(2)[1], 2)
+            self.send(0, self.halves(3, a)[0], 1)
+            self.send(2, self.halves(3, a)[1], 2)
+            self.send(1, self.halves(1, a)[0], 1)
+            self.send(3, self.halves(2, a)[1], 2)
         else:
             for d in range(1, self.n):
-                self.send(d - 1, self.a.at[self.me ^ d], d)
+                self.send(d - 1, a.at[self.me ^ d], d)
 
     def middle(self):
         if self.n == 4:
@@ -349,40 +242,190 @@
             copy.wait_send()
 
 
-def out_rs_kernel(n, a_ref, w_ref, x_ref, g_ref, after_ref, h_ref, sbuf, rbuf, ss, rs):
+def front_kernel(n, ctx, x_hbm, g_ref, wq_hbm, wk_hbm, wv_hbm, c_ref, s_ref, xq_ref, xo_ref, ctx_ref, xk_hbm, xv_hbm,
+                 h_hbm, q_hbm, k_hbm, v_hbm, o_ref, lse_ref, xqa_ref, xoa_ref, kva_ref,
+                 kv_own, sq, rq, so, ro, sk, rk, fsq, frq, fso, fro, local,
+                 x_buf, wq_buf, wk_buf, wv_buf, xk_buf, xv_buf, lsem, h_ref, q_ref, k_ref, v_ref, osem):
+    xk, xv, x, wq, wk, wv = (
+        Late(src, dst, lsem.at[i])
+        for i, (src, dst) in enumerate(
+            (
+                (xk_hbm, xk_buf),
+                (xv_hbm, xv_buf),
+                (x_hbm, x_buf),
+                (wq_hbm, wq_buf),
+                (wk_hbm, wk_buf),
+                (wv_hbm, wv_buf),
+            )
+        )
+    )
     me = lax.axis_index("tensor")
-    C = x_ref.shape[0]
+    dp = lax.axis_index("dp")
+    core = dp % 2
+    partner = dp + 1 - 2 * core
+    T, D = x_hbm.shape
+    W = q_ref.shape[1]
+    KP = ctx_ref.shape[0]
+    greet(n, me, [partner])
+
+    rows_q = pl.ds(pl.multiple_of(core * (D // 2), 16), D // 2)
+    rows_o = pl.ds(pl.multiple_of(core * (W // 2), 16), W // 2)
+    def quarter(ref, rows):
+        return lambda t, i: ref.at[t, pl.ds(pl.multiple_of(core * (rows // 2) + i * (rows // 4), 16), rows // 4)]
+
+    gq = Gather(n, me, xq_ref.at[rows_q], lambda t: xqa_ref.at[t, rows_q], quarter(xqa_ref, D), sq, rq)
+    go = Gather(n, me, xo_ref.at[rows_o], lambda t: xoa_ref.at[t, rows_o], quarter(xoa_ref, W), so, ro)
+    gk = Gather(n, me, kv_own, lambda t: kva_ref.at[t], lambda t, i: kva_ref.at[t, pl.ds(i * KP, KP)], sk, rk)
+    gq.start()
+    go.start()
+    own = [
+        pltpu.make_async_copy(xq_ref, xqa_ref.at[me], local.at[0]),
+        pltpu.make_async_copy(xo_ref, xoa_ref.at[me], local.at[1]),
+    ]
+    for copy in own:
+        copy.start()
+    kv_own[:KP] = nn(ctx_ref[...], xk()[...]).astype(BF)
+    kv_own[KP:] = nn(ctx_ref[...], xv()[...]).astype(BF)
+    gk.start()
+    kva_ref[me] = kv_own[...]
+
+    tb = 256
+    reps = W // c_ref.shape[1]
+    x_ref, wq_ref, wk_ref, wv_ref = x(), wq(), wk(), wv()
+
+    def project(i, carry):
+        rows = pl.ds(pl.multiple_of(i * tb, tb), tb)
+        u, _ = unit(x_ref[rows, :].astype(F32))
+        h = (u * g_ref[...].reshape(1, D)).astype(BF)
+        h_ref[rows, :] = h
+        c = jnp.concatenate([c_ref[rows, :]] * reps, 1)
+        s = jnp.concatenate([s_ref[rows, :]] * reps, 1)
+        for w_ref, out_ref in ((wq_ref, q_ref), (wk_ref, k_ref)):
+            a = nn(h, w_ref[...])
+            out_ref[rows, :] = (a * c + turned(a) * s).astype(BF)
+        v_ref[rows, :] = nn(h, wv_ref[...]).astype(BF)
+        return carry
+
+    lax.fori_loop(0, T // tb, project, 0)
+    kept = [
+        pltpu.make_async_copy(src, dst, osem.at[i])
+        for i, (src, dst) in enumerate(((h_ref, h_hbm), (q_ref, q_hbm), (k_ref, k_hbm), (v_ref, v_hbm)))
+    ]
+    for copy in kept:
+        copy.start()
+    gq.relay()
+
+    G = lane_group(W)
+    mult = SCALE * LOG2E
+    masks = [m.astype(BF) for m in head_masks(1, G)]
+    lane = lax.broadcasted_iota(jnp.int32, (tb, G), 1) // HEAD_DIM
+    stat_lane = lax.broadcasted_iota(jnp.int32, (tb, 128), 1)
+
+    def heads(g, carry):
+        cols = pl.ds(pl.multiple_of(g * G, G), G) if G < W else slice(None)
+        k, v = k_ref[:, cols], v_ref[:, cols]
+
+        def block(i, inner):
+            rows = pl.ds(pl.multiple_of(i * tb, tb), tb)
+            q = q_ref[rows, cols]
+            out = jnp.zeros((tb, G), F32)
+            stats = jnp.zeros((tb, 128), F32)
+            for h in range(G // HEAD_DIM):
+                s = nt(q * masks[h], k)
+                top = jnp.max(s, axis=-1, keepdims=True) * mult
+                p = jnp.exp2(s * mult - top)
+                total = jnp.sum(p, axis=-1, keepdims=True)
+                o = nn(p.astype(BF), v) / total
+                out = jnp.where(lane == h, o, out)
+                stats = jnp.where(stat_lane == h, top + jnp.log2(total), stats)
+            o_ref[rows, cols] = out.astype(BF)
+            lse_ref[g, :, rows] = jnp.transpose(stats)[:8]
+            return inner
+
+        return lax.fori_loop(0, T // tb, block, carry)
+
+    lax.fori_loop(0, W // G, heads, 0)
+
+    go.relay()
+    gk.relay()
+    passed = []
+    for gather, ref, rows, send, recv in ((gq, xqa_ref, rows_q, fsq, frq), (go, xoa_ref, rows_o, fso, fro)):
+        for d in range(1, n):
+            gather.wait(d)
+            block = ref.at[me ^ d, rows]
+            copy = to_dp(block, block, send.at[d - 1], recv.at[d - 1], partner)
+            copy.start()
+            passed.append(copy)
+    for copy in (*own, *kept):
+        copy.wait()
+    for d in range(1, n):
+        gk.wait(d)
+    for copy in passed:
+        copy.wait_recv()
+    for copy in (gq, go, gk):
+        copy.finish()
+    for copy in passed:
+        copy.wait_send()
+
+
+def front(n, ctx, x, gain, wq, wk, wv, cs, sn, xq, xo, ctx_rows, xk, xv):
+    T, D = x.shape
+    W = wq.shape[1]
+    KP = ctx_rows.shape[0]
+    groups = W // lane_group(W)
+    link, pair = pltpu.SemaphoreType.DMA((links(n),)), pltpu.SemaphoreType.DMA((n - 1,))
+    return pl.pallas_call(
+        functools.partial(front_kernel, n, ctx),
+        in_specs=[ANYSPEC, VSPEC] + [ANYSPEC] * 3 + [VSPEC] * 5 + [ANYSPEC] * 2,
+        out_specs=[ANYSPEC] * 4 + [VSPEC] * 2 + [ANYSPEC] * 2 + [VSPEC],
+        out_shape=[sds((T, D), BF)]
+        + [sds((T, W), BF)] * 4
+        + [sds((groups, 8, T), F32), sds((n, D, W), BF), sds((n, W, D), BF), sds((n, 2 * KP, W), BF)],
+        scratch_shapes=[pltpu.VMEM((2 * KP, W), BF)] + [link] * 6 + [pair] * 4 + [pltpu.SemaphoreType.DMA((2,))]
+        + held(x, wq, wk, wv, xk, xv)
+        + held(sds((T, D), BF), *[sds((T, W), BF)] * 3),
+        compiler_params=params(collective_id=4, has_side_effects=True),
+        cost_estimate=cost(6 * T * D * W, 4 * T * D + 6 * D * W + 6 * T * W),
+        name="front",
+    )(x, gain, wq, wk, wv, cs, sn, xq, xo, ctx_rows, xk, xv)
+
+
+def out_rs_kernel(n, a_ref, w_ref, x_hbm, g_ref, after_ref, h_ref, sbuf, rbuf, ss, rs, x_buf, lsem):
+    me = lax.axis_index("tensor")
+    C, D = x_buf.shape
+    x = Late(rows_of(x_hbm, me, C), x_buf, lsem.at[0])
     greet(n, me)
 
     def part(t):
         return nn(a_ref[pl.ds(pl.multiple_of(t * C, C), C), :], w_ref[...])
 
     total, copies = reduce_parts(n, me, part, lambda: None, sbuf, rbuf, ss, rs)
-    after = x_ref[...].astype(F32) + total
+    after = x()[...].astype(F32) + total
     after_ref[...] = after
     u, _ = unit(after)
-    h_ref[...] = (u * g_ref[...]).astype(BF)
+    h_ref[...] = (u * g_ref[...].reshape(1, D)).astype(BF)
     for copy in copies.values():
         copy.wait_send()
 
 
 def out_rs(n, a, w, x, gain):
-    C, D = x.shape
-    T, W = a.shape
+    T, D = x.shape
+    C = T // n
+    W = a.shape[1]
     return pl.pallas_call(
         functools.partial(out_rs_kernel, n),
-        in_specs=[VSPEC] * 4,
+        in_specs=[VSPEC, VSPEC, ANYSPEC, VSPEC],
         out_specs=[VSPEC] * 2,
         out_shape=[sds((C, D), F32), sds((C, D), BF)],
-        scratch_shapes=reduce_bufs(n, C, D),
+        scratch_shapes=reduce_bufs(n, C, D) + held(sds((C, D), BF)),
         compiler_params=params(collective_id=0, has_side_effects=True),
         cost_estimate=cost(2 * T * W * D + 2e10, 8 * C * D),
         name="out_rs",
     )(a, w, x, gain)
 
 
-def ff_kernel(n, h_in, gb_hbm, wg_hbm, wu_hbm, wd_hbm, h_ref, hid_ref, dgu_ref, dh_ref,
-              gb_ref, wg_ref, wu_ref, wd_ref, sbuf, rbuf, ss, rs, ss2, rs2, ls):
+def ff_kernel(n, h_in, gb_hbm, wg_hbm, wu_hbm, wd_hbm, h_hbm, hid_hbm, dgu_hbm, dh_ref,
+              gb_ref, wg_ref, wu_ref, wd_ref, sbuf, rbuf, ss, rs, ss2, rs2, ls, h_ref, hid_ref, dgu_ref, osem):
     me = lax.axis_index("tensor")
     C, D = h_in.shape
     F = wg_ref.shape[1]
@@ -429,7 +472,17 @@
     def store_own(cols, val):
         dh_ref[:, cols] = val
 
+    kept = []
+
+    def keep(i, t):
+        pieces = [(h_ref.at[t], h_hbm.at[t])]
+        pieces += [(rows_of(a, t, C), rows_of(b, t, C)) for a, b in ((hid_ref, hid_hbm), (dgu_ref, dgu_hbm))]
+        for k, (src, dst) in enumerate(pieces):
+            kept.append(pltpu.make_async_copy(src, dst, osem.at[i, k]))
+            kept[-1].start()
+
     chunk(me, store_own)
+    keep(0, me)
     gather.relay()
     copies = {}
     for d in range(1, n):
@@ -440,6 +493,7 @@
             sbuf[d - 1, :, cols] = val.astype(BF)
 
         chunk(t, store_sent)
+        keep(d, t)
         copies[d] = remote(sbuf.at[d - 1], rbuf.at[d - 1], ss2.at[d - 1], rs2.at[d - 1], t)
         copies[d].start()
     gather.finish()
@@ -448,6 +502,8 @@
         dh_ref[...] += rbuf[d - 1].astype(F32)
     for d in range(1, n):
         copies[d].wait_send()
+    for copy in kept:
+        copy.wait()
 
 
 def ff(n, h, gb, wg, wu, wd):
@@ -457,7 +513,7 @@
     return pl.pallas_call(
         functools.partial(ff_kernel, n),
         in_specs=[VSPEC] + [ANYSPEC] * 4,
-        out_specs=[VSPEC] * 4,
+        out_specs=[ANYSPEC] * 3 + [VSPEC],
         out_shape=[sds((n, C, D), BF), sds((T, F), BF), sds((T, 2 * F), BF), sds((C, D), F32)],
         scratch_shapes=[
             pltpu.VMEM((T, D), BF),
@@ -469,7 +525,9 @@
         ]
         + [pltpu.SemaphoreType.DMA((links(n),))] * 2
         + [pltpu.SemaphoreType.DMA((n - 1,))] * 2
-        + [pltpu.SemaphoreType.DMA((4,))],
+        + [pltpu.SemaphoreType.DMA((4,))]
+        + [pltpu.VMEM((n, C, D), BF), pltpu.VMEM((T, F), BF), pltpu.VMEM((T, 2 * F), BF)]
+        + [pltpu.SemaphoreType.DMA((n, 3))],
         compiler_params=params(collective_id=1, has_side_effects=True),
         cost_estimate=cost(10 * T * D * F + 3e10, 6 * D * F + 8 * T * D),
         name="ff",
@@ -507,8 +565,13 @@
     )(gb, hidden)
 
 
-def feed_kernel(n, hid_ref, wd_ref, after_ref, h_ref, dgu_ref, out_ref, gr_ref, sbuf, rbuf, ss, rs):
+def feed_kernel(n, hid_ref, wd_ref, after_hbm, h_hbm, dgu_hbm, out_ref, gr_hbm,
+                sbuf, rbuf, ss, rs, h_ref, dgu_ref, after_ref, lsem, gr_ref, osem):
     me = lax.axis_index("tensor")
+    h, dgu, after = (
+        Late(src, dst, lsem.at[i])
+        for i, (src, dst) in enumerate(((h_hbm, h_ref), (dgu_hbm, dgu_ref), (after_hbm, after_ref)))
+    )
     C, D = after_ref.shape
     F2 = dgu_ref.shape[1]
     greet(n, me)
@@ -523,15 +586,24 @@
         for i in range(D // tb):
             rows = slice(i * tb, (i + 1) * tb)
             gr_ref[rows, cols] = tn(h_ref[:, rows], dgu_ref[:, cols]).astype(BF)
+        leave(j).start()
         return carry
 
+    def leave(j):
+        cols = pl.ds(pl.multiple_of(j * tf, tf), tf)
+        return pltpu.make_async_copy(gr_ref.at[:, cols], gr_hbm.at[:, cols], osem.at[j])
+
     def filler():
+        h()
+        dgu()
         lax.fori_loop(0, F2 // tf, tile, 0)
 
     total, copies = reduce_parts(n, me, part, filler, sbuf, rbuf, ss, rs)
-    out_ref[...] = (after_ref[...] + total).astype(BF)
+    out_ref[...] = (after()[...] + total).astype(BF)
     for copy in copies.values():
         copy.wait_send()
+    for j in range(F2 // tf):
+        leave(j).wait()
 
 
 def feed_grads(n, hidden, wd, after, h, dgu):
@@ -539,18 +611,20 @@
     T, F2 = dgu.shape
     return pl.pallas_call(
         functools.partial(feed_kernel, n),
-        in_specs=[VSPEC] * 5,
-        out_specs=[VSPEC] * 2,
+        in_specs=[VSPEC] * 2 + [ANYSPEC] * 3,
+        out_specs=[VSPEC, ANYSPEC],
         out_shape=[sds((C, D), BF), sds((D, F2), BF)],
-        scratch_shapes=reduce_bufs(n, C, D),
+        scratch_shapes=reduce_bufs(n, C, D)
+        + held(h, dgu, after)
+        + [pltpu.VMEM((D, F2), BF), pltpu.SemaphoreType.DMA((F2 // 512,))],
         compiler_params=params(collective_id=6, has_side_effects=True),
         cost_estimate=cost(3 * T * D * F2, 6 * D * F2),
         name="feed_grads",
     )(hidden, wd, after, h, dgu)
 
 
-def gather_kernel(n, ndp, x_in, w_ref, h2_ref, dcq_ref, cb_ref, ca_ref, dkv_ref, ctx_ref, x_ref, da_ref, gr_ref, kv_ref,
-                  buf, other, ksend, krecv, ss, rs, ss2, rs2, pair):
+def gather_kernel(n, ndp, x_in, w_ref, h2_ref, dcq_ref, cb_ref, ca_ref, dkv_ref, ctx_ref, at_ref, x_hbm, da_ref, gr_hbm, kv_ref,
+                  buf, other, ksend, krecv, ss, rs, ss2, rs2, pair, x_ref, acc, gr_ref, osem, gsem):
     me = lax.axis_index("tensor")
     dp = lax.axis_index("dp")
     core = dp % 2
@@ -568,11 +642,22 @@
         kv[d] = remote(ksend.at[d - 1], krecv.at[d - 1], ss2.at[d - 1], rs2.at[d - 1], me ^ d)
         kv[d].start()
 
-    def back(t, x):
-        da_ref[pl.ds(pl.multiple_of(t * C, C), C), :] = nt(x, w_ref[...]).astype(BF)
+    kept = []
+
+    def back(i, t):
+        rows = pl.ds(pl.multiple_of(t * C, C), C)
+        x = x_ref[t]
+        kept.append(pltpu.make_async_copy(x_ref.at[t], x_hbm.at[t], osem.at[i]))
+        kept[-1].start()
+        da_ref[rows, :] = nt(x, w_ref[...]).astype(BF)
+        term = tn(x, at_ref[rows, :])
+        if i == 0:
+            acc[...] = term
+        else:
+            acc[...] += term
 
     x_ref[me] = x_in[...]
-    back(me, x_in[...])
+    back(0, me)
 
     for j in range(ndp // 2):
         h2, cb = h2_ref[:, 2 * R * j : 2 * R * (j + 1)], cb_ref[:, 2 * R * j : 2 * R * (j + 1)]
@@ -596,46 +681,60 @@
         kvg = tn(ctx_ref[...], dkv[half * KP : (half + 1) * KP].astype(BF)).astype(BF)
         S = kvg.shape[0] // ndp
         for i in range(ndp):
-            kv_ref[(2 * i + half) * S : (2 * i + half + 1) * S] = kvg[i * S : (i + 1) * S]
-    for d in range(1, n):
+            kv_ref[(2 * i + half) * S : (2 * i + half + 1) * S, W:] = kvg[i * S : (i + 1) * S]
+    for d in range(1, n - 1):
         gather.wait(d)
-        back(me ^ d, x_ref[me ^ d])
+        back(d, me ^ d)
     swap.wait_recv()
+
+    def leave(t):
+        return pltpu.make_async_copy(gr_ref.at[t], gr_hbm.at[t], gsem.at[t])
 
     def add(t, carry):
         gr_ref[t] = (buf[core, t].astype(F32) + other[t].astype(F32)).astype(BF)
+        leave(t).start()
         return carry
 
     lax.fori_loop(0, n, add, 0)
+    gather.wait(n - 1)
+    back(n - 1, me ^ (n - 1))
+    kv_ref[:, :W] = acc[...].astype(BF)
     gather.finish()
+    for copy in kept:
+        copy.wait()
+    for t in range(n):
+        leave(t).wait()
     for d in range(1, n):
         kv[d].wait_send()
     swap.wait_send()
 
 
-def gather_back(n, ndp, x, w, h2, dcq, cb, ca, dkv, ctx):
+def gather_back(n, ndp, x, w, h2, dcq, cb, ca, dkv, ctx, attn):
     C, D = x.shape
     W = w.shape[0]
     KP = ctx.shape[0]
     half = (n, D // 2, 2 * W)
     return pl.pallas_call(
         functools.partial(gather_kernel, n, ndp),
-        in_specs=[VSPEC] * 8,
-        out_specs=[VSPEC] * 4,
-        out_shape=[sds((n, C, D), BF), sds((n * C, W), BF), sds(half, BF), sds((2 * ctx.shape[1], W), BF)],
+        in_specs=[VSPEC] * 9,
+        out_specs=[ANYSPEC, VSPEC, ANYSPEC, VSPEC],
+        out_shape=[sds((n, C, D), BF), sds((n * C, W), BF), sds(half, BF), sds((D, 2 * W), BF)],
         scratch_shapes=[pltpu.VMEM((2, *half), BF), pltpu.VMEM(half, BF)]
         + [pltpu.VMEM((n - 1, 2 * KP, W), BF)] * 2
         + [pltpu.SemaphoreType.DMA((links(n),))] * 2
         + [pltpu.SemaphoreType.DMA((n - 1,))] * 2
-        + [pltpu.SemaphoreType.DMA((2,))],
+        + [pltpu.SemaphoreType.DMA((2,))]
+        + [pltpu.VMEM((n, C, D), BF), pltpu.VMEM((D, W), F32), pltpu.VMEM(half, BF)]
+        + [pltpu.SemaphoreType.DMA((n,))] * 2,
         compiler_params=params(collective_id=2, has_side_effects=True),
         cost_estimate=cost(2 * n * C * W * D + 2e10, 8 * C * D),
         name="gather_back",
-    )(x, w, h2, dcq, cb, ca, dkv, ctx)
-
-
-def attn_bwd_kernel(n, q_ref, k_ref, v_ref, o_ref, do_ref, lse_ref, c_ref, s_ref, h_ref, sb_ref, kv_ref, a_ref,
-                    dq_ref, dk_ref, dv_ref, gr_ref, x_ref, dk_acc, dv_acc, kt_ref, sbuf, rbuf, ss, rs):
+    )(x, w, h2, dcq, cb, ca, dkv, ctx, attn)
+
+
+def attn_bwd_kernel(n, q_ref, k_ref, v_ref, o_ref, do_ref, lse_ref, c_ref, s_ref, h_hbm, a_hbm,
+                    dq_ref, dk_ref, dv_ref, gr_hbm, x_ref, dk_acc, dv_acc, kt_ref, sbuf, rbuf, ss, rs,
+                    a_ref, h_ref, lsem, gr_ref, osem):
     me = lax.axis_index("tensor")
     T, W = q_ref.shape
     G = lane_group(W)
@@ -644,7 +743,8 @@
     nh = G // HEAD_DIM
     greet(n, me)
     shards = ShardSum(n, me, a_ref, sbuf, rbuf, ss, rs)
-    shards.start()
+    shards.start(a_hbm)
+    a, h_all = Late(a_hbm, a_ref, lsem.at[0]), Late(h_hbm, h_ref, lsem.at[1])
     masks = [m.astype(BF) for m in head_masks(1, G)]
     head_rows = jnp.where(
         lax.broadcasted_iota(jnp.int32, (16, G), 0) == lax.broadcasted_iota(jnp.int32, (16, G), 1) // HEAD_DIM, 1.0, 0.0
@@ -687,23 +787,30 @@
         return outer
 
     lax.fori_loop(0, W // G, heads, 0)
+    a()
     shards.middle()
+    h_all()
     tf = 256
+
+    def leave(j):
+        rows = pl.ds(pl.multiple_of(j * tf, tf), tf)
+        return pltpu.make_async_copy(gr_ref.at[rows], gr_hbm.at[rows], osem.at[j])
 
     def weights(j, carry):
         rows = pl.ds(pl.multiple_of(j * tf, tf), tf)
         h = h_ref[:, rows]
         for i, g_ref in enumerate((dq_ref, dk_ref, dv_ref)):
             gr_ref[rows, i * W : (i + 1) * W] = tn(h, g_ref[...]).astype(BF)
-        gr_ref[rows, 3 * W : 4 * W] = tn(sb_ref[:, rows], o_ref[...]).astype(BF)
-        gr_ref[rows, 4 * W :] = kv_ref[rows, :]
+        leave(j).start()
         return carry
 
     lax.fori_loop(0, gr_ref.shape[0] // tf, weights, 0)
     shards.store(x_ref)
-
-
-def attn_bwd(n, q, k, v, o, do, lse, cs, sn, h, sb, kv, a):
+    for j in range(gr_ref.shape[0] // tf):
+        leave(j).wait()
+
+
+def attn_bwd(n, q, k, v, o, do, lse, cs, sn, h, a):
     T, W = q.shape
     D = h.shape[1]
     G = lane_group(W)
@@ -712,23 +819,26 @@
     H = R // 2 if n == 4 else R
     return pl.pallas_call(
         functools.partial(attn_bwd_kernel, n),
-        in_specs=[VSPEC] * 12,
-        out_specs=[VSPEC] * 5,
-        out_shape=[sds((T, W), BF)] * 3 + [sds((D, 5 * W), BF), sds((R, N), BF)],
+        in_specs=[VSPEC] * 8 + [ANYSPEC] * 2,
+        out_specs=[VSPEC] * 3 + [ANYSPEC, VSPEC],
+        out_shape=[sds((T, W), BF)] * 3 + [sds((D, 3 * W), BF), sds((R, N), BF)],
         scratch_shapes=[pltpu.VMEM((T, G), F32), pltpu.VMEM((T, G), F32), pltpu.VMEM((G, T), BF)]
         + [pltpu.VMEM((2, H, N), BF), pltpu.VMEM((slots, H, N), BF)]
-        + [pltpu.SemaphoreType.DMA((slots,))] * 2,
+        + [pltpu.SemaphoreType.DMA((slots,))] * 2
+        + held(a, h)
+        + [pltpu.VMEM((D, 3 * W), BF), pltpu.SemaphoreType.DMA((D // 256,))],
         compiler_params=params(collective_id=5, has_side_effects=True),
         cost_estimate=cost(40 * T * T * W, 16 * T * W, T * T * W // HEAD_DIM),
         name="attn_bwd",
-    )(q, k, v, o, do, lse, cs, sn, h, sb, kv, a)
-
-
-def last_kernel(n, ndp, dq_ref, dk_ref, dv_ref, wq_ref, wk_ref, wv_ref, x_ref, da_ref, g_ref, gg_in,
-                lbuf, gg_ref, sbuf, rbuf, gbuf, gsum, gown, gall, ss, rs, ss2, rs2, ss3, rs3, ss4, rs4):
+    )(q, k, v, o, do, lse, cs, sn, h, a)
+
+
+def last_kernel(n, ndp, dq_ref, dk_ref, dv_ref, wq_ref, wk_ref, wv_ref, x_hbm, da_ref, g_ref, gg_in,
+                lbuf, gg_ref, sbuf, rbuf, gbuf, gsum, gown, gall, ss, rs, ss2, rs2, ss3, rs3, ss4, rs4, x_buf, lsem):
     me = lax.axis_index("tensor")
     dp = lax.axis_index("dp")
-    C, D = x_ref.shape
+    C, D = x_buf.shape
+    x = Late(rows_of(x_hbm, me, C), x_buf, lsem.at[0])
     R = D // ndp
     others = [(dp + i) % ndp for i in range(1, ndp)]
     greet(n, me, others)
@@ -738,18 +848,18 @@
         return nt(dq_ref[rows, :], wq_ref[...]) + nt(dk_ref[rows, :], wk_ref[...]) + nt(dv_ref[rows, :], wv_ref[...])
 
     total, copies = reduce_parts(n, me, part, lambda: None, sbuf, rbuf, ss, rs)
-    u, inverse = unit(x_ref[...].astype(F32))
-    lbuf[me] = (da_ref[...] + norm_back(total, u, inverse, g_ref[...])).astype(BF)
-    gather = Gather(
-        n, me, lbuf.at[me], lambda t: lbuf.at[t], lambda t, i: lbuf.at[t, pl.ds(i * C // 2, C // 2)], ss2, rs2
-    )
-    gather.start()
+    u, inverse = unit(x()[...].astype(F32))
     row = lax.broadcasted_iota(jnp.int32, (8, D), 0)
     gsum[...] = gg_in[...] + jnp.where(row == 2, jnp.sum(total * u, axis=0, keepdims=True), 0.0)
     small = {}
     for d in range(1, n):
         small[d] = remote(gsum, gbuf.at[d - 1], ss3.at[d - 1], rs3.at[d - 1], me ^ d)
         small[d].start()
+    lbuf[me] = (da_ref[...] + norm_back(total, u, inverse, g_ref[...].reshape(1, D))).astype(BF)
+    gather = Gather(
+        n, me, lbuf.at[me], lambda t: lbuf.at[t], lambda t, i: lbuf.at[t, pl.ds(i * C // 2, C // 2)], ss2, rs2
+    )
+    gather.start()
     gains = gsum[...]
     for d in range(1, n):
         small[d].wait_recv()
@@ -760,12 +870,12 @@
     for i, other in enumerate(others):
         sums.append(to_dp(gown.at[other], gall.at[i], ss4.at[i], rs4.at[i], other))
         sums[i].start()
+    gather.relay()
     mine = gown[dp]
     for i in range(ndp - 1):
         sums[i].wait_recv()
         mine = mine + gall[i]
     gg_ref[...] = mine
-    gather.relay()
     for d in range(1, n):
         gather.wait(d)
     gather.finish()
@@ -774,11 +884,11 @@
 
 
 def last(n, ndp, dq, dk, dv, wq, wk, wv, x, da, gain, gains):
-    C, D = x.shape
     T, W = dq.shape
+    C, D = da.shape
     return pl.pallas_call(
         functools.partial(last_kernel, n, ndp),
-        in_specs=[VSPEC] * 10,
+        in_specs=[VSPEC] * 6 + [ANYSPEC] + [VSPEC] * 3,
         out_specs=[VSPEC] * 2,
         out_shape=[sds((n, C, D), BF), sds((8, D // ndp), F32)],
         scratch_shapes=reduce_bufs(n, C, D)[:2]
@@ -787,14 +897,16 @@
         + reduce_bufs(n, C, D)[2:]
         + [pltpu.SemaphoreType.DMA((links(n),))] * 2
         + [pltpu.SemaphoreType.DMA((n - 1,))] * 2
-        + [pltpu.SemaphoreType.DMA((ndp - 1,))] * 2,
+        + [pltpu.SemaphoreType.DMA((ndp - 1,))] * 2
+        + held(sds((C, D), BF)),
         compiler_params=params(collective_id=3, has_side_effects=True),
         cost_estimate=cost(6 * T * W * D + 4e10, 8 * T * D),
         name="last",
     )(dq, dk, dv, wq, wk, wv, x, da, gain, gains)
 
 
-def cross_fwd_kernel(n, ctx, h_ref, x_ref, wq_ref, kv_ref, wo_ref, g_ref, q_ref, o_ref, after_ref, h3_ref):
+def cross_fwd_kernel(n, ctx, h_ref, x_ref, wq_ref, kv_ref, wo_hbm, g_ref, q_ref, o_ref, after_ref, h3_ref, wo_ref, lsem):
+    wo = Late(wo_hbm, wo_ref, lsem.at[0])
     _, C, W = q_ref.shape
     KP = kv_ref.shape[1] // 2
     mult = SCALE * LOG2E
@@ -822,6 +934,7 @@
     lax.fori_loop(0, n * per, group, 0)
     D = h_ref.shape[1]
     tf = 256
+    wo()
 
     def project(j, carry):
         cols = pl.ds(pl.multiple_of(j * tf, tf), tf)
@@ -833,7 +946,7 @@
 
     lax.fori_loop(0, D // tf, project, 0)
     u, _ = unit(after_ref[...])
-    h3_ref[...] = (u * g_ref[...]).astype(BF)
+    h3_ref[...] = (u * g_ref[...].reshape(1, D)).astype(BF)
 
 
 def cross_fwd(ctx, h, x, wq, kv, wo, gain):
@@ -841,18 +954,31 @@
     n, W = wq.shape[0], wq.shape[2]
     return pl.pallas_call(
         functools.partial(cross_fwd_kernel, n, ctx),
-        in_specs=[VSPEC] * 6,
+        in_specs=[VSPEC] * 4 + [ANYSPEC, VSPEC],
         out_specs=[VSPEC] * 4,
         out_shape=[sds((n, C, W), BF), sds((n, C, W), BF), sds((C, D), F32), sds((C, D), BF)],
+        scratch_shapes=held(wo),
         compiler_params=params(),
         cost_estimate=cost(4 * C * D * n * W + 16 * C * 256 * n * W, 8 * D * n * W),
         name="cross_fwd",
     )(h, x, wq, kv, wo, gain)
 
 
-def cross_bwd_kernel(n, ctx, dh3_ref, after2_ref, cot_ref, g3_ref, wo_ref, q_ref, kv_ref, wq_ref, after1_ref, g2_ref, bo_in,
-                     cb_ref, dq_ref, dkv_ref, da_ref, sb_ref, gg_ref, bo_ref, dh2_ref, ss, rs):
+def cross_bwd_kernel(n, ctx, dh3_ref, after2_ref, cot_hbm, g3_ref, wo_hbm, q_ref, kv_ref, wq_hbm, after1_hbm, g2_ref, bo_in,
+                     cb_ref, dq_ref, dkv_ref, da_ref, sb_ref, gg_ref, bo_ref, dh2_ref, ss, rs,
+                     cot_buf, wo_ref, wq_ref, after1_buf, lsem):
     me = lax.axis_index("tensor")
+    cot, wo, wq, after1 = (
+        Late(src, dst, lsem.at[i])
+        for i, (src, dst) in enumerate(
+            (
+                (rows_of(cot_hbm, me, cot_buf.shape[0]), cot_buf),
+                (wo_hbm, wo_ref),
+                (wq_hbm, wq_ref),
+                (after1_hbm, after1_buf),
+            )
+        )
+    )
     _, C, W = q_ref.shape
     KP = kv_ref.shape[1] // 2
     D = da_ref.shape[1]
@@ -869,9 +995,10 @@
     dh3 = dh3_ref[...]
     u3, inv3 = unit(after2_ref[...])
     gain3 = jnp.sum(dh3 * u3, axis=0, keepdims=True)
-    da2 = cot_ref[...].astype(F32) + norm_back(dh3, u3, inv3, g3_ref[...])
+    da2 = cot()[...].astype(F32) + norm_back(dh3, u3, inv3, g3_ref[...].reshape(1, D))
     da_ref[...] = da2
     cb_ref[...] = da2.astype(BF)
+    wo()
 
     def group(g, carry):
         t = g // per
@@ -899,6 +1026,7 @@
 
     lax.fori_loop(0, n * per, group, 0)
     gather.relay()
+    wq()
     tf = 256
 
     def project(j, carry):
@@ -911,9 +1039,9 @@
 
     lax.fori_loop(0, D // tf, project, 0)
     dh2 = dh2_ref[...]
-    u2, inv2 = unit(after1_ref[...])
+    u2, inv2 = unit(after1()[...])
     gain2 = jnp.sum(dh2 * u2, axis=0, keepdims=True)
-    da1 = da_ref[...] + norm_back(dh2, u2, inv2, g2_ref[...])
+    da1 = da_ref[...] + norm_back(dh2, u2, inv2, g2_ref[...].reshape(1, D))
     da_ref[...] = da1
     sb_ref[...] = da1.astype(BF)
     row = lax.broadcasted_iota(jnp.int32, (8, D), 0)
@@ -928,7 +1056,7 @@
     n, W = wq.shape[0], wq.shape[2]
     return pl.pallas_call(
         functools.partial(cross_bwd_kernel, n, ctx),
-        in_specs=[VSPEC] * 11,
+        in_specs=[VSPEC, VSPEC, ANYSPEC, VSPEC, ANYSPEC, VSPEC, VSPEC, ANYSPEC, ANYSPEC, VSPEC, VSPEC],
         out_specs=[VSPEC] * 7,
         out_shape=[
             sds((C, D), BF),
@@ -939,7 +1067,9 @@
             sds((8, D), F32),
             sds((n, C, D), BF),
         ],
-        scratch_shapes=[pltpu.VMEM((C, D), F32)] + [pltpu.SemaphoreType.DMA((links(n),))] * 2,
+        scratch_shapes=[pltpu.VMEM((C, D), F32)]
+        + [pltpu.SemaphoreType.DMA((links(n),))] * 2
+        + held(sds((C, D), BF), wo, wq, after1),
         compiler_params=params(collective_id=7, has_side_effects=True),
         cost_estimate=cost(4 * C * D * n * W + 40 * C * 256 * n * W, 8 * D * n * W),
         name="cross_bwd",
@@ -952,19 +1082,15 @@
     W = wq.shape[1]
     F = wg.shape[1]
     C = T // n
-    me = lax.axis_index("tensor")
     x = latents.reshape(T, D)
     gb = cotangent.reshape(T, D)
     ctx_rows = context.reshape(ctx, -1)
     KP = -(-ctx // 16) * 16
     cs, sn = tables(T, lane_group(W))
-    g1, g2, g3 = (g.reshape(1, D) for g in (g1, g2, g3))
-    own = lambda a: lax.dynamic_slice_in_dim(a, me * C, C, 0)
 
     ctx_pad = jnp.pad(ctx_rows, ((0, KP - ctx), (0, 0)))
     h1, q, k, v, attn, lse, xq_all, xo_all, kv_all = front(n, ctx, x, g1, wq, wk, wv, cs, sn, xq, xo, ctx_pad, xk, xv)
-    x_own = own(x)
-    after1, h2 = out_rs(n, attn, wo, x_own, g2)
+    after1, h2 = out_rs(n, attn, wo, x, g2)
     cq, cattn, after2, h3_own = cross_fwd(ctx, h2, after1, xq_all, kv_all, xo_all, g3)
     h3, hidden, dgu, dh3 = ff(n, h3_own, gb, wg, wu, wd)
     h3 = h3.reshape(T, D)
@@ -980,35 +1106,39 @@
     gu_grad = scatter(gu_part, "dp")
 
     cb, dcq, dckv, dafter1, sb_own, gains, block_out = cross_bwd(
-        ctx, dh3, after2, own(gb), g3, xo_all, cq, kv_all, xq_all, after1, g2, out_own
+        ctx, dh3, after2, gb, g3, xo_all, cq, kv_all, xq_all, after1, g2, out_own
     )
     sb_own, down_grad = lax.optimization_barrier((sb_own, down_grad))
-    sb, dattn, cross_part, kv_part = gather_back(n, ndp, sb_own, wo, h2, dcq, cb, cattn, dckv, ctx_pad)
-    sb = sb.reshape(T, D)
-    dq, dk, dv, self_part, cross_part = attn_bwd(
-        n, q, k, v, attn, dattn, lse, cs, sn, h1, sb, kv_part, cross_part
-    )
+    sb, dattn, cross_part, early_part = gather_back(n, ndp, sb_own, wo, h2, dcq, cb, cattn, dckv, ctx_pad, attn)
+    early_grads = scatter(early_part, "dp")
+    dq, dk, dv, self_part, cross_part = attn_bwd(n, q, k, v, attn, dattn, lse, cs, sn, h1, cross_part)
     cores = [[i for i in range(ndp) if i % 2 == c] for c in range(2)]
     cross_grads = lax.psum_scatter(cross_part, "dp", scatter_dimension=0, axis_index_groups=cores, tiled=True)
     self_grads = scatter(self_part, "dp")
     dq, gu_grad = lax.optimization_barrier((dq, gu_grad))
-    latent_grad, gains = last(n, ndp, dq, dk, dv, wq, wk, wv, x_own, dafter1, g1, gains)
-
-    cross_grads, self_grads, gains = lax.optimization_barrier((cross_grads, self_grads, gains))
+    latent_grad, gains = last(n, ndp, dq, dk, dv, wq, wk, wv, x, dafter1, g1, gains)
+
+    latent_grad = latent_grad.astype(F32)
     gu_grad = gu_grad.astype(F32)
     gate_grad, up_grad, down_grad = gu_grad[:, :F], gu_grad[:, F:], down_grad.astype(F32).T
+    early_grads, gains, latent_grad, gate_grad, up_grad = lax.optimization_barrier(
+        (early_grads, gains, latent_grad, gate_grad, up_grad)
+    )
+    early_grads = early_grads.astype(F32)
+    so_grad, kv_grads = early_grads[:, :W].T, early_grads[:, W:].reshape(2, D // ndp // 2, W)
+    cross_grads, so_grad, kv_grads = lax.optimization_barrier((cross_grads, so_grad, kv_grads))
     cross_grads = cross_grads.astype(F32)
     xq_grad, xo_grad = cross_grads[:, :W], cross_grads[:, W:].T
+    self_grads, xq_grad, xo_grad = lax.optimization_barrier((self_grads, xq_grad, xo_grad))
     self_grads = self_grads.astype(F32)
-    kv_grads = self_grads[:, 4 * W :].reshape(2, D // ndp // 2, W)
     return (
         block_out.reshape(1, T, D),
-        latent_grad.astype(F32).reshape(1, T, D),
+        latent_grad.reshape(1, T, D),
         gains[2],
         self_grads[:, :W],
         self_grads[:, W : 2 * W],
         self_grads[:, 2 * W : 3 * W],
-        self_grads[:, 3 * W : 4 * W].T,
+        so_grad,
         gains[1],
         xq_grad,
         kv_grads[0],

time: 516 us -> 491 us (0.952)
  Pallas kernels: 447 us -> 415 us
  waiting for transfers between devices: 15.8 us -> 27.2 us
  local copies, waits for them, and re-layouts: 22.4 us -> 13.8 us
    reduce_scatter x3 -> x4, waiting for transfers between devices: 15.4 us -> 26.6 us  [scatter(): return lax.psum_scatter(a, axis, scatter_dimension=0, tiled=True)]
    pallas_call x3, Pallas kernels: 131 us -> 120 us  [the longest x1 54.4 us: front(): pl.pallas_call(functools.partial(front_kernel, n, ctx), in_specs=[ANYSPEC...]
    convert_element_type x1 -> x2, other arithmetic: 0.1 us -> 6.56 us  [the longest x1 5.56 us: body(): latent_grad = latent_grad.astype(F32)]
    pallas_call x1, Pallas kernels: 73.5 us -> 68 us  [last(): pl.pallas_call(functools.partial(last_kernel, n, ndp), in_specs=[VSPEC] *...]
    pallas_call x1, Pallas kernels: 50.3 us -> 45.1 us  [attn_bwd(): pl.pallas_call(functools.partial(attn_bwd_kernel, n), in_specs=[VSPEC] *...]
  transfers between devices with their start and end apart: 4 -> 5, of which waited for: 1 -> 1; matrix products, arithmetic and copies ran while one was open for 1% -> 3% of each run, Pallas kernels for 49% -> 47%
where the time goes in v6:
time: 491 us; the launch traced here: 482 us
  Pallas kernels  415 us (85%)
  waiting for transfers between devices  27.2 us (6%)
  between operations  14.4 us (3%)
  local copies, waits for them, and re-layouts  13.8 us (3%)
  other arithmetic  11.5 us (2%)
    pallas_call x1, Pallas kernels, ff(): pl.pallas_call(functools.partial(ff_kernel, n), in_specs=[VSPEC] + [ANYSP...  74 us
    pallas_call x1, Pallas kernels, last(): pl.pallas_call(functools.partial(last_kernel, n, ndp), in_specs=[VSPEC] *...  68 us
    pallas_call x1, Pallas kernels, front(): pl.pallas_call(functools.partial(front_kernel, n, ctx), in_specs=[ANYSPEC...  54.4 us
    pallas_call x1, Pallas kernels, attn_bwd(): pl.pallas_call(functools.partial(attn_bwd_kernel, n), in_specs=[VSPEC] *...  45.1 us
    pallas_call x1, Pallas kernels, gather_back(): pl.pallas_call(functools.partial(gather_kernel, n, ndp), in_specs=[VSPEC]...  43.1 us
    pallas_call x1, Pallas kernels, cross_bwd(): pl.pallas_call(functools.partial(cross_bwd_kernel, n, ctx), in_specs=[VSP...  36.4 us
    pallas_call x1, Pallas kernels, out_rs(): pl.pallas_call(functools.partial(out_rs_kernel, n), in_specs=[VSPEC, VSPE...  33.6 us
    pallas_call x1, Pallas kernels, feed_grads(): pl.pallas_call(functools.partial(feed_kernel, n), in_specs=[VSPEC] * 2 +...  32.3 us
  transfers between devices with their start and end apart: 5, of which 1 were waited for; matrix products, arithmetic and copies ran while one was open for 3% of the time, Pallas kernels for 47%

profile of v6, /device:TPU:0, one launch (start us, length us, event | category | flops | bytes accessed | tf_op | source)
XLA Modules:
  0.0 482.5 jit_solution(12912453078703154985)
XLA Ops:
  7.2 0.0 reduce-scatter.6.cloned.1.call-start
  7.3 0.1 mul.33
  7.4 1.6 pad.4.ctx_ref
  9.0 2.8 sine_multiply_fusion
  11.8 54.4 %front.1 = (bf16[1024,1536]{1,0:T(8,128)(2,1)}, bf16[1024,384]{1,0:T(8,128)(2,1)}, bf16[1024,384]{1,0:T(8,128)(2,1)}, bf16[1024,384]{1,0:T(8,128)(2,1)}, bf16[10...) custom-call(bf16[1024,1536]{1,0:T(8,128)(2,1)} %bitcast.20, ...), custom_call_target="tpu_custom_call" | custom-call | flops 1000 | bytes 1000 | tf_op jit(solution)/shard_map/front/pallas_call | solution.py:377
  66.2 33.6 %out_rs.1 = (f32[256,1536]{1,0:T(8,128)}, bf16[256,1536]{1,0:T(8,128)(2,1)}) custom-call(bf16[1024,384]{1,0:T(8,128)(2,1)} %get-tuple-element.73.a_ref.at_ref.o_ref, bf16[384,1536]{1,0:T(8,128)(2,1)} %w_ref.3, bf16[1024,1536]{1,0:T(8,128)(2,1)} %bitcast.21, f32[1536]{0:T(1024)} %g2_ref.1), custom_call_target="tpu_custom_call" | custom-call | flops 1000 | bytes 1000 | tf_op jit(solution)/shard_map/out_rs/pallas_call | solution.py:415
  99.9 16.5 %cross_fwd.1 = (bf16[4,256,384]{2,1,0:T(8,128)(2,1)}, bf16[4,256,384]{2,1,0:T(8,128)(2,1)}, f32[256,1536]{1,0:T(8,128)}, bf16[256,1536]{1,0:T(8,128)(2,1)}) custom-call(bf16[256,1536]{1,0:T(8,128)(2,1)} %get-tuple-element.74.h_ref.h2_ref, f32[256,1536]{1,0:T(8,128)} %get-tuple-element.75.x_ref.after1_hbm, ...), custom_call_target="tpu_custom_call" | custom-call | flops 1000 | bytes 1000 | tf_op jit(solution)/shard_map/cross_fwd/pallas_call | solution.py:955
  116.4 74.0 %ff.1 = (bf16[4,256,1536]{2,1,0:T(8,128)(2,1)}, bf16[1024,1536]{1,0:T(8,128)(2,1)}, bf16[1024,3072]{1,0:T(8,128)(2,1)}, f32[256,1536]{1,0:T(8,128)}) custom-call(bf16[256,1536]{1,0:T(8,128)(2,1)} %get-tuple-element.79.h_in, bf16[1024,1536]{1,0:T(8,128)(2,1)} %bitcast.23, bf16[1536,1536]{1,0:T(8,128)(2,1)} %wg_hbm.1, bf16[1536,1536]{1,0:T(8,128)(2,1)} %wu_hbm.1, ...), custom_call_target="tpu_custom_call" | custom-call | flops 1000 | bytes 1000 | tf_op jit(solution)/shard_map/ff/pallas_call | solution.py:513
  190.4 11.9 %down_grads.1 = bf16[1536,1536]{1,0:T(8,128)(2,1)} custom-call(bf16[1024,1536]{1,0:T(8,128)(2,1)} %bitcast.24, bf16[1024,1536]{1,0:T(8,128)(2,1)} %get-tuple-element.81.hid_ref), custom_call_target="tpu_custom_call" | custom-call | flops 1000 | bytes 1000 | tf_op jit(solution)/shard_map/down_grads/pallas_call | solution.py:553
  202.3 0.0 reduce-scatter.6.cloned.1.call-update
  202.3 0.0 reduce-scatter.10.cloned.1.call-start
  202.4 32.3 %feed_grads.1 = (bf16[256,1536]{1,0:T(8,128)(2,1)}, bf16[1536,3072]{1,0:T(8,128)(2,1)}) custom-call(bf16[1024,1536]{1,0:T(8,128)(2,1)} %get-tuple-element.81.hid_ref, bf16[1536,1536]{1,0:T(8,128)(2,1)} %wd_ref.1, f32[256,1536]{1,0:T(8,128)} %get-tuple-element.82.after_hbm.after2_ref, bf16[1024,1536]{1,0:T(8,128)(2,1)} %bitcast.27, ...), custom_call_target="tpu_custom_call" | custom-call | flops 1000 | bytes 1000 | tf_op jit(solution)/shard_map/feed_grads/pallas_call | solution.py:612
  234.7 0.0 reduce-scatter.10.cloned.1.call-update
  234.7 0.0 reduce-scatter.8.cloned.1.call-start
  234.7 36.4 %cross_bwd.1 = (bf16[256,1536]{1,0:T(8,128)(2,1)}, bf16[4,256,384]{2,1,0:T(8,128)(2,1)}, f32[4,288,384]{2,1,0:T(8,128)}, f32[256,1536]{1,0:T(8,128)}, bf16[256,1...) custom-call(f32[256,1536]{1,0:T(8,128)} %get-tuple-element.87.dh3_ref, ...), custom_call_target="tpu_custom_call" | custom-call | flops 1000 | bytes 1000 | tf_op jit(solution)/shard_map/cross_bwd/pallas_call | solution.py:1057
  271.2 0.0 reduce-scatter.6.cloned.1.call-done
  271.2 43.1 %gather_back.1 = (bf16[4,256,1536]{2,1,0:T(8,128)(2,1)}, bf16[1024,384]{1,0:T(8,128)(2,1)}, bf16[4,768,768]{2,1,0:T(8,128)(2,1)}, bf16[1536,768]{1,0:T(8,128)(2,1)}) custom-call(bf16[256,1536]{1,0:T(8,128)(2,1)} %get-tuple-element.93.x_in, bf16[384,1536]{1,0:T(8,128)(2,1)} %w_ref.3, bf16[256,1536]{1,0:T(8,128)(2,1)} %get-tuple-element.74.h_ref.h2_ref, ...), custom_call_target="tpu_custom_call" | custom-call | flops 1000 | bytes 1000 | tf_op jit(solution)/shard_map/gather_back/pallas_call | solution.py:717
  314.3 0.0 reduce-scatter.8.cloned.1.call-update
  314.3 0.0 reduce-scatter.14.cloned.1.call-start
  314.4 45.1 %attn_bwd.1 = (bf16[1024,384]{1,0:T(8,128)(2,1)}, bf16[1024,384]{1,0:T(8,128)(2,1)}, bf16[1024,384]{1,0:T(8,128)(2,1)}, bf16[1536,1152]{1,0:T(8,128)(2,1)}, bf16[768,768]{1,0:T(8,128)(2,1)}) custom-call(bf16[1024,384]{1,0:T(8,128)(2,1)} %get-tuple-element.99.q_ref, bf16[1024,384]{1,0:T(8,128)(2,1)} %get-tuple-element.100.k_ref, ...), custom_call_target="tpu_custom_call" | custom-call | flops 1000 | bytes 1000 | tf_op jit(solution)/shard_map/attn_bwd/pallas_call | solution.py:820
  359.5 0.0 copy-start.2
  359.5 0.0 reduce-scatter.14.cloned.1.call-update
  359.5 0.0 reduce-scatter.12.cloned.1.call-start
  359.5 0.5 reduce-scatter.12.cloned.1.call-update
  360.1 0.4 copy-done.2
  360.5 1.1 convert_bitcast_fusion
  361.7 0.0 reduce-scatter.10.cloned.1.call-done
  361.7 68.0 %last.1 = (bf16[4,256,1536]{2,1,0:T(8,128)(2,1)}, f32[8,192]{1,0:T(8,128)}) custom-call(bf16[1024,384]{1,0:T(8,128)(2,1)} %get-tuple-element.108.dq_ref, bf16[1024,384]{1,0:T(8,128)(2,1)} %get-tuple-element.109.dk_ref, bf16[1024,384]{1,0:T(8,128)(2,1)} %get-tuple-element.110.dv_ref, bf16[1536,384]{1,0:T(8,128)(2,1)} %wq_ref.1, bf16[1536,384]{1,0:T(8,128)(2,1)} %wk_ref.1, ...), custom_call_target="tpu_custom_call" | custom-call | flops 1000 | bytes 1000 | tf_op jit(solution)/shard_map/last/pallas_call | solution.py:889
  429.6 0.0 copy-start
  429.7 5.6 %convert_element_type.18 = f32[4,256,1536]{2,1,0:T(8,128)} convert(bf16[4,256,1536]{2,1,0:T(8,128)(2,1)} %get-tuple-element.114) | non-fusion elementwise | flops 1572864 | bytes 9437184 | tf_op jit(solution)/shard_map/convert_element_type | solution.py:1121
  435.2 0.0 copy-done
  435.2 1.7 fusion.1
  436.9 0.0 reduce-scatter.8.cloned.1.call-done
  436.9 0.9 slice.59
  437.9 1.0 convert_element_type.20
  438.9 0.7 slice_bitcast_fusion.1
  439.6 0.0 copy-start.1
  439.6 0.0 reduce-scatter.14.cloned.1.call-done
  439.6 1.8 slice.60
  441.4 1.0 convert_element_type.21
  442.4 1.4 fusion.3
  443.8 0.7 slice_bitcast_fusion
  444.5 26.6 %reduce-scatter.12.cloned.1.call-done = bf16[192,1152]{1,0:T(8,128)(2,1)} async-done(((bf16[1536,1152]{1,0:T(8,128)(2,1)}), bf16[192,1152]{1,0:T(8,128)(2,1)}) %reduce-scatter.12.cloned.1.call-update) | async-done | bytes 442384 | tf_op jit(solution)/shard_map/reduce_scatter | solution.py:1099
  471.1 0.7 slice_bitcast_fusion.2
  471.8 2.0 fusion.2
  473.8 0.0 copy-done.1
  473.8 1.7 copy.34
  (4 shorter events, 0.0 us)
Async XLA Ops:
  7.2 264.0 %reduce-scatter.6.cloned.1.call-start = ((), (), s32[]{:S(2)}) async-start(), calls=%async_computation.5 | async-start | bytes 5308416 | tf_op jit(solution)/shard_map/reduce_scatter | solution.py:1099
  202.3 159.4 %reduce-scatter.10.cloned.1.call-start = ((), (), s32[]{:S(2)}) async-start(), calls=%async_computation.7 | async-start | bytes 10616832 | tf_op jit(solution)/shard_map/reduce_scatter | solution.py:1099
  234.7 202.2 %reduce-scatter.8.cloned.1.call-start = ((), (), s32[]{:S(2)}) async-start(), calls=%async_computation.6 | async-start | bytes 2654208 | tf_op jit(solution)/shard_map/reduce_scatter | solution.py:1099
  314.3 125.3 %reduce-scatter.14.cloned.1.call-start = ((), (), s32[]{:S(2)}) async-start(), calls=%async_computation.9 | async-start | bytes 1474560 | tf_op jit(solution)/shard_map/reduce_scatter | solution.py:1116
  359.5 1.1 copy-start.2
  359.5 111.6 %reduce-scatter.12.cloned.1.call-start = ((), (), s32[]{:S(2)}) async-start(), calls=%async_computation.8 | async-start | bytes 3981312 | tf_op jit(solution)/shard_map/reduce_scatter | solution.py:1099
  429.6 5.6 %copy-start = (bf16[192,3072]{1,0:T(8,128)(2,1)S(1)}, bf16[192,3072]{1,0:T(8,128)(2,1)}, u32[]{:S(2)}) copy-start(bf16[192,3072]{1,0:T(8,128)(2,1)} %reduce-scatter.10.cloned.1.call-done) | copy-start | bytes 3538948
  439.6 34.2 %copy-start.1 = (bf16[4,256,1536]{2,1,0:T(8,128)(2,1)S(1)}, bf16[4,256,1536]{2,1,0:T(8,128)(2,1)}, u32[]{:S(2)}) copy-start(bf16[4,256,1536]{2,1,0:T(8,128)(2,1)} %get-tuple-element.90) | copy-start | bytes 9437188
Sparse Core Ops, SparseCore 0:
  202.4 55.1 reduce-scatter.5
  259.9 97.8 reduce-scatter.9
  360.2 35.5 reduce-scatter.7
  397.9 28.1 reduce-scatter.13
  428.3 42.7 reduce-scatter.11

commit v7 on v6

--- a/solution.py
+++ b/solution.py
@@ -441,7 +441,7 @@
     h_ref[me] = h_in[...]
     for c in loads:
         c.wait()
-    tf = 256
+    tf = 512
 
     def chunk(t, store):
         rows = pl.ds(pl.multiple_of(t * C, C), C)
@@ -549,7 +549,7 @@
 def down_grads(gb, hidden):
     T, D = gb.shape
     F = hidden.shape[1]
-    tb = 256
+    tb = 512
     return pl.pallas_call(
         down_kernel,
         grid=(D // tb,),
@@ -579,7 +579,7 @@
     def part(t):
         return nn(hid_ref[pl.ds(pl.multiple_of(t * C, C), C), :], wd_ref[...])
 
-    tb, tf = 256, 512
+    tb, tf = 512, 512
 
     def tile(j, carry):
         cols = pl.ds(pl.multiple_of(j * tf, tf), tf)
@@ -732,9 +732,9 @@
     )(x, w, h2, dcq, cb, ca, dkv, ctx, attn)
 
 
-def attn_bwd_kernel(n, q_ref, k_ref, v_ref, o_ref, do_ref, lse_ref, c_ref, s_ref, h_hbm, a_hbm,
+def attn_bwd_kernel(n, q_ref, k_ref, v_ref, o_ref, do_ref, lse_ref, c_ref, s_ref, h_hbm, e_hbm, a_hbm,
                     dq_ref, dk_ref, dv_ref, gr_hbm, x_ref, dk_acc, dv_acc, kt_ref, sbuf, rbuf, ss, rs,
-                    a_ref, h_ref, lsem, gr_ref, osem):
+                    a_ref, h_ref, e_ref, lsem, gr_ref, osem):
     me = lax.axis_index("tensor")
     T, W = q_ref.shape
     G = lane_group(W)
@@ -744,7 +744,9 @@
     greet(n, me)
     shards = ShardSum(n, me, a_ref, sbuf, rbuf, ss, rs)
     shards.start(a_hbm)
-    a, h_all = Late(a_hbm, a_ref, lsem.at[0]), Late(h_hbm, h_ref, lsem.at[1])
+    a, h_all, early = (
+        Late(src, dst, lsem.at[i]) for i, (src, dst) in enumerate(((a_hbm, a_ref), (h_hbm, h_ref), (e_hbm, e_ref)))
+    )
     masks = [m.astype(BF) for m in head_masks(1, G)]
     head_rows = jnp.where(
         lax.broadcasted_iota(jnp.int32, (16, G), 0) == lax.broadcasted_iota(jnp.int32, (16, G), 1) // HEAD_DIM, 1.0, 0.0
@@ -790,6 +792,7 @@
     a()
     shards.middle()
     h_all()
+    early()
     tf = 256
 
     def leave(j):
@@ -801,6 +804,7 @@
         h = h_ref[:, rows]
         for i, g_ref in enumerate((dq_ref, dk_ref, dv_ref)):
             gr_ref[rows, i * W : (i + 1) * W] = tn(h, g_ref[...]).astype(BF)
+        gr_ref[rows, 3 * W :] = e_ref[rows, :]
         leave(j).start()
         return carry
 
@@ -810,7 +814,7 @@
         leave(j).wait()
 
 
-def attn_bwd(n, q, k, v, o, do, lse, cs, sn, h, a):
+def attn_bwd(n, q, k, v, o, do, lse, cs, sn, h, early, a):
     T, W = q.shape
     D = h.shape[1]
     G = lane_group(W)
@@ -819,18 +823,18 @@
     H = R // 2 if n == 4 else R
     return pl.pallas_call(
         functools.partial(attn_bwd_kernel, n),
-        in_specs=[VSPEC] * 8 + [ANYSPEC] * 2,
+        in_specs=[VSPEC] * 8 + [ANYSPEC] * 3,
         out_specs=[VSPEC] * 3 + [ANYSPEC, VSPEC],
-        out_shape=[sds((T, W), BF)] * 3 + [sds((D, 3 * W), BF), sds((R, N), BF)],
+        out_shape=[sds((T, W), BF)] * 3 + [sds((D, 5 * W), BF), sds((R, N), BF)],
         scratch_shapes=[pltpu.VMEM((T, G), F32), pltpu.VMEM((T, G), F32), pltpu.VMEM((G, T), BF)]
         + [pltpu.VMEM((2, H, N), BF), pltpu.VMEM((slots, H, N), BF)]
         + [pltpu.SemaphoreType.DMA((slots,))] * 2
-        + held(a, h)
-        + [pltpu.VMEM((D, 3 * W), BF), pltpu.SemaphoreType.DMA((D // 256,))],
+        + held(a, h, early)
+        + [pltpu.VMEM((D, 5 * W), BF), pltpu.SemaphoreType.DMA((D // 256,))],
         compiler_params=params(collective_id=5, has_side_effects=True),
         cost_estimate=cost(40 * T * T * W, 16 * T * W, T * T * W // HEAD_DIM),
         name="attn_bwd",
-    )(q, k, v, o, do, lse, cs, sn, h, a)
+    )(q, k, v, o, do, lse, cs, sn, h, early, a)
 
 
 def last_kernel(n, ndp, dq_ref, dk_ref, dv_ref, wq_ref, wk_ref, wv_ref, x_hbm, da_ref, g_ref, gg_in,
@@ -916,9 +920,8 @@
     lane = lax.broadcasted_iota(jnp.int32, (C, G), 1) // HEAD_DIM
     valid = lax.broadcasted_iota(jnp.int32, (C, KP), 1) < ctx
 
-    def group(g, carry):
-        t = g // per
-        cols = pl.ds(pl.multiple_of(g % per * G, G), G) if per > 1 else slice(None)
+    def group(t, j):
+        cols = slice(j * G, (j + 1) * G)
         q = nn(h_ref[...], wq_ref[t, :, cols]).astype(BF)
         q_ref[t, :, cols] = q
         k, v = kv_ref[t, :KP, cols], kv_ref[t, KP:, cols]
@@ -929,9 +932,13 @@
             o = nn(p.astype(BF), v) / jnp.sum(p, axis=-1, keepdims=True)
             out = jnp.where(lane == h, o, out)
         o_ref[t, :, cols] = out.astype(BF)
+
+    def shard(t, carry):
+        for j in range(per):
+            group(t, j)
         return carry
 
-    lax.fori_loop(0, n * per, group, 0)
+    lax.fori_loop(0, n, shard, 0)
     D = h_ref.shape[1]
     tf = 256
     wo()
@@ -1000,9 +1007,8 @@
     cb_ref[...] = da2.astype(BF)
     wo()
 
-    def group(g, carry):
-        t = g // per
-        cols = pl.ds(pl.multiple_of(g % per * G, G), G) if per > 1 else slice(None)
+    def group(t, j):
+        cols = slice(j * G, (j + 1) * G)
         do = nt(cb_ref[...], wo_ref[t, cols, :]).astype(BF)
         q, k, v = q_ref[t, :, cols], kv_ref[t, :KP, cols], kv_ref[t, KP:, cols]
         dq = jnp.zeros((C, G), F32)
@@ -1022,9 +1028,13 @@
         dq_ref[t, :, cols] = (dq * SCALE).astype(BF)
         dkv_ref[t, :KP, cols] = dk * SCALE
         dkv_ref[t, KP:, cols] = dv
+
+    def shard(t, carry):
+        for j in range(per):
+            group(t, j)
         return carry
 
-    lax.fori_loop(0, n * per, group, 0)
+    lax.fori_loop(0, n, shard, 0)
     gather.relay()
     wq()
     tf = 256
@@ -1110,8 +1120,7 @@
     )
     sb_own, down_grad = lax.optimization_barrier((sb_own, down_grad))
     sb, dattn, cross_part, early_part = gather_back(n, ndp, sb_own, wo, h2, dcq, cb, cattn, dckv, ctx_pad, attn)
-    early_grads = scatter(early_part, "dp")
-    dq, dk, dv, self_part, cross_part = attn_bwd(n, q, k, v, attn, dattn, lse, cs, sn, h1, cross_part)
+    dq, dk, dv, self_part, cross_part = attn_bwd(n, q, k, v, attn, dattn, lse, cs, sn, h1, early_part, cross_part)
     cores = [[i for i in range(ndp) if i % 2 == c] for c in range(2)]
     cross_grads = lax.psum_scatter(cross_part, "dp", scatter_dimension=0, axis_index_groups=cores, tiled=True)
     self_grads = scatter(self_part, "dp")
@@ -1121,16 +1130,14 @@
     latent_grad = latent_grad.astype(F32)
     gu_grad = gu_grad.astype(F32)
     gate_grad, up_grad, down_grad = gu_grad[:, :F], gu_grad[:, F:], down_grad.astype(F32).T
-    early_grads, gains, latent_grad, gate_grad, up_grad = lax.optimization_barrier(
-        (early_grads, gains, latent_grad, gate_grad, up_grad)
+    cross_grads, gains, latent_grad, gate_grad, up_grad = lax.optimization_barrier(
+        (cross_grads, gains, latent_grad, gate_grad, up_grad)
     )
-    early_grads = early_grads.astype(F32)
-    so_grad, kv_grads = early_grads[:, :W].T, early_grads[:, W:].reshape(2, D // ndp // 2, W)
-    cross_grads, so_grad, kv_grads = lax.optimization_barrier((cross_grads, so_grad, kv_grads))
     cross_grads = cross_grads.astype(F32)
     xq_grad, xo_grad = cross_grads[:, :W], cross_grads[:, W:].T
     self_grads, xq_grad, xo_grad = lax.optimization_barrier((self_grads, xq_grad, xo_grad))
     self_grads = self_grads.astype(F32)
+    so_grad, kv_grads = self_grads[:, 3 * W : 4 * W].T, self_grads[:, 4 * W :].reshape(2, D // ndp // 2, W)
     return (
         block_out.reshape(1, T, D),
         latent_grad.reshape(1, T, D),

time: 491 us -> 473 us (0.963)
  waiting for transfers between devices: 27.2 us -> 16.3 us
  Pallas kernels: 415 us -> 409 us
    reduce_scatter x4 -> x3, waiting for transfers between devices: 26.6 us -> 15.7 us  [scatter(): return lax.psum_scatter(a, axis, scatter_dimension=0, tiled=True)]
  transfers between devices with their start and end apart: 5 -> 4, of which waited for: 1 -> 1; matrix products, arithmetic and copies ran while one was open for 3% -> 3% of each run, Pallas kernels for 47% -> 48%
where the time goes in v7:
time: 473 us; the launch traced here: 464 us
  Pallas kernels  409 us (86%)
  waiting for transfers between devices  16.3 us (3%)
  between operations  14.1 us (3%)
  local copies, waits for them, and re-layouts  14 us (3%)
  other arithmetic  10.6 us (2%)
    pallas_call x1, Pallas kernels, ff(): pl.pallas_call(functools.partial(ff_kernel, n), in_specs=[VSPEC] + [ANYSP...  71.6 us
    pallas_call x1, Pallas kernels, last(): pl.pallas_call(functools.partial(last_kernel, n, ndp), in_specs=[VSPEC] *...  67.7 us
    pallas_call x1, Pallas kernels, front(): pl.pallas_call(functools.partial(front_kernel, n, ctx), in_specs=[ANYSPEC...  54.4 us
    pallas_call x1, Pallas kernels, attn_bwd(): pl.pallas_call(functools.partial(attn_bwd_kernel, n), in_specs=[VSPEC] *...  45.2 us
    pallas_call x1, Pallas kernels, gather_back(): pl.pallas_call(functools.partial(gather_kernel, n, ndp), in_specs=[VSPEC]...  43 us
    pallas_call x1, Pallas kernels, cross_bwd(): pl.pallas_call(functools.partial(cross_bwd_kernel, n, ctx), in_specs=[VSP...  35 us
    pallas_call x1, Pallas kernels, out_rs(): pl.pallas_call(functools.partial(out_rs_kernel, n), in_specs=[VSPEC, VSPE...  33.6 us
    pallas_call x1, Pallas kernels, feed_grads(): pl.pallas_call(functools.partial(feed_kernel, n), in_specs=[VSPEC] * 2 +...  32.3 us
  transfers between devices with their start and end apart: 4, of which 1 were waited for; matrix products, arithmetic and copies ran while one was open for 3% of the time, Pallas kernels for 48%

profile of v7, /device:TPU:0, one launch (start us, length us, event | category | flops | bytes accessed | tf_op | source)
XLA Modules:
  0.0 463.8 jit_solution(10143117376839601455)
XLA Ops:
  7.2 0.0 reduce-scatter.5.cloned.1.call-start
  7.3 0.1 mul.33
  7.4 1.6 pad.4.ctx_ref
  9.0 2.8 sine_multiply_fusion
  11.8 54.4 %front.1 = (bf16[1024,1536]{1,0:T(8,128)(2,1)}, bf16[1024,384]{1,0:T(8,128)(2,1)}, bf16[1024,384]{1,0:T(8,128)(2,1)}, bf16[1024,384]{1,0:T(8,128)(2,1)}, bf16[10...) custom-call(bf16[1024,1536]{1,0:T(8,128)(2,1)} %bitcast.15, ...), custom_call_target="tpu_custom_call" | custom-call | flops 1000 | bytes 1000 | tf_op jit(solution)/shard_map/front/pallas_call | solution.py:377
  66.2 33.6 %out_rs.1 = (f32[256,1536]{1,0:T(8,128)}, bf16[256,1536]{1,0:T(8,128)(2,1)}) custom-call(bf16[1024,384]{1,0:T(8,128)(2,1)} %get-tuple-element.70.a_ref.at_ref.o_ref, bf16[384,1536]{1,0:T(8,128)(2,1)} %w_ref.3, bf16[1024,1536]{1,0:T(8,128)(2,1)} %bitcast.16, f32[1536]{0:T(1024)} %g2_ref.1), custom_call_target="tpu_custom_call" | custom-call | flops 1000 | bytes 1000 | tf_op jit(solution)/shard_map/out_rs/pallas_call | solution.py:415
  99.8 15.4 %cross_fwd.1 = (bf16[4,256,384]{2,1,0:T(8,128)(2,1)}, bf16[4,256,384]{2,1,0:T(8,128)(2,1)}, f32[256,1536]{1,0:T(8,128)}, bf16[256,1536]{1,0:T(8,128)(2,1)}) custom-call(bf16[256,1536]{1,0:T(8,128)(2,1)} %get-tuple-element.71.h_ref.h2_ref, f32[256,1536]{1,0:T(8,128)} %get-tuple-element.72.x_ref.after1_hbm, ...), custom_call_target="tpu_custom_call" | custom-call | flops 1000 | bytes 1000 | tf_op jit(solution)/shard_map/cross_fwd/pallas_call | solution.py:962
  115.3 71.6 %ff.1 = (bf16[4,256,1536]{2,1,0:T(8,128)(2,1)}, bf16[1024,1536]{1,0:T(8,128)(2,1)}, bf16[1024,3072]{1,0:T(8,128)(2,1)}, f32[256,1536]{1,0:T(8,128)}) custom-call(bf16[256,1536]{1,0:T(8,128)(2,1)} %get-tuple-element.76.h_in, bf16[1024,1536]{1,0:T(8,128)(2,1)} %bitcast.18, bf16[1536,1536]{1,0:T(8,128)(2,1)} %wg_hbm.1, bf16[1536,1536]{1,0:T(8,128)(2,1)} %wu_hbm.1, ...), custom_call_target="tpu_custom_call" | custom-call | flops 1000 | bytes 1000 | tf_op jit(solution)/shard_map/ff/pallas_call | solution.py:513
  186.9 10.3 %down_grads.1 = bf16[1536,1536]{1,0:T(8,128)(2,1)} custom-call(bf16[1024,1536]{1,0:T(8,128)(2,1)} %bitcast.19, bf16[1024,1536]{1,0:T(8,128)(2,1)} %get-tuple-element.78.hid_ref), custom_call_target="tpu_custom_call" | custom-call | flops 1000 | bytes 1000 | tf_op jit(solution)/shard_map/down_grads/pallas_call | solution.py:553
  197.2 0.0 reduce-scatter.5.cloned.1.call-update
  197.2 0.0 reduce-scatter.9.cloned.1.call-start
  197.3 32.3 %feed_grads.1 = (bf16[256,1536]{1,0:T(8,128)(2,1)}, bf16[1536,3072]{1,0:T(8,128)(2,1)}) custom-call(bf16[1024,1536]{1,0:T(8,128)(2,1)} %get-tuple-element.78.hid_ref, bf16[1536,1536]{1,0:T(8,128)(2,1)} %wd_ref.1, f32[256,1536]{1,0:T(8,128)} %get-tuple-element.79.after_hbm.after2_ref, bf16[1024,1536]{1,0:T(8,128)(2,1)} %bitcast.22, ...), custom_call_target="tpu_custom_call" | custom-call | flops 1000 | bytes 1000 | tf_op jit(solution)/shard_map/feed_grads/pallas_call | solution.py:612
  229.6 0.0 reduce-scatter.9.cloned.1.call-update
  229.6 0.0 reduce-scatter.7.cloned.1.call-start
  229.7 35.0 %cross_bwd.1 = (bf16[256,1536]{1,0:T(8,128)(2,1)}, bf16[4,256,384]{2,1,0:T(8,128)(2,1)}, f32[4,288,384]{2,1,0:T(8,128)}, f32[256,1536]{1,0:T(8,128)}, bf16[256,1...) custom-call(f32[256,1536]{1,0:T(8,128)} %get-tuple-element.84.dh3_ref, ...), custom_call_target="tpu_custom_call" | custom-call | flops 1000 | bytes 1000 | tf_op jit(solution)/shard_map/cross_bwd/pallas_call | solution.py:1067
  264.7 0.0 reduce-scatter.5.cloned.1.call-done
  264.7 43.0 %gather_back.1 = (bf16[4,256,1536]{2,1,0:T(8,128)(2,1)}, bf16[1024,384]{1,0:T(8,128)(2,1)}, bf16[4,768,768]{2,1,0:T(8,128)(2,1)}, bf16[1536,768]{1,0:T(8,128)(2,1)}) custom-call(bf16[256,1536]{1,0:T(8,128)(2,1)} %get-tuple-element.93.x_in, bf16[384,1536]{1,0:T(8,128)(2,1)} %w_ref.3, bf16[256,1536]{1,0:T(8,128)(2,1)} %get-tuple-element.71.h_ref.h2_ref, ...), custom_call_target="tpu_custom_call" | custom-call | flops 1000 | bytes 1000 | tf_op jit(solution)/shard_map/gather_back/pallas_call | solution.py:717
  307.7 45.2 %attn_bwd.1 = (bf16[1024,384]{1,0:T(8,128)(2,1)}, bf16[1024,384]{1,0:T(8,128)(2,1)}, bf16[1024,384]{1,0:T(8,128)(2,1)}, bf16[1536,1920]{1,0:T(8,128)(2,1)}, bf16[768,768]{1,0:T(8,128)(2,1)}) custom-call(bf16[1024,384]{1,0:T(8,128)(2,1)} %get-tuple-element.88.q_ref, bf16[1024,384]{1,0:T(8,128)(2,1)} %get-tuple-element.89.k_ref, ...), custom_call_target="tpu_custom_call" | custom-call | flops 1000 | bytes 1000 | tf_op jit(solution)/shard_map/attn_bwd/pallas_call | solution.py:824
  353.0 0.0 reduce-scatter.7.cloned.1.call-update
  353.0 0.0 reduce-scatter.11.cloned.1.call-start
  353.0 0.0 copy-start.3
  353.1 0.5 reduce-scatter.11.cloned.1.call-update
  353.6 0.5 copy-done.3
  354.1 1.1 convert_bitcast_fusion
  355.3 0.0 reduce-scatter.9.cloned.1.call-done
  355.3 67.7 %last.1 = (bf16[4,256,1536]{2,1,0:T(8,128)(2,1)}, f32[8,192]{1,0:T(8,128)}) custom-call(bf16[1024,384]{1,0:T(8,128)(2,1)} %get-tuple-element.106.dq_ref, bf16[1024,384]{1,0:T(8,128)(2,1)} %get-tuple-element.107.dk_ref, bf16[1024,384]{1,0:T(8,128)(2,1)} %get-tuple-element.108.dv_ref, bf16[1536,384]{1,0:T(8,128)(2,1)} %wq_ref.1, bf16[1536,384]{1,0:T(8,128)(2,1)} %wk_ref.1, ...), custom_call_target="tpu_custom_call" | custom-call | flops 1000 | bytes 1000 | tf_op jit(solution)/shard_map/last/pallas_call | solution.py:893
  423.0 0.0 copy-start.1
  423.0 5.6 %convert_element_type.15 = f32[4,256,1536]{2,1,0:T(8,128)} convert(bf16[4,256,1536]{2,1,0:T(8,128)(2,1)} %get-tuple-element.112) | non-fusion elementwise | flops 1572864 | bytes 9437184 | tf_op jit(solution)/shard_map/convert_element_type | solution.py:1130
  428.6 0.0 copy-done.1
  428.6 1.7 fusion.1
  430.3 0.0 reduce-scatter.7.cloned.1.call-done
  430.3 1.6 slice.59
  431.9 1.0 convert_element_type.17
  432.9 1.4 fusion.4
  434.3 0.7 slice_bitcast_fusion.1
  435.0 15.7 %reduce-scatter.11.cloned.1.call-done = bf16[192,1920]{1,0:T(8,128)(2,1)} async-done(((bf16[1536,1920]{1,0:T(8,128)(2,1)}), bf16[192,1920]{1,0:T(8,128)(2,1)}) %reduce-scatter.11.cloned.1.call-update) | async-done | bytes 737296 | tf_op jit(solution)/shard_map/reduce_scatter | solution.py:1109
  450.8 0.0 copy-start
  450.8 1.7 fusion.2
  452.5 0.0 copy-start.2
  452.5 2.1 fusion.3
  454.6 0.0 copy-done
  454.6 0.1 convert_element_type.18
  454.7 0.7 slice_bitcast_fusion
  455.5 0.0 copy-done.2
  455.5 1.7 copy.34
  (4 shorter events, 0.0 us)
Async XLA Ops:
  7.2 257.6 %reduce-scatter.5.cloned.1.call-start = ((), (), s32[]{:S(2)}) async-start(), calls=%async_computation.4 | async-start | bytes 5308416 | tf_op jit(solution)/shard_map/reduce_scatter | solution.py:1109
  197.2 158.0 %reduce-scatter.9.cloned.1.call-start = ((), (), s32[]{:S(2)}) async-start(), calls=%async_computation.6 | async-start | bytes 10616832 | tf_op jit(solution)/shard_map/reduce_scatter | solution.py:1109
  229.6 200.7 %reduce-scatter.7.cloned.1.call-start = ((), (), s32[]{:S(2)}) async-start(), calls=%async_computation.5 | async-start | bytes 1474560 | tf_op jit(solution)/shard_map/reduce_scatter | solution.py:1125
  353.0 97.8 %reduce-scatter.11.cloned.1.call-start = ((), (), s32[]{:S(2)}) async-start(), calls=%async_computation.7 | async-start | bytes 6635520 | tf_op jit(solution)/shard_map/reduce_scatter | solution.py:1109
  353.0 1.1 copy-start.3
  423.0 5.6 %copy-start.1 = (bf16[192,3072]{1,0:T(8,128)(2,1)S(1)}, bf16[192,3072]{1,0:T(8,128)(2,1)}, u32[]{:S(2)}) copy-start(bf16[192,3072]{1,0:T(8,128)(2,1)} %reduce-scatter.9.cloned.1.call-done) | copy-start | bytes 3538948
  450.8 3.9 copy-start
  452.5 3.0 copy-start.2
Sparse Core Ops, SparseCore 0:
  197.3 55.1 reduce-scatter.4
  254.8 97.9 reduce-scatter.8
  355.1 27.7 reduce-scatter.6
  385.1 65.6 reduce-scatter.10

commit v8 on v7

--- a/solution.py
+++ b/solution.py
@@ -424,8 +424,8 @@
     )(a, w, x, gain)
 
 
-def ff_kernel(n, h_in, gb_hbm, wg_hbm, wu_hbm, wd_hbm, h_hbm, hid_hbm, dgu_hbm, dh_ref,
-              gb_ref, wg_ref, wu_ref, wd_ref, sbuf, rbuf, ss, rs, ss2, rs2, ls, h_ref, hid_ref, dgu_ref, osem):
+def ff_kernel(n, h_in, gb_hbm, wg_hbm, wu_hbm, wd_hbm, h_hbm, hid_hbm, dgu_hbm, dh_ref, gd_hbm,
+              gb_ref, wg_ref, wu_ref, wd_ref, sbuf, rbuf, ss, rs, ss2, rs2, ls, h_ref, hid_ref, dgu_ref, osem, gd_ref, gsem):
     me = lax.axis_index("tensor")
     C, D = h_in.shape
     F = wg_ref.shape[1]
@@ -497,6 +497,22 @@
         copies[d] = remote(sbuf.at[d - 1], rbuf.at[d - 1], ss2.at[d - 1], rs2.at[d - 1], t)
         copies[d].start()
     gather.finish()
+
+    def leave(i):
+        return pltpu.make_async_copy(rows_of(gd_ref, i, td), rows_of(gd_hbm, i, td), gsem.at[i])
+
+    td = 512
+    tg = 512 if F % 512 == 0 else 256
+
+    def down(i, carry):
+        g = gb_ref[:, pl.ds(pl.multiple_of(i * td, td), td)]
+        for j in range(F // tg):
+            cols = slice(j * tg, (j + 1) * tg)
+            gd_ref[pl.ds(pl.multiple_of(i * td, td), td), cols] = tn(g, hid_ref[:, cols]).astype(BF)
+        leave(i).start()
+        return carry
+
+    lax.fori_loop(0, D // td, down, 0)
     for d in range(1, n):
         copies[d].wait_recv()
         dh_ref[...] += rbuf[d - 1].astype(F32)
@@ -504,6 +520,8 @@
         copies[d].wait_send()
     for copy in kept:
         copy.wait()
+    for i in range(D // td):
+        leave(i).wait()
 
 
 def ff(n, h, gb, wg, wu, wd):
@@ -513,8 +531,8 @@
     return pl.pallas_call(
         functools.partial(ff_kernel, n),
         in_specs=[VSPEC] + [ANYSPEC] * 4,
-        out_specs=[ANYSPEC] * 3 + [VSPEC],
-        out_shape=[sds((n, C, D), BF), sds((T, F), BF), sds((T, 2 * F), BF), sds((C, D), F32)],
+        out_specs=[ANYSPEC] * 3 + [VSPEC, ANYSPEC],
+        out_shape=[sds((n, C, D), BF), sds((T, F), BF), sds((T, 2 * F), BF), sds((C, D), F32), sds((D, F), BF)],
         scratch_shapes=[
             pltpu.VMEM((T, D), BF),
             pltpu.VMEM((D, F), BF),
@@ -527,42 +545,12 @@
         + [pltpu.SemaphoreType.DMA((n - 1,))] * 2
         + [pltpu.SemaphoreType.DMA((4,))]
         + [pltpu.VMEM((n, C, D), BF), pltpu.VMEM((T, F), BF), pltpu.VMEM((T, 2 * F), BF)]
-        + [pltpu.SemaphoreType.DMA((n, 3))],
+        + [pltpu.SemaphoreType.DMA((n, 3))]
+        + [pltpu.VMEM((D, F), BF), pltpu.SemaphoreType.DMA((D // 512,))],
         compiler_params=params(collective_id=1, has_side_effects=True),
         cost_estimate=cost(10 * T * D * F + 3e10, 6 * D * F + 8 * T * D),
         name="ff",
     )(h, gb, wg, wu, wd)
-
-
-def down_kernel(gb_ref, hid_ref, o_ref):
-    gb = gb_ref[...]
-    tf = 512 if hid_ref.shape[1] % 512 == 0 else 256
-
-    def down(j, carry):
-        cols = pl.ds(pl.multiple_of(j * tf, tf), tf)
-        o_ref[:, cols] = tn(gb, hid_ref[:, cols]).astype(BF)
-        return carry
-
-    lax.fori_loop(0, hid_ref.shape[1] // tf, down, 0)
-
-
-def down_grads(gb, hidden):
-    T, D = gb.shape
-    F = hidden.shape[1]
-    tb = 512
-    return pl.pallas_call(
-        down_kernel,
-        grid=(D // tb,),
-        in_specs=[
-            pl.BlockSpec((T, tb), lambda i: (0, i)),
-            pl.BlockSpec(hidden.shape, lambda i: (0, 0), pipeline_mode=pl.Buffered(1)),
-        ],
-        out_specs=pl.BlockSpec((tb, F), lambda i: (i, 0)),
-        out_shape=sds((D, F), BF),
-        compiler_params=params(),
-        cost_estimate=cost(2 * T * D * F, 2 * D * F),
-        name="down_grads",
-    )(gb, hidden)
 
 
 def feed_kernel(n, hid_ref, wd_ref, after_hbm, h_hbm, dgu_hbm, out_ref, gr_hbm,
@@ -732,9 +720,9 @@
     )(x, w, h2, dcq, cb, ca, dkv, ctx, attn)
 
 
-def attn_bwd_kernel(n, q_ref, k_ref, v_ref, o_ref, do_ref, lse_ref, c_ref, s_ref, h_hbm, e_hbm, a_hbm,
-                    dq_ref, dk_ref, dv_ref, gr_hbm, x_ref, dk_acc, dv_acc, kt_ref, sbuf, rbuf, ss, rs,
-                    a_ref, h_ref, e_ref, lsem, gr_ref, osem):
+def attn_bwd_kernel(n, ndp, q_ref, k_ref, v_ref, o_ref, do_ref, lse_ref, c_ref, s_ref, h_hbm, e_hbm, a_hbm,
+                    dq_ref, dk_ref, dv_ref, gr_hbm, dk_acc, dv_acc, kt_ref, sbuf, rbuf, ss, rs,
+                    a_ref, h_ref, e_ref, lsem, gr_ref, osem, x_ref):
     me = lax.axis_index("tensor")
     T, W = q_ref.shape
     G = lane_group(W)
@@ -794,27 +782,38 @@
     h_all()
     early()
     tf = 256
+    cut = 5 * W if W % 128 == 0 else 0
 
     def leave(j):
         rows = pl.ds(pl.multiple_of(j * tf, tf), tf)
-        return pltpu.make_async_copy(gr_ref.at[rows], gr_hbm.at[rows], osem.at[j])
+        return pltpu.make_async_copy(gr_ref.at[rows, :cut], gr_hbm.at[rows, :cut], osem.at[j])
 
     def weights(j, carry):
         rows = pl.ds(pl.multiple_of(j * tf, tf), tf)
         h = h_ref[:, rows]
         for i, g_ref in enumerate((dq_ref, dk_ref, dv_ref)):
             gr_ref[rows, i * W : (i + 1) * W] = tn(h, g_ref[...]).astype(BF)
-        gr_ref[rows, 3 * W :] = e_ref[rows, :]
-        leave(j).start()
+        gr_ref[rows, 3 * W : 5 * W] = e_ref[rows, :]
+        if cut:
+            leave(j).start()
         return carry
 
     lax.fori_loop(0, gr_ref.shape[0] // tf, weights, 0)
     shards.store(x_ref)
-    for j in range(gr_ref.shape[0] // tf):
-        leave(j).wait()
-
-
-def attn_bwd(n, q, k, v, o, do, lse, cs, sn, h, early, a):
+    core = lax.axis_index("dp") % 2
+    R = gr_ref.shape[0] // ndp
+    for i in range(ndp // 2):
+        gr_ref[pl.ds(pl.multiple_of((2 * i + core) * R, 16), R), 5 * W :] = x_ref[i * R : (i + 1) * R]
+        gr_ref[pl.ds(pl.multiple_of((2 * i + 1 - core) * R, 16), R), 5 * W :] = jnp.zeros((R, 2 * W), BF)
+    final = pltpu.make_async_copy(gr_ref.at[:, cut:], gr_hbm.at[:, cut:], osem.at[gr_ref.shape[0] // tf])
+    final.start()
+    if cut:
+        for j in range(gr_ref.shape[0] // tf):
+            leave(j).wait()
+    final.wait()
+
+
+def attn_bwd(n, ndp, q, k, v, o, do, lse, cs, sn, h, early, a):
     T, W = q.shape
     D = h.shape[1]
     G = lane_group(W)
@@ -822,15 +821,15 @@
     slots = 6 if n == 4 else n - 1
     H = R // 2 if n == 4 else R
     return pl.pallas_call(
-        functools.partial(attn_bwd_kernel, n),
+        functools.partial(attn_bwd_kernel, n, ndp),
         in_specs=[VSPEC] * 8 + [ANYSPEC] * 3,
-        out_specs=[VSPEC] * 3 + [ANYSPEC, VSPEC],
-        out_shape=[sds((T, W), BF)] * 3 + [sds((D, 5 * W), BF), sds((R, N), BF)],
+        out_specs=[VSPEC] * 3 + [ANYSPEC],
+        out_shape=[sds((T, W), BF)] * 3 + [sds((D, 7 * W), BF)],
         scratch_shapes=[pltpu.VMEM((T, G), F32), pltpu.VMEM((T, G), F32), pltpu.VMEM((G, T), BF)]
         + [pltpu.VMEM((2, H, N), BF), pltpu.VMEM((slots, H, N), BF)]
         + [pltpu.SemaphoreType.DMA((slots,))] * 2
         + held(a, h, early)
-        + [pltpu.VMEM((D, 5 * W), BF), pltpu.SemaphoreType.DMA((D // 256,))],
+        + [pltpu.VMEM((D, 7 * W), BF), pltpu.SemaphoreType.DMA((D // 256 + 1,)), pltpu.VMEM((R, N), BF)],
         compiler_params=params(collective_id=5, has_side_effects=True),
         cost_estimate=cost(40 * T * T * W, 16 * T * W, T * T * W // HEAD_DIM),
         name="attn_bwd",
@@ -1102,14 +1101,12 @@
     h1, q, k, v, attn, lse, xq_all, xo_all, kv_all = front(n, ctx, x, g1, wq, wk, wv, cs, sn, xq, xo, ctx_pad, xk, xv)
     after1, h2 = out_rs(n, attn, wo, x, g2)
     cq, cattn, after2, h3_own = cross_fwd(ctx, h2, after1, xq_all, kv_all, xo_all, g3)
-    h3, hidden, dgu, dh3 = ff(n, h3_own, gb, wg, wu, wd)
+    h3, hidden, dgu, dh3, down_part = ff(n, h3_own, gb, wg, wu, wd)
     h3 = h3.reshape(T, D)
 
     def scatter(a, axis):
         return lax.psum_scatter(a, axis, scatter_dimension=0, tiled=True)
 
-    down_part = down_grads(gb, hidden)
-    down_part, dgu = lax.optimization_barrier((down_part, dgu))
     down_grad = scatter(down_part, "dp")
     out_own, gu_part = feed_grads(n, hidden, wd, after2, h3, dgu)
     dh3, gu_part = lax.optimization_barrier((dh3, gu_part))
@@ -1120,9 +1117,7 @@
     )
     sb_own, down_grad = lax.optimization_barrier((sb_own, down_grad))
     sb, dattn, cross_part, early_part = gather_back(n, ndp, sb_own, wo, h2, dcq, cb, cattn, dckv, ctx_pad, attn)
-    dq, dk, dv, self_part, cross_part = attn_bwd(n, q, k, v, attn, dattn, lse, cs, sn, h1, early_part, cross_part)
-    cores = [[i for i in range(ndp) if i % 2 == c] for c in range(2)]
-    cross_grads = lax.psum_scatter(cross_part, "dp", scatter_dimension=0, axis_index_groups=cores, tiled=True)
+    dq, dk, dv, self_part = attn_bwd(n, ndp, q, k, v, attn, dattn, lse, cs, sn, h1, early_part, cross_part)
     self_grads = scatter(self_part, "dp")
     dq, gu_grad = lax.optimization_barrier((dq, gu_grad))
     latent_grad, gains = last(n, ndp, dq, dk, dv, wq, wk, wv, x, dafter1, g1, gains)
@@ -1130,14 +1125,12 @@
     latent_grad = latent_grad.astype(F32)
     gu_grad = gu_grad.astype(F32)
     gate_grad, up_grad, down_grad = gu_grad[:, :F], gu_grad[:, F:], down_grad.astype(F32).T
-    cross_grads, gains, latent_grad, gate_grad, up_grad = lax.optimization_barrier(
-        (cross_grads, gains, latent_grad, gate_grad, up_grad)
+    self_grads, gains, latent_grad, gate_grad, up_grad, down_grad = lax.optimization_barrier(
+        (self_grads, gains, latent_grad, gate_grad, up_grad, down_grad)
     )
-    cross_grads = cross_grads.astype(F32)
-    xq_grad, xo_grad = cross_grads[:, :W], cross_grads[:, W:].T
-    self_grads, xq_grad, xo_grad = lax.optimization_barrier((self_grads, xq_grad, xo_grad))
     self_grads = self_grads.astype(F32)
-    so_grad, kv_grads = self_grads[:, 3 * W : 4 * W].T, self_grads[:, 4 * W :].reshape(2, D // ndp // 2, W)
+    so_grad, kv_grads = self_grads[:, 3 * W : 4 * W].T, self_grads[:, 4 * W : 5 * W].reshape(2, D // ndp // 2, W)
+    xq_grad, xo_grad = self_grads[:, 5 * W : 6 * W], self_grads[:, 6 * W :].T
     return (
         block_out.reshape(1, T, D),
         latent_grad.reshape(1, T, D),

time: 473 us -> 464 us (0.981)
    pallas_call x2 -> x1, Pallas kernels: 55.6 us -> 46.8 us  [attn_bwd(): pl.pallas_call(functools.partial(attn_bwd_kernel, n, ndp), in_specs=[VSPE...]
    pallas_call x1, Pallas kernels: 32.3 us -> 40.2 us  [feed_grads(): pl.pallas_call(functools.partial(feed_kernel, n), in_specs=[VSPEC] * 2 +...]
  transfers between devices with their start and end apart: 4 -> 3, of which waited for: 1 -> 1; matrix products, arithmetic and copies ran while one was open for 3% -> 2% of each run, Pallas kernels for 48% -> 51%
where the time goes in v8:
time: 464 us; the launch traced here: 456 us
  Pallas kernels  407 us (88%)
  between operations  14.3 us (3%)
  local copies, waits for them, and re-layouts  12.3 us (3%)
  waiting for transfers between devices  12.3 us (3%)
  other arithmetic  9.67 us (2%)
    pallas_call x1, Pallas kernels, ff(): pl.pallas_call(functools.partial(ff_kernel, n), in_specs=[VSPEC] + [ANYSP...  71.7 us
    pallas_call x1, Pallas kernels, last(): pl.pallas_call(functools.partial(last_kernel, n, ndp), in_specs=[VSPEC] *...  67.9 us
    pallas_call x1, Pallas kernels, front(): pl.pallas_call(functools.partial(front_kernel, n, ctx), in_specs=[ANYSPEC...  54.4 us
    pallas_call x1, Pallas kernels, attn_bwd(): pl.pallas_call(functools.partial(attn_bwd_kernel, n, ndp), in_specs=[VSPE...  46.8 us
    pallas_call x1, Pallas kernels, gather_back(): pl.pallas_call(functools.partial(gather_kernel, n, ndp), in_specs=[VSPEC]...  43 us
    pallas_call x1, Pallas kernels, feed_grads(): pl.pallas_call(functools.partial(feed_kernel, n), in_specs=[VSPEC] * 2 +...  40.2 us
    pallas_call x1, Pallas kernels, cross_bwd(): pl.pallas_call(functools.partial(cross_bwd_kernel, n, ctx), in_specs=[VSP...  33.7 us
    pallas_call x1, Pallas kernels, out_rs(): pl.pallas_call(functools.partial(out_rs_kernel, n), in_specs=[VSPEC, VSPE...  33.7 us
  transfers between devices with their start and end apart: 3, of which 1 were waited for; matrix products, arithmetic and copies ran while one was open for 2% of the time, Pallas kernels for 51%

profile of v8, /device:TPU:0, one launch (start us, length us, event | category | flops | bytes accessed | tf_op | source)
XLA Modules:
  0.0 455.5 jit_solution(704991241643695455)
XLA Ops:
  7.2 0.0 reduce-scatter.4.cloned.1.call-start
  7.3 0.1 mul.33
  7.4 1.6 pad.4.ctx_ref
  9.0 2.8 sine_multiply_fusion
  11.8 54.4 %front.1 = (bf16[1024,1536]{1,0:T(8,128)(2,1)}, bf16[1024,384]{1,0:T(8,128)(2,1)}, bf16[1024,384]{1,0:T(8,128)(2,1)}, bf16[1024,384]{1,0:T(8,128)(2,1)}, bf16[10...) custom-call(bf16[1024,1536]{1,0:T(8,128)(2,1)} %bitcast.15, ...), custom_call_target="tpu_custom_call" | custom-call | flops 1000 | bytes 1000 | tf_op jit(solution)/shard_map/front/pallas_call | solution.py:377
  66.2 33.7 %out_rs.1 = (f32[256,1536]{1,0:T(8,128)}, bf16[256,1536]{1,0:T(8,128)(2,1)}) custom-call(bf16[1024,384]{1,0:T(8,128)(2,1)} %get-tuple-element.66.a_ref.at_ref.o_ref, bf16[384,1536]{1,0:T(8,128)(2,1)} %w_ref.3, bf16[1024,1536]{1,0:T(8,128)(2,1)} %bitcast.16, f32[1536]{0:T(1024)} %g2_ref.1), custom_call_target="tpu_custom_call" | custom-call | flops 1000 | bytes 1000 | tf_op jit(solution)/shard_map/out_rs/pallas_call | solution.py:415
  99.9 15.4 %cross_fwd.1 = (bf16[4,256,384]{2,1,0:T(8,128)(2,1)}, bf16[4,256,384]{2,1,0:T(8,128)(2,1)}, f32[256,1536]{1,0:T(8,128)}, bf16[256,1536]{1,0:T(8,128)(2,1)}) custom-call(bf16[256,1536]{1,0:T(8,128)(2,1)} %get-tuple-element.67.h_ref.h2_ref, f32[256,1536]{1,0:T(8,128)} %get-tuple-element.68.x_ref.after1_hbm, ...), custom_call_target="tpu_custom_call" | custom-call | flops 1000 | bytes 1000 | tf_op jit(solution)/shard_map/cross_fwd/pallas_call | solution.py:961
  115.3 71.7 %ff.1 = (bf16[4,256,1536]{2,1,0:T(8,128)(2,1)}, bf16[1024,1536]{1,0:T(8,128)(2,1)}, bf16[1024,3072]{1,0:T(8,128)(2,1)}, f32[256,1536]{1,0:T(8,128)}, bf16[1536,1536]{1,0:T(8,128)(2,1)}) custom-call(bf16[256,1536]{1,0:T(8,128)(2,1)} %get-tuple-element.72.h_in, bf16[1024,1536]{1,0:T(8,128)(2,1)} %bitcast.18, bf16[1536,1536]{1,0:T(8,128)(2,1)} %wg_hbm.1, ...), custom_call_target="tpu_custom_call" | custom-call | flops 1000 | bytes 1000 | tf_op jit(solution)/shard_map/ff/pallas_call | solution.py:531
  187.1 0.0 reduce-scatter.4.cloned.1.call-update
  187.1 0.0 reduce-scatter.8.cloned.1.call-start
  187.2 40.2 %feed_grads.1 = (bf16[256,1536]{1,0:T(8,128)(2,1)}, bf16[1536,3072]{1,0:T(8,128)(2,1)}) custom-call(bf16[1024,1536]{1,0:T(8,128)(2,1)} %get-tuple-element.74.hid_ref, bf16[1536,1536]{1,0:T(8,128)(2,1)} %wd_ref.1, f32[256,1536]{1,0:T(8,128)} %get-tuple-element.75.after_hbm.after2_ref, bf16[1024,1536]{1,0:T(8,128)(2,1)} %bitcast.21, ...), custom_call_target="tpu_custom_call" | custom-call | flops 1000 | bytes 1000 | tf_op jit(solution)/shard_map/feed_grads/pallas_call | solution.py:600
  227.4 0.0 reduce-scatter.8.cloned.1.call-update
  227.4 0.0 reduce-scatter.6.cloned.1.call-start
  227.4 33.7 %cross_bwd.1 = (bf16[256,1536]{1,0:T(8,128)(2,1)}, bf16[4,256,384]{2,1,0:T(8,128)(2,1)}, f32[4,288,384]{2,1,0:T(8,128)}, f32[256,1536]{1,0:T(8,128)}, bf16[256,1...) custom-call(f32[256,1536]{1,0:T(8,128)} %get-tuple-element.79.dh3_ref, ...), custom_call_target="tpu_custom_call" | custom-call | flops 1000 | bytes 1000 | tf_op jit(solution)/shard_map/cross_bwd/pallas_call | solution.py:1066
  261.2 0.0 reduce-scatter.4.cloned.1.call-done
  261.2 43.0 %gather_back.1 = (bf16[4,256,1536]{2,1,0:T(8,128)(2,1)}, bf16[1024,384]{1,0:T(8,128)(2,1)}, bf16[4,768,768]{2,1,0:T(8,128)(2,1)}, bf16[1536,768]{1,0:T(8,128)(2,1)}) custom-call(bf16[256,1536]{1,0:T(8,128)(2,1)} %get-tuple-element.88.x_in, bf16[384,1536]{1,0:T(8,128)(2,1)} %w_ref.3, bf16[256,1536]{1,0:T(8,128)(2,1)} %get-tuple-element.67.h_ref.h2_ref, ...), custom_call_target="tpu_custom_call" | custom-call | flops 1000 | bytes 1000 | tf_op jit(solution)/shard_map/gather_back/pallas_call | solution.py:705
  304.2 46.8 %attn_bwd.1 = (bf16[1024,384]{1,0:T(8,128)(2,1)}, bf16[1024,384]{1,0:T(8,128)(2,1)}, bf16[1024,384]{1,0:T(8,128)(2,1)}, bf16[1536,2688]{1,0:T(8,128)(2,1)}) custom-call(bf16[1024,384]{1,0:T(8,128)(2,1)} %get-tuple-element.83.q_ref, bf16[1024,384]{1,0:T(8,128)(2,1)} %get-tuple-element.84.k_ref, bf16[1024,384]{1,0:T(8,128)(2,1)} %get-tuple-element.85.v_ref, ...), custom_call_target="tpu_custom_call" | custom-call | flops 1000 | bytes 1000 | tf_op jit(solution)/shard_map/attn_bwd/pallas_call | solution.py:823
  350.9 0.0 copy-start.3
  350.9 0.0 reduce-scatter.6.cloned.1.call-update
  351.0 1.0 copy-done.3
  352.0 1.1 convert_bitcast_fusion
  353.2 0.0 reduce-scatter.8.cloned.1.call-done
  353.2 67.9 %last.1 = (bf16[4,256,1536]{2,1,0:T(8,128)(2,1)}, f32[8,192]{1,0:T(8,128)}) custom-call(bf16[1024,384]{1,0:T(8,128)(2,1)} %get-tuple-element.101.dq_ref, bf16[1024,384]{1,0:T(8,128)(2,1)} %get-tuple-element.102.dk_ref, bf16[1024,384]{1,0:T(8,128)(2,1)} %get-tuple-element.103.dv_ref, bf16[1536,384]{1,0:T(8,128)(2,1)} %wq_ref.1, bf16[1536,384]{1,0:T(8,128)(2,1)} %wk_ref.1, ...), custom_call_target="tpu_custom_call" | custom-call | flops 1000 | bytes 1000 | tf_op jit(solution)/shard_map/last/pallas_call | solution.py:892
  421.0 0.0 copy-start.1
  421.1 5.6 %convert_element_type.12 = f32[4,256,1536]{2,1,0:T(8,128)} convert(bf16[4,256,1536]{2,1,0:T(8,128)(2,1)} %get-tuple-element.107) | non-fusion elementwise | flops 1572864 | bytes 9437184 | tf_op jit(solution)/shard_map/convert_element_type | solution.py:1125
  426.6 0.0 copy-done.1
  426.6 1.7 fusion.1
  428.3 12.3 %reduce-scatter.6.cloned.1.call-done = bf16[192,2688]{1,0:T(8,128)(2,1)} async-done(((bf16[1536,2688]{1,0:T(8,128)(2,1)}), bf16[192,2688]{1,0:T(8,128)(2,1)}) %reduce-scatter.6.cloned.1.call-update) | async-done | bytes 1032208 | tf_op jit(solution)/shard_map/reduce_scatter | solution.py:1108
  440.6 0.0 copy-start
  440.6 1.7 fusion.2
  442.3 2.2 fusion.3
  444.5 0.0 copy-done
  444.5 0.0 copy-start.2
  444.5 0.1 convert_element_type.14
  444.6 1.5 fusion.4
  446.1 0.8 slice_bitcast_fusion
  446.9 0.0 copy-done.2
  446.9 1.7 copy.34
  (4 shorter events, 0.0 us)
Async XLA Ops:
  7.2 254.0 %reduce-scatter.4.cloned.1.call-start = ((), (), s32[]{:S(2)}) async-start(), calls=%async_computation.3 | async-start | bytes 5308416 | tf_op jit(solution)/shard_map/reduce_scatter | solution.py:1108
  187.1 166.0 %reduce-scatter.8.cloned.1.call-start = ((), (), s32[]{:S(2)}) async-start(), calls=%async_computation.5 | async-start | bytes 10616832 | tf_op jit(solution)/shard_map/reduce_scatter | solution.py:1108
  227.4 213.2 %reduce-scatter.6.cloned.1.call-start = ((), (), s32[]{:S(2)}) async-start(), calls=%async_computation.4 | async-start | bytes 9289728 | tf_op jit(solution)/shard_map/reduce_scatter | solution.py:1108
  350.9 1.1 copy-start.3
  421.0 5.6 %copy-start.1 = (bf16[192,3072]{1,0:T(8,128)(2,1)S(1)}, bf16[192,3072]{1,0:T(8,128)(2,1)}, u32[]{:S(2)}) copy-start(bf16[192,3072]{1,0:T(8,128)(2,1)} %reduce-scatter.8.cloned.1.call-done) | copy-start | bytes 3538948
  440.6 3.9 copy-start
  444.5 2.4 copy-start.2
Sparse Core Ops, SparseCore 0:
  187.2 55.1 reduce-scatter.3
  244.7 97.8 reduce-scatter.7
  351.1 89.4 reduce-scatter.5

commit v9 on v8

--- a/solution.py
+++ b/solution.py
@@ -1125,8 +1125,9 @@
     latent_grad = latent_grad.astype(F32)
     gu_grad = gu_grad.astype(F32)
     gate_grad, up_grad, down_grad = gu_grad[:, :F], gu_grad[:, F:], down_grad.astype(F32).T
-    self_grads, gains, latent_grad, gate_grad, up_grad, down_grad = lax.optimization_barrier(
-        (self_grads, gains, latent_grad, gate_grad, up_grad, down_grad)
+    block_out = jnp.maximum(block_out, jnp.finfo(BF).min)
+    self_grads, gains, latent_grad, gate_grad, up_grad, down_grad, block_out = lax.optimization_barrier(
+        (self_grads, gains, latent_grad, gate_grad, up_grad, down_grad, block_out)
     )
     self_grads = self_grads.astype(F32)
     so_grad, kv_grads = self_grads[:, 3 * W : 4 * W].T, self_grads[:, 4 * W : 5 * W].reshape(2, D // ndp // 2, W)

time: 464 us -> 463 us (level)
  no operation moved by 1% of the time
where the time goes in v9:
time: 463 us; the launch traced here: 454 us
  Pallas kernels  408 us (88%)
  between operations  14.3 us (3%)
  other arithmetic  11.6 us (3%)
  local copies, waits for them, and re-layouts  11.4 us (2%)
  waiting for transfers between devices  8.86 us (2%)
    pallas_call x1, Pallas kernels, ff(): pl.pallas_call(functools.partial(ff_kernel, n), in_specs=[VSPEC] + [ANYSP...  71.7 us
    pallas_call x1, Pallas kernels, last(): pl.pallas_call(functools.partial(last_kernel, n, ndp), in_specs=[VSPEC] *...  68.6 us
    pallas_call x1, Pallas kernels, front(): pl.pallas_call(functools.partial(front_kernel, n, ctx), in_specs=[ANYSPEC...  54.4 us
    pallas_call x1, Pallas kernels, attn_bwd(): pl.pallas_call(functools.partial(attn_bwd_kernel, n, ndp), in_specs=[VSPE...  46.8 us
    pallas_call x1, Pallas kernels, gather_back(): pl.pallas_call(functools.partial(gather_kernel, n, ndp), in_specs=[VSPEC]...  43 us
    pallas_call x1, Pallas kernels, feed_grads(): pl.pallas_call(functools.partial(feed_kernel, n), in_specs=[VSPEC] * 2 +...  40.2 us
    pallas_call x1, Pallas kernels, cross_bwd(): pl.pallas_call(functools.partial(cross_bwd_kernel, n, ctx), in_specs=[VSP...  33.7 us
    pallas_call x1, Pallas kernels, out_rs(): pl.pallas_call(functools.partial(out_rs_kernel, n), in_specs=[VSPEC, VSPE...  33.7 us
  transfers between devices with their start and end apart: 3, of which 1 were waited for; matrix products, arithmetic and copies ran while one was open for 2% of the time, Pallas kernels for 51%

profile of v9, /device:TPU:0, one launch (start us, length us, event | category | flops | bytes accessed | tf_op | source)
XLA Modules:
  0.0 453.8 jit_solution(12580245953470261039)
XLA Ops:
  7.2 0.0 reduce-scatter.4.cloned.1.call-start
  7.3 0.1 mul.33
  7.4 1.6 pad.4.ctx_ref
  9.0 2.8 sine_multiply_fusion
  11.8 54.4 %front.1 = (bf16[1024,1536]{1,0:T(8,128)(2,1)}, bf16[1024,384]{1,0:T(8,128)(2,1)}, bf16[1024,384]{1,0:T(8,128)(2,1)}, bf16[1024,384]{1,0:T(8,128)(2,1)}, bf16[10...) custom-call(bf16[1024,1536]{1,0:T(8,128)(2,1)} %bitcast.15, ...), custom_call_target="tpu_custom_call" | custom-call | flops 1000 | bytes 1000 | tf_op jit(solution)/shard_map/front/pallas_call | solution.py:377
  66.2 33.7 %out_rs.1 = (f32[256,1536]{1,0:T(8,128)}, bf16[256,1536]{1,0:T(8,128)(2,1)}) custom-call(bf16[1024,384]{1,0:T(8,128)(2,1)} %get-tuple-element.70.a_ref.at_ref.o_ref, bf16[384,1536]{1,0:T(8,128)(2,1)} %w_ref.3, bf16[1024,1536]{1,0:T(8,128)(2,1)} %bitcast.16, f32[1536]{0:T(1024)} %g2_ref.1), custom_call_target="tpu_custom_call" | custom-call | flops 1000 | bytes 1000 | tf_op jit(solution)/shard_map/out_rs/pallas_call | solution.py:415
  99.9 15.4 %cross_fwd.1 = (bf16[4,256,384]{2,1,0:T(8,128)(2,1)}, bf16[4,256,384]{2,1,0:T(8,128)(2,1)}, f32[256,1536]{1,0:T(8,128)}, bf16[256,1536]{1,0:T(8,128)(2,1)}) custom-call(bf16[256,1536]{1,0:T(8,128)(2,1)} %get-tuple-element.71.h_ref.h2_ref, f32[256,1536]{1,0:T(8,128)} %get-tuple-element.72.x_ref.after1_hbm, ...), custom_call_target="tpu_custom_call" | custom-call | flops 1000 | bytes 1000 | tf_op jit(solution)/shard_map/cross_fwd/pallas_call | solution.py:961
  115.3 71.7 %ff.1 = (bf16[4,256,1536]{2,1,0:T(8,128)(2,1)}, bf16[1024,1536]{1,0:T(8,128)(2,1)}, bf16[1024,3072]{1,0:T(8,128)(2,1)}, f32[256,1536]{1,0:T(8,128)}, bf16[1536,1536]{1,0:T(8,128)(2,1)}) custom-call(bf16[256,1536]{1,0:T(8,128)(2,1)} %get-tuple-element.76.h_in, bf16[1024,1536]{1,0:T(8,128)(2,1)} %bitcast.18, bf16[1536,1536]{1,0:T(8,128)(2,1)} %wg_hbm.1, ...), custom_call_target="tpu_custom_call" | custom-call | flops 1000 | bytes 1000 | tf_op jit(solution)/shard_map/ff/pallas_call | solution.py:531
  187.1 0.0 reduce-scatter.4.cloned.1.call-update
  187.1 0.0 reduce-scatter.8.cloned.1.call-start
  187.2 40.2 %feed_grads.1 = (bf16[256,1536]{1,0:T(8,128)(2,1)}, bf16[1536,3072]{1,0:T(8,128)(2,1)}) custom-call(bf16[1024,1536]{1,0:T(8,128)(2,1)} %get-tuple-element.78.hid_ref, bf16[1536,1536]{1,0:T(8,128)(2,1)} %wd_ref.1, f32[256,1536]{1,0:T(8,128)} %get-tuple-element.79.after_hbm.after2_ref, bf16[1024,1536]{1,0:T(8,128)(2,1)} %bitcast.21, ...), custom_call_target="tpu_custom_call" | custom-call | flops 1000 | bytes 1000 | tf_op jit(solution)/shard_map/feed_grads/pallas_call | solution.py:600
  227.4 0.0 reduce-scatter.8.cloned.1.call-update
  227.4 0.0 reduce-scatter.6.cloned.1.call-start
  227.4 33.7 %cross_bwd.1 = (bf16[256,1536]{1,0:T(8,128)(2,1)}, bf16[4,256,384]{2,1,0:T(8,128)(2,1)}, f32[4,288,384]{2,1,0:T(8,128)}, f32[256,1536]{1,0:T(8,128)}, bf16[256,1...) custom-call(f32[256,1536]{1,0:T(8,128)} %get-tuple-element.83.dh3_ref, ...), custom_call_target="tpu_custom_call" | custom-call | flops 1000 | bytes 1000 | tf_op jit(solution)/shard_map/cross_bwd/pallas_call | solution.py:1066
  261.2 0.0 reduce-scatter.4.cloned.1.call-done
  261.2 43.0 %gather_back.1 = (bf16[4,256,1536]{2,1,0:T(8,128)(2,1)}, bf16[1024,384]{1,0:T(8,128)(2,1)}, bf16[4,768,768]{2,1,0:T(8,128)(2,1)}, bf16[1536,768]{1,0:T(8,128)(2,1)}) custom-call(bf16[256,1536]{1,0:T(8,128)(2,1)} %get-tuple-element.88.x_in, bf16[384,1536]{1,0:T(8,128)(2,1)} %w_ref.3, bf16[256,1536]{1,0:T(8,128)(2,1)} %get-tuple-element.71.h_ref.h2_ref, ...), custom_call_target="tpu_custom_call" | custom-call | flops 1000 | bytes 1000 | tf_op jit(solution)/shard_map/gather_back/pallas_call | solution.py:705
  304.2 46.8 %attn_bwd.1 = (bf16[1024,384]{1,0:T(8,128)(2,1)}, bf16[1024,384]{1,0:T(8,128)(2,1)}, bf16[1024,384]{1,0:T(8,128)(2,1)}, bf16[1536,2688]{1,0:T(8,128)(2,1)}) custom-call(bf16[1024,384]{1,0:T(8,128)(2,1)} %get-tuple-element.67.q_ref, bf16[1024,384]{1,0:T(8,128)(2,1)} %get-tuple-element.68.k_ref, bf16[1024,384]{1,0:T(8,128)(2,1)} %get-tuple-element.69.v_ref, ...), custom_call_target="tpu_custom_call" | custom-call | flops 1000 | bytes 1000 | tf_op jit(solution)/shard_map/attn_bwd/pallas_call | solution.py:823
  350.9 0.0 copy-start.2
  350.9 0.0 reduce-scatter.6.cloned.1.call-update
  351.0 1.9 copy-done.2
  352.8 0.0 copy-start.3
  352.8 1.9 broadcast_maximum_fusion
  354.8 0.0 copy-done.3
  354.8 1.1 convert_bitcast_fusion
  355.9 0.0 reduce-scatter.8.cloned.1.call-done
  355.9 68.6 %last.1 = (bf16[4,256,1536]{2,1,0:T(8,128)(2,1)}, f32[8,192]{1,0:T(8,128)}) custom-call(bf16[1024,384]{1,0:T(8,128)(2,1)} %get-tuple-element.101.dq_ref, bf16[1024,384]{1,0:T(8,128)(2,1)} %get-tuple-element.102.dk_ref, bf16[1024,384]{1,0:T(8,128)(2,1)} %get-tuple-element.103.dv_ref, bf16[1536,384]{1,0:T(8,128)(2,1)} %wq_ref.1, bf16[1536,384]{1,0:T(8,128)(2,1)} %wk_ref.1, ...), custom_call_target="tpu_custom_call" | custom-call | flops 1000 | bytes 1000 | tf_op jit(solution)/shard_map/last/pallas_call | solution.py:892
  424.5 0.0 copy-start.1
  424.6 5.6 %convert_element_type.12 = f32[4,256,1536]{2,1,0:T(8,128)} convert(bf16[4,256,1536]{2,1,0:T(8,128)(2,1)} %get-tuple-element.107) | non-fusion elementwise | flops 1572864 | bytes 9437184 | tf_op jit(solution)/shard_map/convert_element_type | solution.py:1125
  430.1 0.0 copy-done.1
  430.1 1.7 fusion.1
  431.8 8.8 %reduce-scatter.6.cloned.1.call-done = bf16[192,2688]{1,0:T(8,128)(2,1)} async-done(((bf16[1536,2688]{1,0:T(8,128)(2,1)}), bf16[192,2688]{1,0:T(8,128)(2,1)}) %reduce-scatter.6.cloned.1.call-update) | async-done | bytes 1032208 | tf_op jit(solution)/shard_map/reduce_scatter | solution.py:1108
  440.6 0.0 copy-start
  440.6 1.7 fusion.2
  442.3 2.2 fusion.3
  444.5 0.0 copy-done
  444.5 0.1 convert_element_type.14
  444.6 1.4 fusion.4
  446.0 0.8 slice_bitcast_fusion
  (4 shorter events, 0.0 us)
Async XLA Ops:
  7.2 254.0 %reduce-scatter.4.cloned.1.call-start = ((), (), s32[]{:S(2)}) async-start(), calls=%async_computation.3 | async-start | bytes 5308416 | tf_op jit(solution)/shard_map/reduce_scatter | solution.py:1108
  187.1 168.8 %reduce-scatter.8.cloned.1.call-start = ((), (), s32[]{:S(2)}) async-start(), calls=%async_computation.5 | async-start | bytes 10616832 | tf_op jit(solution)/shard_map/reduce_scatter | solution.py:1108
  227.4 213.2 %reduce-scatter.6.cloned.1.call-start = ((), (), s32[]{:S(2)}) async-start(), calls=%async_computation.4 | async-start | bytes 9289728 | tf_op jit(solution)/shard_map/reduce_scatter | solution.py:1108
  350.9 1.9 copy-start.2
  352.8 1.9 copy-start.3
  424.5 5.6 %copy-start.1 = (bf16[192,3072]{1,0:T(8,128)(2,1)S(1)}, bf16[192,3072]{1,0:T(8,128)(2,1)}, u32[]{:S(2)}) copy-start(bf16[192,3072]{1,0:T(8,128)(2,1)} %reduce-scatter.8.cloned.1.call-done) | copy-start | bytes 3538948
  440.6 3.9 copy-start
Sparse Core Ops, SparseCore 0:
  187.2 55.1 reduce-scatter.3
  244.7 97.8 reduce-scatter.7
  351.1 89.4 reduce-scatter.5
